TPU v7x, 32 devices: a whole 2x2x4 slice. The times are simulated.
32 devices in a mesh: grp: 4 (over y, x), ctx: 8 (over z, core).
Axes of the slice: x: 2, y: 2, z: 4, core: 2. Of those that a mesh axis runs over, the one named last changes fastest.
Arguments:
- layer_input: bfloat16 [8192, 768], P(('grp', 'ctx')), may hold values from -6 to 6
- block_table: int32 [4, 16], P('grp'), may hold values from 0 to 15, each once within a row
- ln1_gain: bfloat16 [768], replicated, may hold values from 0.5 to 1.5
- ln1_bias: bfloat16 [768], replicated, may hold values from -2 to 2
- ln2_gain: bfloat16 [768], replicated, may hold values from 0.5 to 1.5
- ln2_bias: bfloat16 [768], replicated, may hold values from -2 to 2
- w_query: bfloat16 [768, 768], replicated, may hold values from -0.21875 to 0.21875
- w_keyval: bfloat16 [768, 128], replicated, may hold values from -0.21875 to 0.21875
- w_out: bfloat16 [768, 768], replicated, may hold values from -3.5 to 3.5
- w_up: bfloat16 [768, 3072], replicated, may hold values from -0.21875 to 0.21875
- w_down: bfloat16 [3072, 768], replicated, may hold values from -0.109375 to 0.109375
- cotangent: bfloat16 [8192, 768], P(('grp', 'ctx')), may hold values from -6 to 6
Outputs:
- layer_output: bfloat16 [8192, 768], P(('grp', 'ctx'))
- in_grad: float32 [8192, 768], P(('grp', 'ctx'))
- grad_ln1_gain: float32 [768], P('ctx')
- grad_ln1_bias: float32 [768], P('ctx')
- grad_ln2_gain: float32 [768], P('ctx')
- grad_ln2_bias: float32 [768], P('ctx')
- grad_w_query: float32 [768, 768], P('ctx')
- grad_w_keyval: float32 [768, 128], P('ctx')
- grad_w_out: float32 [768, 768], P('ctx')
- grad_w_up: float32 [768, 3072], P('ctx')
- grad_w_down: float32 [3072, 768], P('ctx')
Inputs may be any that keep to these rules, and one draw needn't show every extreme that they name: Each row of block_table names every block of 0 to 15 once.
All inputs are finite; a program needn't handle non-finite values.
Results may differ from a plain program's by a relative error of at most 0.012.
Values may be sent and summed in bfloat16 or wider, within the bound.
No kernel may reach another device: no remote copies, remote signals or barrier semaphores. Data moves between devices by JAX's collectives and lax.ppermute only.
A program may use at most 192 MiB of HBM per device.

v0:
```python
import jax
import jax.numpy as jnp
from jax import lax
from jax.sharding import PartitionSpec as P

ROT = 16
BLK = 128
CONT = 1024


EPS = 1e-05
key_span = 2048


def token_meta(canon, group_len):
    prompt_len = group_len // 2
    cont_span = min(CONT, prompt_len)
    after = canon - prompt_len
    segment = jnp.where(canon < prompt_len, 0, 1 + after // cont_span)
    position = jnp.where(canon < prompt_len, canon, prompt_len + after % cont_span)
    return (segment, position)


def rope_tables(position):
    half = ROT // 2
    inverse = 10000.0 ** (-(2.0 * jnp.arange(half, dtype=jnp.float32)) / ROT)
    angles = position.astype(jnp.float32)[:, None] * inverse[None, :]
    return (jnp.cos(angles), jnp.sin(angles))


def rotate(values, cosine, sine):
    half = ROT // 2
    first = values[..., :half]
    second = values[..., half:ROT]
    cos_b = cosine[:, None, :]
    sin_b = sine[:, None, :]
    return jnp.concatenate(
        [first * cos_b - second * sin_b, second * cos_b + first * sin_b, values[..., ROT:]], -1
    )


def rotate_back(values, cosine, sine):
    half = ROT // 2
    first = values[..., :half]
    second = values[..., half:ROT]
    cos_b = cosine[:, None, :]
    sin_b = sine[:, None, :]
    return jnp.concatenate(
        [first * cos_b + second * sin_b, second * cos_b - first * sin_b, values[..., ROT:]], -1
    )


def layer_norm(values, gain, bias):
    center = jnp.mean(values, -1, keepdims=True)
    shifted = values - center
    spread = jnp.mean(shifted * shifted, -1, keepdims=True)
    scale = lax.rsqrt(spread + EPS)
    normed = shifted * scale
    return (normed * gain + bias, normed, scale)


def norm_back(grad_h, normed, scale, gain):
    grad_hat = grad_h * gain
    first = jnp.mean(grad_hat, -1, keepdims=True)
    second = jnp.mean(grad_hat * normed, -1, keepdims=True)
    grad_x = scale * (grad_hat - first - normed * second)
    return (grad_x, jnp.sum(grad_h * normed, 0), jnp.sum(grad_h, 0))


def times_right(left, right):
    return lax.dot_general(
        left, right, (((1,), (1,)), ((), ())), preferred_element_type=jnp.float32
    )


def rows_summed(left, right):
    return lax.dot_general(
        left, right, (((0,), (0,)), ((), ())), preferred_element_type=jnp.float32
    )


def over_blocks(step, carry, piece, start):
    total = piece.shape[0]
    count = total // key_span
    parts = piece.reshape(count, key_span, piece.shape[1])
    starts = start + jnp.arange(count, dtype=jnp.int32) * key_span

    def advance(state, member):
        return (step(state, member[0], member[1]), None)

    result, unused = lax.scan(advance, carry, (parts, starts))
    return result


def shards(
    layer_input,
    block_table,
    ln1_gain,
    ln1_bias,
    ln2_gain,
    ln2_bias,
    w_query,
    w_keyval,
    w_out,
    w_up,
    w_down,
    cotangent,
):
    rows, width = layer_input.shape
    head_size = w_keyval.shape[1] // 2
    heads = width // head_size
    group_len = block_table.shape[1] * BLK
    device = lax.axis_index("ctx")
    per_device = rows // BLK
    offsets = jnp.arange(BLK, dtype=jnp.int32)
    own_blocks = lax.dynamic_slice_in_dim(block_table[0], device * per_device, per_device)
    query_seg, query_pos = token_meta(
        (own_blocks[:, None] * BLK + offsets[None, :]).reshape(rows), group_len
    )
    key_seg, key_pos = token_meta(
        (block_table[0][:, None] * BLK + offsets[None, :]).reshape(group_len), group_len
    )
    cosine, sine = rope_tables(query_pos)
    x_full = layer_input.astype(jnp.float32)
    gain_one = ln1_gain.astype(jnp.float32)
    gain_two = ln2_gain.astype(jnp.float32)
    normed_one, hat_one, scale_one = layer_norm(x_full, gain_one, ln1_bias.astype(jnp.float32))
    normed_two, hat_two, scale_two = layer_norm(x_full, gain_two, ln2_bias.astype(jnp.float32))
    h_one = normed_one.astype(jnp.bfloat16)
    h_two = normed_two.astype(jnp.bfloat16)
    q_raw = jnp.dot(h_one, w_query, preferred_element_type=jnp.float32).reshape(
        rows, heads, head_size
    )
    kv_raw = jnp.dot(h_one, w_keyval, preferred_element_type=jnp.float32)
    queries = rotate(q_raw, cosine, sine).astype(jnp.bfloat16)
    key_rot = rotate(kv_raw[:, None, :head_size], cosine, sine)[:, 0, :]
    kv_low = jnp.concatenate([key_rot, kv_raw[:, head_size:]], -1).astype(jnp.bfloat16)
    up_val = jnp.dot(h_two, w_up, preferred_element_type=jnp.float32)
    act = jax.nn.gelu(up_val, approximate=False).astype(jnp.bfloat16)
    ffn_out = jnp.dot(act, w_down, preferred_element_type=jnp.float32)

    def block_scores(kv_block, block_start):
        size = kv_block.shape[0]
        seg_block = lax.dynamic_slice_in_dim(key_seg, block_start, size)
        pos_block = lax.dynamic_slice_in_dim(key_pos, block_start, size)
        visible = ((seg_block[None, :] == 0) | (seg_block[None, :] == query_seg[:, None])) & (
            pos_block[None, :] <= query_pos[:, None]
        )
        scores = (
            jnp.einsum(
                "rhd,bd->hrb", queries, kv_block[:, :head_size], preferred_element_type=jnp.float32
            )
            * 0.125
        )
        return (scores, visible[None])

    def stats_step(state, kv_block, block_start):
        running, totals = state
        scores, visible = block_scores(kv_block, block_start)
        newest = jnp.maximum(running, jnp.max(jnp.where(visible, scores, -1e30), -1))
        terms = jnp.where(visible, jnp.exp(scores - newest[..., None]), 0.0)
        return (newest, totals * jnp.exp(running - newest) + jnp.sum(terms, -1))

    stats_init = (
        jnp.full((heads, rows), -1e30, jnp.float32),
        jnp.zeros((heads, rows), jnp.float32),
    )
    kv_all = lax.all_gather(kv_low, "ctx", axis=0, tiled=True)
    running, totals = over_blocks(stats_step, stats_init, kv_all, 0)
    log_total = running + jnp.log(totals)

    def mix_step(accum, kv_block, block_start):
        scores, visible = block_scores(kv_block, block_start)
        chance = jnp.where(visible, jnp.exp(scores - log_total[..., None]), 0.0).astype(
            jnp.bfloat16
        )
        return accum + jnp.einsum(
            "hrb,bd->rhd", chance, kv_block[:, head_size:], preferred_element_type=jnp.float32
        )

    mix_init = jnp.zeros((rows, heads, head_size), jnp.float32)
    mixed_full = over_blocks(mix_step, mix_init, kv_all, 0)
    mixed = mixed_full.reshape(rows, width).astype(jnp.bfloat16)
    attn_out = jnp.dot(mixed, w_out, preferred_element_type=jnp.float32)
    layer_output = (x_full + attn_out + ffn_out).astype(jnp.bfloat16)
    grad_act = times_right(cotangent, w_down)
    grad_w_down = rows_summed(act, cotangent)
    cdf_val = 0.5 * (1.0 + lax.erf(up_val * 0.7071067811865476))
    pdf_val = jnp.exp(-0.5 * up_val * up_val) * 0.3989422804014327
    grad_up = (grad_act * (cdf_val + up_val * pdf_val)).astype(jnp.bfloat16)
    grad_w_up = rows_summed(h_two, grad_up)
    grad_h_two = times_right(grad_up, w_up)
    grad_x_two, grad_gain_two, grad_bias_two = norm_back(grad_h_two, hat_two, scale_two, gain_two)
    grad_w_out = rows_summed(mixed, cotangent)
    grad_mixed = times_right(cotangent, w_out).astype(jnp.bfloat16).reshape(rows, heads, head_size)
    delta = jnp.transpose(jnp.sum(grad_mixed.astype(jnp.float32) * mixed_full, -1))

    def back_step(state, kv_block, block_start):
        grad_query, grad_keyval = state
        size = kv_block.shape[0]
        scores, visible = block_scores(kv_block, block_start)
        chance = jnp.where(visible, jnp.exp(scores - log_total[..., None]), 0.0)
        chance_low = chance.astype(jnp.bfloat16)
        grad_values = jnp.einsum(
            "hrb,rhd->bd", chance_low, grad_mixed, preferred_element_type=jnp.float32
        )
        grad_chance = jnp.einsum(
            "rhd,bd->hrb", grad_mixed, kv_block[:, head_size:], preferred_element_type=jnp.float32
        )
        grad_scores = (chance * (grad_chance - delta[..., None])).astype(jnp.bfloat16)
        grad_query = (
            grad_query
            + jnp.einsum(
                "hrb,bd->rhd",
                grad_scores,
                kv_block[:, :head_size],
                preferred_element_type=jnp.float32,
            )
            * 0.125
        )
        grad_keys = (
            jnp.einsum("hrb,rhd->bd", grad_scores, queries, preferred_element_type=jnp.float32)
            * 0.125
        )
        current = lax.dynamic_slice_in_dim(grad_keyval, block_start, size, 0)
        updated = current + jnp.concatenate([grad_keys, grad_values], -1)
        return (grad_query, lax.dynamic_update_slice_in_dim(grad_keyval, updated, block_start, 0))

    back_init = (
        jnp.zeros((rows, heads, head_size), jnp.float32),
        jnp.zeros((group_len, 2 * head_size), jnp.float32),
    )
    grad_query, grad_keyval_all = over_blocks(back_step, back_init, kv_all, 0)
    grad_keyval = lax.psum_scatter(grad_keyval_all, "ctx", scatter_dimension=0, tiled=True)
    grad_key_raw = rotate_back(grad_keyval[:, None, :head_size], cosine, sine)[:, 0, :]
    keyval_low = jnp.concatenate([grad_key_raw, grad_keyval[:, head_size:]], -1).astype(
        jnp.bfloat16
    )
    query_low = rotate_back(grad_query, cosine, sine).reshape(rows, width).astype(jnp.bfloat16)
    grad_w_query = rows_summed(h_one, query_low)
    grad_w_keyval = rows_summed(h_one, keyval_low)
    grad_h_one = times_right(query_low, w_query) + times_right(keyval_low, w_keyval)
    grad_x_one, grad_gain_one, grad_bias_one = norm_back(grad_h_one, hat_one, scale_one, gain_one)
    in_grad = cotangent.astype(jnp.float32) + grad_x_one + grad_x_two
    shares_all = (
        lax.psum_scatter(grad_w_query, "ctx", scatter_dimension=0, tiled=True),
        lax.psum_scatter(grad_w_keyval, "ctx", scatter_dimension=0, tiled=True),
        lax.psum_scatter(grad_w_out, "ctx", scatter_dimension=0, tiled=True),
        lax.psum_scatter(grad_w_up, "ctx", scatter_dimension=0, tiled=True),
        lax.psum_scatter(grad_w_down, "ctx", scatter_dimension=0, tiled=True),
        lax.psum_scatter(grad_gain_one, "ctx", scatter_dimension=0, tiled=True),
        lax.psum_scatter(grad_bias_one, "ctx", scatter_dimension=0, tiled=True),
        lax.psum_scatter(grad_gain_two, "ctx", scatter_dimension=0, tiled=True),
        lax.psum_scatter(grad_bias_two, "ctx", scatter_dimension=0, tiled=True),
    )
    totals_all = (
        lax.psum(shares_all[0].astype(jnp.bfloat16), "grp").astype(jnp.float32),
        lax.psum(shares_all[1].astype(jnp.bfloat16), "grp").astype(jnp.float32),
        lax.psum(shares_all[2].astype(jnp.bfloat16), "grp").astype(jnp.float32),
        lax.psum(shares_all[3].astype(jnp.bfloat16), "grp").astype(jnp.float32),
        lax.psum(shares_all[4].astype(jnp.bfloat16), "grp").astype(jnp.float32),
        lax.psum(shares_all[5].astype(jnp.bfloat16), "grp").astype(jnp.float32),
        lax.psum(shares_all[6].astype(jnp.bfloat16), "grp").astype(jnp.float32),
        lax.psum(shares_all[7].astype(jnp.bfloat16), "grp").astype(jnp.float32),
        lax.psum(shares_all[8].astype(jnp.bfloat16), "grp").astype(jnp.float32),
    )
    (
        total_query,
        total_keyval,
        total_out,
        total_up,
        total_down,
        total_gain_one,
        total_bias_one,
        total_gain_two,
        total_bias_two,
    ) = totals_all
    return (
        layer_output,
        in_grad,
        total_gain_one,
        total_bias_one,
        total_gain_two,
        total_bias_two,
        total_query,
        total_keyval,
        total_out,
        total_up,
        total_down,
    )


def solution(mesh):
    return jax.shard_map(
        shards,
        mesh=mesh,
        in_specs=(
            P(("grp", "ctx"), None),
            P("grp", None),
            P(),
            P(),
            P(),
            P(),
            P(),
            P(),
            P(),
            P(),
            P(),
            P(("grp", "ctx"), None),
        ),
        out_specs=(
            P(("grp", "ctx"), None),
            P(("grp", "ctx"), None),
            P("ctx"),
            P("ctx"),
            P("ctx"),
            P("ctx"),
            P("ctx", None),
            P("ctx", None),
            P("ctx", None),
            P("ctx", None),
            P("ctx", None),
        ),
        check_vma=False,
    )
```

profile of v0, /device:TPU:0, one launch (start us, length us, event | category | flops | bytes accessed | tf_op | source)
XLA Modules:
  0.0 522.3 jit_solution(18059078337386753023)
XLA Ops:
  18.9 17.5 %all_gather.3 = bf16[2048,128]{0,1:T(8,128)(2,1)} all-gather(bf16[256,128]{0,1:T(8,128)(2,1)S(1)} %pad_maximum_fusion.5), channel_id=1, replica_groups=mesh['grp'=4,'ctx'=8] {'ctx'}, dimensions={0}, use_global_device_ids=true | all-gather | bytes 589824 | tf_op jit(solution)/shard_map/all_gather | solution.py:168
  37.1 2.6 compare_and_fusion
  39.7 4.8 fusion.2
  44.5 7.1 %fusion.5 = f32[12,256]{1,0:T(8,128)S(1)} fusion(f32[2048,256,12]{1,0,2:T(8,128)S(1)} %get-tuple-element.146, f32[12,256]{1,0:T(8,128)S(1)} %broadcast_maximum_fusion, pred[256,2048]{0,1:T(8,128)(4,1)} %compare_and_fusion), kind=kLoop, calls=%fused_computation.9 | loop fusion | flops 25162752 | bytes 25714688 | tf_op jit(solution)/shard_map/while/body/eval_jaxpr/reduce_sum | solution.py:162
  54.0 10.9 %multiply_reduce_fusion = (f32[256,12]{0,1:T(8,128)S(1)}, bf16[256,12,64]{0,2,1:T(8,128)(2,1)S(1)}) fusion(bf16[256,12,64]{0,2,1:T(8,128)(2,1)} %bitcast.164, f32[2048,256,12]{1,0,2:T(8,128)} %copy-done.1, f32[12,256]{1,0:T(8,128)} %log_add_fusion, pred[256,2048]{0,1:T(8,128)(4,1)} %compare_and_fusion, bf16[2048,128]{0,1:T(8,128)(2,1)} %all_gather.3), kind=kOutput, calls=%fused_computation.79 | convolution fusion | flops 831255552 | bytes 26767360 | tf_op jit(solution)/shard_map/while/body/eval_jaxpr/hrb,bd->rhd/dot_general | solution.py:177
  64.9 11.5 %convolution_bitcast_fusion = f32[2048,64]{0,1:T(8,128)} fusion(bf16[256,12,64]{0,2,1:T(8,128)(2,1)S(1)} %bitcast.165, f32[2048,256,12]{1,0,2:T(8,128)} %copy-done.1, f32[12,256]{1,0:T(8,128)S(1)} %copy-done.24, pred[256,2048]{0,1:T(8,128)(4,1)S(1)} %copy-done.5), kind=kOutput, calls=%fused_computation.39 | convolution fusion | flops 830472192 | bytes 26619904 | tf_op jit(solution)/shard_map/while/body/eval_jaxpr/hrb,rhd->bd/dot_general | solution.py:204
  76.4 17.1 %fusion.1 = bf16[12,256,2048]{1,2,0:T(8,128)(2,1)} fusion(f32[2048,256,12]{1,0,2:T(8,128)} %copy-done.1, f32[12,256]{1,0:T(8,128)S(1)} %bitcast.167, f32[12,256]{1,0:T(8,128)S(1)} %copy-done.24, pred[256,2048]{0,1:T(8,128)(4,1)S(1)} %copy-done.5, bf16[256,12,64]{0,2,1:T(8,128)(2,1)S(1)} %bitcast.166, bf16[2048,128]{0,1:T(8,128)(2,1)} %all_gather.3), kind=kOutput, calls=%fused_computation.2 | convolution fusion | flops 843055104 | bytes 38952960 | tf_op jit(solution)/shard_map/while/body/eval_jaxpr/rhd,bd->hrb/dot_general | solution.py:207
  93.5 8.5 %fusion.24 = f32[2048,64]{0,1:T(8,128)S(1)} fusion(bf16[12,256,2048]{1,2,0:T(8,128)(2,1)} %fusion.1, bf16[256,12,48]{0,2,1:T(8,128)(2,1)S(1)} %slice.136, bf16[256,12,8]{0,2,1:T(8,128)(2,1)S(1)} %get-tuple-element.133, bf16[256,12,8]{0,2,1:T(8,128)(2,1)S(1)} %get-tuple-element.132), kind=kOutput, calls=%fused_computation.41 | convolution fusion | flops 806617088 | bytes 13500416 | tf_op jit(solution)/shard_map/while/body/eval_jaxpr/hrb,rhd->bd/dot_general | solution.py:222
  103.2 6.8 %fusion.25 = f32[256,12,64]{0,2,1:T(8,128)S(1)} fusion(bf16[12,256,2048]{1,2,0:T(8,128)(2,1)} %fusion.1, bf16[2048,128]{0,1:T(8,128)(2,1)S(1)} %copy-done.9), kind=kOutput, calls=%fused_computation.44 | convolution fusion | flops 805502976 | bytes 13631488 | tf_op jit(solution)/shard_map/while/body/eval_jaxpr/hrb,bd->rhd/dot_general | solution.py:213
  114.3 10.8 %fusion.12 = (bf16[256,3072]{1,0:T(8,128)(2,1)}, f32[256,3072]{1,0:T(8,128)S(1)}) fusion(bf16[768,3072]{1,0:T(8,128)(2,1)} %param.21, bf16[256,768]{1,0:T(8,128)(2,1)S(1)} %copy-done.2, f32[768]{0:T(1024)S(1)} %convert_element_type.132, f32[768]{0:T(1024)S(1)} %convert_element_type.131, f32[256]{0:T(256)S(1)} %copy-done.23, f32[256]{0:T(256)S(1)} %copy-done.21), kind=kOutput, calls=%fused_computation.19 | convolution fusion | flops 1260257280 | bytes 9838592 | tf_op jit(solution)/shard_map/dot_general | solution.py:138
  125.0 4.2 fusion.9
  130.4 5.2 fusion.88
  135.7 6.5 %fusion.100 = f32[3072,768]{1,0:T(8,128)} fusion(bf16[256,3072]{1,0:T(8,128)(2,1)} %get-tuple-element.143, bf16[256,768]{1,0:T(8,128)(2,1)S(1)} %copy-done.3), kind=kOutput, calls=%fused_computation.185 | convolution fusion | flops 1207959552 | bytes 11403264 | tf_op jit(solution)/shard_map/dot_general | solution.py:77
  148.7 4.4 fusion.95
  154.5 20.2 %reduce-scatter.9.cloned.1.call-done = f32[96,768]{1,0:T(8,128)} async-done(((f32[768,768]{1,0:T(8,128)}), f32[96,768]{1,0:T(8,128)}) %reduce-scatter.9.cloned.1.call-update) | async-done | bytes 294928 | tf_op jit(solution)/shard_map/reduce_scatter | solution.py:246
  176.3 36.6 %reduce-scatter.13.cloned.1.call-done = f32[96,768]{1,0:T(8,128)} async-done(((f32[768,768]{1,0:T(8,128)}), f32[96,768]{1,0:T(8,128)}) %reduce-scatter.13.cloned.1.call-update) | async-done | bytes 294928 | tf_op jit(solution)/shard_map/reduce_scatter | solution.py:248
  214.5 98.9 %reduce-scatter.15.cloned.1.call-done = f32[96,3072]{1,0:T(8,128)} async-done(((f32[768,3072]{1,0:T(8,128)}), f32[96,3072]{1,0:T(8,128)}) %reduce-scatter.15.cloned.1.call-update) | async-done | bytes 1179664 | tf_op jit(solution)/shard_map/reduce_scatter | solution.py:249
  315.6 98.0 %reduce-scatter.17.cloned.1.call-done = f32[384,768]{1,0:T(8,128)} async-done(((f32[3072,768]{1,0:T(8,128)}), f32[384,768]{1,0:T(8,128)}) %reduce-scatter.17.cloned.1.call-update) | async-done | bytes 1179664 | tf_op jit(solution)/shard_map/reduce_scatter | solution.py:250
  415.7 4.3 fusion.97
  421.6 25.9 %all-reduce.4 = (bf16[768]{0:T(1024)(128)(2,1)S(1)}, bf16[768]{0:T(1024)(128)(2,1)S(1)}, bf16[768]{0:T(1024)(128)(2,1)S(1)}, bf16[768]{0:T(1024)(128)(2,1)S(1)}) all-reduce(f32[768]{0:T(1024)S(1)} %get-tuple-element.79, f32[768]{0:T(1024)S(1)} %get-tuple-element.96, ...), channel_id=3, replica_groups=mesh['grp'=4,'ctx'=8] {'ctx'}, use_global_device_ids=true, to_apply=%region_11.12.clone | all-reduce | flops 3072 | bytes 18432
  447.9 2.5 fusion.46
  451.2 17.3 %all-reduce.5 = (bf16[96]{0:T(256)(128)(2,1)S(1)}, bf16[96]{0:T(256)(128)(2,1)S(1)}, bf16[96]{0:T(256)(128)(2,1)S(1)}, bf16[96]{0:T(256)(128)(2,1)S(1)}, bf16[96,128]{1,0:T(8,128)(2,1)S(1)}) all-reduce(bf16[96]{0:T(256)(128)(2,1)S(1)} %dynamic-slice.17, ...), channel_id=1, replica_groups=mesh['grp'=4,'ctx'=8] {'grp'}, use_global_device_ids=true, to_apply=%region_12.13 | all-reduce | flops 12672 | bytes 50688 | tf_op jit(solution)/shard_map/psum | solution.py:262
  471.1 36.7 %all-reduce.9.cloned.1.call-done = (bf16[96,768]{1,0:T(8,128)(2,1)}, bf16[96,768]{1,0:T(8,128)(2,1)}, bf16[96,3072]{1,0:T(8,128)(2,1)}, bf16[384,768]{1,0:T(8,128)(2,1)}) async-done(((bf16[96,768]{1,0:T(8,128)(2,1)}, bf16[96,768]{1,0:T(8,128)(2,1)}, bf16[96,3072]{1,0:T(8,128)(2,1)}, bf16[384,768]{1,0:T(8,128)(2,1)}), (bf16[96,768]{1,0:T(8,128)(2,1)}, bf16[96,768]{1,0:T(8,128)(2,1)}, ...) | async-done | bytes 1474576 | tf_op jit(solution)/shard_map/psum | solution.py:257
  511.1 2.2 convert_element_type.157
  (145 shorter events, 46.5 us)
Async XLA Ops:
  7.2 29.2 %copy-start = (bf16[768,768]{1,0:T(8,128)(2,1)S(1)}, bf16[768,768]{1,0:T(8,128)(2,1)}, u32[]{:S(2)}) copy-start(bf16[768,768]{1,0:T(8,128)(2,1)} %param.18) | copy-start | bytes 3538948
  7.2 138.3 %reduce-scatter.7.cloned.1.call-start = ((), (), s32[]{:S(2)}) async-start(), calls=%async_computation.6 | async-start | bytes 1179648 | tf_op jit(solution)/shard_map/reduce_scatter | solution.py:234
  7.3 8.2 %copy-start.27 = (f32[8]{0:T(128)}, f32[8]{0:T(128)S(1)}, u32[]{:S(2)}) copy-start(f32[8]{0:T(128)S(1)} %multiply_power_fusion) | copy-start | bytes 100
  44.5 8.9 %copy-start.1 = (f32[2048,256,12]{1,0,2:T(8,128)}, f32[2048,256,12]{1,0,2:T(8,128)S(1)}, u32[]{:S(2)}) copy-start(f32[2048,256,12]{1,0,2:T(8,128)S(1)} %get-tuple-element.146) | copy-start | bytes 75497472
  54.0 10.9 %copy-start.5 = (pred[256,2048]{0,1:T(8,128)(4,1)S(1)}, pred[256,2048]{0,1:T(8,128)(4,1)}, u32[]{:S(2)}) copy-start(pred[256,2048]{0,1:T(8,128)(4,1)} %compare_and_fusion) | copy-start | bytes 1572868
  54.0 10.9 %copy-start.12 = (bf16[256,768]{0,1:T(8,128)(2,1)S(1)}, bf16[256,768]{0,1:T(8,128)(2,1)}, u32[]{:S(2)}) copy-start(bf16[256,768]{0,1:T(8,128)(2,1)} %copy.39) | copy-start | bytes 1179652
  54.0 10.9 %copy-start.24 = (f32[12,256]{1,0:T(8,128)S(1)}, f32[12,256]{1,0:T(8,128)}, u32[]{:S(2)}) copy-start(f32[12,256]{1,0:T(8,128)} %log_add_fusion) | copy-start | bytes 36868
  64.9 47.3 %copy-start.6 = (bf16[256,12,64]{0,2,1:T(8,128)(2,1)}, bf16[256,12,64]{0,2,1:T(8,128)(2,1)S(1)}, u32[]{:S(2)}) copy-start(bf16[256,12,64]{0,2,1:T(8,128)(2,1)S(1)} %get-tuple-element.135) | copy-start | bytes 1179652
  93.5 8.5 %copy-start.11 = (f32[2048,64]{0,1:T(8,128)S(1)}, f32[2048,64]{0,1:T(8,128)}, u32[]{:S(2)}) copy-start(f32[2048,64]{0,1:T(8,128)} %convolution_bitcast_fusion) | copy-start | bytes 1572868
  103.1 71.5 %reduce-scatter.9.cloned.1.call-start = ((), (), s32[]{:S(2)}) async-start(), calls=%async_computation.7 | async-start | bytes 2654208 | tf_op jit(solution)/shard_map/reduce_scatter | solution.py:246
  112.1 100.8 %reduce-scatter.13.cloned.1.call-start = ((), (), s32[]{:S(2)}) async-start(), calls=%async_computation.9 | async-start | bytes 2654208 | tf_op jit(solution)/shard_map/reduce_scatter | solution.py:248
  114.2 199.2 %reduce-scatter.15.cloned.1.call-start = ((), (), s32[]{:S(2)}) async-start(), calls=%async_computation.10 | async-start | bytes 10616832 | tf_op jit(solution)/shard_map/reduce_scatter | solution.py:249
  135.6 277.9 %reduce-scatter.17.cloned.1.call-start = ((), (), s32[]{:S(2)}) async-start(), calls=%async_computation.11 | async-start | bytes 10616832 | tf_op jit(solution)/shard_map/reduce_scatter | solution.py:250
  142.2 5.0 copy-start.26
  142.2 5.0 copy-start.28
  142.2 308.2 %reduce-scatter.11.cloned.1.call-start = ((), (), s32[]{:S(2)}) async-start(), calls=%async_computation.8 | async-start | bytes 442368 | tf_op jit(solution)/shard_map/reduce_scatter | solution.py:247
  148.4 4.8 copy-start.4
  148.4 4.7 copy-start.7
  148.4 359.4 %all-reduce.9.cloned.1.call-start = ((), (), s32[]{:S(2)}) async-start(), calls=%async_computation.12 | async-start | bytes 2949120 | tf_op jit(solution)/shard_map/psum | solution.py:257
  415.7 4.4 copy-start.10
  415.7 4.4 copy-start.13
  415.7 4.4 copy-start.15
  415.7 4.4 copy-start.17
  415.7 4.4 copy-start.19
  (15 other events, 23.4 us)
Sparse Core Ops, SparseCore 0:
  103.2 33.7 reduce-scatter.6
  139.3 35.2 reduce-scatter.8
  177.0 35.9 reduce-scatter.12
  215.1 98.3 reduce-scatter.14
  315.6 97.9 reduce-scatter.16
  415.6 29.4 reduce-scatter.10
  449.7 58.0 all-reduce.8
where the time goes:
time: 524 us; the launch traced here: 522 us
  waiting for transfers between devices  290 us (55%)
  matrix products  108 us (21%)
  blocking collectives  60.8 us (12%)
  other arithmetic  39.8 us (8%)
  between operations  15.4 us (3%)
  local copies, waits for them, and re-layouts  7.6 us (1%)
    reduce_scatter x1, waiting for transfers between devices, shards(): lax.psum_scatter(grad_w_up, 'ctx', scatter_dimension=0, tiled=True)  98.9 us
    reduce_scatter x1, waiting for transfers between devices, shards(): lax.psum_scatter(grad_w_down, 'ctx', scatter_dimension=0, tiled=True)  98 us
    psum x1, waiting for transfers between devices, shards(): lax.psum(shares_all[0].astype(jnp.bfloat16), 'grp').astype(jnp.float32)  36.7 us
    reduce_scatter x1, waiting for transfers between devices, shards(): lax.psum_scatter(grad_w_out, 'ctx', scatter_dimension=0, tiled=True)  36.6 us
    unnamed x1, blocking collectives  25.9 us
    reduce_scatter x1, waiting for transfers between devices, shards(): lax.psum_scatter(grad_w_query, 'ctx', scatter_dimension=0, tiled=True)  20.2 us
    all_gather x1, blocking collectives, shards(): kv_all = lax.all_gather(kv_low, 'ctx', axis=0, tiled=True)  17.5 us
    psum x1, blocking collectives, shards(): lax.psum(shares_all[5].astype(jnp.bfloat16), 'grp').astype(jnp.float32)  17.3 us
  transfers between devices with their start and end apart: 7, of which 5 were waited for; matrix products, arithmetic and copies ran while one was open for 13% of the time, Pallas kernels for 0%

commit v1 on v0

v1 whole, which is shorter than its diff:
```python
import functools

import jax
import jax.numpy as jnp
from jax import lax
from jax.experimental import pallas as pl
from jax.experimental.pallas import tpu as pltpu
from jax.sharding import PartitionSpec as P

ROT = 16
BLK = 128
CONT = 1024
TILE = 256
EPS = 1e-05
LOG2E = 1.4426950408889634
LN2 = 0.6931471805599453
BF = jnp.bfloat16
F32 = jnp.float32


def dot(left, right, dims=((1,), (0,))):
    return lax.dot_general(left, right, (dims, ((), ())), preferred_element_type=F32)


def rope_tables(position):
    half = ROT // 2
    inverse = 10000.0 ** (-(2.0 * jnp.arange(half, dtype=F32)) / ROT)
    angles = inverse[:, None] * position.astype(F32)[None, :]
    return (jnp.cos(angles), jnp.sin(angles))


def rotate_rows(values, cosine, sine):
    half = ROT // 2
    first, second = values[:, :half], values[:, half:ROT]
    cos_t, sin_t = cosine.T, sine.T
    return jnp.concatenate(
        [first * cos_t - second * sin_t, second * cos_t + first * sin_t, values[:, ROT:]], -1
    )


def attn_kernel(
    table,
    place,
    q_ref,
    do_ref,
    cos_ref,
    sin_ref,
    kv_ref,
    mix_ref,
    dq_ref,
    dkv_ref,
    kv_c,
    kv_t,
    s_scr,
    p_scr,
    rq,
    rd,
    rqt,
    rdt,
    o_acc,
    dq_acc,
    dkv_acc,
    *,
    blocks,
    heads,
    size,
):
    step, group = pl.program_id(0), pl.program_id(1)
    lanes = heads * BLK
    prompt_blocks = blocks // 2
    prompt_tiles = prompt_blocks * BLK // TILE
    cont_blocks = min(CONT, prompt_blocks * BLK) // BLK

    @pl.when((step == 0) & (group == 0))
    def _():
        ones = jnp.ones((16, BLK), BF)

        def place_block(slot, carry):
            block = table[slot]
            rows = kv_ref[pl.ds(pl.multiple_of(slot * BLK, BLK), BLK), :]
            kv_c[pl.ds(pl.multiple_of(block * BLK, BLK), BLK), :] = rows
            turned = jnp.concatenate([rows.T, ones], 0)

            @pl.when(block % 2 == 0)
            def _():
                kv_t[block // 2, :, 0:BLK] = turned

            @pl.when(block % 2 == 1)
            def _():
                kv_t[block // 2, :, BLK:TILE] = turned

            return carry

        lax.fori_loop(0, blocks, place_block, 0)
        dkv_acc[...] = jnp.zeros_like(dkv_acc)

    block = table[place[0] + step]
    last = block // 2
    in_prompt = block < prompt_blocks
    seg_tile = (prompt_blocks + (block - prompt_blocks) // cont_blocks * cont_blocks) // 2
    full = jnp.where(in_prompt, last, prompt_tiles + last - seg_tile)

    def tile_of(i):
        return jnp.where(i < prompt_tiles, jnp.minimum(i, last), i - prompt_tiles + seg_tile)

    def key_rows(tile):
        return pl.ds(pl.multiple_of(tile * TILE, TILE), TILE)

    for h in range(heads):
        rq[0:size, h * BLK : (h + 1) * BLK] = q_ref[h * size : (h + 1) * size, :]
    rq[size : 2 * size, :] = jnp.zeros((size, lanes), BF)

    def scores(tile):
        return dot(kv_c[key_rows(tile), :], rq[...])

    def fold(values):
        return jnp.max(values.reshape(TILE // 8, 8, lanes), 0)

    def first_pass(i, top):
        part = scores(tile_of(i))
        s_scr[i] = part
        return jnp.maximum(top, fold(part))

    top = lax.fori_loop(0, full, first_pass, jnp.full((8, lanes), -1e30, F32))
    part = scores(last)
    key_at = last * TILE + lax.broadcasted_iota(jnp.int32, (TILE, lanes), 0)
    row_at = block * BLK + lax.rem(lax.broadcasted_iota(jnp.int32, (TILE, lanes), 1), BLK)
    part = jnp.where(key_at <= row_at, part, -1e30)
    s_scr[full] = part
    top = jnp.max(jnp.maximum(top, fold(part)), 0, keepdims=True)

    o_acc[...] = jnp.zeros_like(o_acc)

    def second_pass(i, carry):
        p = jnp.exp2(s_scr[i] - top).astype(BF)
        p_scr[i] = p
        o_acc[...] += dot(kv_t[jnp.where(i == full, last, tile_of(i)), size : 2 * size + 16, :], p)
        return carry

    lax.fori_loop(0, full + 1, second_pass, 0)

    inverse = 1.0 / o_acc[size : size + 1, :]
    mixed = o_acc[0:size, :] * inverse
    grads = []
    for h in range(heads):
        at = slice(h * BLK, (h + 1) * BLK)
        mix_ref[h * size : (h + 1) * size, :] = mixed[:, at].astype(BF)
        grads.append(do_ref[h * size : (h + 1) * size, :])
    scaled = (jnp.concatenate(grads, 1) * inverse).astype(BF)
    delta = jnp.sum(mixed * scaled.astype(F32), 0, keepdims=True)
    rd[0:size, :] = jnp.zeros((size, lanes), BF)
    rd[size : 2 * size, :] = scaled
    rqt[...] = rq[...].T
    rdt[...] = rd[...].T
    dq_acc[...] = jnp.zeros_like(dq_acc)

    def third_pass(i, carry):
        tile = jnp.where(i == full, last, tile_of(i))
        p = p_scr[i]
        d_probs = dot(kv_c[key_rows(tile), :], rd[...])
        ds = (p.astype(F32) * (d_probs - delta)).astype(BF)
        dq_acc[...] += dot(kv_t[tile, 0:size, :], ds)
        dkv_acc[key_rows(tile), :] += dot(p, rdt[...]) + dot(ds, rqt[...])
        return carry

    lax.fori_loop(0, full + 1, third_pass, 0)

    half = ROT // 2
    cosine, sine = cos_ref[...], sin_ref[...]
    for h in range(heads):
        part = dq_acc[:, h * BLK : (h + 1) * BLK] * 0.125
        first, second = part[0:half, :], part[half:ROT, :]
        turned = jnp.concatenate(
            [first * cosine + second * sine, second * cosine - first * sine, part[ROT:, :]], 0
        )
        dq_ref[h * size : (h + 1) * size, :] = turned.astype(BF)

    @pl.when((step == pl.num_programs(0) - 1) & (group == pl.num_programs(1) - 1))
    def _():
        scale = jnp.where(
            lax.broadcasted_iota(jnp.int32, (BLK, 2 * size), 1) < size, F32(LN2), F32(1.0)
        )

        def give_block(slot, carry):
            rows = dkv_acc[pl.ds(pl.multiple_of(table[slot] * BLK, BLK), BLK), :]
            dkv_ref[pl.ds(pl.multiple_of(slot * BLK, BLK), BLK), :] = (rows * scale).astype(BF)
            return carry

        lax.fori_loop(0, blocks, give_block, 0)


def attention(table, place, q_t, do_t, cosine, sine, kv_all):
    width, rows = q_t.shape
    keys = kv_all.shape[0]
    size = kv_all.shape[1] // 2
    all_heads = width // size
    blocks = keys // BLK
    heads = all_heads if keys <= 4096 else 2
    lanes = heads * BLK
    cont = min(CONT, keys // 2)
    most = (keys // 2 + cont) // TILE
    tiles = keys // TILE
    whole = lambda *shape: pl.BlockSpec(shape, lambda i, j, *_: (0,) * len(shape))
    return pl.pallas_call(
        functools.partial(attn_kernel, blocks=blocks, heads=heads, size=size),
        out_shape=(
            jax.ShapeDtypeStruct((width, rows), BF),
            jax.ShapeDtypeStruct((width, rows), BF),
            jax.ShapeDtypeStruct((keys, 2 * size), BF),
        ),
        grid_spec=pltpu.PrefetchScalarGridSpec(
            num_scalar_prefetch=2,
            grid=(rows // BLK, all_heads // heads),
            in_specs=[
                pl.BlockSpec((heads * size, BLK), lambda i, j, *_: (j, i)),
                pl.BlockSpec((heads * size, BLK), lambda i, j, *_: (j, i)),
                pl.BlockSpec((ROT // 2, BLK), lambda i, j, *_: (0, i)),
                pl.BlockSpec((ROT // 2, BLK), lambda i, j, *_: (0, i)),
                whole(keys, 2 * size),
            ],
            out_specs=[
                pl.BlockSpec((heads * size, BLK), lambda i, j, *_: (j, i)),
                pl.BlockSpec((heads * size, BLK), lambda i, j, *_: (j, i)),
                whole(keys, 2 * size),
            ],
            scratch_shapes=[
                pltpu.VMEM((keys, 2 * size), BF),
                pltpu.VMEM((tiles, 2 * size + 16, TILE), BF),
                pltpu.VMEM((most, TILE, lanes), F32),
                pltpu.VMEM((most, TILE, lanes), BF),
                pltpu.VMEM((2 * size, lanes), BF),
                pltpu.VMEM((2 * size, lanes), BF),
                pltpu.VMEM((lanes, 2 * size), BF),
                pltpu.VMEM((lanes, 2 * size), BF),
                pltpu.VMEM((size + 16, lanes), F32),
                pltpu.VMEM((size, lanes), F32),
                pltpu.VMEM((keys, 2 * size), F32),
            ],
        ),
        compiler_params=pltpu.CompilerParams(vmem_limit_bytes=60 * 1024 * 1024),
        cost_estimate=pl.CostEstimate(
            flops=8 * width * rows * keys, bytes_accessed=4 * width * rows * 4, transcendentals=0
        ),
        name="attention",
    )(table, place, q_t, do_t, cosine, sine, kv_all)


class Links:
    def __init__(self, n_grp, n_ctx):
        self.n_grp, self.n_ctx, self.n_pair = n_grp, n_ctx, n_ctx // 2
        self.small = (n_grp, n_ctx) == (4, 8)
        self.ctx = lax.axis_index("ctx")
        self.grp = lax.axis_index("grp")
        self.core = self.ctx % 2
        self.chip = self.ctx // 2
        self.groups = [[2 * z + c for z in range(self.n_pair)] for c in range(2)]

    def swap(self, value):
        return lax.ppermute(value, "ctx", [(i, i ^ 1) for i in range(self.n_ctx)])

    def permute(self, value, target):
        pairs = []
        for g in range(self.n_grp):
            for i in range(self.n_ctx):
                y, x, z, c = target(g // 2, g % 2, i // 2, i % 2)
                pairs.append((g * self.n_ctx + i, (2 * y + x) * self.n_ctx + 2 * z + c))
        return lax.ppermute(value, ("grp", "ctx"), pairs)

    def shift(self, value, k):
        return self.permute(value, lambda y, x, z, c: (y, x, (z + k) % 4, c))

    def cross(self, value, stage):
        return self.permute(
            value, lambda y, x, z, c: (y, 1 - x, z, c) if c == stage else (1 - y, x, z, c)
        )

    def bit(self, stage):
        y, x = self.grp // 2, self.grp % 2
        return jnp.where(self.core == stage, x, y)

    def spread(self, parts):
        total = lax.dynamic_index_in_dim(parts, self.chip, 0, False).astype(F32)
        for k in range(1, 4):
            out = lax.dynamic_index_in_dim(parts, (self.chip + k) % 4, 0, False)
            total = total + self.shift(out, k).astype(F32)
        return total

    def reduce(self, parts):
        if not self.small:
            moved = lax.all_to_all(parts, "ctx", 0, 0, axis_index_groups=self.groups)
            own = jnp.sum(moved.astype(F32), 0)
            return lax.psum(own.astype(BF), "grp").astype(F32)
        for stage in range(2):
            rows = parts.shape[1] // 2
            bit = self.bit(stage)
            send = lax.dynamic_slice_in_dim(parts, (1 - bit) * rows, rows, 1)
            keep = lax.dynamic_slice_in_dim(parts, bit * rows, rows, 1)
            got = self.cross(send, stage)
            parts = (keep.astype(F32) + got.astype(F32)).astype(BF)
        own = self.spread(parts).astype(BF)
        for stage in (1, 0):
            got = self.cross(own, stage)
            low = self.bit(stage) == 0
            own = jnp.concatenate([jnp.where(low, own, got), jnp.where(low, got, own)], 0)
        return own.astype(F32)

    def reduce_few(self, parts):
        if not self.small:
            return self.reduce(parts)
        own = self.spread(parts).astype(BF)
        total = own.astype(F32)
        total = total + self.permute(own, lambda y, x, z, c: (y, 1 - x, z, c)).astype(F32)
        total = total + self.permute(own, lambda y, x, z, c: (1 - y, x, z, c)).astype(F32)
        return total + self.permute(own, lambda y, x, z, c: (1 - y, 1 - x, z, c)).astype(F32)

    def gather_pairs(self, value):
        if not self.small:
            return lax.all_gather(value, "ctx", axis=0, axis_index_groups=self.groups)
        parts = [value] + [self.shift(value, k) for k in range(1, 4)]
        stacked = jnp.stack([parts[0], parts[3], parts[2], parts[1]] * 2)
        return lax.dynamic_slice_in_dim(stacked, (4 - self.chip) % 4, 4, 0)


def column_sums(values):
    return jnp.sum(values, 0)


def shards(
    layer_input,
    block_table,
    ln1_gain,
    ln1_bias,
    ln2_gain,
    ln2_bias,
    w_query,
    w_keyval,
    w_out,
    w_up,
    w_down,
    cotangent,
    *,
    n_grp,
    n_ctx,
):
    links = Links(n_grp, n_ctx)
    core, chip, n_pair = links.core, links.chip, links.n_pair
    rows, width = layer_input.shape
    size = w_keyval.shape[1] // 2
    hidden = w_up.shape[1]
    group_len = block_table.shape[1] * BLK
    part_rows = width // n_ctx
    part_hidden = hidden // n_ctx
    half_width = width // 2
    half_hidden = hidden // 2
    pair_blocks = 2 * rows // BLK
    table = block_table[0]

    def both(own, other):
        return jnp.concatenate(
            [jnp.where(core == 0, own, other), jnp.where(core == 0, other, own)], 0
        )

    def mine(value, own_core):
        return lax.dynamic_slice_in_dim(value, own_core * rows, rows, 0)

    x_two = both(layer_input, links.swap(layer_input))
    g_two = both(cotangent, links.swap(cotangent))

    canon = (
        lax.dynamic_slice_in_dim(table, chip * pair_blocks, pair_blocks)[:, None] * BLK
        + jnp.arange(BLK, dtype=jnp.int32)[None, :]
    ).reshape(2 * rows)
    prompt_len = group_len // 2
    cont_span = min(CONT, prompt_len)
    position = jnp.where(
        canon < prompt_len, canon, prompt_len + (canon - prompt_len) % cont_span
    )
    cosine, sine = rope_tables(position)

    gain_one, gain_two = ln1_gain.astype(F32), ln2_gain.astype(F32)
    x_full = x_two.astype(F32)
    shifted = x_full - jnp.mean(x_full, -1, keepdims=True)
    scale = lax.rsqrt(jnp.mean(shifted * shifted, -1, keepdims=True) + EPS)
    hat = shifted * scale
    h_one = (hat * gain_one + ln1_bias.astype(F32)).astype(BF)
    h_two = (hat * gain_two + ln2_bias.astype(F32)).astype(BF)

    kv_raw = dot(h_one, w_keyval)
    kv_low = jnp.concatenate(
        [rotate_rows(kv_raw[:, :size], cosine, sine), kv_raw[:, size:]], -1
    ).astype(BF)
    kv_all = links.gather_pairs(kv_low).reshape(group_len, 2 * size)

    up_half = lax.dynamic_index_in_dim(
        w_up.reshape(width, n_pair, 2, part_hidden), core, 2, False
    ).reshape(width, half_hidden)
    down_half = lax.dynamic_index_in_dim(
        w_down.reshape(n_pair, 2, part_hidden, width), core, 1, False
    ).reshape(half_hidden, width)
    up_val = dot(h_two, up_half)
    cdf_val = 0.5 * (1.0 + lax.erf(up_val * 0.7071067811865476))
    pdf_val = jnp.exp(-0.5 * up_val * up_val) * 0.3989422804014327
    act = (up_val * cdf_val).astype(BF)
    grad_down = dot(act, g_two, ((0,), (0,))).astype(BF)
    total_down = links.reduce(grad_down.reshape(n_pair, part_hidden, width))
    grad_act = dot(g_two, down_half, ((1,), (1,)))
    grad_up = (grad_act * (cdf_val + up_val * pdf_val)).astype(BF)
    grad_up_w = dot(h_two, grad_up, ((0,), (0,))).astype(BF)

    def parity(value, which):
        return lax.dynamic_index_in_dim(
            value.reshape(n_pair, 2, part_rows, value.shape[-1]), which, 1, False
        )

    up_own = parity(grad_up_w, core)
    up_got = links.swap(parity(grad_up_w, 1 - core))
    up_parts = jnp.concatenate(
        [jnp.where(core == 0, up_own, up_got), jnp.where(core == 0, up_got, up_own)], -1
    )
    total_up = links.reduce(up_parts)
    total_up = (
        total_up.reshape(part_rows, 2, n_pair, part_hidden)
        .transpose(0, 2, 1, 3)
        .reshape(part_rows, hidden)
    )

    query_half = lax.dynamic_slice_in_dim(w_query, core * half_width, half_width, 1)
    out_half = lax.dynamic_slice_in_dim(w_out, core * half_width, half_width, 0)
    q_raw = dot(query_half, h_one, ((0,), (1,))).reshape(-1, size, 2 * rows) * (0.125 * LOG2E)
    half = ROT // 2
    first, second = q_raw[:, :half], q_raw[:, half:ROT]
    q_t = (
        jnp.concatenate(
            [first * cosine - second * sine, second * cosine + first * sine, q_raw[:, ROT:]], 1
        )
        .astype(BF)
        .reshape(half_width, 2 * rows)
    )
    do_t = dot(out_half, g_two, ((1,), (1,)))
    place = jnp.reshape(chip * pair_blocks, (1,)).astype(jnp.int32)
    mix_t, dq_t, dkv_part = attention(table, place, q_t, do_t, cosine, sine, kv_all)

    dkv_part = dkv_part.reshape(n_pair, 2, rows, 2 * size)
    dkv_own = lax.dynamic_index_in_dim(dkv_part, core, 1, False).astype(F32)
    dkv_got = links.swap(lax.dynamic_index_in_dim(dkv_part, 1 - core, 1, False)).astype(F32)
    dkv_sum = (dkv_own + dkv_got).astype(BF)
    if links.small:
        dkv = links.spread(dkv_sum)
    else:
        dkv = jnp.sum(
            lax.all_to_all(dkv_sum, "ctx", 0, 0, axis_index_groups=links.groups).astype(F32), 0
        )
    cos_own = lax.dynamic_slice_in_dim(cosine, core * rows, rows, 1)
    sin_own = lax.dynamic_slice_in_dim(sine, core * rows, rows, 1)
    dkv_low = jnp.concatenate(
        [rotate_rows(dkv[:, :size], cos_own, -sin_own), dkv[:, size:]], -1
    ).astype(BF)

    grad_q_w = dot(h_one, dq_t, ((0,), (1,))).astype(BF)
    grad_out_w = dot(mix_t, g_two).astype(BF)
    out_parts = grad_out_w.reshape(n_pair // 2, 2, part_rows, width)

    def pack(which):
        rows_out = lax.dynamic_index_in_dim(out_parts, which, 1, False)
        rows_out = rows_out.reshape(n_pair // 2, part_rows, 2, half_width).transpose(0, 2, 1, 3)
        return jnp.concatenate(
            [parity(grad_q_w, which), rows_out.reshape(n_pair, part_rows, half_width)], -1
        )

    own, got = pack(core), links.swap(pack(1 - core))
    low = jnp.where(core == 0, own, got)
    high = jnp.where(core == 0, got, own)
    query_parts = jnp.concatenate([low[..., :half_width], high[..., :half_width]], -1)

    def unpack(value):
        value = value[..., half_width:].reshape(n_pair // 2, 2, part_rows, half_width)
        return value.transpose(0, 2, 1, 3).reshape(n_pair // 2, part_rows, width)

    late_parts = jnp.concatenate(
        [query_parts, jnp.concatenate([unpack(low), unpack(high)], 0)], -1
    )
    total_late = links.reduce(late_parts)

    out_part = dot(act, down_half) + dot(mix_t, out_half, ((0,), (0,)))
    out_got = links.swap(mine(out_part, 1 - core).astype(BF))
    layer_output = (
        layer_input.astype(F32) + mine(out_part, core) + out_got.astype(F32)
    ).astype(BF)

    d_two = dot(grad_up, up_half, ((1,), (1,)))
    d_one = dot(dq_t, query_half, ((0,), (1,)))
    d_kv = dot(dkv_low, w_keyval, ((1,), (1,)))
    row_core = lax.broadcasted_iota(jnp.int32, (2 * rows, 1), 0) // rows
    d_one = d_one + jnp.where(row_core == core, jnp.concatenate([d_kv, d_kv], 0), 0.0)
    sums = jnp.stack(
        [column_sums(d_one * hat), column_sums(d_one), column_sums(d_two * hat), column_sums(d_two)]
    )
    d_hat = d_one * gain_one + d_two * gain_two
    hat_got = links.swap(mine(d_hat, 1 - core).astype(BF))
    d_hat = mine(d_hat, core) + hat_got.astype(F32)
    hat_own = mine(hat, core)
    in_grad = cotangent.astype(F32) + mine(scale, core) * (
        d_hat
        - jnp.mean(d_hat, -1, keepdims=True)
        - hat_own * jnp.mean(d_hat * hat_own, -1, keepdims=True)
    )

    grad_kv_w = dot(mine(h_one, core), dkv_low, ((0,), (0,)))
    sum_rows = sums.reshape(4, n_pair, 2, part_rows).transpose(1, 2, 0, 3)
    sum_rows = jnp.pad(sum_rows, ((0, 0), (0, 0), (0, 12), (0, 2 * size - part_rows)))
    few = jnp.concatenate([grad_kv_w.reshape(n_pair, 2, part_rows, 2 * size), sum_rows], 2)
    few_own = lax.dynamic_index_in_dim(few, core, 1, False)
    few_got = links.swap(lax.dynamic_index_in_dim(few, 1 - core, 1, False).astype(BF))
    total_few = links.reduce_few((few_own + few_got.astype(F32)).astype(BF))
    norm_sums = total_few[part_rows : part_rows + 4, :part_rows]
    return (
        layer_output,
        in_grad,
        norm_sums[0],
        norm_sums[1],
        norm_sums[2],
        norm_sums[3],
        total_late[:, :width],
        total_few[:part_rows],
        total_late[:, width:],
        total_up,
        total_down,
    )


def solution(mesh):
    return jax.shard_map(
        functools.partial(shards, n_grp=mesh.shape["grp"], n_ctx=mesh.shape["ctx"]),
        mesh=mesh,
        in_specs=(P(("grp", "ctx"), None), P("grp", None))
        + (P(),) * 9
        + (P(("grp", "ctx"), None),),
        out_specs=(P(("grp", "ctx"), None),) * 2 + (P("ctx"),) * 4 + (P("ctx", None),) * 5,
        check_vma=False,
    )
```

time: 524 us -> 210 us (0.40)
  waiting for transfers between devices: 290 us -> 57.5 us
  matrix products: 108 us -> 23.5 us
  blocking collectives: 60.8 us -> 0 us
  starting transfers between devices: 0.55 us -> 54.8 us
  local copies, waits for them, and re-layouts: 7.6 us -> 29.9 us
  Pallas kernels: 0 us -> 21.1 us
  other arithmetic: 39.8 us -> 19.1 us
  between operations: 15.4 us -> 1.69 us
    reduce_scatter x6 -> x0, waiting for transfers between devices: 254 us -> none  [the longest x1 98.9 us: shards(): lax.psum_scatter(grad_w_up, 'ctx', scatter_dimension=0, tiled=True)]
    dot_general x21 -> x15, matrix products: 108 us -> 23.5 us  [dot(): lax.dot_general(left, right, (dims, ((), ())), preferred_element_type=F32)]
    ppermute x0 -> x41, waiting for transfers between devices: none -> 57.5 us  [the longest x33 57.4 us: permute(): return lax.ppermute(value, ('grp', 'ctx'), pairs)]
    ppermute x0 -> x41, starting transfers between devices: none -> 54.8 us  [the longest x33 53.1 us: permute(): return lax.ppermute(value, ('grp', 'ctx'), pairs)]
    psum x1 -> x0, waiting for transfers between devices: 36.7 us -> none  [shards(): lax.psum(shares_all[0].astype(jnp.bfloat16), 'grp').astype(jnp.float32)]
    unnamed x1 -> x0, blocking collectives: 25.9 us -> none
    pallas_call x0 -> x1, Pallas kernels: none -> 21.1 us  [attention(): pl.pallas_call(functools.partial(attn_kernel, blocks=blocks, heads=heads,...]
    all_gather x1 -> x0, blocking collectives: 17.5 us -> none  [shards(): kv_all = lax.all_gather(kv_low, 'ctx', axis=0, tiled=True)]
  transfers between devices with their start and end apart: 7 -> 41, of which waited for: 5 -> 20; matrix products, arithmetic and copies ran while one was open for 13% -> 32% of each run, Pallas kernels for 0% -> 10%
where the time goes in v1:
time: 210 us; the launch traced here: 208 us
  waiting for transfers between devices  57.5 us (27%)
  starting transfers between devices  54.8 us (26%)
  local copies, waits for them, and re-layouts  29.9 us (14%)
  matrix products  23.5 us (11%)
  Pallas kernels  21.1 us (10%)
  other arithmetic  19.1 us (9%)
    ppermute x33, waiting for transfers between devices, permute(): return lax.ppermute(value, ('grp', 'ctx'), pairs)  57.4 us
    ppermute x33, starting transfers between devices, permute(): return lax.ppermute(value, ('grp', 'ctx'), pairs)  53.1 us
    dot_general x15, matrix products, dot(): lax.dot_general(left, right, (dims, ((), ())), preferred_element_type=F32)  23.5 us
    pallas_call x1, Pallas kernels, attention(): pl.pallas_call(functools.partial(attn_kernel, blocks=blocks, heads=heads,...  21.1 us
    unnamed x83, local copies, waits for them, and re-layouts  11.6 us
  transfers between devices with their start and end apart: 41, of which 20 were waited for; matrix products, arithmetic and copies ran while one was open for 32% of the time, Pallas kernels for 10%

profile of v1, /device:TPU:0, one launch (start us, length us, event | category | flops | bytes accessed | tf_op | source)
XLA Modules:
  0.0 207.6 jit_solution(7362827507913158447)
XLA Ops:
  5.4 6.7 %copy.36 = bf16[768,3072]{0,1:T(8,128)(2,1)} copy(bf16[768,3072]{1,0:T(8,128)(2,1)} %param.21) | data formatting | bytes 9437184 | tf_op args[9]
  17.7 3.0 %collective-permute-start.4 = (bf16[512,128]{0,1:T(8,128)(2,1)S(1)}, bf16[512,128]{0,1:T(8,128)(2,1)S(1)}, u32[]{:S(2)}, u32[]{:S(2)}) collective-permute-start(bf16[512,128]{0,1:T(8,128)(2,1)S(1)} %pad_maximum_fusion.8), channel_id=1, source_target_pairs={{0,2},{1,3},{2,4},{3,5},{4,6},{5,7},{6,0},{7,1},{8,10},{9,11},{10,... | collective-permute-start | bytes 393224 | tf_op jit(solution)/shard_map/ppermute | solution.py:267
  20.8 2.6 %collective-permute-start.3 = (bf16[512,128]{0,1:T(8,128)(2,1)S(1)}, bf16[512,128]{0,1:T(8,128)(2,1)S(1)}, u32[]{:S(2)}, u32[]{:S(2)}) collective-permute-start(bf16[512,128]{0,1:T(8,128)(2,1)S(1)} %pad_maximum_fusion.8), channel_id=1, source_target_pairs={{0,4},{1,5},{2,6},{3,7},{4,0},{5,1},{6,2},{7,3},{8,12},{9,13},{10,... | collective-permute-start | bytes 393224 | tf_op jit(solution)/shard_map/ppermute | solution.py:267
  26.3 2.6 %fusion.70 = f32[512,768]{1,0:T(8,128)} fusion(bf16[512,1536]{1,0:T(8,128)(2,1)S(1)} %get-tuple-element.86, bf16[1536,768]{1,0:T(8,128)(2,1)S(1)} %bitcast.176), kind=kOutput, calls=%fused_computation.221 | convolution fusion | flops 1207959552 | bytes 5505024 | tf_op jit(solution)/shard_map/dot_general | solution.py:22
  31.5 2.5 %fusion.4 = bf16[512,1536]{1,0:T(8,128)(2,1)S(1)} fusion(f32[512,1536]{1,0:T(8,128)S(1)} %get-tuple-element.87, bf16[1536,768]{1,0:T(8,128)(2,1)S(1)} %bitcast.177, bf16[256,768]{1,0:T(8,128)(2,1)S(1)} %get-tuple-element.34, bf16[256,768]{1,0:T(8,128)(2,1)S(1)} %get-tuple-element.33), kind=kOutput, calls=%fused_computation.10 | convolution fusion | flops 1217396736 | bytes 7864320 | tf_op jit(solution)/shard_map/dot_general | solution.py:22
  34.0 2.6 %fusion.72 = f32[512,768]{1,0:T(8,128)} fusion(bf16[512,1536]{1,0:T(8,128)(2,1)S(1)} %fusion.4, bf16[768,1536]{0,1:T(8,128)(2,1)S(1)} %bitcast.175), kind=kOutput, calls=%fused_computation.223 | convolution fusion | flops 1207959552 | bytes 5505024 | tf_op jit(solution)/shard_map/dot_general | solution.py:22
  46.7 21.1 %attention.1 = (bf16[384,512]{1,0:T(8,128)(2,1)}, bf16[384,512]{1,0:T(8,128)(2,1)}, bf16[2048,128]{1,0:T(8,128)(2,1)}) custom-call(s32[16]{0:T(128)} %bitcast.198, s32[1]{0:T(128)} %bitcast.5.place, bf16[384,512]{1,0:T(8,128)(2,1)} %bitcast.193, f32[384,512]{1,0:T(8,128)} %fusion.13.do_ref, f32[8,512]{1,0:T(8,128)} %copy-done.22, f32[8,512]{1,0:T(8,128)} %copy-done.24, ...), custom_call_target="tpu_custom_call" | custom-call | flops 3221225472 | bytes 3145728 | tf_op jit(solution)/shard_map/attention/pallas_call | solution.py:204
  81.1 8.6 %collective-permute-start.7 = (bf16[256,128]{0,1:T(8,128)(2,1)S(1)}, bf16[256,128]{0,1:T(8,128)(2,1)S(1)}, u32[]{:S(2)}, u32[]{:S(2)}) collective-permute-start(bf16[256,128]{0,1:T(8,128)(2,1)S(1)} %get-tuple-element.70), channel_id=1, source_target_pairs={{0,2},{1,3},{2,4},{3,5},{4,6},{5,7},{6,0},{7,1},{8,10},{9,11},{10,... | collective-permute-start | bytes 196616 | tf_op jit(solution)/shard_map/ppermute | solution.py:267
  94.8 3.4 %collective-permute-done.8 = bf16[256,128]{0,1:T(8,128)(2,1)S(1)} collective-permute-done((bf16[256,128]{0,1:T(8,128)(2,1)S(1)}, bf16[256,128]{0,1:T(8,128)(2,1)S(1)}, u32[]{:S(2)}, u32[]{:S(2)}) %collective-permute-start.8) | collective-permute-done | bytes 65568 | tf_op jit(solution)/shard_map/ppermute | solution.py:267
  99.7 2.9 %multiply_reduce_fusion.1 = (f32[768]{0:T(1024)S(1)}, f32[768]{0:T(1024)S(1)}, f32[768]{0:T(1024)S(1)}, f32[768]{0:T(1024)S(1)}, f32[512,768]{1,0:T(8,128)S(1)}, /*index=5*/f32[512,768]{1,0:T(8,128)}) fusion(f32[512]{0:T(512)S(1)} %copy-done.31, f32[512]{0:T(512)S(1)} %copy-done.27, bf16[256,768]{1,0:T(8,128)(2,1)S(1)} %get-tuple-element.36, ...), kind=kOutput, calls=%fused_computation.25 | convolution fusion | flops 309064704 | bytes 7299588 | tf_op jit(solution)/shard_map/dot_general | solution.py:22
  105.6 3.8 %collective-permute-start.14 = (bf16[112,128]{1,0:T(8,128)(2,1)S(1)}, bf16[112,128]{1,0:T(8,128)(2,1)S(1)}, u32[]{:S(2)}, u32[]{:S(2)}) collective-permute-start(bf16[112,128]{1,0:T(8,128)(2,1)S(1)} %get-tuple-element.78), channel_id=1, source_target_pairs={{0,6},{1,7},{2,0},{3,1},{4,2},{5,3},{6,4},{7,5},{8,14},{9,15},{10,... | collective-permute-start | bytes 86024 | tf_op jit(solution)/shard_map/ppermute | solution.py:267
  111.5 2.7 %collective-permute-done.13 = bf16[112,128]{1,0:T(8,128)(2,1)S(1)} collective-permute-done((bf16[112,128]{1,0:T(8,128)(2,1)S(1)}, bf16[112,128]{1,0:T(8,128)(2,1)S(1)}, u32[]{:S(2)}, u32[]{:S(2)}) %collective-permute-start.13) | collective-permute-done | bytes 28704 | tf_op jit(solution)/shard_map/ppermute | solution.py:267
  114.3 5.5 %collective-permute-start.16 = (bf16[112,128]{1,0:T(8,128)(2,1)S(1)}, bf16[112,128]{1,0:T(8,128)(2,1)S(1)}, u32[]{:S(2)}, u32[]{:S(2)}) collective-permute-start(bf16[112,128]{1,0:T(8,128)(2,1)S(1)} %fusion.35), channel_id=1, source_target_pairs={{0,16},{1,17},{2,18},{3,19},{4,20},{5,21},{6,22},{7,23},{8,24},{9,... | collective-permute-start | bytes 86024 | tf_op jit(solution)/shard_map/ppermute | solution.py:267
  129.1 6.3 %collective-permute-done.19 = bf16[4,48,1536]{2,1,0:T(8,128)(2,1)S(1)} collective-permute-done((bf16[4,48,1536]{2,1,0:T(8,128)(2,1)S(1)}, bf16[4,48,1536]{2,1,0:T(8,128)(2,1)S(1)}, u32[]{:S(2)}, u32[]{:S(2)}) %collective-permute-start.19) | collective-permute-done | bytes 589856 | tf_op jit(solution)/shard_map/ppermute | solution.py:267
  137.7 7.9 %collective-permute-done.20 = bf16[4,24,1536]{2,1,0:T(8,128)(2,1)S(1)} collective-permute-done((bf16[4,24,1536]{2,1,0:T(8,128)(2,1)S(1)}, bf16[4,24,1536]{2,1,0:T(8,128)(2,1)S(1)}, u32[]{:S(2)}, u32[]{:S(2)}) %collective-permute-start.20) | collective-permute-done | bytes 294944 | tf_op jit(solution)/shard_map/ppermute | solution.py:267
  145.8 3.8 %collective-permute-start.23 = (bf16[24,1536]{1,0:T(8,128)(2,1)S(1)}, bf16[24,1536]{1,0:T(8,128)(2,1)S(1)}, u32[]{:S(2)}, u32[]{:S(2)}) collective-permute-start(bf16[24,1536]{1,0:T(8,128)(2,1)S(1)} %get-tuple-element.66), channel_id=1, source_target_pairs={{0,6},{1,7},{2,0},{3,1},{4,2},{5,3},{6,4},{7,5},{8,14},{9,15},{10,... | collective-permute-start | bytes 221192 | tf_op jit(solution)/shard_map/ppermute | solution.py:267
  151.9 2.9 %collective-permute-done.22 = bf16[24,1536]{1,0:T(8,128)(2,1)S(1)} collective-permute-done((bf16[24,1536]{1,0:T(8,128)(2,1)S(1)}, bf16[24,1536]{1,0:T(8,128)(2,1)S(1)}, u32[]{:S(2)}, u32[]{:S(2)}) %collective-permute-start.22) | collective-permute-done | bytes 73760 | tf_op jit(solution)/shard_map/ppermute | solution.py:267
  159.9 5.7 %collective-permute-done.35 = bf16[4,96,768]{2,1,0:T(8,128)(2,1)S(1)} collective-permute-done((bf16[4,96,768]{2,1,0:T(8,128)(2,1)S(1)}, bf16[4,96,768]{2,1,0:T(8,128)(2,1)S(1)}, u32[]{:S(2)}, u32[]{:S(2)}) %collective-permute-start.35) | collective-permute-done | bytes 589856 | tf_op jit(solution)/shard_map/ppermute | solution.py:267
  165.9 3.8 %collective-permute-start.38 = (bf16[96,768]{1,0:T(8,128)(2,1)S(1)}, bf16[96,768]{1,0:T(8,128)(2,1)S(1)}, u32[]{:S(2)}, u32[]{:S(2)}) collective-permute-start(bf16[96,768]{1,0:T(8,128)(2,1)S(1)} %get-tuple-element.40), channel_id=1, source_target_pairs={{0,6},{1,7},{2,0},{3,1},{4,2},{5,3},{6,4},{7,5},{8,14},{9,15},{10,... | collective-permute-start | bytes 442376 | tf_op jit(solution)/shard_map/ppermute | solution.py:267
  172.5 7.6 %collective-permute-done.28 = bf16[4,24,3072]{2,1,0:T(8,128)(2,1)S(1)} collective-permute-done((bf16[4,24,3072]{2,1,0:T(8,128)(2,1)S(1)}, bf16[4,24,3072]{2,1,0:T(8,128)(2,1)S(1)}, u32[]{:S(2)}, u32[]{:S(2)}) %collective-permute-start.28) | collective-permute-done | bytes 589856 | tf_op jit(solution)/shard_map/ppermute | solution.py:267
  180.9 3.3 %collective-permute-start.31 = (bf16[24,3072]{1,0:T(8,128)(2,1)S(1)}, bf16[24,3072]{1,0:T(8,128)(2,1)S(1)}, u32[]{:S(2)}, u32[]{:S(2)}) collective-permute-start(bf16[24,3072]{1,0:T(8,128)(2,1)S(1)} %get-tuple-element.45), channel_id=1, source_target_pairs={{0,6},{1,7},{2,0},{3,1},{4,2},{5,3},{6,4},{7,5},{8,14},{9,15},{10,... | collective-permute-start | bytes 442376 | tf_op jit(solution)/shard_map/ppermute | solution.py:267
  188.5 3.5 %collective-permute-done.30 = bf16[24,3072]{1,0:T(8,128)(2,1)S(1)} collective-permute-done((bf16[24,3072]{1,0:T(8,128)(2,1)S(1)}, bf16[24,3072]{1,0:T(8,128)(2,1)S(1)}, u32[]{:S(2)}, u32[]{:S(2)}) %collective-permute-start.30) | collective-permute-done | bytes 147488 | tf_op jit(solution)/shard_map/ppermute | solution.py:267
  194.2 3.1 %collective-permute-done.32 = bf16[24,3072]{1,0:T(8,128)(2,1)S(1)} collective-permute-done((bf16[24,3072]{1,0:T(8,128)(2,1)S(1)}, bf16[24,3072]{1,0:T(8,128)(2,1)S(1)}, u32[]{:S(2)}, u32[]{:S(2)}) %collective-permute-start.32) | collective-permute-done | bytes 147488 | tf_op jit(solution)/shard_map/ppermute | solution.py:267
  201.6 2.6 %collective-permute-done.33 = bf16[48,3072]{1,0:T(8,128)(2,1)S(1)} collective-permute-done((bf16[48,3072]{1,0:T(8,128)(2,1)S(1)}, bf16[48,3072]{1,0:T(8,128)(2,1)S(1)}, u32[]{:S(2)}, u32[]{:S(2)}) %collective-permute-start.33) | collective-permute-done | bytes 294944 | tf_op jit(solution)/shard_map/ppermute | solution.py:267
  (262 shorter events, 87.4 us)
Async XLA Ops:
  0.7 14.8 %collective-permute-start = (bf16[256,768]{1,0:T(8,128)(2,1)}, bf16[256,768]{1,0:T(8,128)(2,1)S(1)}, u32[]{:S(2)}, u32[]{:S(2)}) collective-permute-start(bf16[256,768]{1,0:T(8,128)(2,1)} %param.12), channel_id=1, source_target_pairs={{0,1},{1,0},{2,3},{3,2},{4,5},{5,4},{6,7},{7,6},{8,9},{9,8},{10,11... | collective-permute-start | bytes 1179656 | tf_op jit(solution)/shard_map/ppermute | solution.py:259
  1.2 27.7 %collective-permute-start.1 = (bf16[256,768]{1,0:T(8,128)(2,1)}, bf16[256,768]{1,0:T(8,128)(2,1)}, u32[]{:S(2)}, u32[]{:S(2)}) collective-permute-start(bf16[256,768]{1,0:T(8,128)(2,1)} %param.23), channel_id=1, source_target_pairs={{0,1},{1,0},{2,3},{3,2},{4,5},{5,4},{6,7},{7,6},{8,9},{9,8},{10,11... | collective-permute-start | bytes 1179656 | tf_op jit(solution)/shard_map/ppermute | solution.py:259
  17.7 27.8 %collective-permute-start.4 = (bf16[512,128]{0,1:T(8,128)(2,1)S(1)}, bf16[512,128]{0,1:T(8,128)(2,1)S(1)}, u32[]{:S(2)}, u32[]{:S(2)}) collective-permute-start(bf16[512,128]{0,1:T(8,128)(2,1)S(1)} %pad_maximum_fusion.8), channel_id=1, source_target_pairs={{0,2},{1,3},{2,4},{3,5},{4,6},{5,7},{6,0},{7,1},{8,10},{9,11},{10,... | collective-permute-start | bytes 393224 | tf_op jit(solution)/shard_map/ppermute | solution.py:267
  20.8 24.7 %collective-permute-start.3 = (bf16[512,128]{0,1:T(8,128)(2,1)S(1)}, bf16[512,128]{0,1:T(8,128)(2,1)S(1)}, u32[]{:S(2)}, u32[]{:S(2)}) collective-permute-start(bf16[512,128]{0,1:T(8,128)(2,1)S(1)} %pad_maximum_fusion.8), channel_id=1, source_target_pairs={{0,4},{1,5},{2,6},{3,7},{4,0},{5,1},{6,2},{7,3},{8,12},{9,13},{10,... | collective-permute-start | bytes 393224 | tf_op jit(solution)/shard_map/ppermute | solution.py:267
  23.4 22.1 %collective-permute-start.2 = (bf16[512,128]{0,1:T(8,128)(2,1)S(1)}, bf16[512,128]{0,1:T(8,128)(2,1)S(1)}, u32[]{:S(2)}, u32[]{:S(2)}) collective-permute-start(bf16[512,128]{0,1:T(8,128)(2,1)S(1)} %pad_maximum_fusion.8), channel_id=1, source_target_pairs={{0,6},{1,7},{2,0},{3,1},{4,2},{5,3},{6,4},{7,5},{8,14},{9,15},{10,... | collective-permute-start | bytes 393224 | tf_op jit(solution)/shard_map/ppermute | solution.py:267
  40.6 109.0 %collective-permute-start.34 = (bf16[4,192,768]{2,1,0:T(8,128)(2,1)}, bf16[4,192,768]{2,1,0:T(8,128)(2,1)}, u32[]{:S(2)}, u32[]{:S(2)}) collective-permute-start(bf16[4,192,768]{2,1,0:T(8,128)(2,1)} %constant_dynamic-slice_fusion.1), channel_id=1, source_target_pairs={{0,8},{1,17},{2,10},{3,19},{4,12},{5,21},{6,14},{7,23},{8,0},{9,25... | collective-permute-start | bytes 3538952 | tf_op jit(solution)/shard_map/ppermute | solution.py:267
  70.6 9.4 %collective-permute-start.6 = (bf16[4,256,128]{1,2,0:T(8,128)(2,1)}, bf16[4,256,128]{1,2,0:T(8,128)(2,1)}, u32[]{:S(2)}, u32[]{:S(2)}) collective-permute-start(bf16[4,256,128]{1,2,0:T(8,128)(2,1)} %bitcast.19), channel_id=1, source_target_pairs={{0,1},{1,0},{2,3},{3,2},{4,5},{5,4},{6,7},{7,6},{8,9},{9,8},{10,11... | collective-permute-start | bytes 786440 | tf_op jit(solution)/shard_map/ppermute | solution.py:259
  78.9 40.9 %collective-permute-start.5 = (bf16[256,768]{1,0:T(8,128)(2,1)}, bf16[256,768]{1,0:T(8,128)(2,1)}, u32[]{:S(2)}, u32[]{:S(2)}) collective-permute-start(bf16[256,768]{1,0:T(8,128)(2,1)} %dynamic-slice_convert_fusion.1), channel_id=1, source_target_pairs={{0,1},{1,0},{2,3},{3,2},{4,5},{5,4},{6,7},{7,6},{8,9},{9,8},{10,11... | collective-permute-start | bytes 1179656 | tf_op jit(solution)/shard_map/ppermute | solution.py:259
  81.1 13.0 %collective-permute-start.7 = (bf16[256,128]{0,1:T(8,128)(2,1)S(1)}, bf16[256,128]{0,1:T(8,128)(2,1)S(1)}, u32[]{:S(2)}, u32[]{:S(2)}) collective-permute-start(bf16[256,128]{0,1:T(8,128)(2,1)S(1)} %get-tuple-element.70), channel_id=1, source_target_pairs={{0,2},{1,3},{2,4},{3,5},{4,6},{5,7},{6,0},{7,1},{8,10},{9,11},{10,... | collective-permute-start | bytes 196616 | tf_op jit(solution)/shard_map/ppermute | solution.py:267
  111.5 13.3 %collective-permute-start.18 = (bf16[4,96,768]{2,1,0:T(8,128)(2,1)S(1)}, bf16[4,96,768]{2,1,0:T(8,128)(2,1)S(1)}, u32[]{:S(2)}, u32[]{:S(2)}) collective-permute-start(bf16[4,96,768]{2,1,0:T(8,128)(2,1)S(1)} %pad_maximum_fusion.3), channel_id=1, source_target_pairs={{0,1},{1,0},{2,3},{3,2},{4,5},{5,4},{6,7},{7,6},{8,9},{9,8},{10,11... | collective-permute-start | bytes 1769480 | tf_op jit(solution)/shard_map/ppermute | solution.py:259
  114.2 7.4 %collective-permute-start.17 = (bf16[112,128]{1,0:T(8,128)(2,1)S(1)}, bf16[112,128]{1,0:T(8,128)(2,1)S(1)}, u32[]{:S(2)}, u32[]{:S(2)}) collective-permute-start(bf16[112,128]{1,0:T(8,128)(2,1)S(1)} %fusion.35), channel_id=1, source_target_pairs={{0,24},{1,25},{2,26},{3,27},{4,28},{5,29},{6,30},{7,31},{8,16},{9,... | collective-permute-start | bytes 86024 | tf_op jit(solution)/shard_map/ppermute | solution.py:267
  114.3 7.4 %collective-permute-start.16 = (bf16[112,128]{1,0:T(8,128)(2,1)S(1)}, bf16[112,128]{1,0:T(8,128)(2,1)S(1)}, u32[]{:S(2)}, u32[]{:S(2)}) collective-permute-start(bf16[112,128]{1,0:T(8,128)(2,1)S(1)} %fusion.35), channel_id=1, source_target_pairs={{0,16},{1,17},{2,18},{3,19},{4,20},{5,21},{6,22},{7,23},{8,24},{9,... | collective-permute-start | bytes 86024 | tf_op jit(solution)/shard_map/ppermute | solution.py:267
  125.5 9.9 %collective-permute-start.19 = (bf16[4,48,1536]{2,1,0:T(8,128)(2,1)S(1)}, bf16[4,48,1536]{2,1,0:T(8,128)(2,1)S(1)}, u32[]{:S(2)}, u32[]{:S(2)}) collective-permute-start(bf16[4,48,1536]{2,1,0:T(8,128)(2,1)S(1)} %constant_dynamic-slice_fusion.4), channel_id=1, source_target_pairs={{0,8},{1,17},{2,10},{3,19},{4,12},{5,21},{6,14},{7,23},{8,0},{9,25... | collective-permute-start | bytes 1769480 | tf_op jit(solution)/shard_map/ppermute | solution.py:267
  135.6 9.9 %collective-permute-start.20 = (bf16[4,24,1536]{2,1,0:T(8,128)(2,1)S(1)}, bf16[4,24,1536]{2,1,0:T(8,128)(2,1)S(1)}, u32[]{:S(2)}, u32[]{:S(2)}) collective-permute-start(bf16[4,24,1536]{2,1,0:T(8,128)(2,1)S(1)} %constant_dynamic-slice_fusion.3), channel_id=1, source_target_pairs={{0,16},{1,9},{2,18},{3,11},{4,20},{5,13},{6,22},{7,15},{8,24},{9,1... | collective-permute-start | bytes 884744 | tf_op jit(solution)/shard_map/ppermute | solution.py:267
  136.1 33.6 %collective-permute-start.27 = (bf16[4,48,3072]{2,1,0:T(8,128)(2,1)S(1)}, bf16[4,48,3072]{2,1,0:T(8,128)(2,1)S(1)}, u32[]{:S(2)}, u32[]{:S(2)}) collective-permute-start(bf16[4,48,3072]{2,1,0:T(8,128)(2,1)S(1)} %fusion.9), channel_id=1, source_target_pairs={{0,8},{1,17},{2,10},{3,19},{4,12},{5,21},{6,14},{7,23},{8,0},{9,25... | collective-permute-start | bytes 3538952 | tf_op jit(solution)/shard_map/ppermute | solution.py:267
  155.3 10.3 %collective-permute-start.35 = (bf16[4,96,768]{2,1,0:T(8,128)(2,1)S(1)}, bf16[4,96,768]{2,1,0:T(8,128)(2,1)S(1)}, u32[]{:S(2)}, u32[]{:S(2)}) collective-permute-start(bf16[4,96,768]{2,1,0:T(8,128)(2,1)S(1)} %constant_dynamic-slice_fusion), channel_id=1, source_target_pairs={{0,16},{1,9},{2,18},{3,11},{4,20},{5,13},{6,22},{7,15},{8,24},{9,1... | collective-permute-start | bytes 1769480 | tf_op jit(solution)/shard_map/ppermute | solution.py:267
  159.3 12.2 %collective-permute-start.25 = (bf16[48,1536]{1,0:T(8,128)(2,1)S(1)}, bf16[48,1536]{1,0:T(8,128)(2,1)S(1)}, u32[]{:S(2)}, u32[]{:S(2)}) collective-permute-start(bf16[48,1536]{1,0:T(8,128)(2,1)S(1)} %pad_maximum_fusion.7), channel_id=1, source_target_pairs={{0,8},{1,17},{2,10},{3,19},{4,12},{5,21},{6,14},{7,23},{8,0},{9,25... | collective-permute-start | bytes 442376 | tf_op jit(solution)/shard_map/ppermute | solution.py:267
  165.8 18.3 %collective-permute-start.36 = (bf16[96,768]{1,0:T(8,128)(2,1)S(1)}, bf16[96,768]{1,0:T(8,128)(2,1)S(1)}, u32[]{:S(2)}, u32[]{:S(2)}) collective-permute-start(bf16[96,768]{1,0:T(8,128)(2,1)S(1)} %get-tuple-element.39), channel_id=1, source_target_pairs={{0,2},{1,3},{2,4},{3,5},{4,6},{5,7},{6,0},{7,1},{8,10},{9,11},{10,... | collective-permute-start | bytes 442376 | tf_op jit(solution)/shard_map/ppermute | solution.py:267
  165.9 19.4 %collective-permute-start.38 = (bf16[96,768]{1,0:T(8,128)(2,1)S(1)}, bf16[96,768]{1,0:T(8,128)(2,1)S(1)}, u32[]{:S(2)}, u32[]{:S(2)}) collective-permute-start(bf16[96,768]{1,0:T(8,128)(2,1)S(1)} %get-tuple-element.40), channel_id=1, source_target_pairs={{0,6},{1,7},{2,0},{3,1},{4,2},{5,3},{6,4},{7,5},{8,14},{9,15},{10,... | collective-permute-start | bytes 442376 | tf_op jit(solution)/shard_map/ppermute | solution.py:267
  169.7 15.6 %collective-permute-start.37 = (bf16[96,768]{1,0:T(8,128)(2,1)S(1)}, bf16[96,768]{1,0:T(8,128)(2,1)S(1)}, u32[]{:S(2)}, u32[]{:S(2)}) collective-permute-start(bf16[96,768]{1,0:T(8,128)(2,1)S(1)} %get-tuple-element.41), channel_id=1, source_target_pairs={{0,4},{1,5},{2,6},{3,7},{4,0},{5,1},{6,2},{7,3},{8,12},{9,13},{10,... | collective-permute-start | bytes 442376 | tf_op jit(solution)/shard_map/ppermute | solution.py:267
  170.1 9.9 %collective-permute-start.28 = (bf16[4,24,3072]{2,1,0:T(8,128)(2,1)S(1)}, bf16[4,24,3072]{2,1,0:T(8,128)(2,1)S(1)}, u32[]{:S(2)}, u32[]{:S(2)}) collective-permute-start(bf16[4,24,3072]{2,1,0:T(8,128)(2,1)S(1)} %constant_dynamic-slice_fusion.2), channel_id=1, source_target_pairs={{0,16},{1,9},{2,18},{3,11},{4,20},{5,13},{6,22},{7,15},{8,24},{9,1... | collective-permute-start | bytes 1769480 | tf_op jit(solution)/shard_map/ppermute | solution.py:267
  180.9 7.6 %collective-permute-start.31 = (bf16[24,3072]{1,0:T(8,128)(2,1)S(1)}, bf16[24,3072]{1,0:T(8,128)(2,1)S(1)}, u32[]{:S(2)}, u32[]{:S(2)}) collective-permute-start(bf16[24,3072]{1,0:T(8,128)(2,1)S(1)} %get-tuple-element.45), channel_id=1, source_target_pairs={{0,6},{1,7},{2,0},{3,1},{4,2},{5,3},{6,4},{7,5},{8,14},{9,15},{10,... | collective-permute-start | bytes 442376 | tf_op jit(solution)/shard_map/ppermute | solution.py:267
  184.1 7.9 %collective-permute-start.30 = (bf16[24,3072]{1,0:T(8,128)(2,1)S(1)}, bf16[24,3072]{1,0:T(8,128)(2,1)S(1)}, u32[]{:S(2)}, u32[]{:S(2)}) collective-permute-start(bf16[24,3072]{1,0:T(8,128)(2,1)S(1)} %get-tuple-element.46), channel_id=1, source_target_pairs={{0,4},{1,5},{2,6},{3,7},{4,0},{5,1},{6,2},{7,3},{8,12},{9,13},{10,... | collective-permute-start | bytes 442376 | tf_op jit(solution)/shard_map/ppermute | solution.py:267
  185.4 8.2 %collective-permute-start.39 = (bf16[96,768]{1,0:T(8,128)(2,1)S(1)}, bf16[96,768]{1,0:T(8,128)(2,1)S(1)}, u32[]{:S(2)}, u32[]{:S(2)}) collective-permute-start(bf16[96,768]{1,0:T(8,128)(2,1)S(1)} %fusion.21), channel_id=1, source_target_pairs={{0,16},{1,9},{2,18},{3,11},{4,20},{5,13},{6,22},{7,15},{8,24},{9,1... | collective-permute-start | bytes 442376 | tf_op jit(solution)/shard_map/ppermute | solution.py:267
  (54 other events, 509.0 us)

commit v2 on v1

v2 whole, which is shorter than its diff:
```python
import functools

import jax
import jax.numpy as jnp
from jax import lax
from jax.experimental import pallas as pl
from jax.experimental.pallas import tpu as pltpu
from jax.sharding import PartitionSpec as P

ROT = 16
HALF = ROT // 2
BLK = 128
CONT = 1024
TILE = 256
LANES = 128
WIDE = 256
EPS = 1e-05
LOG2E = 1.4426950408889634
LN2 = 0.6931471805599453
BF = jnp.bfloat16
F32 = jnp.float32
MIB = 1024 * 1024
VM = pl.BlockSpec(memory_space=pltpu.VMEM)
HBM = pl.BlockSpec(memory_space=pltpu.HBM)


def dot(left, right, dims=((1,), (0,))):
    return lax.dot_general(left, right, (dims, ((), ())), preferred_element_type=F32)


def shape(dims, dtype):
    return jax.ShapeDtypeStruct(dims, dtype)


def tie(value, *others):
    return lax.optimization_barrier((value,) + others)[0]


def rope_tables(position):
    inverse = 10000.0 ** (-(2.0 * jnp.arange(HALF, dtype=F32)) / ROT)
    angles = inverse[:, None] * position.astype(F32)[None, :]
    return (jnp.cos(angles), jnp.sin(angles))


def turn(values, cosine, sine):
    first, second = values[:HALF], values[HALF:ROT]
    return jnp.concatenate(
        [first * cosine - second * sine, second * cosine + first * sine, values[ROT:]], 0
    )


def normed(values):
    shifted = values - jnp.mean(values, -1, keepdims=True)
    scale = lax.rsqrt(jnp.mean(shifted * shifted, -1, keepdims=True) + EPS)
    return (shifted * scale, scale)


def gelu_parts(value):
    cdf = 0.5 * (1.0 + lax.erf(value * 0.7071067811865476))
    pdf = jnp.exp(-0.5 * value * value) * 0.3989422804014327
    return value * cdf, cdf + value * pdf


def call(kernel, name, outs, specs, out_specs, scratch, limit, flops=1000000):
    return pl.pallas_call(
        kernel,
        out_shape=outs,
        grid_spec=pltpu.PrefetchScalarGridSpec(
            num_scalar_prefetch=1, in_specs=specs, out_specs=out_specs, scratch_shapes=scratch
        ),
        compiler_params=pltpu.CompilerParams(vmem_limit_bytes=limit * MIB),
        cost_estimate=pl.CostEstimate(flops=flops, bytes_accessed=flops // 200, transcendentals=0),
        name=name,
    )


def attn_kernel(table, place, *refs, blocks, heads, size, n_kv, per_chip, last_call, first_call):
    q_ref, do_ref, cos_ref, sin_ref = refs[:4]
    kv_refs = refs[4 : 4 + n_kv]
    refs = refs[4 + n_kv :]
    if not first_call:
        sum_ref, refs = refs[0], refs[1:]
    mix_ref, dq_ref = refs[:2]
    outs = refs[2:-11]
    kv_c, kv_t, s_scr, p_scr, rq, rd, rqt, rdt, o_acc, dq_acc, dkv_acc = refs[-11:]
    step, group = pl.program_id(0), pl.program_id(1)
    lanes = heads * BLK
    prompt_blocks = blocks // 2
    prompt_tiles = prompt_blocks * BLK // TILE
    cont_blocks = min(CONT, prompt_blocks * BLK) // BLK

    def block_rows(block):
        return pl.ds(pl.multiple_of(block * BLK, BLK), BLK)

    @pl.when((step == 0) & (group == 0))
    def _():
        ones = jnp.ones((16, BLK), BF)
        share = blocks // n_kv

        for n, kv_ref in enumerate(kv_refs):

            def place_block(at, carry, n=n, kv_ref=kv_ref):
                spot = n * share + at
                block = table[((spot // per_chip) ^ place[2]) * per_chip + spot % per_chip]
                rows = kv_ref[block_rows(at), :]
                kv_c[block_rows(block), :] = rows
                turned = jnp.concatenate([rows.T, ones], 0)

                @pl.when(block % 2 == 0)
                def _():
                    kv_t[block // 2, :, 0:BLK] = turned

                @pl.when(block % 2 == 1)
                def _():
                    kv_t[block // 2, :, BLK:TILE] = turned

                return carry

            lax.fori_loop(0, share, place_block, 0)
        dkv_acc[...] = jnp.zeros_like(dkv_acc) if first_call else sum_ref[...]

    block = table[place[0] + lax.rem(place[3] + step + place[1], per_chip)]
    last = block // 2
    in_prompt = block < prompt_blocks
    seg_tile = (prompt_blocks + (block - prompt_blocks) // cont_blocks * cont_blocks) // 2
    full = jnp.where(in_prompt, last, prompt_tiles + last - seg_tile)

    def tile_of(i):
        return jnp.where(i < prompt_tiles, jnp.minimum(i, last), i - prompt_tiles + seg_tile)

    def key_rows(tile):
        return pl.ds(pl.multiple_of(tile * TILE, TILE), TILE)

    for h in range(heads):
        rq[0:size, h * BLK : (h + 1) * BLK] = q_ref[h * size : (h + 1) * size, :]
    rq[size : 2 * size, :] = jnp.zeros((size, lanes), BF)

    def scores(tile):
        return dot(kv_c[key_rows(tile), :], rq[...])

    def fold(values):
        return jnp.max(values.reshape(TILE // 8, 8, lanes), 0)

    def first_pass(i, top):
        part = scores(tile_of(i))
        s_scr[i] = part
        return jnp.maximum(top, fold(part))

    top = lax.fori_loop(0, full, first_pass, jnp.full((8, lanes), -1e30, F32))
    part = scores(last)
    key_at = last * TILE + lax.broadcasted_iota(jnp.int32, (TILE, lanes), 0)
    row_at = block * BLK + lax.rem(lax.broadcasted_iota(jnp.int32, (TILE, lanes), 1), BLK)
    part = jnp.where(key_at <= row_at, part, -1e30)
    s_scr[full] = part
    top = jnp.max(jnp.maximum(top, fold(part)), 0, keepdims=True)

    o_acc[...] = jnp.zeros_like(o_acc)

    def second_pass(i, carry):
        p = jnp.exp2(s_scr[i] - top).astype(BF)
        p_scr[i] = p
        o_acc[...] += dot(kv_t[jnp.where(i == full, last, tile_of(i)), size : 2 * size + 16, :], p)
        return carry

    lax.fori_loop(0, full + 1, second_pass, 0)

    inverse = 1.0 / o_acc[size : size + 1, :]
    mixed = o_acc[0:size, :] * inverse
    grads = []
    for h in range(heads):
        at = slice(h * BLK, (h + 1) * BLK)
        mix_ref[h * size : (h + 1) * size, :] = mixed[:, at].astype(BF)
        grads.append(do_ref[h * size : (h + 1) * size, :])
    scaled = (jnp.concatenate(grads, 1) * inverse).astype(BF)
    delta = jnp.sum(mixed * scaled.astype(F32), 0, keepdims=True)
    rd[0:size, :] = jnp.zeros((size, lanes), BF)
    rd[size : 2 * size, :] = scaled
    rqt[...] = rq[...].T
    rdt[...] = rd[...].T
    dq_acc[...] = jnp.zeros_like(dq_acc)

    def third_pass(i, carry):
        tile = jnp.where(i == full, last, tile_of(i))
        p = p_scr[i]
        d_probs = dot(kv_c[key_rows(tile), :], rd[...])
        ds = (p.astype(F32) * (d_probs - delta)).astype(BF)
        dq_acc[...] += dot(kv_t[tile, 0:size, :], ds)
        dkv_acc[key_rows(tile), :] += dot(p, rdt[...]) + dot(ds, rqt[...])
        return carry

    lax.fori_loop(0, full + 1, third_pass, 0)

    cosine, sine = cos_ref[...], sin_ref[...]
    for h in range(heads):
        part = dq_acc[:, h * BLK : (h + 1) * BLK] * 0.125
        dq_ref[h * size : (h + 1) * size, :] = turn(part, cosine, -sine).astype(BF)

    @pl.when((step == pl.num_programs(0) - 1) & (group == pl.num_programs(1) - 1))
    def _():
        if not last_call:
            outs[0][...] = dkv_acc[...]
            return
        scale = jnp.where(
            lax.broadcasted_iota(jnp.int32, (BLK, 2 * size), 1) < size, F32(LN2), F32(1.0)
        )

        def rows_of(slot):
            return (dkv_acc[block_rows(table[slot]), :] * scale).astype(BF)

        if len(outs) == 1:

            def give_block(slot, carry):
                outs[0][block_rows(slot), :] = rows_of(slot)
                return carry

            lax.fori_loop(0, blocks, give_block, 0)
            return
        per_core = per_chip // 2
        for low in range(2):
            for high in range(2):
                chip = place[2] ^ (low + 2 * high)
                for n in range(per_core):
                    here = slice(n * BLK, (n + 1) * BLK)
                    base = chip * per_chip + n
                    outs[0][low, high, here, :] = rows_of(base + per_core - place[1])
                    outs[1][low, high, here, :] = rows_of(base + place[1])


def attention(
    table, place, q_t, do_t, cosine, sine, kvs, carried, start, count, per_chip, last_call, split
):
    width = q_t.shape[0]
    rows = count * BLK
    first_call = carried is None
    size = kvs[0].shape[1] // 2
    keys = sum(kv.shape[0] for kv in kvs)
    all_heads = width // size
    blocks = keys // BLK
    heads = all_heads if keys <= 4096 else 2
    lanes = heads * BLK
    cont = min(CONT, keys // 2)
    most = (keys // 2 + cont) // TILE
    tiles = keys // TILE

    def whole(dims):
        return pl.BlockSpec(dims, lambda i, j, *_: (0,) * len(dims))

    if not last_call:
        dkv_shapes = [shape((keys, 2 * size), F32)]
    elif split:
        dkv_shapes = [shape((2, 2, keys // 8, 2 * size), BF)] * 2
    else:
        dkv_shapes = [shape((keys, 2 * size), BF)]
    extra = [] if first_call else [carried]
    column = pl.BlockSpec((heads * size, BLK), lambda i, j, *_: (j, i + start))
    angle = pl.BlockSpec((HALF, BLK), lambda i, j, *_: (0, i + start))
    out_column = pl.BlockSpec((heads * size, BLK), lambda i, j, *_: (j, i))
    return pl.pallas_call(
        functools.partial(
            attn_kernel,
            blocks=blocks,
            heads=heads,
            size=size,
            n_kv=len(kvs),
            per_chip=per_chip,
            last_call=last_call,
            first_call=first_call,
        ),
        out_shape=[shape((width, rows), BF)] * 2 + dkv_shapes,
        grid_spec=pltpu.PrefetchScalarGridSpec(
            num_scalar_prefetch=2,
            grid=(count, all_heads // heads),
            in_specs=[column, column, angle, angle]
            + [whole(kv.shape) for kv in kvs]
            + [whole(e.shape) for e in extra],
            out_specs=[out_column, out_column] + [whole(s.shape) for s in dkv_shapes],
            scratch_shapes=[
                pltpu.VMEM((keys, 2 * size), BF),
                pltpu.VMEM((tiles, 2 * size + 16, TILE), BF),
                pltpu.VMEM((most, TILE, lanes), F32),
                pltpu.VMEM((most, TILE, lanes), BF),
                pltpu.VMEM((2 * size, lanes), BF),
                pltpu.VMEM((2 * size, lanes), BF),
                pltpu.VMEM((lanes, 2 * size), BF),
                pltpu.VMEM((lanes, 2 * size), BF),
                pltpu.VMEM((size + 16, lanes), F32),
                pltpu.VMEM((size, lanes), F32),
                pltpu.VMEM((keys, 2 * size), F32),
            ],
        ),
        compiler_params=pltpu.CompilerParams(
            vmem_limit_bytes=(24 if keys <= 4096 else 60) * MIB
        ),
        cost_estimate=pl.CostEstimate(
            flops=24 * width * rows * keys, bytes_accessed=4 * width * rows * 4, transcendentals=0
        ),
        name="attention",
    )(table, place + jnp.array([0, 0, 0, start], jnp.int32), q_t, do_t, cosine, sine, *kvs, *extra)


def prologue_kernel(
    sc, xo, xt, go, gt, g1, c1, g2, c2, w_kv, cos_ref, sin_ref, h1_ref, h2_ref, gg_ref, kv_ref
):
    rows = xo.shape[0]
    gain_one, bias_one = g1[...].astype(F32), c1[...].astype(F32)
    gain_two, bias_two = g2[...].astype(F32), c2[...].astype(F32)
    for n, (x, g) in enumerate(((xo, go), (xt, gt))):
        for t in range(rows // 128):
            here = slice(n * rows + t * 128, n * rows + (t + 1) * 128)
            hat, unused = normed(x[t * 128 : (t + 1) * 128, :].astype(F32))
            h1_ref[here, :] = (hat * gain_one + bias_one).astype(BF)
            h2_ref[here, :] = (hat * gain_two + bias_two).astype(BF)
        gg_ref[n * rows : (n + 1) * rows, :] = g[...]
    raw = dot(h1_ref[...], w_kv[...])
    kv = turn(raw.T, cos_ref[...], sin_ref[...]).T.astype(BF)
    kv_ref[pl.ds(pl.multiple_of(sc[0] * rows, rows), rows), :] = kv[:rows]
    kv_ref[pl.ds(pl.multiple_of((1 - sc[0]) * rows, rows), rows), :] = kv[rows:]


def half_copies(sc, w_query, w_out, query_s, out_s, sem):
    half = out_s.shape[0]
    at = pl.ds(pl.multiple_of(sc[0] * half, 128), half)
    return [
        pltpu.make_async_copy(w_query.at[:, at], query_s, sem.at[0]),
        pltpu.make_async_copy(w_out.at[at, :], out_s, sem.at[1]),
    ]


def project_kernel(
    sc, h_ref, g_ref, cos_ref, sin_ref, w_query, w_out, q_ref, do_ref, query_s, out_s, sem, *, size
):
    copies = half_copies(sc, w_query, w_out, query_s, out_s, sem)
    for copy in copies:
        copy.start()
    cosine, sine = cos_ref[...], sin_ref[...]
    copies[0].wait()
    raw = (dot(h_ref[...], query_s[...]) * (0.125 * LOG2E)).T
    for h in range(raw.shape[0] // size):
        at = slice(h * size, (h + 1) * size)
        q_ref[at, :] = turn(raw[at], cosine, sine).astype(BF)
    copies[1].wait()
    do_ref[...] = dot(out_s[...], g_ref[...], ((1,), (1,)))


def hidden_copies(sc, piece, w_up, w_down, up_s, down_s, sems, part, n_pair):
    copies = []
    for j in range(n_pair):
        source = pl.ds(pl.multiple_of((2 * j + sc[0]) * part + piece * LANES, LANES), LANES)
        at = slice(j * LANES, (j + 1) * LANES)
        if w_up is not None:
            copies.append(
                pltpu.make_async_copy(w_up.at[:, source], up_s.at[:, at], sems.at[0])
            )
        if w_down is not None:
            copies.append(
                pltpu.make_async_copy(w_down.at[source, :], down_s.at[at, :], sems.at[1])
            )
    return copies


def piece_of(sc, n):
    return 0 if n == 0 else (2 - sc[2] if n == 1 else 1 + sc[2])


def ffn_kernel(
    sc, h_ref, g_ref, w_up, w_down, act_ref, dup_ref, *refs, n, part, n_pair
):
    up_s, down_s, grad_s, sems = refs[-4:]
    outs = refs[:-4]
    rows, width = h_ref.shape
    copies = hidden_copies(sc, piece_of(sc, n), w_up, w_down, up_s, down_s, sems, part, n_pair)
    for copy in copies:
        copy.start()
    for copy in copies:
        copy.wait()

    def row_tile(r, carry):
        tile = pl.ds(pl.multiple_of(r * 128, 128), 128)
        act, slope = gelu_parts(dot(h_ref[tile, :], up_s[...]))
        act_ref[tile, :] = act.astype(BF)
        d_act = dot(g_ref[tile, :], down_s[...], ((1,), (1,)))
        dup_ref[tile, :] = (d_act * slope).astype(BF)
        return carry

    lax.fori_loop(0, rows // 128, row_tile, 0, unroll=2)
    up_rows = width // n_pair
    block_rows = width // WIDE * LANES

    def give(low, high, kind, first, value):
        here = slice(first, first + value.shape[0])
        if n == 0:
            outs[1 - low][high, kind * block_rows + first : kind * block_rows + here.stop, :] = value
        else:
            outs[0][kind ^ sc[3], low, high, here, :] = value

    grad_s[0 : n_pair * LANES, :] = dot(act_ref[...], g_ref[...], ((0,), (0,))).astype(BF)
    for low in range(2):
        for high in range(2):
            chip = sc[1] ^ (low + 2 * high)
            rows_at = pl.ds(pl.multiple_of(chip * LANES, LANES), LANES)
            for b in range(width // WIDE):
                give(low, high, 0, b * LANES, grad_s[rows_at, b * WIDE : (b + 1) * WIDE])
    span = n_pair * LANES
    grad_s[:, 0:span] = dot(h_ref[...], dup_ref[...], ((0,), (0,))).astype(BF)
    for low in range(2):
        for high in range(2):
            chip = sc[1] ^ (low + 2 * high)
            rows_at = pl.ds(pl.multiple_of(chip * up_rows, 64), up_rows)
            for b in range(span // WIDE):
                give(low, high, 1, b * up_rows, grad_s[rows_at, b * WIDE : (b + 1) * WIDE])


def ffn_gradients(sc, h_two, g_two, w_up, w_down, n, part, n_pair):
    rows, width = h_two.shape
    span = n_pair * LANES
    block = width // WIDE * LANES
    if n == 0:
        outs = [shape((2, 2 * block, WIDE), BF)] * 2
    else:
        outs = [shape((2, 2, 2, block, WIDE), BF)]
    return call(
        functools.partial(ffn_kernel, n=n, part=part, n_pair=n_pair),
        "ffn_gradients",
        [shape((rows, span), BF)] * 2 + outs,
        [VM, VM, HBM, HBM],
        [VM] * (2 + len(outs)),
        [
            pltpu.VMEM((width, span), BF),
            pltpu.VMEM((span, width), BF),
            pltpu.VMEM((width, width), BF),
            pltpu.SemaphoreType.DMA((2,)),
        ],
        20,
        8 * rows * width * span,
    )(sc, h_two, g_two, w_up, w_down)


def late_kernel(sc, h_ref, dq0, dq1, mix0, mix1, got0, got1, g_ref, send_ref, keep_ref, mix_s, dq_s, both_s, *, n_pair):
    half = mix0.shape[0]
    rows = mix0.shape[1]
    width = 2 * half
    own = pl.multiple_of(sc[0] * half, 128)
    other = pl.multiple_of((1 - sc[0]) * half, 128)
    mix_s[pl.ds(own, half), 0:rows] = mix0[...]
    mix_s[pl.ds(own, half), rows : 2 * rows] = mix1[...]
    mix_s[pl.ds(other, half), 0:rows] = got1[...]
    mix_s[pl.ds(other, half), rows : 2 * rows] = got0[...]
    dq_s[:, 0:rows] = dq0[...]
    dq_s[:, rows : 2 * rows] = dq1[...]
    both_s[:, 0:half] = dot(h_ref[...], dq_s[...], ((0,), (1,))).astype(BF)
    both_s[:, half:width] = dot(mix_s[...], g_ref[:, pl.ds(own, half)]).astype(BF)
    block = width // n_pair
    quarter = keep_ref.shape[3]
    unit = 48
    for low in range(2):
        for high in range(2):
            chip = sc[1] ^ (low + 2 * high)
            for first in range(2):
                ref = send_ref if first else keep_ref
                for second in range(2):
                    part = 2 * (first ^ sc[2]) + (second ^ sc[3])
                    for r in range(quarter // unit):
                        at = part * quarter + r * unit
                        col, row = at // block, at % block
                        source = pl.ds(pl.multiple_of(chip * block + row, 16), unit)
                        lane = pl.ds(pl.multiple_of(col * WIDE, WIDE), WIDE)
                        ref[second, low, high, r * unit : (r + 1) * unit, :] = both_s[source, lane]


def late_gradients(sc, h_one, dqs, mixes, gots, g_two, n_pair):
    half = dqs[0].shape[0]
    width = 2 * half
    rows = h_one.shape[0]
    quarter = width // n_pair * (width // WIDE) // 4
    return call(
        functools.partial(late_kernel, n_pair=n_pair),
        "late_gradients",
        [shape((2, 2, 2, quarter, WIDE), BF)] * 2,
        [VM] * 8,
        [VM] * 2,
        [
            pltpu.VMEM((width, rows), BF),
            pltpu.VMEM((half, rows), BF),
            pltpu.VMEM((width, width), BF),
        ],
        16,
        2 * rows * width * width,
    )(sc, h_one, *dqs, *mixes, *gots, g_two)


def out_kernel(sc, a0, a1, a2, mix0, mix1, x_ref, w_down, w_out, own_ref, send_ref, down_s, out_s, sems, *, part, n_pair):
    half = out_s.shape[0]
    rows = x_ref.shape[0]
    span = n_pair * LANES
    copies = [
        pltpu.make_async_copy(
            w_out.at[pl.ds(pl.multiple_of(sc[0] * half, 128), half), :], out_s, sems.at[0]
        )
    ]
    for n in range(3):
        copies += hidden_copies(
            sc, piece_of(sc, n), None, w_down, None, down_s.at[n], sems, part, n_pair
        )
    for copy in copies:
        copy.start()
    for copy in copies:
        copy.wait()
    for n, mix in enumerate((mix0, mix1)):
        here = slice(n * rows, (n + 1) * rows)
        total = dot(mix[...], out_s[...], ((0,), (0,)))
        for k, act in enumerate((a0, a1, a2)):
            total = total + dot(act[here, :], down_s[k])
        if n == 0:
            own_ref[...] = total + x_ref[...].astype(F32)
        else:
            send_ref[...] = total.astype(BF)


def hat_kernel(sc, d0, d1, d2, dq0, dq1, xo, xt, g1, g2, w_up, w_query, own_ref, send_ref, sum_ref, up_s, query_s, sems, *, part, n_pair):
    half = query_s.shape[1]
    rows, width = xo.shape
    copies = [
        pltpu.make_async_copy(
            w_query.at[:, pl.ds(pl.multiple_of(sc[0] * half, 128), half)], query_s, sems.at[1]
        )
    ]
    for n in range(3):
        copies += hidden_copies(
            sc, piece_of(sc, n), w_up, None, up_s.at[n], None, sems, part, n_pair
        )
    for copy in copies:
        copy.start()
    for copy in copies:
        copy.wait()
    gain_one, gain_two = g1[...].astype(F32), g2[...].astype(F32)
    sums = [jnp.zeros((1, width), F32)] * 4
    for n, (x, dq) in enumerate(((xo, dq0), (xt, dq1))):
        here = slice(n * rows, (n + 1) * rows)
        two = dot(d0[here, :], up_s[0], ((1,), (1,)))
        two = two + dot(d1[here, :], up_s[1], ((1,), (1,)))
        two = two + dot(d2[here, :], up_s[2], ((1,), (1,)))
        one = dot(dq[...], query_s[...], ((0,), (1,)))
        hat, unused = normed(x[...].astype(F32))
        for k, value in enumerate((one * hat, one, two * hat, two)):
            sums[k] = sums[k] + jnp.sum(value, 0, keepdims=True)
        total = one * gain_one + two * gain_two
        if n == 0:
            own_ref[...] = total
        else:
            send_ref[...] = total.astype(BF)
    sum_ref[...] = jnp.concatenate(sums + [jnp.zeros((4, width), F32)], 0)


def last_kernel(sc, dkv_a, dkv_b, cos_ref, sin_ref, w_kv, h_ref, x_ref, g1, hat_own, hat_got, sum_ref, g_ref, grad_ref, send_ref, keep_ref, *, n_pair):
    rows, width = x_ref.shape
    dkv = (dkv_a[...] + dkv_b[...].astype(F32)).T
    low_t = turn(dkv, cos_ref[:, 0:rows], -sin_ref[:, 0:rows]).astype(BF)
    low = low_t.T
    weight = dot(low_t, h_ref[0:rows, :]).T.astype(BF)
    d_kv = dot(low, w_kv[...], ((1,), (1,)))
    hat, scale = normed(x_ref[...].astype(F32))
    gain = g1[...].astype(F32)
    total = hat_own[...] + hat_got[...].astype(F32) + d_kv * gain
    grad_ref[...] = g_ref[...].astype(F32) + scale * (
        total
        - jnp.mean(total, -1, keepdims=True)
        - hat * jnp.mean(total * hat, -1, keepdims=True)
    )
    sums = jnp.concatenate(
        [
            sum_ref[0:1, :] + jnp.sum(d_kv * hat, 0, keepdims=True),
            sum_ref[1:2, :] + jnp.sum(d_kv, 0, keepdims=True),
            sum_ref[2:4, :],
            jnp.zeros((4, width), F32),
        ],
        0,
    ).astype(BF)
    part = width // (2 * n_pair)
    lanes = weight.shape[1]
    for chip in range(n_pair):
        rel = chip ^ sc[1]
        low_bit, high_bit = rel % 2, rel // 2
        blocks = []
        for core in range(2):
            at = (2 * chip + core) * part
            piece = weight[at : at + part, :]
            blocks.append(jnp.concatenate([piece[: part // 2], piece[part // 2 :]], 1))
            row = sums[:, at : at + part]
            blocks.append(jnp.concatenate([row, jnp.zeros((8, 2 * lanes - part), BF)], 1))
        block = jnp.concatenate(blocks, 0)

        @pl.when(low_bit == 1)
        def _():
            send_ref[high_bit] = block

        @pl.when(low_bit == 0)
        def _():
            keep_ref[high_bit] = block


def down_kernel(sc, send_ref, got_ref, out_ref, *, width):
    block = width // WIDE * LANES
    for k in range(3):
        for b in range(width // WIDE):
            here = slice(b * LANES, (b + 1) * LANES)
            if k == 0:
                at = slice(2 * block + b * LANES, 2 * block + (b + 1) * LANES)
                value = send_ref[at, :].astype(F32) + got_ref[at, :].astype(F32)
            else:
                at = pl.ds(pl.multiple_of(sc[3] * block + b * LANES, LANES), LANES)
                mine = send_ref[at, :].astype(F32)
                value = jnp.where(sc[2] == k - 1, mine, got_ref[at, :].astype(F32))
            out_ref[k * LANES : (k + 1) * LANES, b * WIDE : (b + 1) * WIDE] = value


def up_block(sc, k, b, parity, early_send, early_got, width, part):
    block = width // WIDE * LANES
    off = b * 2 * part + parity * part
    if k == 0:
        at = pl.ds(pl.multiple_of(3 * block + off, 32), part)
        return early_send[at, :].astype(F32) + early_got[at, :].astype(F32)
    at = pl.ds(pl.multiple_of((1 - sc[3]) * block + off, 32), part)
    return jnp.where(
        sc[2] == k - 1, early_send[at, :].astype(F32), early_got[at, :].astype(F32)
    )


def late_block(sc, b, parity, send, got, part, quarter):
    pieces = []
    for r in range(2):
        at = b * 2 * part + parity * part + r * (part // 2)
        first, second = at // (2 * quarter), at // quarter % 2
        rel = (second ^ sc[3]) * quarter + at % quarter
        source = pl.ds(pl.multiple_of(rel, 16), part // 2)
        pieces.append(
            jnp.where(
                first == sc[2], send[source, :].astype(F32), got[source, :].astype(F32)
            )
        )
    return jnp.concatenate(pieces, 0)


def pack_kernel(sc, early_send, early_got, last_send, last_got, out_ref, own_ref, *, width, part, quarter):
    for which, ref in ((1, out_ref), (0, own_ref)):
        parity = sc[0] if which == 0 else 1 - sc[0]
        at = 0
        for k in range(3):
            for b in range(2):
                ref[at : at + part, :] = up_block(
                    sc, k, b, parity, early_send, early_got, width, part
                ).astype(BF)
                at += part
        for b in range(width // WIDE):
            ref[at : at + part, :] = late_block(
                sc, b, parity, last_send, last_got, part, quarter
            ).astype(BF)
            at += part
        few = (last_send.shape[0] - 2 * quarter) // 2
        source = pl.ds(pl.multiple_of(2 * quarter + parity * few, 8), few)
        ref[at : at + few, :] = (
            last_send[source, :].astype(F32) + last_got[source, :].astype(F32)
        ).astype(BF)


def final_kernel(sc, own_ref, got_ref, up_ref, query_ref, proj_ref, kv_ref, norm_ref, *, part, n_pair):
    part_hidden = up_ref.shape[1] // (2 * n_pair)
    half = query_ref.shape[1] // 2
    for which, ref in enumerate((own_ref, got_ref)):
        core = sc[0] if which == 0 else 1 - sc[0]
        at = 0
        for k in range(3):
            for j in range(n_pair):
                lane = (2 * j + core) * part_hidden + k * LANES
                rows = slice((2 * k + j // 2) * part, (2 * k + j // 2 + 1) * part)
                cols = slice(j % 2 * LANES, (j % 2 + 1) * LANES)
                up_ref[:, pl.ds(pl.multiple_of(lane, LANES), LANES)] = ref[rows, cols].astype(F32)
        base = 6 * part
        for n in range(2 * half // LANES):
            rows = slice(base + n // 2 * part, base + (n // 2 + 1) * part)
            value = ref[rows, n % 2 * LANES : (n % 2 + 1) * LANES].astype(F32)
            to, m = (query_ref, n) if n < half // LANES else (proj_ref, n - half // LANES)
            to[:, pl.ds(pl.multiple_of(core * half + m * LANES, LANES), LANES)] = value
    base = 9 * part
    few = own_ref[base:, :].astype(F32) + got_ref[base:, :].astype(F32)
    kv_ref[0 : part // 2, :] = few[0 : part // 2, 0:LANES]
    kv_ref[part // 2 : part, :] = few[0 : part // 2, LANES:WIDE]
    norm_ref[...] = few[part // 2 : part // 2 + 8, :]


class Links:
    def __init__(self, n_grp, n_ctx):
        self.n_grp, self.n_ctx, self.n_pair = n_grp, n_ctx, n_ctx // 2
        self.small = (n_grp, n_ctx) == (4, 8)
        self.ctx = lax.axis_index("ctx")
        self.grp = lax.axis_index("grp")
        self.core = self.ctx % 2
        self.chip = self.ctx // 2
        self.groups = [[2 * z + c for z in range(self.n_pair)] for c in range(2)]

    def swap(self, value):
        return lax.ppermute(value, "ctx", [(i, i ^ 1) for i in range(self.n_ctx)])

    def permute(self, value, target):
        pairs = []
        for g in range(self.n_grp):
            for i in range(self.n_ctx):
                y, x, z, c = target(g // 2, g % 2, i // 2, i % 2)
                pairs.append((g * self.n_ctx + i, (2 * y + x) * self.n_ctx + 2 * z + c))
        return lax.ppermute(value, ("grp", "ctx"), pairs)

    def cross(self, value, stage):
        return self.permute(
            value, lambda y, x, z, c: (y, 1 - x, z, c) if c == stage else (1 - y, x, z, c)
        )

    def bit(self, stage):
        y, x = self.grp // 2, self.grp % 2
        return jnp.where(self.core == stage, x, y)

    def flip(self, value, bit):
        return self.permute(value, lambda y, x, z, c: (y, x, z ^ bit, c))

    def reduce(self, parts):
        moved = lax.all_to_all(parts, "ctx", 0, 0, axis_index_groups=self.groups)
        return lax.psum(jnp.sum(moved.astype(F32), 0).astype(BF), "grp")


def add(keep, got):
    return keep.astype(F32) + got.astype(F32)


def low(value):
    return value.astype(BF)


def shards_small(
    layer_input, block_table, ln1_gain, ln1_bias, ln2_gain, ln2_bias,
    w_query, w_keyval, w_out, w_up, w_down, cotangent, *, n_grp, n_ctx,
):
    links = Links(n_grp, n_ctx)
    core, chip, n_pair = links.core, links.chip, links.n_pair
    rows, width = layer_input.shape
    lanes = w_keyval.shape[1]
    size = lanes // 2
    hidden = w_up.shape[1]
    group_len = block_table.shape[1] * BLK
    part, part_hidden = width // n_ctx, hidden // n_ctx
    half = width // 2
    per_chip = 2 * rows // BLK
    table = block_table[0]
    sc = jnp.stack([core, chip, links.bit(0), links.bit(1)]).astype(jnp.int32)
    g1, c1, g2, c2 = (v.reshape(1, width) for v in (ln1_gain, ln1_bias, ln2_gain, ln2_bias))

    x_other, g_other = links.swap(layer_input), links.swap(cotangent)
    own_slots = lax.dynamic_slice_in_dim(table, chip * per_chip, per_chip).reshape(2, -1)
    slots = jnp.concatenate([own_slots[core], own_slots[1 - core]])
    canon = (slots[:, None] * BLK + jnp.arange(BLK, dtype=jnp.int32)[None, :]).reshape(2 * rows)
    prompt_len = group_len // 2
    cont_span = min(CONT, prompt_len)
    position = jnp.where(
        canon < prompt_len, canon, prompt_len + (canon - prompt_len) % cont_span
    )
    cosine, sine = rope_tables(position)

    h_one, h_two, g_two, kv_low = call(
        prologue_kernel,
        "prologue",
        [shape((2 * rows, width), BF)] * 3 + [shape((2 * rows, lanes), BF)],
        [VM] * 11,
        [VM] * 4,
        [],
        16,
    )(sc, layer_input, x_other, cotangent, g_other, g1, c1, g2, c2, w_keyval, cosine, sine)

    kv_got = links.flip(kv_low, 1)
    ffn = functools.partial(
        ffn_gradients, sc, w_up=w_up, w_down=w_down, part=part_hidden, n_pair=n_pair
    )
    act_0, dup_0, a_send, a_keep = ffn(h_two, g_two, n=0)
    a_got = links.flip(a_send, 1)
    kv_near = jnp.concatenate([kv_low, kv_got], 0)
    kv_far = links.flip(kv_near, 2)
    act_1, dup_1, b_send = ffn(tie(h_two, a_keep, kv_near), g_two, n=1)
    b_got = links.cross(b_send, 0)
    act_2, dup_2, b_keep = ffn(tie(h_two, b_send), g_two, n=2)

    q_t, do_t = call(
        functools.partial(project_kernel, size=size),
        "project",
        [shape((half, 2 * rows), BF), shape((half, 2 * rows), F32)],
        [VM] * 4 + [HBM] * 2,
        [VM] * 2,
        [
            pltpu.VMEM((width, half), BF),
            pltpu.VMEM((half, width), BF),
            pltpu.SemaphoreType.DMA((2,)),
        ],
        16,
    )(sc, tie(h_one, b_keep), g_two, cosine, sine, w_query, w_out)

    place = jnp.stack([chip * per_chip, core * (rows // BLK), chip, 0 * chip]).astype(jnp.int32)
    count = rows // BLK
    attend = functools.partial(
        attention, table, place, do_t=do_t, cosine=cosine, sine=sine, kvs=(kv_near, kv_far),
        count=count, per_chip=per_chip, split=True,
    )
    mix_0, dq_0, carried = attend(q_t=q_t, carried=None, start=0, last_call=False)
    mix_0_got = links.swap(mix_0)
    a_sum = add(a_keep, tie(a_got, carried))
    a_got_2 = links.flip(low(a_sum[1]), 2)
    b_sum = add(b_keep, tie(b_got, carried))
    b_got_2 = links.cross(low(b_sum[1]), 1)
    mix_1, dq_1, dkv_send, dkv_keep = attend(
        q_t=tie(q_t, a_got, b_got), carried=carried, start=count, last_call=True
    )

    dkv_got = links.swap(dkv_send)
    mix_1_got = links.swap(mix_1)
    late_send, late_keep = late_gradients(
        sc, h_one, (dq_0, dq_1), (mix_0, mix_1), (mix_0_got, mix_1_got), g_two, n_pair
    )
    late_got = links.cross(late_send, 0)
    dkv_sum = add(dkv_keep, dkv_got)
    dkv_got_2 = links.flip(low(dkv_sum[1]), 1)
    b_sum = add(b_sum[0], tie(b_got_2, late_send))
    b_got_3 = links.flip(low(b_sum[1]), 1)

    w_specs = [HBM] * 2
    out_own, out_send = call(
        functools.partial(out_kernel, part=part_hidden, n_pair=n_pair),
        "outputs",
        [shape((rows, width), F32), shape((rows, width), BF)],
        [VM] * 6 + w_specs,
        [VM] * 2,
        [
            pltpu.VMEM((3, n_pair * LANES, width), BF),
            pltpu.VMEM((half, width), BF),
            pltpu.SemaphoreType.DMA((2,)),
        ],
        16,
    )(sc, act_0, act_1, tie(act_2, late_send, dkv_got), mix_0, mix_1, layer_input, w_down, w_out)
    out_got = links.swap(out_send)
    dkv_sum = add(dkv_sum[0], tie(dkv_got_2, out_send))
    dkv_got_3 = links.flip(low(dkv_sum[1]), 2)
    hat_own, hat_send, sums = call(
        functools.partial(hat_kernel, part=part_hidden, n_pair=n_pair),
        "norms",
        [shape((rows, width), F32), shape((rows, width), BF), shape((8, width), F32)],
        [VM] * 9 + w_specs,
        [VM] * 3,
        [
            pltpu.VMEM((3, width, n_pair * LANES), BF),
            pltpu.VMEM((width, half), BF),
            pltpu.SemaphoreType.DMA((2,)),
        ],
        24,
    )(
        sc, dup_0, dup_1, tie(dup_2, out_send, dkv_got_2), dq_0, dq_1, layer_input, x_other, g1, g2,
        w_up, w_query,
    )
    hat_got = links.swap(hat_send)
    layer_output = low(out_own + out_got.astype(F32))

    late_sum = add(late_keep, tie(late_got, hat_send))
    late_got_2 = links.cross(low(late_sum[1]), 1)
    b_sum = add(b_sum[0], tie(b_got_3, hat_send))
    b_got_4 = links.flip(low(b_sum[1]), 2)
    a_sum = add(a_sum[0], tie(a_got_2, hat_send))

    few = part // 2 + 8
    in_grad, few_send, few_keep = call(
        functools.partial(last_kernel, n_pair=n_pair),
        "last",
        [shape((rows, width), F32)] + [shape((2, 2 * few, 2 * lanes), BF)] * 2,
        [VM] * 12,
        [VM] * 3,
        [],
        16,
    )(
        sc, dkv_sum[0], dkv_got_3, cosine, sine, w_keyval, h_one, layer_input, g1, hat_own, hat_got,
        sums, cotangent,
    )

    late_sum = add(late_sum[0], tie(late_got_2, few_send))
    quarter = late_sum.shape[2]
    last = jnp.concatenate([late_sum, jnp.stack([few_keep, few_send]).astype(F32)], 2)
    last_got = links.flip(low(last[1]), 1)
    early = jnp.concatenate([low(add(b_sum[0], tie(b_got_4, last_got))), low(a_sum)], 0)
    block = early.shape[0] // 3
    early_got = links.cross(early, 1)
    last = add(last[0], last_got)
    last_got = links.flip(low(last[1]), 2)
    early = jnp.concatenate(
        [early[:block], early_got[:block], low(add(early[block:], early_got[block:]))], 0
    )
    early_got = links.cross(early, 0)
    last = low(add(last[0], last_got))
    last_got = links.cross(last, 1)
    last = jnp.concatenate(
        [last[:quarter], last_got[:quarter], low(add(last[quarter:], last_got[quarter:]))], 0
    )
    last_got = links.cross(last, 0)
    total_down = call(
        functools.partial(down_kernel, width=width),
        "down", shape((part_hidden, width), F32), [VM] * 2, VM, [], 8,
    )(sc, early, early_got)
    size_out = 9 * part + few
    other, own = call(
        functools.partial(pack_kernel, width=width, part=part, quarter=quarter),
        "pack", [shape((size_out, WIDE), BF)] * 2, [VM] * 4, [VM] * 2, [], 8,
    )(sc, early, early_got, last, last_got)
    got = links.swap(other)
    total_up, total_query, total_out, total_kv, norm = call(
        functools.partial(final_kernel, part=part, n_pair=n_pair),
        "final",
        [
            shape((part, hidden), F32),
            shape((part, width), F32),
            shape((part, width), F32),
            shape((part, lanes), F32),
            shape((8, WIDE), F32),
        ],
        [VM] * 2,
        [VM] * 5,
        [],
        8,
    )(sc, own, got)
    norms = [norm[n, :part] for n in range(4)]
    return (layer_output, in_grad, *norms, total_query, total_kv, total_out, total_up, total_down)


def rotate_rows(values, cosine, sine):
    return turn(values.T, cosine, sine).T


def shards(
    layer_input, block_table, ln1_gain, ln1_bias, ln2_gain, ln2_bias,
    w_query, w_keyval, w_out, w_up, w_down, cotangent, *, n_grp, n_ctx,
):
    links = Links(n_grp, n_ctx)
    core, chip, n_pair = links.core, links.chip, links.n_pair
    rows, width = layer_input.shape
    size = w_keyval.shape[1] // 2
    hidden = w_up.shape[1]
    group_len = block_table.shape[1] * BLK
    part_rows, part_hidden = width // n_ctx, hidden // n_ctx
    half_width, half_hidden = width // 2, hidden // 2
    per_chip = 2 * rows // BLK
    table = block_table[0]

    def both(own, other):
        return jnp.concatenate(
            [jnp.where(core == 0, own, other), jnp.where(core == 0, other, own)], 0
        )

    def mine(value, own_core):
        return lax.dynamic_slice_in_dim(value, own_core * rows, rows, 0)

    x_two = both(layer_input, links.swap(layer_input))
    g_two = both(cotangent, links.swap(cotangent))
    canon = (
        lax.dynamic_slice_in_dim(table, chip * per_chip, per_chip)[:, None] * BLK
        + jnp.arange(BLK, dtype=jnp.int32)[None, :]
    ).reshape(2 * rows)
    prompt_len = group_len // 2
    cont_span = min(CONT, prompt_len)
    position = jnp.where(
        canon < prompt_len, canon, prompt_len + (canon - prompt_len) % cont_span
    )
    cosine, sine = rope_tables(position)
    gain_one, gain_two = ln1_gain.astype(F32), ln2_gain.astype(F32)
    hat, scale = normed(x_two.astype(F32))
    h_one = low(hat * gain_one + ln1_bias.astype(F32))
    h_two = low(hat * gain_two + ln2_bias.astype(F32))
    kv_raw = dot(h_one, w_keyval)
    kv_low = low(
        jnp.concatenate([rotate_rows(kv_raw[:, :size], cosine, sine), kv_raw[:, size:]], -1)
    )
    kv_all = lax.all_gather(kv_low, "ctx", axis=0, axis_index_groups=links.groups, tiled=True)

    up_half = lax.dynamic_index_in_dim(
        w_up.reshape(width, n_pair, 2, part_hidden), core, 2, False
    ).reshape(width, half_hidden)
    down_half = lax.dynamic_index_in_dim(
        w_down.reshape(n_pair, 2, part_hidden, width), core, 1, False
    ).reshape(half_hidden, width)
    act, slope = gelu_parts(dot(h_two, up_half))
    act = low(act)
    grad_down = low(dot(act, g_two, ((0,), (0,))))
    total_down = links.reduce(grad_down.reshape(n_pair, part_hidden, width))
    grad_up = low(dot(g_two, down_half, ((1,), (1,))) * slope)
    grad_up_w = low(dot(h_two, grad_up, ((0,), (0,))))
    total_up = links.reduce(grad_up_w.reshape(n_pair, 2 * part_rows, half_hidden))

    query_half = lax.dynamic_slice_in_dim(w_query, core * half_width, half_width, 1)
    out_half = lax.dynamic_slice_in_dim(w_out, core * half_width, half_width, 0)
    q_raw = dot(query_half, h_one, ((0,), (1,))) * (0.125 * LOG2E)
    q_t = low(
        jax.vmap(turn, (0, None, None))(q_raw.reshape(-1, size, 2 * rows), cosine, sine)
    ).reshape(half_width, 2 * rows)
    do_t = dot(out_half, g_two, ((1,), (1,)))
    place = jnp.stack([chip * per_chip, 0 * chip, 0 * chip, 0 * chip]).astype(jnp.int32)
    mix_t, dq_t, dkv_part = attention(
        table, place, q_t, do_t, cosine, sine, (kv_all,), None, 0, per_chip, per_chip, True, False
    )

    dkv_part = dkv_part.reshape(n_pair, 2, rows, 2 * size)
    dkv_own = lax.dynamic_index_in_dim(dkv_part, core, 1, False)
    dkv_got = links.swap(lax.dynamic_index_in_dim(dkv_part, 1 - core, 1, False))
    moved = lax.all_to_all(
        low(add(dkv_own, dkv_got)), "ctx", 0, 0, axis_index_groups=links.groups
    )
    dkv = jnp.sum(moved.astype(F32), 0)
    cos_own = lax.dynamic_slice_in_dim(cosine, core * rows, rows, 1)
    sin_own = lax.dynamic_slice_in_dim(sine, core * rows, rows, 1)
    dkv_low = low(
        jnp.concatenate([rotate_rows(dkv[:, :size], cos_own, -sin_own), dkv[:, size:]], -1)
    )

    mix_got = links.swap(mix_t)
    mix_all = jnp.concatenate(
        [jnp.where(core == 0, mix_t, mix_got), jnp.where(core == 0, mix_got, mix_t)], 0
    )
    g_half = lax.dynamic_slice_in_dim(g_two, core * half_width, half_width, 1)
    grad_q_w = low(dot(h_one, dq_t, ((0,), (1,))))
    grad_out_w = low(dot(mix_all, g_half))
    late = jnp.concatenate([grad_q_w, grad_out_w], 1).reshape(n_pair, 2 * part_rows, width)
    total_late = links.reduce(late)

    out_part = dot(act, down_half) + dot(mix_t, out_half, ((0,), (0,)))
    out_got = links.swap(low(mine(out_part, 1 - core)))
    layer_output = low(layer_input.astype(F32) + mine(out_part, core) + out_got.astype(F32))

    d_two = dot(grad_up, up_half, ((1,), (1,)))
    d_one = dot(dq_t, query_half, ((0,), (1,)))
    d_kv = dot(dkv_low, w_keyval, ((1,), (1,)))
    row_core = lax.broadcasted_iota(jnp.int32, (2 * rows, 1), 0) // rows
    d_one = d_one + jnp.where(row_core == core, jnp.concatenate([d_kv, d_kv], 0), 0.0)
    sums = jnp.stack([jnp.sum(v, 0) for v in (d_one * hat, d_one, d_two * hat, d_two)])
    d_hat = d_one * gain_one + d_two * gain_two
    hat_got = links.swap(low(mine(d_hat, 1 - core)))
    d_hat = mine(d_hat, core) + hat_got.astype(F32)
    hat_own = mine(hat, core)
    in_grad = cotangent.astype(F32) + mine(scale, core) * (
        d_hat
        - jnp.mean(d_hat, -1, keepdims=True)
        - hat_own * jnp.mean(d_hat * hat_own, -1, keepdims=True)
    )

    grad_kv_w = dot(mine(h_one, core), dkv_low, ((0,), (0,)))
    sum_rows = sums.reshape(4, n_pair, 2, part_rows).transpose(1, 2, 0, 3)
    sum_rows = jnp.pad(sum_rows, ((0, 0), (0, 0), (0, 0), (0, 2 * size - part_rows)))
    few = jnp.concatenate([grad_kv_w.reshape(n_pair, 2, part_rows, 2 * size), sum_rows], 2)
    few = links.reduce(low(few).reshape(n_pair, 2 * (part_rows + 4), 2 * size))
    few = few.reshape(2, part_rows + 4, 2 * size)
    few_got = links.swap(lax.dynamic_index_in_dim(few, 1 - core, 0, False))
    few = add(lax.dynamic_index_in_dim(few, core, 0, False), few_got)

    halves = jnp.concatenate(
        [total_up.reshape(2, part_rows, half_hidden), total_late.reshape(2, part_rows, width)], -1
    )
    own = lax.dynamic_index_in_dim(halves, core, 0, False)
    got = links.swap(lax.dynamic_index_in_dim(halves, 1 - core, 0, False))
    sides = jnp.stack([jnp.where(core == 0, own, got), jnp.where(core == 0, got, own)]).astype(F32)
    ups = sides[:, :, :half_hidden].reshape(2, part_rows, n_pair, part_hidden)
    total_up = ups.transpose(1, 2, 0, 3).reshape(part_rows, hidden)
    lates = sides[:, :, half_hidden:]
    total_query = lates[:, :, :half_width].transpose(1, 0, 2).reshape(part_rows, width)
    total_out = lates[:, :, half_width:].transpose(1, 0, 2).reshape(part_rows, width)
    norms = [few[part_rows + n, :part_rows] for n in range(4)]
    total_kv = few[:part_rows]
    total_down = total_down.astype(F32)
    return (layer_output, in_grad, *norms, total_query, total_kv, total_out, total_up, total_down)


def solution(mesh):
    n_grp, n_ctx = mesh.shape["grp"], mesh.shape["ctx"]
    body = shards_small if (n_grp, n_ctx) == (4, 8) else shards
    return jax.shard_map(
        functools.partial(body, n_grp=n_grp, n_ctx=n_ctx),
        mesh=mesh,
        in_specs=(P(("grp", "ctx"), None), P("grp", None))
        + (P(),) * 9
        + (P(("grp", "ctx"), None),),
        out_specs=(P(("grp", "ctx"), None),) * 2 + (P("ctx"),) * 4 + (P("ctx", None),) * 5,
        check_vma=False,
    )
```

time: 210 us -> 182 us (0.87)
  Pallas kernels: 21.1 us -> 65.5 us
  matrix products: 23.5 us -> 0 us
  starting transfers between devices: 54.8 us -> 34.8 us
  other arithmetic: 19.1 us -> 4.98 us
  local copies, waits for them, and re-layouts: 29.9 us -> 21.8 us
  waiting for transfers between devices: 57.5 us -> 51.3 us
    pallas_call x0 -> x12, Pallas kernels: none -> 36.4 us  [the longest x3 15.2 us: ffn_gradients(): call(functools.partial(ffn_kernel, n=n, part=part, n_pair=n_pair), 'ffn_g...]
    ppermute x33 -> x18, starting transfers between devices: 53.1 us -> 29 us  [permute(): return lax.ppermute(value, ('grp', 'ctx'), pairs)]
    dot_general x15 -> x0, matrix products: 23.5 us -> none  [dot(): lax.dot_general(left, right, (dims, ((), ())), preferred_element_type=F32)]
    convert_element_type x20 -> x8, other arithmetic: 9.82 us -> 1.2 us  [the longest x7 1.17 us: low(): return value.astype(BF)]
    pallas_call x1 -> x2, Pallas kernels: 21.1 us -> 29.1 us  [attention(): pl.pallas_call(functools.partial(attn_kernel, blocks=blocks, heads=heads,...]
    ppermute x33 -> x18, waiting for transfers between devices: 57.4 us -> 51.2 us  [permute(): return lax.ppermute(value, ('grp', 'ctx'), pairs)]
    unnamed x83 -> x75, local copies, waits for them, and re-layouts: 11.6 us -> 17.4 us
    dynamic_slice x11 -> x1, local copies, waits for them, and re-layouts: 6.38 us -> 0.75 us  [shards_small(): lax.dynamic_slice_in_dim(table, chip * per_chip, per_chip).reshape(2, -1)]
  transfers between devices with their start and end apart: 41 -> 26, of which waited for: 20 -> 10; matrix products, arithmetic and copies ran while one was open for 32% -> 5% of each run, Pallas kernels for 10% -> 31%
where the time goes in v2:
time: 182 us; the launch traced here: 180 us
  Pallas kernels  65.5 us (36%)
  waiting for transfers between devices  51.3 us (28%)
  starting transfers between devices  34.8 us (19%)
  local copies, waits for them, and re-layouts  21.8 us (12%)
  other arithmetic  4.98 us (3%)
    ppermute x18, waiting for transfers between devices, permute(): return lax.ppermute(value, ('grp', 'ctx'), pairs)  51.2 us
    pallas_call x2, Pallas kernels, attention(): pl.pallas_call(functools.partial(attn_kernel, blocks=blocks, heads=heads,...  29.1 us
    ppermute x18, starting transfers between devices, permute(): return lax.ppermute(value, ('grp', 'ctx'), pairs)  29 us
    unnamed x75, local copies, waits for them, and re-layouts  17.4 us
    pallas_call x3, Pallas kernels, ffn_gradients(): call(functools.partial(ffn_kernel, n=n, part=part, n_pair=n_pair), 'ffn_g...  15.2 us
    ppermute x8, starting transfers between devices, swap(): return lax.ppermute(value, 'ctx', [(i, i ^ 1) for i in range(self.n_ctx)])  5.74 us
    pallas_call x1, Pallas kernels, shards_small(): call(functools.partial(out_kernel, part=part_hidden, n_pair=n_pair), 'out...  5.57 us
  transfers between devices with their start and end apart: 26, of which 10 were waited for; matrix products, arithmetic and copies ran while one was open for 5% of the time, Pallas kernels for 31%

profile of v2, /device:TPU:0, one launch (start us, length us, event | category | flops | bytes accessed | tf_op | source)
XLA Modules:
  0.0 179.7 jit_solution(3358404151996187363)
XLA Ops:
  9.8 3.1 %collective-permute-start.2 = (bf16[512,128]{1,0:T(8,128)(2,1)S(1)}, bf16[512,128]{1,0:T(8,128)(2,1)S(1)}, u32[]{:S(2)}, u32[]{:S(2)}) collective-permute-start(bf16[512,128]{1,0:T(8,128)(2,1)S(1)} %get-tuple-element.70), channel_id=1, source_target_pairs={{0,2},{1,3},{2,0},{3,1},{4,6},{5,7},{6,4},{7,5},{8,10},{9,11},{10,... | collective-permute-start | bytes 393224 | tf_op jit(solution)/shard_map/ppermute | solution.py:709
  17.5 4.7 %ffn_gradients.3 = (bf16[512,512]{1,0:T(8,128)(2,1)S(1)}, bf16[512,512]{1,0:T(8,128)(2,1)S(1)}, bf16[2,768,256]{2,1,0:T(8,128)(2,1)S(1)}, bf16[2,768,256]{2,1,0:T(8,128)(2,1)S(1)}) custom-call(s32[4]{0:T(128)S(1)} %pad_add_fusion.sc, bf16[512,768]{1,0:T(8,128)(2,1)S(1)} %get-tuple-element.74.h_ref, bf16[512,768]{1,0:T(8,128)(2,1)S(1)} %get-tuple-element.67.g_ref, ...), custom_call_target="tpu_custom_call" | custom-call | flops 1610612736 | bytes 8053063 | tf_op jit(solution)/shard_map/ffn_gradients/pallas_call | solution.py:421
  24.8 5.8 %ffn_gradients.4 = (bf16[512,512]{1,0:T(8,128)(2,1)S(1)}, bf16[512,512]{1,0:T(8,128)(2,1)S(1)}, bf16[2,2,2,384,256]{4,3,2,1,0:T(8,128)(2,1)}) custom-call(s32[4]{0:T(128)S(1)} %pad_add_fusion.sc, bf16[512,768]{1,0:T(8,128)(2,1)S(1)} %get-tuple-element.74.h_ref, bf16[512,768]{1,0:T(8,128)(2,1)S(1)} %get-tuple-element.67.g_ref, ...), custom_call_target="tpu_custom_call" | custom-call | flops 1610612736 | bytes 8053063 | tf_op jit(solution)/shard_map/ffn_gradients/pallas_call | solution.py:421
  34.2 2.6 %collective-permute-start.3 = (bf16[1024,128]{1,0:T(8,128)(2,1)}, bf16[1024,128]{1,0:T(8,128)(2,1)S(1)}, u32[]{:S(2)}, u32[]{:S(2)}) collective-permute-start(bf16[1024,128]{1,0:T(8,128)(2,1)} %copy-done.25), channel_id=1, source_target_pairs={{0,4},{1,5},{2,6},{3,7},{4,0},{5,1},{6,2},{7,3},{8,12},{9,13},{10,... | collective-permute-start | bytes 786440 | tf_op jit(solution)/shard_map/ppermute | solution.py:709
  42.8 4.7 %ffn_gradients.5 = (bf16[512,512]{1,0:T(8,128)(2,1)S(1)}, bf16[512,512]{1,0:T(8,128)(2,1)S(1)}, bf16[2,2,2,384,256]{4,3,2,1,0:T(8,128)(2,1)S(1)}) custom-call(s32[4]{0:T(128)S(1)} %copy-done.23, bf16[512,768]{1,0:T(8,128)(2,1)S(1)} %get-tuple-element.74.h_ref, bf16[512,768]{1,0:T(8,128)(2,1)S(1)} %get-tuple-element.67.g_ref, ...), custom_call_target="tpu_custom_call" | custom-call | flops 1610612736 | bytes 8053063 | tf_op jit(solution)/shard_map/ffn_gradients/pallas_call | solution.py:421
  49.5 7.1 %collective-permute-done.3.refs_5_ = bf16[1024,128]{1,0:T(8,128)(2,1)S(1)} collective-permute-done((bf16[1024,128]{1,0:T(8,128)(2,1)}, bf16[1024,128]{1,0:T(8,128)(2,1)S(1)}, u32[]{:S(2)}, u32[]{:S(2)}) %collective-permute-start.3) | collective-permute-done | bytes 262176 | tf_op jit(solution)/shard_map/ppermute | solution.py:709
  56.6 11.7 %attention.2 = (bf16[384,256]{1,0:T(8,128)(2,1)S(1)}, bf16[384,256]{1,0:T(8,128)(2,1)S(1)}, f32[2048,128]{1,0:T(8,128)S(1)}) custom-call(s32[16]{0:T(128)S(1)} %bitcast.92, s32[4]{0:T(128)S(1)} %get-tuple-element.122.place, bf16[384,512]{1,0:T(8,128)(2,1)S(1)} %get-tuple-element.83.refs_0_, f32[384,512]{1,0:T(8,128)S(1)} %get-tuple-element.80.refs_1_, ...), custom_call_target="tpu_custom_call" | custom-call | flops 4831838208 | bytes 1572864 | tf_op jit(solution)/shard_map/attention/pallas_call | solution.py:258
  68.3 4.4 %collective-permute-start.6 = (bf16[384,256]{1,0:T(8,128)(2,1)S(1)}, bf16[384,256]{1,0:T(8,128)(2,1)S(1)}, u32[]{:S(2)}, u32[]{:S(2)}) collective-permute-start(bf16[384,256]{1,0:T(8,128)(2,1)S(1)} %get-tuple-element.86.mix0), channel_id=1, source_target_pairs={{0,1},{1,0},{2,3},{3,2},{4,5},{5,4},{6,7},{7,6},{8,9},{9,8},{10,11... | collective-permute-start | bytes 589832 | tf_op jit(solution)/shard_map/ppermute | solution.py:701
  72.9 17.5 %attention.3 = (bf16[384,256]{1,0:T(8,128)(2,1)S(1)}, bf16[384,256]{1,0:T(8,128)(2,1)S(1)}, bf16[2,2,256,128]{3,2,1,0:T(8,128)(2,1)S(1)}, bf16[2,2,256,128]{3,2,1,0:T(8,128)(2,1)S(1)}) custom-call(s32[16]{0:T(128)S(1)} %bitcast.93, s32[4]{0:T(128)S(1)} %get-tuple-element.121.place, bf16[384,512]{1,0:T(8,128)(2,1)S(1)} %get-tuple-element.83.refs_0_, ...), custom_call_target="tpu_custom_call" | custom-call | flops 4831838208 | bytes 1572864 | tf_op jit(solution)/shard_map/attention/pallas_call | solution.py:258
  93.0 6.0 %collective-permute-start.10 = (bf16[2,256,128]{2,1,0:T(8,128)(2,1)S(1)}, bf16[2,256,128]{2,1,0:T(8,128)(2,1)S(1)}, u32[]{:S(2)}, u32[]{:S(2)}) collective-permute-start(bf16[2,256,128]{2,1,0:T(8,128)(2,1)S(1)} %fusion.20), channel_id=1, source_target_pairs={{0,2},{1,3},{2,0},{3,1},{4,6},{5,7},{6,4},{7,5},{8,10},{9,11},{10,... | collective-permute-start | bytes 393224 | tf_op jit(solution)/shard_map/ppermute | solution.py:709
  99.0 2.4 %collective-permute-start.19 = (bf16[768,256]{1,0:T(8,128)(2,1)S(1)}, bf16[768,256]{1,0:T(8,128)(2,1)S(1)}, u32[]{:S(2)}, u32[]{:S(2)}) collective-permute-start(bf16[768,256]{1,0:T(8,128)(2,1)S(1)} %fusion.11), channel_id=1, source_target_pairs={{0,4},{1,5},{2,6},{3,7},{4,0},{5,1},{6,2},{7,3},{8,12},{9,13},{10,... | collective-permute-start | bytes 1179656 | tf_op jit(solution)/shard_map/ppermute | solution.py:709
  103.6 5.6 %outputs.1 = (f32[256,768]{1,0:T(8,128)S(1)}, bf16[256,768]{1,0:T(8,128)(2,1)S(1)}) custom-call(s32[4]{0:T(128)S(1)} %copy-done.24, bf16[512,512]{1,0:T(8,128)(2,1)S(1)} %copy-done.17, bf16[512,512]{1,0:T(8,128)(2,1)S(1)} %copy-done.19, bf16[512,512]{1,0:T(8,128)(2,1)S(1)} %get-tuple-element.90.a2, bf16[384,256]{1,0:T(8,128)(2,1)S(1)} %get-tuple-element.86.mix0, ...), custom_call_target="tpu_custom_call" | custom-call | flops 1000000 | bytes 5000 | tf_op jit(solution)/shard_map/outputs/pallas_call | solution.py:829
  109.2 3.4 %norms.1 = (f32[256,768]{1,0:T(8,128)S(1)}, bf16[256,768]{1,0:T(8,128)(2,1)S(1)}, f32[8,768]{1,0:T(8,128)S(1)}) custom-call(s32[4]{0:T(128)S(1)} %copy-done.24, bf16[512,512]{1,0:T(8,128)(2,1)S(1)} %copy-done.13, bf16[512,512]{1,0:T(8,128)(2,1)S(1)} %copy-done.15, bf16[512,512]{1,0:T(8,128)(2,1)S(1)} %get-tuple-element.98.d2, ...), custom_call_target="tpu_custom_call" | custom-call | flops 1000000 | bytes 5000 | tf_op jit(solution)/shard_map/norms/pallas_call | solution.py:845
  113.4 7.9 %collective-permute-done.19 = bf16[768,256]{1,0:T(8,128)(2,1)S(1)} collective-permute-done((bf16[768,256]{1,0:T(8,128)(2,1)S(1)}, bf16[768,256]{1,0:T(8,128)(2,1)S(1)}, u32[]{:S(2)}, u32[]{:S(2)}) %collective-permute-start.19) | collective-permute-done | bytes 393248 | tf_op jit(solution)/shard_map/ppermute | solution.py:709
  122.5 2.5 %last.1 = (f32[256,768]{1,0:T(8,128)}, bf16[2,112,256]{2,1,0:T(8,128)(2,1)S(1)}, bf16[2,112,256]{2,1,0:T(8,128)(2,1)S(1)}) custom-call(s32[4]{0:T(128)S(1)} %copy-done.24, f32[256,128]{1,0:T(8,128)S(1)} %slice_bitcast_fusion.7.dkv_a, bf16[256,128]{1,0:T(8,128)(2,1)S(1)} %collective-permute-done.11.dkv_b, f32[8,512]{1,0:T(8,128)S(1)} %copy-done.21, ...), custom_call_target="tpu_custom_call" | custom-call | flops 1000000 | bytes 5000 | tf_op jit(solution)/shard_map/last/pallas_call | solution.py:871
  125.1 3.4 %collective-permute-done.17 = bf16[2,2,144,256]{3,2,1,0:T(8,128)(2,1)S(1)} collective-permute-done((bf16[2,2,144,256]{3,2,1,0:T(8,128)(2,1)S(1)}, bf16[2,2,144,256]{3,2,1,0:T(8,128)(2,1)S(1)}, u32[]{:S(2)}, u32[]{:S(2)}) %collective-permute-start.17) | collective-permute-done | bytes 294944 | tf_op jit(solution)/shard_map/ppermute | solution.py:709
  128.7 5.4 %collective-permute-done.14 = bf16[2,384,256]{2,1,0:T(8,128)(2,1)S(1)} collective-permute-done((bf16[2,384,256]{2,1,0:T(8,128)(2,1)S(1)}, bf16[2,384,256]{2,1,0:T(8,128)(2,1)S(1)}, u32[]{:S(2)}, u32[]{:S(2)}) %collective-permute-start.14) | collective-permute-done | bytes 393248 | tf_op jit(solution)/shard_map/ppermute | solution.py:709
  136.6 4.4 %collective-permute-done.18 = bf16[2,256,256]{2,1,0:T(8,128)(2,1)S(1)} collective-permute-done((bf16[2,256,256]{2,1,0:T(8,128)(2,1)S(1)}, bf16[2,256,256]{2,1,0:T(8,128)(2,1)S(1)}, u32[]{:S(2)}, u32[]{:S(2)}) %collective-permute-start.18) | collective-permute-done | bytes 262176 | tf_op jit(solution)/shard_map/ppermute | solution.py:709
  141.0 2.7 %collective-permute-done.15 = bf16[384,256]{1,0:T(8,128)(2,1)S(1)} collective-permute-done((bf16[384,256]{1,0:T(8,128)(2,1)S(1)}, bf16[384,256]{1,0:T(8,128)(2,1)S(1)}, u32[]{:S(2)}, u32[]{:S(2)}) %collective-permute-start.15) | collective-permute-done | bytes 196640 | tf_op jit(solution)/shard_map/ppermute | solution.py:709
  143.8 4.9 %collective-permute-start.20 = (bf16[1152,256]{1,0:T(8,128)(2,1)S(1)}, bf16[1152,256]{1,0:T(8,128)(2,1)S(1)}, u32[]{:S(2)}, u32[]{:S(2)}) collective-permute-start(bf16[1152,256]{1,0:T(8,128)(2,1)S(1)} %pad_maximum_fusion.1), channel_id=1, source_target_pairs={{0,16},{1,9},{2,18},{3,11},{4,20},{5,13},{6,22},{7,15},{8,24},{9,1... | collective-permute-start | bytes 1769480 | tf_op jit(solution)/shard_map/ppermute | solution.py:709
  148.8 10.7 %collective-permute-done.20 = bf16[1152,256]{1,0:T(8,128)(2,1)S(1)} collective-permute-done((bf16[1152,256]{1,0:T(8,128)(2,1)S(1)}, bf16[1152,256]{1,0:T(8,128)(2,1)S(1)}, u32[]{:S(2)}, u32[]{:S(2)}) %collective-permute-start.20) | collective-permute-done | bytes 589856 | tf_op jit(solution)/shard_map/ppermute | solution.py:709
  159.8 2.5 %collective-permute-start.23 = (bf16[256,256]{1,0:T(8,128)(2,1)S(1)}, bf16[256,256]{1,0:T(8,128)(2,1)S(1)}, u32[]{:S(2)}, u32[]{:S(2)}) collective-permute-start(bf16[256,256]{1,0:T(8,128)(2,1)S(1)} %fusion.17), channel_id=1, source_target_pairs={{0,16},{1,9},{2,18},{3,11},{4,20},{5,13},{6,22},{7,15},{8,24},{9,1... | collective-permute-start | bytes 393224 | tf_op jit(solution)/shard_map/ppermute | solution.py:709
  162.4 4.3 %collective-permute-done.23 = bf16[256,256]{1,0:T(8,128)(2,1)S(1)} collective-permute-done((bf16[256,256]{1,0:T(8,128)(2,1)S(1)}, bf16[256,256]{1,0:T(8,128)(2,1)S(1)}, u32[]{:S(2)}, u32[]{:S(2)}) %collective-permute-start.23) | collective-permute-done | bytes 131104 | tf_op jit(solution)/shard_map/ppermute | solution.py:709
  168.7 5.2 %collective-permute-done.24.last_got = bf16[400,256]{1,0:T(8,128)(2,1)S(1)} collective-permute-done((bf16[400,256]{1,0:T(8,128)(2,1)S(1)}, bf16[400,256]{1,0:T(8,128)(2,1)S(1)}, u32[]{:S(2)}, u32[]{:S(2)}) %collective-permute-start.24) | collective-permute-done | bytes 204832 | tf_op jit(solution)/shard_map/ppermute | solution.py:709
  (166 shorter events, 45.6 us)
Async XLA Ops:
  0.6 4.6 %collective-permute-start = (bf16[256,768]{1,0:T(8,128)(2,1)}, bf16[256,768]{1,0:T(8,128)(2,1)S(1)}, u32[]{:S(2)}, u32[]{:S(2)}) collective-permute-start(bf16[256,768]{1,0:T(8,128)(2,1)} %x_ref.3), channel_id=1, source_target_pairs={{0,1},{1,0},{2,3},{3,2},{4,5},{5,4},{6,7},{7,6},{8,9},{9,8},{10,11... | collective-permute-start | bytes 1179656 | tf_op jit(solution)/shard_map/ppermute | solution.py:701
  1.2 4.1 %collective-permute-start.1 = (bf16[256,768]{1,0:T(8,128)(2,1)}, bf16[256,768]{1,0:T(8,128)(2,1)S(1)}, u32[]{:S(2)}, u32[]{:S(2)}) collective-permute-start(bf16[256,768]{1,0:T(8,128)(2,1)} %g_ref.1), channel_id=1, source_target_pairs={{0,1},{1,0},{2,3},{3,2},{4,5},{5,4},{6,7},{7,6},{8,9},{9,8},{10,11... | collective-permute-start | bytes 1179656 | tf_op jit(solution)/shard_map/ppermute | solution.py:701
  9.8 14.9 %collective-permute-start.2 = (bf16[512,128]{1,0:T(8,128)(2,1)S(1)}, bf16[512,128]{1,0:T(8,128)(2,1)S(1)}, u32[]{:S(2)}, u32[]{:S(2)}) collective-permute-start(bf16[512,128]{1,0:T(8,128)(2,1)S(1)} %get-tuple-element.70), channel_id=1, source_target_pairs={{0,2},{1,3},{2,0},{3,1},{4,6},{5,7},{6,4},{7,5},{8,10},{9,11},{10,... | collective-permute-start | bytes 393224 | tf_op jit(solution)/shard_map/ppermute | solution.py:709
  32.2 40.7 %collective-permute-start.5 = (bf16[2,2,2,384,256]{4,3,2,1,0:T(8,128)(2,1)}, bf16[2,2,2,384,256]{4,3,2,1,0:T(8,128)(2,1)}, u32[]{:S(2)}, u32[]{:S(2)}) collective-permute-start(bf16[2,2,2,384,256]{4,3,2,1,0:T(8,128)(2,1)} %get-tuple-element.73), channel_id=1, source_target_pairs={{0,8},{1,17},{2,10},{3,19},{4,12},{5,21},{6,14},{7,23},{8,0},{9,25... | collective-permute-start | bytes 4718600 | tf_op jit(solution)/shard_map/ppermute | solution.py:709
  33.7 39.0 %collective-permute-start.4 = (bf16[2,768,256]{2,1,0:T(8,128)(2,1)}, bf16[2,768,256]{2,1,0:T(8,128)(2,1)S(1)}, u32[]{:S(2)}, u32[]{:S(2)}) collective-permute-start(bf16[2,768,256]{2,1,0:T(8,128)(2,1)} %copy-done.31), channel_id=1, source_target_pairs={{0,2},{1,3},{2,0},{3,1},{4,6},{5,7},{6,4},{7,5},{8,10},{9,11},{10,... | collective-permute-start | bytes 2359304 | tf_op jit(solution)/shard_map/ppermute | solution.py:709
  34.2 22.5 %collective-permute-start.3 = (bf16[1024,128]{1,0:T(8,128)(2,1)}, bf16[1024,128]{1,0:T(8,128)(2,1)S(1)}, u32[]{:S(2)}, u32[]{:S(2)}) collective-permute-start(bf16[1024,128]{1,0:T(8,128)(2,1)} %copy-done.25), channel_id=1, source_target_pairs={{0,4},{1,5},{2,6},{3,7},{4,0},{5,1},{6,2},{7,3},{8,12},{9,13},{10,... | collective-permute-start | bytes 786440 | tf_op jit(solution)/shard_map/ppermute | solution.py:709
  68.3 33.2 %collective-permute-start.6 = (bf16[384,256]{1,0:T(8,128)(2,1)S(1)}, bf16[384,256]{1,0:T(8,128)(2,1)S(1)}, u32[]{:S(2)}, u32[]{:S(2)}) collective-permute-start(bf16[384,256]{1,0:T(8,128)(2,1)S(1)} %get-tuple-element.86.mix0), channel_id=1, source_target_pairs={{0,1},{1,0},{2,3},{3,2},{4,5},{5,4},{6,7},{7,6},{8,9},{9,8},{10,11... | collective-permute-start | bytes 589832 | tf_op jit(solution)/shard_map/ppermute | solution.py:701
  90.5 11.0 %collective-permute-start.7 = (bf16[384,256]{1,0:T(8,128)(2,1)S(1)}, bf16[384,256]{1,0:T(8,128)(2,1)S(1)}, u32[]{:S(2)}, u32[]{:S(2)}) collective-permute-start(bf16[384,256]{1,0:T(8,128)(2,1)S(1)} %get-tuple-element.87.mix1), channel_id=1, source_target_pairs={{0,1},{1,0},{2,3},{3,2},{4,5},{5,4},{6,7},{7,6},{8,9},{9,8},{10,11... | collective-permute-start | bytes 589832 | tf_op jit(solution)/shard_map/ppermute | solution.py:701
  92.8 28.5 %collective-permute-start.13 = (bf16[2,2,384,256]{3,2,1,0:T(8,128)(2,1)S(1)}, bf16[2,2,384,256]{3,2,1,0:T(8,128)(2,1)S(1)}, u32[]{:S(2)}, u32[]{:S(2)}) collective-permute-start(bf16[2,2,384,256]{3,2,1,0:T(8,128)(2,1)S(1)} %fusion.1), channel_id=1, source_target_pairs={{0,16},{1,9},{2,18},{3,11},{4,20},{5,13},{6,22},{7,15},{8,24},{9,1... | collective-permute-start | bytes 2359304 | tf_op jit(solution)/shard_map/ppermute | solution.py:709
  93.0 16.2 %collective-permute-start.10 = (bf16[2,256,128]{2,1,0:T(8,128)(2,1)S(1)}, bf16[2,256,128]{2,1,0:T(8,128)(2,1)S(1)}, u32[]{:S(2)}, u32[]{:S(2)}) collective-permute-start(bf16[2,256,128]{2,1,0:T(8,128)(2,1)S(1)} %fusion.20), channel_id=1, source_target_pairs={{0,2},{1,3},{2,0},{3,1},{4,6},{5,7},{6,4},{7,5},{8,10},{9,11},{10,... | collective-permute-start | bytes 393224 | tf_op jit(solution)/shard_map/ppermute | solution.py:709
  99.0 22.2 %collective-permute-start.19 = (bf16[768,256]{1,0:T(8,128)(2,1)S(1)}, bf16[768,256]{1,0:T(8,128)(2,1)S(1)}, u32[]{:S(2)}, u32[]{:S(2)}) collective-permute-start(bf16[768,256]{1,0:T(8,128)(2,1)S(1)} %fusion.11), channel_id=1, source_target_pairs={{0,4},{1,5},{2,6},{3,7},{4,0},{5,1},{6,2},{7,3},{8,12},{9,13},{10,... | collective-permute-start | bytes 1179656 | tf_op jit(solution)/shard_map/ppermute | solution.py:709
  103.4 18.1 %collective-permute-start.16 = (bf16[2,2,2,144,256]{4,3,2,1,0:T(8,128)(2,1)S(1)}, bf16[2,2,2,144,256]{4,3,2,1,0:T(8,128)(2,1)S(1)}, u32[]{:S(2)}, u32[]{:S(2)}) collective-permute-start(bf16[2,2,2,144,256]{4,3,2,1,0:T(8,128)(2,1)S(1)} %get-tuple-element.88), channel_id=1, source_target_pairs={{0,8},{1,17},{2,10},{3,19},{4,12},{5,21},{6,14},{7,23},{8,0},{9,25... | collective-permute-start | bytes 1769480 | tf_op jit(solution)/shard_map/ppermute | solution.py:709
  112.6 9.7 %collective-permute-start.12 = (bf16[256,768]{1,0:T(8,128)(2,1)S(1)}, bf16[256,768]{1,0:T(8,128)(2,1)S(1)}, u32[]{:S(2)}, u32[]{:S(2)}) collective-permute-start(bf16[256,768]{1,0:T(8,128)(2,1)S(1)} %get-tuple-element.100), channel_id=1, source_target_pairs={{0,1},{1,0},{2,3},{3,2},{4,5},{5,4},{6,7},{7,6},{8,9},{9,8},{10,11... | collective-permute-start | bytes 1179656 | tf_op jit(solution)/shard_map/ppermute | solution.py:701
  112.7 9.5 %collective-permute-start.11 = (bf16[256,128]{1,0:T(8,128)(2,1)S(1)}, bf16[256,128]{1,0:T(8,128)(2,1)S(1)}, u32[]{:S(2)}, u32[]{:S(2)}) collective-permute-start(bf16[256,128]{1,0:T(8,128)(2,1)S(1)} %fusion.22), channel_id=1, source_target_pairs={{0,4},{1,5},{2,6},{3,7},{4,0},{5,1},{6,2},{7,3},{8,12},{9,13},{10,... | collective-permute-start | bytes 196616 | tf_op jit(solution)/shard_map/ppermute | solution.py:709
  121.7 6.8 %collective-permute-start.17 = (bf16[2,2,144,256]{3,2,1,0:T(8,128)(2,1)S(1)}, bf16[2,2,144,256]{3,2,1,0:T(8,128)(2,1)S(1)}, u32[]{:S(2)}, u32[]{:S(2)}) collective-permute-start(bf16[2,2,144,256]{3,2,1,0:T(8,128)(2,1)S(1)} %fusion.14), channel_id=1, source_target_pairs={{0,16},{1,9},{2,18},{3,11},{4,20},{5,13},{6,22},{7,15},{8,24},{9,1... | collective-permute-start | bytes 884744 | tf_op jit(solution)/shard_map/ppermute | solution.py:709
  122.0 12.1 %collective-permute-start.14 = (bf16[2,384,256]{2,1,0:T(8,128)(2,1)S(1)}, bf16[2,384,256]{2,1,0:T(8,128)(2,1)S(1)}, u32[]{:S(2)}, u32[]{:S(2)}) collective-permute-start(bf16[2,384,256]{2,1,0:T(8,128)(2,1)S(1)} %fusion.10), channel_id=1, source_target_pairs={{0,2},{1,3},{2,0},{3,1},{4,6},{5,7},{6,4},{7,5},{8,10},{9,11},{10,... | collective-permute-start | bytes 1179656 | tf_op jit(solution)/shard_map/ppermute | solution.py:709
  128.6 12.4 %collective-permute-start.18 = (bf16[2,256,256]{2,1,0:T(8,128)(2,1)S(1)}, bf16[2,256,256]{2,1,0:T(8,128)(2,1)S(1)}, u32[]{:S(2)}, u32[]{:S(2)}) collective-permute-start(bf16[2,256,256]{2,1,0:T(8,128)(2,1)S(1)} %fusion.15), channel_id=1, source_target_pairs={{0,2},{1,3},{2,0},{3,1},{4,6},{5,7},{6,4},{7,5},{8,10},{9,11},{10,... | collective-permute-start | bytes 786440 | tf_op jit(solution)/shard_map/ppermute | solution.py:709
  134.2 9.5 %collective-permute-start.15 = (bf16[384,256]{1,0:T(8,128)(2,1)S(1)}, bf16[384,256]{1,0:T(8,128)(2,1)S(1)}, u32[]{:S(2)}, u32[]{:S(2)}) collective-permute-start(bf16[384,256]{1,0:T(8,128)(2,1)S(1)} %fusion.19), channel_id=1, source_target_pairs={{0,4},{1,5},{2,6},{3,7},{4,0},{5,1},{6,2},{7,3},{8,12},{9,13},{10,... | collective-permute-start | bytes 589832 | tf_op jit(solution)/shard_map/ppermute | solution.py:709
  143.8 15.7 %collective-permute-start.20 = (bf16[1152,256]{1,0:T(8,128)(2,1)S(1)}, bf16[1152,256]{1,0:T(8,128)(2,1)S(1)}, u32[]{:S(2)}, u32[]{:S(2)}) collective-permute-start(bf16[1152,256]{1,0:T(8,128)(2,1)S(1)} %pad_maximum_fusion.1), channel_id=1, source_target_pairs={{0,16},{1,9},{2,18},{3,11},{4,20},{5,13},{6,22},{7,15},{8,24},{9,1... | collective-permute-start | bytes 1769480 | tf_op jit(solution)/shard_map/ppermute | solution.py:709
  148.8 11.0 %collective-permute-start.22 = (bf16[256,256]{1,0:T(8,128)(2,1)S(1)}, bf16[256,256]{1,0:T(8,128)(2,1)S(1)}, u32[]{:S(2)}, u32[]{:S(2)}) collective-permute-start(bf16[256,256]{1,0:T(8,128)(2,1)S(1)} %fusion.21), channel_id=1, source_target_pairs={{0,4},{1,5},{2,6},{3,7},{4,0},{5,1},{6,2},{7,3},{8,12},{9,13},{10,... | collective-permute-start | bytes 393224 | tf_op jit(solution)/shard_map/ppermute | solution.py:709
  159.7 14.3 %collective-permute-start.21 = (bf16[1536,256]{1,0:T(8,128)(2,1)S(1)}, bf16[1536,256]{1,0:T(8,128)(2,1)S(1)}, u32[]{:S(2)}, u32[]{:S(2)}) collective-permute-start(bf16[1536,256]{1,0:T(8,128)(2,1)S(1)} %pad_maximum_fusion.early_send.send_ref), channel_id=1, source_target_pairs={{0,8},{1,17},{2,10},{3,19},{4,12},{5,21},{6,14},{7,23},{8,0},{9,25... | collective-permute-start | bytes 2359304 | tf_op jit(solution)/shard_map/ppermute | solution.py:709
  159.8 6.9 %collective-permute-start.23 = (bf16[256,256]{1,0:T(8,128)(2,1)S(1)}, bf16[256,256]{1,0:T(8,128)(2,1)S(1)}, u32[]{:S(2)}, u32[]{:S(2)}) collective-permute-start(bf16[256,256]{1,0:T(8,128)(2,1)S(1)} %fusion.17), channel_id=1, source_target_pairs={{0,16},{1,9},{2,18},{3,11},{4,20},{5,13},{6,22},{7,15},{8,24},{9,1... | collective-permute-start | bytes 393224 | tf_op jit(solution)/shard_map/ppermute | solution.py:709
  166.8 7.2 %collective-permute-start.24 = (bf16[400,256]{1,0:T(8,128)(2,1)S(1)}, bf16[400,256]{1,0:T(8,128)(2,1)S(1)}, u32[]{:S(2)}, u32[]{:S(2)}) collective-permute-start(bf16[400,256]{1,0:T(8,128)(2,1)S(1)} %pad_maximum_fusion.3.last_send), channel_id=1, source_target_pairs={{0,8},{1,17},{2,10},{3,19},{4,12},{5,21},{6,14},{7,23},{8,0},{9,25... | collective-permute-start | bytes 614408 | tf_op jit(solution)/shard_map/ppermute | solution.py:709
  168.7 6.1 %collective-permute-start.9 = (bf16[256,768]{1,0:T(8,128)(2,1)S(1)}, bf16[256,768]{1,0:T(8,128)(2,1)S(1)}, u32[]{:S(2)}, u32[]{:S(2)}) collective-permute-start(bf16[256,768]{1,0:T(8,128)(2,1)S(1)} %get-tuple-element.92), channel_id=1, source_target_pairs={{0,1},{1,0},{2,3},{3,2},{4,5},{5,4},{6,7},{7,6},{8,9},{9,8},{10,11... | collective-permute-start | bytes 1179656 | tf_op jit(solution)/shard_map/ppermute | solution.py:701
  (39 other events, 228.5 us)

commit v3 on v2

--- a/solution.py
+++ b/solution.py
@@ -299,22 +299,33 @@
 
 
 def prologue_kernel(
-    sc, xo, xt, go, gt, g1, c1, g2, c2, w_kv, cos_ref, sin_ref, h1_ref, h2_ref, gg_ref, kv_ref
+    sc, x_hbm, xt, g_hbm, gt, gains, w_hbm, cos_ref, sin_ref, h1_ref, h2_ref, gg_ref, kv_ref, xo, w_kv, sem
 ):
-    rows = xo.shape[0]
-    gain_one, bias_one = g1[...].astype(F32), c1[...].astype(F32)
-    gain_two, bias_two = g2[...].astype(F32), c2[...].astype(F32)
-    for n, (x, g) in enumerate(((xo, go), (xt, gt))):
+    rows = xt.shape[0]
+    copies = [
+        pltpu.make_async_copy(x_hbm, xo, sem.at[0]),
+        pltpu.make_async_copy(w_hbm, w_kv, sem.at[1]),
+        pltpu.make_async_copy(g_hbm, gg_ref.at[0:rows, :], sem.at[2]),
+    ]
+    for copy in copies:
+        copy.start()
+    gg_ref[rows : 2 * rows, :] = gt[...]
+    gain_one, bias_one = gains[0:1, :].astype(F32), gains[1:2, :].astype(F32)
+    gain_two, bias_two = gains[2:3, :].astype(F32), gains[3:4, :].astype(F32)
+    for n, x in ((1, xt), (0, xo)):
+        if n == 0:
+            copies[0].wait()
         for t in range(rows // 128):
             here = slice(n * rows + t * 128, n * rows + (t + 1) * 128)
             hat, unused = normed(x[t * 128 : (t + 1) * 128, :].astype(F32))
             h1_ref[here, :] = (hat * gain_one + bias_one).astype(BF)
             h2_ref[here, :] = (hat * gain_two + bias_two).astype(BF)
-        gg_ref[n * rows : (n + 1) * rows, :] = g[...]
+    copies[1].wait()
     raw = dot(h1_ref[...], w_kv[...])
     kv = turn(raw.T, cos_ref[...], sin_ref[...]).T.astype(BF)
     kv_ref[pl.ds(pl.multiple_of(sc[0] * rows, rows), rows), :] = kv[:rows]
     kv_ref[pl.ds(pl.multiple_of((1 - sc[0]) * rows, rows), rows), :] = kv[rows:]
+    copies[2].wait()
 
 
 def half_copies(sc, w_query, w_out, query_s, out_s, sem):
@@ -369,9 +380,9 @@
     outs = refs[:-4]
     rows, width = h_ref.shape
     copies = hidden_copies(sc, piece_of(sc, n), w_up, w_down, up_s, down_s, sems, part, n_pair)
-    for copy in copies:
+    for copy in copies[0::2] + copies[1::2]:
         copy.start()
-    for copy in copies:
+    for copy in copies[0::2] + copies[1::2]:
         copy.wait()
 
     def row_tile(r, carry):
@@ -430,7 +441,7 @@
             pltpu.VMEM((width, width), BF),
             pltpu.SemaphoreType.DMA((2,)),
         ],
-        20,
+        56,
         8 * rows * width * span,
     )(sc, h_two, g_two, w_up, w_down)
 
@@ -516,7 +527,7 @@
             send_ref[...] = total.astype(BF)
 
 
-def hat_kernel(sc, d0, d1, d2, dq0, dq1, xo, xt, g1, g2, w_up, w_query, own_ref, send_ref, sum_ref, up_s, query_s, sems, *, part, n_pair):
+def hat_kernel(sc, d0, d1, d2, dq0, dq1, xo, xt, gains, w_up, w_query, own_ref, send_ref, sum_ref, up_s, query_s, sems, *, part, n_pair):
     half = query_s.shape[1]
     rows, width = xo.shape
     copies = [
@@ -532,7 +543,7 @@
         copy.start()
     for copy in copies:
         copy.wait()
-    gain_one, gain_two = g1[...].astype(F32), g2[...].astype(F32)
+    gain_one, gain_two = gains[0:1, :].astype(F32), gains[2:3, :].astype(F32)
     sums = [jnp.zeros((1, width), F32)] * 4
     for n, (x, dq) in enumerate(((xo, dq0), (xt, dq1))):
         here = slice(n * rows, (n + 1) * rows)
@@ -551,15 +562,15 @@
     sum_ref[...] = jnp.concatenate(sums + [jnp.zeros((4, width), F32)], 0)
 
 
-def last_kernel(sc, dkv_a, dkv_b, cos_ref, sin_ref, w_kv, h_ref, x_ref, g1, hat_own, hat_got, sum_ref, g_ref, grad_ref, send_ref, keep_ref, *, n_pair):
+def last_kernel(sc, dkv_a, dkv_b, cos_ref, sin_ref, w_kv, h_ref, x_ref, gains, hat_own, hat_got, sum_ref, g_ref, grad_ref, send_ref, keep_ref, *, n_pair):
     rows, width = x_ref.shape
-    dkv = (dkv_a[...] + dkv_b[...].astype(F32)).T
+    dkv = (dkv_a[...].astype(F32) + dkv_b[...].astype(F32)).T
     low_t = turn(dkv, cos_ref[:, 0:rows], -sin_ref[:, 0:rows]).astype(BF)
     low = low_t.T
     weight = dot(low_t, h_ref[0:rows, :]).T.astype(BF)
     d_kv = dot(low, w_kv[...], ((1,), (1,)))
     hat, scale = normed(x_ref[...].astype(F32))
-    gain = g1[...].astype(F32)
+    gain = gains[0:1, :].astype(F32)
     total = hat_own[...] + hat_got[...].astype(F32) + d_kv * gain
     grad_ref[...] = g_ref[...].astype(F32) + scale * (
         total
@@ -726,7 +737,7 @@
 
 
 def add(keep, got):
-    return keep.astype(F32) + got.astype(F32)
+    return (keep.astype(F32) + got.astype(F32)).astype(BF)
 
 
 def low(value):
@@ -749,7 +760,7 @@
     per_chip = 2 * rows // BLK
     table = block_table[0]
     sc = jnp.stack([core, chip, links.bit(0), links.bit(1)]).astype(jnp.int32)
-    g1, c1, g2, c2 = (v.reshape(1, width) for v in (ln1_gain, ln1_bias, ln2_gain, ln2_bias))
+    gains = jnp.stack([ln1_gain, ln1_bias, ln2_gain, ln2_bias])
 
     x_other, g_other = links.swap(layer_input), links.swap(cotangent)
     own_slots = lax.dynamic_slice_in_dim(table, chip * per_chip, per_chip).reshape(2, -1)
@@ -766,11 +777,15 @@
         prologue_kernel,
         "prologue",
         [shape((2 * rows, width), BF)] * 3 + [shape((2 * rows, lanes), BF)],
-        [VM] * 11,
+        [HBM, VM, HBM, VM, VM, HBM, VM, VM],
         [VM] * 4,
-        [],
+        [
+            pltpu.VMEM((rows, width), BF),
+            pltpu.VMEM((width, lanes), BF),
+            pltpu.SemaphoreType.DMA((3,)),
+        ],
         16,
-    )(sc, layer_input, x_other, cotangent, g_other, g1, c1, g2, c2, w_keyval, cosine, sine)
+    )(sc, layer_input, x_other, cotangent, g_other, gains, w_keyval, cosine, sine)
 
     kv_got = links.flip(kv_low, 1)
     ffn = functools.partial(
@@ -806,13 +821,15 @@
     )
     mix_0, dq_0, carried = attend(q_t=q_t, carried=None, start=0, last_call=False)
     mix_0_got = links.swap(mix_0)
-    a_sum = add(a_keep, tie(a_got, carried))
-    a_got_2 = links.flip(low(a_sum[1]), 2)
-    b_sum = add(b_keep, tie(b_got, carried))
-    b_got_2 = links.cross(low(b_sum[1]), 1)
+    a_got, b_got = tie(a_got, carried), tie(b_got, carried)
+    a_send = add(a_keep[1], a_got[1])
+    a_got_2 = links.flip(a_send, 2)
+    b_send = add(b_keep[1], b_got[1])
+    b_got_2 = links.cross(b_send, 1)
     mix_1, dq_1, dkv_send, dkv_keep = attend(
-        q_t=tie(q_t, a_got, b_got), carried=carried, start=count, last_call=True
-    )
+        q_t=tie(q_t, a_send, b_send), carried=carried, start=count, last_call=True
+    )
+    a_keep, b_keep = add(a_keep[0], a_got[0]), add(b_keep[0], b_got[0])
 
     dkv_got = links.swap(dkv_send)
     mix_1_got = links.swap(mix_1)
@@ -820,10 +837,11 @@
         sc, h_one, (dq_0, dq_1), (mix_0, mix_1), (mix_0_got, mix_1_got), g_two, n_pair
     )
     late_got = links.cross(late_send, 0)
-    dkv_sum = add(dkv_keep, dkv_got)
-    dkv_got_2 = links.flip(low(dkv_sum[1]), 1)
-    b_sum = add(b_sum[0], tie(b_got_2, late_send))
-    b_got_3 = links.flip(low(b_sum[1]), 1)
+    dkv_got_2 = links.flip(add(dkv_keep[1], dkv_got[1]), 1)
+    dkv_keep = add(dkv_keep[0], dkv_got[0])
+    b_got_2 = tie(b_got_2, late_send)
+    b_got_3 = links.flip(add(b_keep[1], b_got_2[1]), 1)
+    b_keep = add(b_keep[0], b_got_2[0])
 
     w_specs = [HBM] * 2
     out_own, out_send = call(
@@ -837,35 +855,38 @@
             pltpu.VMEM((half, width), BF),
             pltpu.SemaphoreType.DMA((2,)),
         ],
-        16,
+        56,
     )(sc, act_0, act_1, tie(act_2, late_send, dkv_got), mix_0, mix_1, layer_input, w_down, w_out)
     out_got = links.swap(out_send)
-    dkv_sum = add(dkv_sum[0], tie(dkv_got_2, out_send))
-    dkv_got_3 = links.flip(low(dkv_sum[1]), 2)
+    dkv_got_2 = tie(dkv_got_2, out_send)
+    dkv_got_3 = links.flip(add(dkv_keep[1], dkv_got_2[1]), 2)
+    dkv_keep = add(dkv_keep[0], dkv_got_2[0])
     hat_own, hat_send, sums = call(
         functools.partial(hat_kernel, part=part_hidden, n_pair=n_pair),
         "norms",
         [shape((rows, width), F32), shape((rows, width), BF), shape((8, width), F32)],
-        [VM] * 9 + w_specs,
+        [VM] * 8 + w_specs,
         [VM] * 3,
         [
             pltpu.VMEM((3, width, n_pair * LANES), BF),
             pltpu.VMEM((width, half), BF),
             pltpu.SemaphoreType.DMA((2,)),
         ],
-        24,
+        56,
     )(
-        sc, dup_0, dup_1, tie(dup_2, out_send, dkv_got_2), dq_0, dq_1, layer_input, x_other, g1, g2,
+        sc, dup_0, dup_1, tie(dup_2, out_send, dkv_got_2), dq_0, dq_1, layer_input, x_other, gains,
         w_up, w_query,
     )
     hat_got = links.swap(hat_send)
     layer_output = low(out_own + out_got.astype(F32))
 
-    late_sum = add(late_keep, tie(late_got, hat_send))
-    late_got_2 = links.cross(low(late_sum[1]), 1)
-    b_sum = add(b_sum[0], tie(b_got_3, hat_send))
-    b_got_4 = links.flip(low(b_sum[1]), 2)
-    a_sum = add(a_sum[0], tie(a_got_2, hat_send))
+    late_got = tie(late_got, hat_send)
+    late_got_2 = links.cross(add(late_keep[1], late_got[1]), 1)
+    late_keep = add(late_keep[0], late_got[0])
+    b_got_3 = tie(b_got_3, hat_send)
+    b_got_4 = links.flip(add(b_keep[1], b_got_3[1]), 2)
+    b_keep = add(b_keep[0], b_got_3[0])
+    a_sum = add(a_keep, tie(a_got_2, hat_send))
 
     few = part // 2 + 8
     in_grad, few_send, few_keep = call(
@@ -877,27 +898,28 @@
         [],
         16,
     )(
-        sc, dkv_sum[0], dkv_got_3, cosine, sine, w_keyval, h_one, layer_input, g1, hat_own, hat_got,
+        sc, dkv_keep, dkv_got_3, cosine, sine, w_keyval, h_one, layer_input, gains, hat_own, hat_got,
         sums, cotangent,
     )
 
-    late_sum = add(late_sum[0], tie(late_got_2, few_send))
-    quarter = late_sum.shape[2]
-    last = jnp.concatenate([late_sum, jnp.stack([few_keep, few_send]).astype(F32)], 2)
-    last_got = links.flip(low(last[1]), 1)
-    early = jnp.concatenate([low(add(b_sum[0], tie(b_got_4, last_got))), low(a_sum)], 0)
+    late_got_2 = tie(late_got_2, few_send)
+    quarter = late_keep.shape[2]
+    last_send = jnp.concatenate([add(late_keep[1], late_got_2[1]), few_send], 1)
+    last_got = links.flip(last_send, 1)
+    last_keep = jnp.concatenate([add(late_keep[0], late_got_2[0]), few_keep], 1)
+    early = jnp.concatenate([add(b_keep, tie(b_got_4, last_send)), a_sum], 0)
     block = early.shape[0] // 3
     early_got = links.cross(early, 1)
-    last = add(last[0], last_got)
-    last_got = links.flip(low(last[1]), 2)
+    last_got_2 = links.flip(add(last_keep[1], last_got[1]), 2)
+    last_keep = add(last_keep[0], last_got[0])
     early = jnp.concatenate(
-        [early[:block], early_got[:block], low(add(early[block:], early_got[block:]))], 0
+        [early[:block], early_got[:block], add(early[block:], early_got[block:])], 0
     )
     early_got = links.cross(early, 0)
-    last = low(add(last[0], last_got))
+    last = add(last_keep, last_got_2)
     last_got = links.cross(last, 1)
     last = jnp.concatenate(
-        [last[:quarter], last_got[:quarter], low(add(last[quarter:], last_got[quarter:]))], 0
+        [last[:quarter], last_got[:quarter], add(last[quarter:], last_got[quarter:])], 0
     )
     last_got = links.cross(last, 0)
     total_down = call(
@@ -1008,7 +1030,7 @@
     dkv_own = lax.dynamic_index_in_dim(dkv_part, core, 1, False)
     dkv_got = links.swap(lax.dynamic_index_in_dim(dkv_part, 1 - core, 1, False))
     moved = lax.all_to_all(
-        low(add(dkv_own, dkv_got)), "ctx", 0, 0, axis_index_groups=links.groups
+        add(dkv_own, dkv_got), "ctx", 0, 0, axis_index_groups=links.groups
     )
     dkv = jnp.sum(moved.astype(F32), 0)
     cos_own = lax.dynamic_slice_in_dim(cosine, core * rows, rows, 1)
@@ -1054,7 +1076,7 @@
     few = links.reduce(low(few).reshape(n_pair, 2 * (part_rows + 4), 2 * size))
     few = few.reshape(2, part_rows + 4, 2 * size)
     few_got = links.swap(lax.dynamic_index_in_dim(few, 1 - core, 0, False))
-    few = add(lax.dynamic_index_in_dim(few, core, 0, False), few_got)
+    few = lax.dynamic_index_in_dim(few, core, 0, False).astype(F32) + few_got.astype(F32)
 
     halves = jnp.concatenate(
         [total_up.reshape(2, part_rows, half_hidden), total_late.reshape(2, part_rows, width)], -1

time: 182 us -> 181 us (level); the launches traced: 180 us -> 182 us
  starting transfers between devices: 34.8 us -> 47.5 us
  local copies, waits for them, and re-layouts: 21.8 us -> 9.1 us
  Pallas kernels: 65.5 us -> 76.8 us
  waiting for transfers between devices: 51.3 us -> 41.4 us
    ppermute x18, starting transfers between devices: 29 us -> 45.3 us  [permute(): return lax.ppermute(value, ('grp', 'ctx'), pairs)]
    unnamed x75 -> x67, local copies, waits for them, and re-layouts: 17.4 us -> 4.96 us
    ppermute x18, waiting for transfers between devices: 51.2 us -> 40.2 us  [permute(): return lax.ppermute(value, ('grp', 'ctx'), pairs)]
    pallas_call x3, Pallas kernels: 15.2 us -> 23.1 us  [ffn_gradients(): call(functools.partial(ffn_kernel, n=n, part=part, n_pair=n_pair), 'ffn_g...]
    convert_element_type x1 -> x14, other arithmetic: 0.03 us -> 4.88 us  [add(): return (keep.astype(F32) + got.astype(F32)).astype(BF)]
    pallas_call x1, Pallas kernels: 3.35 us -> 6.91 us  [shards_small(): call(functools.partial(hat_kernel, part=part_hidden, n_pair=n_pair), 'nor...]
    ppermute x8, starting transfers between devices: 5.74 us -> 2.28 us  [swap(): return lax.ppermute(value, 'ctx', [(i, i ^ 1) for i in range(self.n_ctx)])]
    reshape x4 -> x0, local copies, waits for them, and re-layouts: 2.74 us -> none  [shards_small(): v.reshape(1, width)]
  transfers between devices with their start and end apart: 26 -> 26, of which waited for: 10 -> 9; matrix products, arithmetic and copies ran while one was open for 5% -> 4% of each run, Pallas kernels for 31% -> 36%
where the time goes in v3:
time: 181 us; the launch traced here: 182 us
  Pallas kernels  76.8 us (42%)
  starting transfers between devices  47.5 us (26%)
  waiting for transfers between devices  41.4 us (23%)
  local copies, waits for them, and re-layouts  9.1 us (5%)
  other arithmetic  6.31 us (3%)
    ppermute x18, starting transfers between devices, permute(): return lax.ppermute(value, ('grp', 'ctx'), pairs)  45.3 us
    ppermute x18, waiting for transfers between devices, permute(): return lax.ppermute(value, ('grp', 'ctx'), pairs)  40.2 us
    pallas_call x2, Pallas kernels, attention(): pl.pallas_call(functools.partial(attn_kernel, blocks=blocks, heads=heads,...  26.9 us
    pallas_call x3, Pallas kernels, ffn_gradients(): call(functools.partial(ffn_kernel, n=n, part=part, n_pair=n_pair), 'ffn_g...  23.1 us
    pallas_call x1, Pallas kernels, shards_small(): call(functools.partial(hat_kernel, part=part_hidden, n_pair=n_pair), 'nor...  6.91 us
    pallas_call x1, Pallas kernels, shards_small(): call(functools.partial(out_kernel, part=part_hidden, n_pair=n_pair), 'out...  6.75 us
    unnamed x67, local copies, waits for them, and re-layouts  4.96 us
    convert_element_type x14, other arithmetic, add(): return (keep.astype(F32) + got.astype(F32)).astype(BF)  4.88 us
  transfers between devices with their start and end apart: 26, of which 9 were waited for; matrix products, arithmetic and copies ran while one was open for 4% of the time, Pallas kernels for 36%

profile of v3, /device:TPU:0, one launch (start us, length us, event | category | flops | bytes accessed | tf_op | source)
XLA Modules:
  0.0 182.4 jit_solution(16082292785811319422)
XLA Ops:
  12.6 3.0 %collective-permute-start.2 = (bf16[512,128]{1,0:T(8,128)(2,1)S(1)}, bf16[512,128]{1,0:T(8,128)(2,1)S(1)}, u32[]{:S(2)}, u32[]{:S(2)}) collective-permute-start(bf16[512,128]{1,0:T(8,128)(2,1)S(1)} %get-tuple-element.70), channel_id=1, source_target_pairs={{0,2},{1,3},{2,0},{3,1},{4,6},{5,7},{6,4},{7,5},{8,10},{9,11},{10,... | collective-permute-start | bytes 393224 | tf_op jit(solution)/shard_map/ppermute | solution.py:720
  15.6 7.5 %ffn_gradients.3 = (bf16[512,512]{1,0:T(8,128)(2,1)}, bf16[512,512]{1,0:T(8,128)(2,1)}, bf16[2,768,256]{2,1,0:T(8,128)(2,1)}, bf16[2,768,256]{2,1,0:T(8,128)(2,1)}) custom-call(s32[4]{0:T(128)} %copy-done.19, bf16[512,768]{1,0:T(8,128)(2,1)} %copy-done.2, bf16[512,768]{1,0:T(8,128)(2,1)} %copy-done, bf16[768,3072]{1,0:T(8,128)(2,1)} %w_up.7, ...), custom_call_target="tpu_custom_call" | custom-call | flops 1610612736 | bytes 8053063 | tf_op jit(solution)/shard_map/ffn_gradients/pallas_call | solution.py:432
  23.3 7.7 %ffn_gradients.4 = (bf16[512,512]{1,0:T(8,128)(2,1)}, bf16[512,512]{1,0:T(8,128)(2,1)}, bf16[2,2,2,384,256]{4,3,2,1,0:T(8,128)(2,1)}) custom-call(s32[4]{0:T(128)} %copy-done.19, bf16[512,768]{1,0:T(8,128)(2,1)} %copy-done.2, bf16[512,768]{1,0:T(8,128)(2,1)} %copy-done, bf16[768,3072]{1,0:T(8,128)(2,1)} %w_up.7, bf16[3072,768]{1,0:T(8,128)(2,1)} %w_down.7), custom_call_target="tpu_custom_call" | custom-call | flops 1610612736 | bytes 8053063 | tf_op jit(solution)/shard_map/ffn_gradients/pallas_call | solution.py:432
  33.0 2.6 %collective-permute-start.3 = (bf16[1024,128]{1,0:T(8,128)(2,1)S(1)}, bf16[1024,128]{1,0:T(8,128)(2,1)S(1)}, u32[]{:S(2)}, u32[]{:S(2)}) collective-permute-start(bf16[1024,128]{1,0:T(8,128)(2,1)S(1)} %constant_dynamic-update-slice_fusion.refs_4_), channel_id=1, source_target_pairs={{0,4},{1,5},{2,6},{3,7},{4,0},{5,1},{6,2},{7,3},{8,12},{9,13},{10,... | collective-permute-start | bytes 786440 | tf_op jit(solution)/shard_map/ppermute | solution.py:720
  35.7 7.9 %ffn_gradients.5 = (bf16[512,512]{1,0:T(8,128)(2,1)}, bf16[512,512]{1,0:T(8,128)(2,1)}, bf16[2,2,2,384,256]{4,3,2,1,0:T(8,128)(2,1)}) custom-call(s32[4]{0:T(128)} %copy-done.19, bf16[512,768]{1,0:T(8,128)(2,1)} %copy-done.2, bf16[512,768]{1,0:T(8,128)(2,1)} %copy-done, bf16[768,3072]{1,0:T(8,128)(2,1)} %w_up.7, bf16[3072,768]{1,0:T(8,128)(2,1)} %w_down.7), custom_call_target="tpu_custom_call" | custom-call | flops 1610612736 | bytes 8053063 | tf_op jit(solution)/shard_map/ffn_gradients/pallas_call | solution.py:432
  45.6 9.5 %collective-permute-done.3.refs_5_ = bf16[1024,128]{1,0:T(8,128)(2,1)S(1)} collective-permute-done((bf16[1024,128]{1,0:T(8,128)(2,1)S(1)}, bf16[1024,128]{1,0:T(8,128)(2,1)S(1)}, u32[]{:S(2)}, u32[]{:S(2)}) %collective-permute-start.3) | collective-permute-done | bytes 262176 | tf_op jit(solution)/shard_map/ppermute | solution.py:720
  55.1 10.5 %attention.2 = (bf16[384,256]{1,0:T(8,128)(2,1)S(1)}, bf16[384,256]{1,0:T(8,128)(2,1)S(1)}, f32[2048,128]{1,0:T(8,128)S(1)}) custom-call(s32[16]{0:T(128)S(1)} %bitcast.103, s32[4]{0:T(128)S(1)} %get-tuple-element.122.place, bf16[384,512]{1,0:T(8,128)(2,1)S(1)} %get-tuple-element.86.refs_0_, f32[384,512]{1,0:T(8,128)S(1)} %get-tuple-element.80.refs_1_, ...), custom_call_target="tpu_custom_call" | custom-call | flops 4831838208 | bytes 1572864 | tf_op jit(solution)/shard_map/attention/pallas_call | solution.py:258
  69.0 16.3 %attention.3 = (bf16[384,256]{1,0:T(8,128)(2,1)S(1)}, bf16[384,256]{1,0:T(8,128)(2,1)S(1)}, bf16[2,2,256,128]{3,2,1,0:T(8,128)(2,1)S(1)}, bf16[2,2,256,128]{3,2,1,0:T(8,128)(2,1)S(1)}) custom-call(s32[16]{0:T(128)S(1)} %bitcast.104, s32[4]{0:T(128)S(1)} %get-tuple-element.121.place, bf16[384,512]{1,0:T(8,128)(2,1)S(1)} %get-tuple-element.86.refs_0_, ...), custom_call_target="tpu_custom_call" | custom-call | flops 4831838208 | bytes 1572864 | tf_op jit(solution)/shard_map/attention/pallas_call | solution.py:258
  89.9 3.4 %collective-permute-start.16 = (bf16[2,2,2,144,256]{4,3,2,1,0:T(8,128)(2,1)S(1)}, bf16[2,2,2,144,256]{4,3,2,1,0:T(8,128)(2,1)S(1)}, u32[]{:S(2)}, u32[]{:S(2)}) collective-permute-start(bf16[2,2,2,144,256]{4,3,2,1,0:T(8,128)(2,1)S(1)} %get-tuple-element.90), channel_id=1, source_target_pairs={{0,8},{1,17},{2,10},{3,19},{4,12},{5,21},{6,14},{7,23},{8,0},{9,25... | collective-permute-start | bytes 1769480 | tf_op jit(solution)/shard_map/ppermute | solution.py:720
  93.4 10.9 %collective-permute-start.10 = (bf16[2,256,128]{2,1,0:T(8,128)(2,1)S(1)}, bf16[2,256,128]{2,1,0:T(8,128)(2,1)S(1)}, u32[]{:S(2)}, u32[]{:S(2)}) collective-permute-start(bf16[2,256,128]{2,1,0:T(8,128)(2,1)S(1)} %get-tuple-element.131), channel_id=1, source_target_pairs={{0,2},{1,3},{2,0},{3,1},{4,6},{5,7},{6,4},{7,5},{8,10},{9,11},{10,... | collective-permute-start | bytes 393224 | tf_op jit(solution)/shard_map/ppermute | solution.py:720
  104.4 6.7 %outputs.1 = (f32[256,768]{1,0:T(8,128)}, bf16[256,768]{1,0:T(8,128)(2,1)}) custom-call(s32[4]{0:T(128)} %copy-done.19, bf16[512,512]{1,0:T(8,128)(2,1)} %get-tuple-element.68.a0, bf16[512,512]{1,0:T(8,128)(2,1)} %get-tuple-element.72.a1, bf16[512,512]{1,0:T(8,128)(2,1)} %get-tuple-element.92.a2, bf16[384,256]{1,0:T(8,128)(2,1)} %copy-done.14, ...), custom_call_target="tpu_custom_call" | custom-call | flops 1000000 | bytes 5000 | tf_op jit(solution)/shard_map/outputs/pallas_call | solution.py:847
  111.1 6.9 %norms.1 = (f32[256,768]{1,0:T(8,128)}, bf16[256,768]{1,0:T(8,128)(2,1)}, f32[8,768]{1,0:T(8,128)}) custom-call(s32[4]{0:T(128)} %copy-done.19, bf16[512,512]{1,0:T(8,128)(2,1)} %get-tuple-element.97.d0, bf16[512,512]{1,0:T(8,128)(2,1)} %get-tuple-element.98.d1, bf16[512,512]{1,0:T(8,128)(2,1)} %get-tuple-element.100.d2, bf16[384,256]{1,0:T(8,128)(2,1)} %copy-done.13, ...), custom_call_target="tpu_custom_call" | custom-call | flops 1000000 | bytes 5000 | tf_op jit(solution)/shard_map/norms/pallas_call | solution.py:864
  119.8 4.3 %collective-permute-start.17 = (bf16[2,2,144,256]{3,2,1,0:T(8,128)(2,1)S(1)}, bf16[2,2,144,256]{3,2,1,0:T(8,128)(2,1)S(1)}, u32[]{:S(2)}, u32[]{:S(2)}) collective-permute-start(bf16[2,2,144,256]{3,2,1,0:T(8,128)(2,1)S(1)} %get-tuple-element.127), channel_id=1, source_target_pairs={{0,16},{1,9},{2,18},{3,11},{4,20},{5,13},{6,22},{7,15},{8,24},{9,1... | collective-permute-start | bytes 884744 | tf_op jit(solution)/shard_map/ppermute | solution.py:720
  124.2 3.0 %collective-permute-start.11 = (bf16[256,128]{1,0:T(8,128)(2,1)S(1)}, bf16[256,128]{1,0:T(8,128)(2,1)S(1)}, u32[]{:S(2)}, u32[]{:S(2)}) collective-permute-start(bf16[256,128]{1,0:T(8,128)(2,1)S(1)} %get-tuple-element.133), channel_id=1, source_target_pairs={{0,4},{1,5},{2,6},{3,7},{4,0},{5,1},{6,2},{7,3},{8,12},{9,13},{10,... | collective-permute-start | bytes 196616 | tf_op jit(solution)/shard_map/ppermute | solution.py:720
  127.3 3.0 %collective-permute-done.11.dkv_b = bf16[256,128]{1,0:T(8,128)(2,1)S(1)} collective-permute-done((bf16[256,128]{1,0:T(8,128)(2,1)S(1)}, bf16[256,128]{1,0:T(8,128)(2,1)S(1)}, u32[]{:S(2)}, u32[]{:S(2)}) %collective-permute-start.11) | collective-permute-done | bytes 65568 | tf_op jit(solution)/shard_map/ppermute | solution.py:720
  130.3 2.5 %last.1 = (f32[256,768]{1,0:T(8,128)}, bf16[2,112,256]{2,1,0:T(8,128)(2,1)S(1)}, bf16[2,112,256]{2,1,0:T(8,128)(2,1)S(1)}) custom-call(s32[4]{0:T(128)S(1)} %copy-done.21, bf16[256,128]{1,0:T(8,128)(2,1)S(1)} %get-tuple-element.134.dkv_a, bf16[256,128]{1,0:T(8,128)(2,1)S(1)} %collective-permute-done.11.dkv_b, ...), custom_call_target="tpu_custom_call" | custom-call | flops 1000000 | bytes 5000 | tf_op jit(solution)/shard_map/last/pallas_call | solution.py:892
  132.9 3.5 %collective-permute-start.15 = (bf16[384,256]{1,0:T(8,128)(2,1)S(1)}, bf16[384,256]{1,0:T(8,128)(2,1)S(1)}, u32[]{:S(2)}, u32[]{:S(2)}) collective-permute-start(bf16[384,256]{1,0:T(8,128)(2,1)S(1)} %fusion.15), channel_id=1, source_target_pairs={{0,4},{1,5},{2,6},{3,7},{4,0},{5,1},{6,2},{7,3},{8,12},{9,13},{10,... | collective-permute-start | bytes 589832 | tf_op jit(solution)/shard_map/ppermute | solution.py:720
  136.5 8.9 %collective-permute-done.15 = bf16[384,256]{1,0:T(8,128)(2,1)S(1)} collective-permute-done((bf16[384,256]{1,0:T(8,128)(2,1)S(1)}, bf16[384,256]{1,0:T(8,128)(2,1)S(1)}, u32[]{:S(2)}, u32[]{:S(2)}) %collective-permute-start.15) | collective-permute-done | bytes 196640 | tf_op jit(solution)/shard_map/ppermute | solution.py:720
  145.6 4.3 %collective-permute-start.19 = (bf16[1152,256]{1,0:T(8,128)(2,1)S(1)}, bf16[1152,256]{1,0:T(8,128)(2,1)S(1)}, u32[]{:S(2)}, u32[]{:S(2)}) collective-permute-start(bf16[1152,256]{1,0:T(8,128)(2,1)S(1)} %pad_maximum_fusion.1), channel_id=1, source_target_pairs={{0,16},{1,9},{2,18},{3,11},{4,20},{5,13},{6,22},{7,15},{8,24},{9,1... | collective-permute-start | bytes 1769480 | tf_op jit(solution)/shard_map/ppermute | solution.py:720
  150.6 5.7 %collective-permute-done.21 = bf16[2,256,256]{2,1,0:T(8,128)(2,1)S(1)} collective-permute-done((bf16[2,256,256]{2,1,0:T(8,128)(2,1)S(1)}, bf16[2,256,256]{2,1,0:T(8,128)(2,1)S(1)}, u32[]{:S(2)}, u32[]{:S(2)}) %collective-permute-start.21) | collective-permute-done | bytes 262176 | tf_op jit(solution)/shard_map/ppermute | solution.py:720
  159.1 4.5 %collective-permute-done.22 = bf16[256,256]{1,0:T(8,128)(2,1)S(1)} collective-permute-done((bf16[256,256]{1,0:T(8,128)(2,1)S(1)}, bf16[256,256]{1,0:T(8,128)(2,1)S(1)}, u32[]{:S(2)}, u32[]{:S(2)}) %collective-permute-start.22) | collective-permute-done | bytes 131104 | tf_op jit(solution)/shard_map/ppermute | solution.py:720
  163.7 3.0 %collective-permute-start.23 = (bf16[256,256]{1,0:T(8,128)(2,1)S(1)}, bf16[256,256]{1,0:T(8,128)(2,1)S(1)}, u32[]{:S(2)}, u32[]{:S(2)}) collective-permute-start(bf16[256,256]{1,0:T(8,128)(2,1)S(1)} %fusion.13), channel_id=1, source_target_pairs={{0,16},{1,9},{2,18},{3,11},{4,20},{5,13},{6,22},{7,15},{8,24},{9,1... | collective-permute-start | bytes 393224 | tf_op jit(solution)/shard_map/ppermute | solution.py:720
  166.7 4.1 %collective-permute-done.23 = bf16[256,256]{1,0:T(8,128)(2,1)S(1)} collective-permute-done((bf16[256,256]{1,0:T(8,128)(2,1)S(1)}, bf16[256,256]{1,0:T(8,128)(2,1)S(1)}, u32[]{:S(2)}, u32[]{:S(2)}) %collective-permute-start.23) | collective-permute-done | bytes 131104 | tf_op jit(solution)/shard_map/ppermute | solution.py:720
  172.1 4.5 %collective-permute-done.24.last_got = bf16[400,256]{1,0:T(8,128)(2,1)S(1)} collective-permute-done((bf16[400,256]{1,0:T(8,128)(2,1)S(1)}, bf16[400,256]{1,0:T(8,128)(2,1)S(1)}, u32[]{:S(2)}, u32[]{:S(2)}) %collective-permute-start.24) | collective-permute-done | bytes 204832 | tf_op jit(solution)/shard_map/ppermute | solution.py:720
  (147 shorter events, 36.8 us)
Async XLA Ops:
  0.6 4.7 %collective-permute-start.1 = (bf16[256,768]{1,0:T(8,128)(2,1)}, bf16[256,768]{1,0:T(8,128)(2,1)S(1)}, u32[]{:S(2)}, u32[]{:S(2)}) collective-permute-start(bf16[256,768]{1,0:T(8,128)(2,1)} %g_ref.1), channel_id=1, source_target_pairs={{0,1},{1,0},{2,3},{3,2},{4,5},{5,4},{6,7},{7,6},{8,9},{9,8},{10,11... | collective-permute-start | bytes 1179656 | tf_op jit(solution)/shard_map/ppermute | solution.py:712
  1.2 4.1 %collective-permute-start = (bf16[256,768]{1,0:T(8,128)(2,1)}, bf16[256,768]{1,0:T(8,128)(2,1)S(1)}, u32[]{:S(2)}, u32[]{:S(2)}) collective-permute-start(bf16[256,768]{1,0:T(8,128)(2,1)} %x_ref.3), channel_id=1, source_target_pairs={{0,1},{1,0},{2,3},{3,2},{4,5},{5,4},{6,7},{7,6},{8,9},{9,8},{10,11... | collective-permute-start | bytes 1179656 | tf_op jit(solution)/shard_map/ppermute | solution.py:712
  12.6 10.6 %collective-permute-start.2 = (bf16[512,128]{1,0:T(8,128)(2,1)S(1)}, bf16[512,128]{1,0:T(8,128)(2,1)S(1)}, u32[]{:S(2)}, u32[]{:S(2)}) collective-permute-start(bf16[512,128]{1,0:T(8,128)(2,1)S(1)} %get-tuple-element.70), channel_id=1, source_target_pairs={{0,2},{1,3},{2,0},{3,1},{4,6},{5,7},{6,4},{7,5},{8,10},{9,11},{10,... | collective-permute-start | bytes 393224 | tf_op jit(solution)/shard_map/ppermute | solution.py:720
  31.0 35.8 %collective-permute-start.5 = (bf16[2,2,2,384,256]{4,3,2,1,0:T(8,128)(2,1)}, bf16[2,2,2,384,256]{4,3,2,1,0:T(8,128)(2,1)}, u32[]{:S(2)}, u32[]{:S(2)}) collective-permute-start(bf16[2,2,2,384,256]{4,3,2,1,0:T(8,128)(2,1)} %get-tuple-element.73), channel_id=1, source_target_pairs={{0,8},{1,17},{2,10},{3,19},{4,12},{5,21},{6,14},{7,23},{8,0},{9,25... | collective-permute-start | bytes 4718600 | tf_op jit(solution)/shard_map/ppermute | solution.py:720
  32.5 33.2 %collective-permute-start.4 = (bf16[2,768,256]{2,1,0:T(8,128)(2,1)S(1)}, bf16[2,768,256]{2,1,0:T(8,128)(2,1)S(1)}, u32[]{:S(2)}, u32[]{:S(2)}) collective-permute-start(bf16[2,768,256]{2,1,0:T(8,128)(2,1)S(1)} %copy-done.31), channel_id=1, source_target_pairs={{0,2},{1,3},{2,0},{3,1},{4,6},{5,7},{6,4},{7,5},{8,10},{9,11},{10,... | collective-permute-start | bytes 2359304 | tf_op jit(solution)/shard_map/ppermute | solution.py:720
  33.0 22.1 %collective-permute-start.3 = (bf16[1024,128]{1,0:T(8,128)(2,1)S(1)}, bf16[1024,128]{1,0:T(8,128)(2,1)S(1)}, u32[]{:S(2)}, u32[]{:S(2)}) collective-permute-start(bf16[1024,128]{1,0:T(8,128)(2,1)S(1)} %constant_dynamic-update-slice_fusion.refs_4_), channel_id=1, source_target_pairs={{0,4},{1,5},{2,6},{3,7},{4,0},{5,1},{6,2},{7,3},{8,12},{9,13},{10,... | collective-permute-start | bytes 786440 | tf_op jit(solution)/shard_map/ppermute | solution.py:720
  68.5 49.6 %collective-permute-start.13 = (bf16[2,2,384,256]{3,2,1,0:T(8,128)(2,1)S(1)}, bf16[2,2,384,256]{3,2,1,0:T(8,128)(2,1)}, u32[]{:S(2)}, u32[]{:S(2)}) collective-permute-start(bf16[2,2,384,256]{3,2,1,0:T(8,128)(2,1)S(1)} %get-tuple-element.124), channel_id=1, source_target_pairs={{0,16},{1,9},{2,18},{3,11},{4,20},{5,13},{6,22},{7,15},{8,24},{9,1... | collective-permute-start | bytes 2359304 | tf_op jit(solution)/shard_map/ppermute | solution.py:720
  85.3 8.0 %collective-permute-start.8 = (bf16[2,2,256,128]{3,2,1,0:T(8,128)(2,1)S(1)}, bf16[2,2,256,128]{3,2,1,0:T(8,128)(2,1)S(1)}, u32[]{:S(2)}, u32[]{:S(2)}) collective-permute-start(bf16[2,2,256,128]{3,2,1,0:T(8,128)(2,1)S(1)} %get-tuple-element.91), channel_id=1, source_target_pairs={{0,1},{1,0},{2,3},{3,2},{4,5},{5,4},{6,7},{7,6},{8,9},{9,8},{10,11... | collective-permute-start | bytes 786440 | tf_op jit(solution)/shard_map/ppermute | solution.py:712
  89.9 29.7 %collective-permute-start.16 = (bf16[2,2,2,144,256]{4,3,2,1,0:T(8,128)(2,1)S(1)}, bf16[2,2,2,144,256]{4,3,2,1,0:T(8,128)(2,1)S(1)}, u32[]{:S(2)}, u32[]{:S(2)}) collective-permute-start(bf16[2,2,2,144,256]{4,3,2,1,0:T(8,128)(2,1)S(1)} %get-tuple-element.90), channel_id=1, source_target_pairs={{0,8},{1,17},{2,10},{3,19},{4,12},{5,21},{6,14},{7,23},{8,0},{9,25... | collective-permute-start | bytes 1769480 | tf_op jit(solution)/shard_map/ppermute | solution.py:720
  93.4 17.7 %collective-permute-start.10 = (bf16[2,256,128]{2,1,0:T(8,128)(2,1)S(1)}, bf16[2,256,128]{2,1,0:T(8,128)(2,1)S(1)}, u32[]{:S(2)}, u32[]{:S(2)}) collective-permute-start(bf16[2,256,128]{2,1,0:T(8,128)(2,1)S(1)} %get-tuple-element.131), channel_id=1, source_target_pairs={{0,2},{1,3},{2,0},{3,1},{4,6},{5,7},{6,4},{7,5},{8,10},{9,11},{10,... | collective-permute-start | bytes 393224 | tf_op jit(solution)/shard_map/ppermute | solution.py:720
  104.4 22.8 %collective-permute-start.18 = (bf16[768,256]{1,0:T(8,128)(2,1)}, bf16[768,256]{1,0:T(8,128)(2,1)S(1)}, u32[]{:S(2)}, u32[]{:S(2)}) collective-permute-start(bf16[768,256]{1,0:T(8,128)(2,1)} %fusion.4), channel_id=1, source_target_pairs={{0,4},{1,5},{2,6},{3,7},{4,0},{5,1},{6,2},{7,3},{8,12},{9,13},{10,... | collective-permute-start | bytes 1179656 | tf_op jit(solution)/shard_map/ppermute | solution.py:720
  118.1 12.2 %collective-permute-start.12 = (bf16[256,768]{1,0:T(8,128)(2,1)}, bf16[256,768]{1,0:T(8,128)(2,1)S(1)}, u32[]{:S(2)}, u32[]{:S(2)}) collective-permute-start(bf16[256,768]{1,0:T(8,128)(2,1)} %get-tuple-element.102), channel_id=1, source_target_pairs={{0,1},{1,0},{2,3},{3,2},{4,5},{5,4},{6,7},{7,6},{8,9},{9,8},{10,11... | collective-permute-start | bytes 1179656 | tf_op jit(solution)/shard_map/ppermute | solution.py:712
  119.5 13.4 %collective-permute-start.14 = (bf16[2,384,256]{2,1,0:T(8,128)(2,1)S(1)}, bf16[2,384,256]{2,1,0:T(8,128)(2,1)S(1)}, u32[]{:S(2)}, u32[]{:S(2)}) collective-permute-start(bf16[2,384,256]{2,1,0:T(8,128)(2,1)S(1)} %get-tuple-element.125), channel_id=1, source_target_pairs={{0,2},{1,3},{2,0},{3,1},{4,6},{5,7},{6,4},{7,5},{8,10},{9,11},{10,... | collective-permute-start | bytes 1179656 | tf_op jit(solution)/shard_map/ppermute | solution.py:720
  119.8 13.0 %collective-permute-start.17 = (bf16[2,2,144,256]{3,2,1,0:T(8,128)(2,1)S(1)}, bf16[2,2,144,256]{3,2,1,0:T(8,128)(2,1)S(1)}, u32[]{:S(2)}, u32[]{:S(2)}) collective-permute-start(bf16[2,2,144,256]{3,2,1,0:T(8,128)(2,1)S(1)} %get-tuple-element.127), channel_id=1, source_target_pairs={{0,16},{1,9},{2,18},{3,11},{4,20},{5,13},{6,22},{7,15},{8,24},{9,1... | collective-permute-start | bytes 884744 | tf_op jit(solution)/shard_map/ppermute | solution.py:720
  124.2 6.1 %collective-permute-start.11 = (bf16[256,128]{1,0:T(8,128)(2,1)S(1)}, bf16[256,128]{1,0:T(8,128)(2,1)S(1)}, u32[]{:S(2)}, u32[]{:S(2)}) collective-permute-start(bf16[256,128]{1,0:T(8,128)(2,1)S(1)} %get-tuple-element.133), channel_id=1, source_target_pairs={{0,4},{1,5},{2,6},{3,7},{4,0},{5,1},{6,2},{7,3},{8,12},{9,13},{10,... | collective-permute-start | bytes 196616 | tf_op jit(solution)/shard_map/ppermute | solution.py:720
  132.9 12.5 %collective-permute-start.15 = (bf16[384,256]{1,0:T(8,128)(2,1)S(1)}, bf16[384,256]{1,0:T(8,128)(2,1)S(1)}, u32[]{:S(2)}, u32[]{:S(2)}) collective-permute-start(bf16[384,256]{1,0:T(8,128)(2,1)S(1)} %fusion.15), channel_id=1, source_target_pairs={{0,4},{1,5},{2,6},{3,7},{4,0},{5,1},{6,2},{7,3},{8,12},{9,13},{10,... | collective-permute-start | bytes 589832 | tf_op jit(solution)/shard_map/ppermute | solution.py:720
  145.6 12.9 %collective-permute-start.19 = (bf16[1152,256]{1,0:T(8,128)(2,1)S(1)}, bf16[1152,256]{1,0:T(8,128)(2,1)S(1)}, u32[]{:S(2)}, u32[]{:S(2)}) collective-permute-start(bf16[1152,256]{1,0:T(8,128)(2,1)S(1)} %pad_maximum_fusion.1), channel_id=1, source_target_pairs={{0,16},{1,9},{2,18},{3,11},{4,20},{5,13},{6,22},{7,15},{8,24},{9,1... | collective-permute-start | bytes 1769480 | tf_op jit(solution)/shard_map/ppermute | solution.py:720
  149.9 6.4 %collective-permute-start.21 = (bf16[2,256,256]{2,1,0:T(8,128)(2,1)S(1)}, bf16[2,256,256]{2,1,0:T(8,128)(2,1)S(1)}, u32[]{:S(2)}, u32[]{:S(2)}) collective-permute-start(bf16[2,256,256]{2,1,0:T(8,128)(2,1)S(1)} %pad_maximum_fusion.2), channel_id=1, source_target_pairs={{0,2},{1,3},{2,0},{3,1},{4,6},{5,7},{6,4},{7,5},{8,10},{9,11},{10,... | collective-permute-start | bytes 786440 | tf_op jit(solution)/shard_map/ppermute | solution.py:720
  156.3 7.3 %collective-permute-start.22 = (bf16[256,256]{1,0:T(8,128)(2,1)S(1)}, bf16[256,256]{1,0:T(8,128)(2,1)S(1)}, u32[]{:S(2)}, u32[]{:S(2)}) collective-permute-start(bf16[256,256]{1,0:T(8,128)(2,1)S(1)} %fusion.20), channel_id=1, source_target_pairs={{0,4},{1,5},{2,6},{3,7},{4,0},{5,1},{6,2},{7,3},{8,12},{9,13},{10,... | collective-permute-start | bytes 393224 | tf_op jit(solution)/shard_map/ppermute | solution.py:720
  158.7 17.9 %collective-permute-start.20 = (bf16[1536,256]{1,0:T(8,128)(2,1)S(1)}, bf16[1536,256]{1,0:T(8,128)(2,1)S(1)}, u32[]{:S(2)}, u32[]{:S(2)}) collective-permute-start(bf16[1536,256]{1,0:T(8,128)(2,1)S(1)} %pad_maximum_fusion.early_send.send_ref), channel_id=1, source_target_pairs={{0,8},{1,17},{2,10},{3,19},{4,12},{5,21},{6,14},{7,23},{8,0},{9,25... | collective-permute-start | bytes 2359304 | tf_op jit(solution)/shard_map/ppermute | solution.py:720
  163.7 7.1 %collective-permute-start.23 = (bf16[256,256]{1,0:T(8,128)(2,1)S(1)}, bf16[256,256]{1,0:T(8,128)(2,1)S(1)}, u32[]{:S(2)}, u32[]{:S(2)}) collective-permute-start(bf16[256,256]{1,0:T(8,128)(2,1)S(1)} %fusion.13), channel_id=1, source_target_pairs={{0,16},{1,9},{2,18},{3,11},{4,20},{5,13},{6,22},{7,15},{8,24},{9,1... | collective-permute-start | bytes 393224 | tf_op jit(solution)/shard_map/ppermute | solution.py:720
  170.8 5.8 %collective-permute-start.24 = (bf16[400,256]{1,0:T(8,128)(2,1)S(1)}, bf16[400,256]{1,0:T(8,128)(2,1)S(1)}, u32[]{:S(2)}, u32[]{:S(2)}) collective-permute-start(bf16[400,256]{1,0:T(8,128)(2,1)S(1)} %pad_maximum_fusion.3.last_send), channel_id=1, source_target_pairs={{0,8},{1,17},{2,10},{3,19},{4,12},{5,21},{6,14},{7,23},{8,0},{9,25... | collective-permute-start | bytes 614408 | tf_op jit(solution)/shard_map/ppermute | solution.py:720
  172.1 5.4 %collective-permute-start.9 = (bf16[256,768]{1,0:T(8,128)(2,1)S(1)}, bf16[256,768]{1,0:T(8,128)(2,1)S(1)}, u32[]{:S(2)}, u32[]{:S(2)}) collective-permute-start(bf16[256,768]{1,0:T(8,128)(2,1)S(1)} %copy-done.32), channel_id=1, source_target_pairs={{0,1},{1,0},{2,3},{3,2},{4,5},{5,4},{6,7},{7,6},{8,9},{9,8},{10,11... | collective-permute-start | bytes 1179656 | tf_op jit(solution)/shard_map/ppermute | solution.py:712
  177.4 2.6 %collective-permute-start.25 = (bf16[920,256]{1,0:T(8,128)(2,1)S(1)}, bf16[920,256]{1,0:T(8,128)(2,1)S(1)}, u32[]{:S(2)}, u32[]{:S(2)}) collective-permute-start(bf16[920,256]{1,0:T(8,128)(2,1)S(1)} %get-tuple-element.115), channel_id=1, source_target_pairs={{0,1},{1,0},{2,3},{3,2},{4,5},{5,4},{6,7},{7,6},{8,9},{9,8},{10,11... | collective-permute-start | bytes 1413128 | tf_op jit(solution)/shard_map/ppermute | solution.py:712
  (35 other events, 320.9 us)

commit v4 on v3

--- a/solution.py
+++ b/solution.py
@@ -36,6 +36,10 @@
     return lax.optimization_barrier((value,) + others)[0]
 
 
+def meet(*values):
+    return lax.optimization_barrier(values)
+
+
 def rope_tables(position):
     inverse = 10000.0 ** (-(2.0 * jnp.arange(HALF, dtype=F32)) / ROT)
     angles = inverse[:, None] * position.astype(F32)[None, :]
@@ -61,17 +65,28 @@
     return value * cdf, cdf + value * pdf
 
 
-def call(kernel, name, outs, specs, out_specs, scratch, limit, flops=1000000):
-    return pl.pallas_call(
+def call(kernel, name, outs, specs, out_specs, scratch, limit, flops=1000):
+    made = pl.pallas_call(
         kernel,
         out_shape=outs,
         grid_spec=pltpu.PrefetchScalarGridSpec(
             num_scalar_prefetch=1, in_specs=specs, out_specs=out_specs, scratch_shapes=scratch
         ),
         compiler_params=pltpu.CompilerParams(vmem_limit_bytes=limit * MIB),
-        cost_estimate=pl.CostEstimate(flops=flops, bytes_accessed=flops // 200, transcendentals=0),
+        cost_estimate=pl.CostEstimate(flops=flops, bytes_accessed=flops, transcendentals=0),
         name=name,
     )
+
+    def placed(scalars, *values):
+        return made(
+            scalars,
+            *(
+                pltpu.with_memory_space_constraint(v, pltpu.HBM) if spec is HBM else v
+                for v, spec in zip(values, specs)
+            ),
+        )
+
+    return placed
 
 
 def attn_kernel(table, place, *refs, blocks, heads, size, n_kv, per_chip, last_call, first_call):
@@ -292,40 +307,41 @@
             vmem_limit_bytes=(24 if keys <= 4096 else 60) * MIB
         ),
         cost_estimate=pl.CostEstimate(
-            flops=24 * width * rows * keys, bytes_accessed=4 * width * rows * 4, transcendentals=0
+            flops=1000, bytes_accessed=1000, transcendentals=0
         ),
         name="attention",
     )(table, place + jnp.array([0, 0, 0, start], jnp.int32), q_t, do_t, cosine, sine, *kvs, *extra)
 
 
 def prologue_kernel(
-    sc, x_hbm, xt, g_hbm, gt, gains, w_hbm, cos_ref, sin_ref, h1_ref, h2_ref, gg_ref, kv_ref, xo, w_kv, sem
+    sc, x_hbm, xt_hbm, g_hbm, gt_hbm, gains, w_hbm, cos_ref, sin_ref, h1_ref, h2_ref, gg_ref, kv_ref, xo, xt, w_kv, sem
 ):
     rows = xt.shape[0]
     copies = [
         pltpu.make_async_copy(x_hbm, xo, sem.at[0]),
-        pltpu.make_async_copy(w_hbm, w_kv, sem.at[1]),
-        pltpu.make_async_copy(g_hbm, gg_ref.at[0:rows, :], sem.at[2]),
+        pltpu.make_async_copy(xt_hbm, xt, sem.at[1]),
+        pltpu.make_async_copy(w_hbm, w_kv, sem.at[2]),
+        pltpu.make_async_copy(g_hbm, gg_ref.at[0:rows, :], sem.at[3]),
+        pltpu.make_async_copy(gt_hbm, gg_ref.at[rows : 2 * rows, :], sem.at[4]),
     ]
     for copy in copies:
         copy.start()
-    gg_ref[rows : 2 * rows, :] = gt[...]
     gain_one, bias_one = gains[0:1, :].astype(F32), gains[1:2, :].astype(F32)
     gain_two, bias_two = gains[2:3, :].astype(F32), gains[3:4, :].astype(F32)
-    for n, x in ((1, xt), (0, xo)):
-        if n == 0:
-            copies[0].wait()
+    for n, x in enumerate((xo, xt)):
+        copies[n].wait()
         for t in range(rows // 128):
             here = slice(n * rows + t * 128, n * rows + (t + 1) * 128)
             hat, unused = normed(x[t * 128 : (t + 1) * 128, :].astype(F32))
             h1_ref[here, :] = (hat * gain_one + bias_one).astype(BF)
             h2_ref[here, :] = (hat * gain_two + bias_two).astype(BF)
-    copies[1].wait()
+    copies[2].wait()
     raw = dot(h1_ref[...], w_kv[...])
     kv = turn(raw.T, cos_ref[...], sin_ref[...]).T.astype(BF)
     kv_ref[pl.ds(pl.multiple_of(sc[0] * rows, rows), rows), :] = kv[:rows]
     kv_ref[pl.ds(pl.multiple_of((1 - sc[0]) * rows, rows), rows), :] = kv[rows:]
-    copies[2].wait()
+    copies[3].wait()
+    copies[4].wait()
 
 
 def half_copies(sc, w_query, w_out, query_s, out_s, sem):
@@ -442,7 +458,6 @@
             pltpu.SemaphoreType.DMA((2,)),
         ],
         56,
-        8 * rows * width * span,
     )(sc, h_two, g_two, w_up, w_down)
 
 
@@ -495,7 +510,6 @@
             pltpu.VMEM((width, width), BF),
         ],
         16,
-        2 * rows * width * width,
     )(sc, h_one, *dqs, *mixes, *gots, g_two)
 
 
@@ -609,14 +623,13 @@
             keep_ref[high_bit] = block
 
 
-def down_kernel(sc, send_ref, got_ref, out_ref, *, width):
+def down_kernel(sc, a_send, a_got, send_ref, got_ref, out_ref, *, width):
     block = width // WIDE * LANES
     for k in range(3):
         for b in range(width // WIDE):
             here = slice(b * LANES, (b + 1) * LANES)
             if k == 0:
-                at = slice(2 * block + b * LANES, 2 * block + (b + 1) * LANES)
-                value = send_ref[at, :].astype(F32) + got_ref[at, :].astype(F32)
+                value = a_send[here, :].astype(F32) + a_got[here, :].astype(F32)
             else:
                 at = pl.ds(pl.multiple_of(sc[3] * block + b * LANES, LANES), LANES)
                 mine = send_ref[at, :].astype(F32)
@@ -624,15 +637,15 @@
             out_ref[k * LANES : (k + 1) * LANES, b * WIDE : (b + 1) * WIDE] = value
 
 
-def up_block(sc, k, b, parity, early_send, early_got, width, part):
+def up_block(sc, k, b, parity, a_send, a_got, b_send, b_got, width, part):
     block = width // WIDE * LANES
     off = b * 2 * part + parity * part
     if k == 0:
-        at = pl.ds(pl.multiple_of(3 * block + off, 32), part)
-        return early_send[at, :].astype(F32) + early_got[at, :].astype(F32)
+        at = pl.ds(pl.multiple_of(block + off, 32), part)
+        return a_send[at, :].astype(F32) + a_got[at, :].astype(F32)
     at = pl.ds(pl.multiple_of((1 - sc[3]) * block + off, 32), part)
     return jnp.where(
-        sc[2] == k - 1, early_send[at, :].astype(F32), early_got[at, :].astype(F32)
+        sc[2] == k - 1, b_send[at, :].astype(F32), b_got[at, :].astype(F32)
     )
 
 
@@ -651,14 +664,14 @@
     return jnp.concatenate(pieces, 0)
 
 
-def pack_kernel(sc, early_send, early_got, last_send, last_got, out_ref, own_ref, *, width, part, quarter):
+def pack_kernel(sc, a_send, a_got, b_send, b_got, last_send, last_got, out_ref, own_ref, *, width, part, quarter):
     for which, ref in ((1, out_ref), (0, own_ref)):
         parity = sc[0] if which == 0 else 1 - sc[0]
         at = 0
         for k in range(3):
             for b in range(2):
                 ref[at : at + part, :] = up_block(
-                    sc, k, b, parity, early_send, early_got, width, part
+                    sc, k, b, parity, a_send, a_got, b_send, b_got, width, part
                 ).astype(BF)
                 at += part
         for b in range(width // WIDE):
@@ -760,7 +773,7 @@
     per_chip = 2 * rows // BLK
     table = block_table[0]
     sc = jnp.stack([core, chip, links.bit(0), links.bit(1)]).astype(jnp.int32)
-    gains = jnp.stack([ln1_gain, ln1_bias, ln2_gain, ln2_bias])
+    gains = jnp.concatenate([ln1_gain, ln1_bias, ln2_gain, ln2_bias]).reshape(4, width)
 
     x_other, g_other = links.swap(layer_input), links.swap(cotangent)
     own_slots = lax.dynamic_slice_in_dim(table, chip * per_chip, per_chip).reshape(2, -1)
@@ -777,27 +790,30 @@
         prologue_kernel,
         "prologue",
         [shape((2 * rows, width), BF)] * 3 + [shape((2 * rows, lanes), BF)],
-        [HBM, VM, HBM, VM, VM, HBM, VM, VM],
+        [HBM] * 4 + [VM, HBM, VM, VM],
         [VM] * 4,
         [
             pltpu.VMEM((rows, width), BF),
+            pltpu.VMEM((rows, width), BF),
             pltpu.VMEM((width, lanes), BF),
-            pltpu.SemaphoreType.DMA((3,)),
+            pltpu.SemaphoreType.DMA((5,)),
         ],
-        16,
+        56,
     )(sc, layer_input, x_other, cotangent, g_other, gains, w_keyval, cosine, sine)
 
     kv_got = links.flip(kv_low, 1)
     ffn = functools.partial(
         ffn_gradients, sc, w_up=w_up, w_down=w_down, part=part_hidden, n_pair=n_pair
     )
-    act_0, dup_0, a_send, a_keep = ffn(h_two, g_two, n=0)
-    a_got = links.flip(a_send, 1)
+    act_1, dup_1, b_send = ffn(h_two, g_two, n=1)
+    b_send, kv_got = meet(b_send, kv_got)
     kv_near = jnp.concatenate([kv_low, kv_got], 0)
     kv_far = links.flip(kv_near, 2)
-    act_1, dup_1, b_send = ffn(tie(h_two, a_keep, kv_near), g_two, n=1)
     b_got = links.cross(b_send, 0)
-    act_2, dup_2, b_keep = ffn(tie(h_two, b_send), g_two, n=2)
+    act_2, dup_2, b_keep = ffn(tie(h_two, b_send, kv_near), g_two, n=2)
+    act_0, dup_0, a_send, a_keep = ffn(tie(h_two, b_keep), g_two, n=0)
+    a_send, kv_far = meet(a_send, kv_far)
+    a_got = links.flip(a_send, 1)
 
     q_t, do_t = call(
         functools.partial(project_kernel, size=size),
@@ -811,7 +827,10 @@
             pltpu.SemaphoreType.DMA((2,)),
         ],
         16,
-    )(sc, tie(h_one, b_keep), g_two, cosine, sine, w_query, w_out)
+    )(sc, tie(h_one, a_send), g_two, cosine, sine, w_query, w_out)
+    q_t, b_got = meet(q_t, b_got)
+    b_send = add(b_keep[1], b_got[1])
+    b_got_2 = links.cross(b_send, 1)
 
     place = jnp.stack([chip * per_chip, core * (rows // BLK), chip, 0 * chip]).astype(jnp.int32)
     count = rows // BLK
@@ -819,48 +838,36 @@
         attention, table, place, do_t=do_t, cosine=cosine, sine=sine, kvs=(kv_near, kv_far),
         count=count, per_chip=per_chip, split=True,
     )
-    mix_0, dq_0, carried = attend(q_t=q_t, carried=None, start=0, last_call=False)
+    mix_0, dq_0, carried = attend(
+        q_t=tie(q_t, b_send), carried=None, start=0, last_call=False
+    )
+    carried, a_got, b_got_2, b_got = meet(carried, a_got, b_got_2, b_got)
     mix_0_got = links.swap(mix_0)
-    a_got, b_got = tie(a_got, carried), tie(b_got, carried)
-    a_send = add(a_keep[1], a_got[1])
+    b_keep = add(b_keep[0], b_got[0])
+    b_send = add(b_keep[1], b_got_2[1])
+    b_got_3 = links.flip(b_send, 1)
+    a_send = add(a_keep[1], tie(a_got, b_send)[1])
     a_got_2 = links.flip(a_send, 2)
-    b_send = add(b_keep[1], b_got[1])
-    b_got_2 = links.cross(b_send, 1)
     mix_1, dq_1, dkv_send, dkv_keep = attend(
-        q_t=tie(q_t, a_send, b_send), carried=carried, start=count, last_call=True
-    )
-    a_keep, b_keep = add(a_keep[0], a_got[0]), add(b_keep[0], b_got[0])
-
+        q_t=tie(q_t, a_send, b_send, carried), carried=carried, start=count, last_call=True
+    )
+    mix_1, dkv_send, mix_0_got, a_got_2 = meet(mix_1, dkv_send, mix_0_got, a_got_2)
     dkv_got = links.swap(dkv_send)
     mix_1_got = links.swap(mix_1)
+    dkv_got, mix_1_got = meet(dkv_got, mix_1_got)
+    dkv_send = add(dkv_keep[1], dkv_got[1])
+    dkv_got_2 = links.flip(dkv_send, 1)
     late_send, late_keep = late_gradients(
-        sc, h_one, (dq_0, dq_1), (mix_0, mix_1), (mix_0_got, mix_1_got), g_two, n_pair
-    )
+        sc, tie(h_one, dkv_send), (dq_0, dq_1), (mix_0, mix_1), (mix_0_got, mix_1_got), g_two, n_pair
+    )
+    late_send, dkv_got, dkv_got_2 = meet(late_send, dkv_got, dkv_got_2)
     late_got = links.cross(late_send, 0)
-    dkv_got_2 = links.flip(add(dkv_keep[1], dkv_got[1]), 1)
     dkv_keep = add(dkv_keep[0], dkv_got[0])
-    b_got_2 = tie(b_got_2, late_send)
-    b_got_3 = links.flip(add(b_keep[1], b_got_2[1]), 1)
-    b_keep = add(b_keep[0], b_got_2[0])
+    dkv_send = add(dkv_keep[1], dkv_got_2[1])
+    dkv_got_3 = links.flip(dkv_send, 2)
+    b_got_3 = links.flip(tie(b_send, dkv_send), 1)
 
     w_specs = [HBM] * 2
-    out_own, out_send = call(
-        functools.partial(out_kernel, part=part_hidden, n_pair=n_pair),
-        "outputs",
-        [shape((rows, width), F32), shape((rows, width), BF)],
-        [VM] * 6 + w_specs,
-        [VM] * 2,
-        [
-            pltpu.VMEM((3, n_pair * LANES, width), BF),
-            pltpu.VMEM((half, width), BF),
-            pltpu.SemaphoreType.DMA((2,)),
-        ],
-        56,
-    )(sc, act_0, act_1, tie(act_2, late_send, dkv_got), mix_0, mix_1, layer_input, w_down, w_out)
-    out_got = links.swap(out_send)
-    dkv_got_2 = tie(dkv_got_2, out_send)
-    dkv_got_3 = links.flip(add(dkv_keep[1], dkv_got_2[1]), 2)
-    dkv_keep = add(dkv_keep[0], dkv_got_2[0])
     hat_own, hat_send, sums = call(
         functools.partial(hat_kernel, part=part_hidden, n_pair=n_pair),
         "norms",
@@ -874,19 +881,15 @@
         ],
         56,
     )(
-        sc, dup_0, dup_1, tie(dup_2, out_send, dkv_got_2), dq_0, dq_1, layer_input, x_other, gains,
+        sc, dup_0, dup_1, tie(dup_2, late_send, dkv_send), dq_0, dq_1, layer_input, x_other, gains,
         w_up, w_query,
     )
+    hat_send, dkv_got_2, dkv_got_3, late_got = meet(hat_send, dkv_got_2, dkv_got_3, late_got)
     hat_got = links.swap(hat_send)
-    layer_output = low(out_own + out_got.astype(F32))
-
-    late_got = tie(late_got, hat_send)
-    late_got_2 = links.cross(add(late_keep[1], late_got[1]), 1)
-    late_keep = add(late_keep[0], late_got[0])
-    b_got_3 = tie(b_got_3, hat_send)
-    b_got_4 = links.flip(add(b_keep[1], b_got_3[1]), 2)
-    b_keep = add(b_keep[0], b_got_3[0])
-    a_sum = add(a_keep, tie(a_got_2, hat_send))
+    dkv_keep = add(dkv_keep[0], dkv_got_2[0])
+    late_send = add(late_keep[1], late_got[1])
+    late_got_2 = links.cross(late_send, 1)
+    late_send, hat_got = meet(late_send, hat_got)
 
     few = part // 2 + 8
     in_grad, few_send, few_keep = call(
@@ -898,24 +901,54 @@
         [],
         16,
     )(
-        sc, dkv_keep, dkv_got_3, cosine, sine, w_keyval, h_one, layer_input, gains, hat_own, hat_got,
-        sums, cotangent,
-    )
-
-    late_got_2 = tie(late_got_2, few_send)
+        sc, dkv_keep, tie(dkv_got_3, late_send), cosine, sine, w_keyval, h_one, layer_input,
+        gains, hat_own, hat_got, sums, cotangent,
+    )
+    few_send, late_got, late_got_2, b_got_2, b_got_3 = meet(
+        few_send, late_got, late_got_2, b_got_2, b_got_3
+    )
+    late_keep = add(late_keep[0], late_got[0])
     quarter = late_keep.shape[2]
     last_send = jnp.concatenate([add(late_keep[1], late_got_2[1]), few_send], 1)
     last_got = links.flip(last_send, 1)
+    b_keep = add(b_keep[0], b_got_2[0])
+    b_send = add(b_keep[1], b_got_3[1])
+    b_got_4 = links.flip(b_send, 2)
+    a_sum = add(add(a_keep[0], a_got[0]), a_got_2)
+    a_got = links.cross(a_sum, 1)
+
+    out_own, out_send = call(
+        functools.partial(out_kernel, part=part_hidden, n_pair=n_pair),
+        "outputs",
+        [shape((rows, width), F32), shape((rows, width), BF)],
+        [VM] * 6 + w_specs,
+        [VM] * 2,
+        [
+            pltpu.VMEM((3, n_pair * LANES, width), BF),
+            pltpu.VMEM((half, width), BF),
+            pltpu.SemaphoreType.DMA((2,)),
+        ],
+        56,
+    )(
+        sc, act_0, act_1, tie(act_2, last_send, b_send, a_sum), mix_0, mix_1,
+        layer_input, w_down, w_out,
+    )
+    out_send, last_got, a_got = meet(out_send, last_got, a_got)
+    out_got = links.swap(out_send)
     last_keep = jnp.concatenate([add(late_keep[0], late_got_2[0]), few_keep], 1)
-    early = jnp.concatenate([add(b_keep, tie(b_got_4, last_send)), a_sum], 0)
-    block = early.shape[0] // 3
-    early_got = links.cross(early, 1)
-    last_got_2 = links.flip(add(last_keep[1], last_got[1]), 2)
+    last_send = add(last_keep[1], last_got[1])
+    last_got_2 = links.flip(last_send, 2)
+    a_sum = add(a_sum, a_got)
+    a_got = links.cross(a_sum, 0)
+    out_got, b_got_4 = meet(out_got, b_got_3, b_got_4, a_sum, last_send)[::2][:2]
+    layer_output = low(out_own + out_got.astype(F32))
+    b_sum = add(add(b_keep[0], b_got_3[0]), b_got_4)
+    b_got = links.cross(b_sum, 1)
     last_keep = add(last_keep[0], last_got[0])
-    early = jnp.concatenate(
-        [early[:block], early_got[:block], add(early[block:], early_got[block:])], 0
-    )
-    early_got = links.cross(early, 0)
+    b_got, layer_output = meet(b_got, layer_output)
+    b_sum = jnp.concatenate([b_sum, b_got], 0)
+    b_got = links.cross(b_sum, 0)
+    last_got_2 = meet(last_got_2, b_sum)[0]
     last = add(last_keep, last_got_2)
     last_got = links.cross(last, 1)
     last = jnp.concatenate(
@@ -924,13 +957,14 @@
     last_got = links.cross(last, 0)
     total_down = call(
         functools.partial(down_kernel, width=width),
-        "down", shape((part_hidden, width), F32), [VM] * 2, VM, [], 8,
-    )(sc, early, early_got)
+        "down", shape((part_hidden, width), F32), [VM] * 4, VM, [], 8,
+    )(sc, tie(a_sum, last), a_got, b_sum, b_got)
+    total_down, last_got = meet(total_down, last_got)
     size_out = 9 * part + few
     other, own = call(
         functools.partial(pack_kernel, width=width, part=part, quarter=quarter),
-        "pack", [shape((size_out, WIDE), BF)] * 2, [VM] * 4, [VM] * 2, [], 8,
-    )(sc, early, early_got, last, last_got)
+        "pack", [shape((size_out, WIDE), BF)] * 2, [VM] * 6, [VM] * 2, [], 8,
+    )(sc, a_sum, a_got, b_sum, b_got, last, last_got)
     got = links.swap(other)
     total_up, total_query, total_out, total_kv, norm = call(
         functools.partial(final_kernel, part=part, n_pair=n_pair),

time: 181 us -> 156 us (0.86); the launches traced: 182 us -> 156 us
  starting transfers between devices: 47.5 us -> 31.6 us
  waiting for transfers between devices: 41.4 us -> 26.7 us
  other arithmetic: 6.31 us -> 11.6 us
  local copies, waits for them, and re-layouts: 9.1 us -> 4.15 us
  Pallas kernels: 76.8 us -> 80.3 us
    ppermute x18 -> x20, starting transfers between devices: 45.3 us -> 26.9 us  [permute(): return lax.ppermute(value, ('grp', 'ctx'), pairs)]
    ppermute x18 -> x20, waiting for transfers between devices: 40.2 us -> 23.4 us  [permute(): return lax.ppermute(value, ('grp', 'ctx'), pairs)]
    pallas_call x12, Pallas kernels: 49.9 us -> 53.4 us  [placed(): made(scalars, *(pltpu.with_memory_space_constraint(v, pltpu.HBM) if spec...]
    convert_element_type x14 -> x19, other arithmetic: 4.88 us -> 8.3 us  [add(): return (keep.astype(F32) + got.astype(F32)).astype(BF)]
    unnamed x67 -> x61, local copies, waits for them, and re-layouts: 4.96 us -> 2.16 us
    another operation x4 -> x0, local copies, waits for them, and re-layouts: 2.74 us -> none  [shards_small(): gains = jnp.stack([ln1_gain, ln1_bias, ln2_gain, ln2_bias])]
    ppermute x8, starting transfers between devices: 2.28 us -> 4.74 us  [swap(): return lax.ppermute(value, 'ctx', [(i, i ^ 1) for i in range(self.n_ctx)])]
    ppermute x8, waiting for transfers between devices: 1.23 us -> 3.36 us  [swap(): return lax.ppermute(value, 'ctx', [(i, i ^ 1) for i in range(self.n_ctx)])]
  transfers between devices with their start and end apart: 26 -> 28, of which waited for: 9 -> 15; matrix products, arithmetic and copies ran while one was open for 4% -> 6% of each run, Pallas kernels for 36% -> 47%
where the time goes in v4:
time: 156 us
  Pallas kernels  80.3 us (51%)
  starting transfers between devices  31.6 us (20%)
  waiting for transfers between devices  26.7 us (17%)
  other arithmetic  11.6 us (7%)
  local copies, waits for them, and re-layouts  4.15 us (3%)
    pallas_call x12, Pallas kernels, placed(): made(scalars, *(pltpu.with_memory_space_constraint(v, pltpu.HBM) if spec...  53.4 us
    ppermute x20, starting transfers between devices, permute(): return lax.ppermute(value, ('grp', 'ctx'), pairs)  26.9 us
    pallas_call x2, Pallas kernels, attention(): pl.pallas_call(functools.partial(attn_kernel, blocks=blocks, heads=heads,...  26.9 us
    ppermute x20, waiting for transfers between devices, permute(): return lax.ppermute(value, ('grp', 'ctx'), pairs)  23.4 us
    convert_element_type x19, other arithmetic, add(): return (keep.astype(F32) + got.astype(F32)).astype(BF)  8.3 us
    ppermute x8, starting transfers between devices, swap(): return lax.ppermute(value, 'ctx', [(i, i ^ 1) for i in range(self.n_ctx)])  4.74 us
    ppermute x8, waiting for transfers between devices, swap(): return lax.ppermute(value, 'ctx', [(i, i ^ 1) for i in range(self.n_ctx)])  3.36 us
  transfers between devices with their start and end apart: 28, of which 15 were waited for; matrix products, arithmetic and copies ran while one was open for 6% of the time, Pallas kernels for 47%

profile of v4, /device:TPU:0, one launch (start us, length us, event | category | flops | bytes accessed | tf_op | source)
XLA Modules:
  0.0 155.6 jit_solution(10290329353403902279)
XLA Ops:
  5.9 5.1 %prologue.1 = (bf16[512,768]{1,0:T(8,128)(2,1)}, bf16[512,768]{1,0:T(8,128)(2,1)}, bf16[512,768]{1,0:T(8,128)(2,1)}, bf16[512,128]{1,0:T(8,128)(2,1)}) custom-call(s32[4]{0:T(128)} %pad_add_fusion.sc, bf16[256,768]{1,0:T(8,128)(2,1)} %x_ref.3, bf16[256,768]{1,0:T(8,128)(2,1)} %copy-done.18, bf16[256,768]{1,0:T(8,128)(2,1)} %g_ref.1, ...), custom_call_target="tpu_custom_call" | custom-call | flops 1000 | bytes 1000 | tf_op jit(solution)/shard_map/prologue/pallas_call | solution.py:81
  11.0 3.1 %collective-permute-start.2 = (bf16[512,128]{1,0:T(8,128)(2,1)}, bf16[512,128]{1,0:T(8,128)(2,1)S(1)}, u32[]{:S(2)}, u32[]{:S(2)}) collective-permute-start(bf16[512,128]{1,0:T(8,128)(2,1)} %get-tuple-element.104), channel_id=1, source_target_pairs={{0,2},{1,3},{2,0},{3,1},{4,6},{5,7},{6,4},{7,5},{8,10},{9,11},{10,... | collective-permute-start | bytes 393224 | tf_op jit(solution)/shard_map/ppermute | solution.py:733
  14.1 7.7 %ffn_gradients.3 = (bf16[512,512]{1,0:T(8,128)(2,1)}, bf16[512,512]{1,0:T(8,128)(2,1)}, bf16[2,2,2,384,256]{4,3,2,1,0:T(8,128)(2,1)}) custom-call(s32[4]{0:T(128)} %pad_add_fusion.sc, bf16[512,768]{1,0:T(8,128)(2,1)} %get-tuple-element.110.h_ref, bf16[512,768]{1,0:T(8,128)(2,1)} %get-tuple-element.102.g_ref, bf16[768,3072]{1,0:T(8,128)(2,1)} %w_up.7, ...), custom_call_target="tpu_custom_call" | custom-call | flops 1000 | bytes 1000 | tf_op jit(solution)/shard_map/ffn_gradients/pallas_call | solution.py:81
  23.4 2.6 %collective-permute-start.3 = (bf16[1024,128]{1,0:T(8,128)(2,1)S(1)}, bf16[1024,128]{1,0:T(8,128)(2,1)S(1)}, u32[]{:S(2)}, u32[]{:S(2)}) collective-permute-start(bf16[1024,128]{1,0:T(8,128)(2,1)S(1)} %constant_dynamic-update-slice_fusion.refs_4_), channel_id=1, source_target_pairs={{0,4},{1,5},{2,6},{3,7},{4,0},{5,1},{6,2},{7,3},{8,12},{9,13},{10,... | collective-permute-start | bytes 786440 | tf_op jit(solution)/shard_map/ppermute | solution.py:733
  26.1 7.6 %ffn_gradients.4 = (bf16[512,512]{1,0:T(8,128)(2,1)}, bf16[512,512]{1,0:T(8,128)(2,1)}, bf16[2,2,2,384,256]{4,3,2,1,0:T(8,128)(2,1)}) custom-call(s32[4]{0:T(128)} %pad_add_fusion.sc, bf16[512,768]{1,0:T(8,128)(2,1)} %get-tuple-element.110.h_ref, bf16[512,768]{1,0:T(8,128)(2,1)} %get-tuple-element.102.g_ref, bf16[768,3072]{1,0:T(8,128)(2,1)} %w_up.7, ...), custom_call_target="tpu_custom_call" | custom-call | flops 1000 | bytes 1000 | tf_op jit(solution)/shard_map/ffn_gradients/pallas_call | solution.py:81
  33.7 7.7 %ffn_gradients.5 = (bf16[512,512]{1,0:T(8,128)(2,1)}, bf16[512,512]{1,0:T(8,128)(2,1)}, bf16[2,768,256]{2,1,0:T(8,128)(2,1)}, bf16[2,768,256]{2,1,0:T(8,128)(2,1)}) custom-call(s32[4]{0:T(128)} %pad_add_fusion.sc, bf16[512,768]{1,0:T(8,128)(2,1)} %get-tuple-element.110.h_ref, bf16[512,768]{1,0:T(8,128)(2,1)} %get-tuple-element.102.g_ref, ...), custom_call_target="tpu_custom_call" | custom-call | flops 1000 | bytes 1000 | tf_op jit(solution)/shard_map/ffn_gradients/pallas_call | solution.py:81
  42.0 2.8 %project.1 = (bf16[384,512]{1,0:T(8,128)(2,1)S(1)}, f32[384,512]{1,0:T(8,128)S(1)}) custom-call(s32[4]{0:T(128)S(1)} %copy-done.13, bf16[512,768]{1,0:T(8,128)(2,1)S(1)} %copy-done.1, bf16[512,768]{1,0:T(8,128)(2,1)S(1)} %copy-done, f32[8,512]{1,0:T(8,128)S(1)} %copy-done.11, f32[8,512]{1,0:T(8,128)S(1)} %copy-done.10, bf16[768,768]{1,0:T(8,128)(2,1)} %w_query.3, ...), custom_call_target="tpu_custom_call" | custom-call | flops 1000 | bytes 1000 | tf_op jit(solution)/shard_map/project/pallas_call | solution.py:81
  48.7 10.5 %attention.2 = (bf16[384,256]{1,0:T(8,128)(2,1)S(1)}, bf16[384,256]{1,0:T(8,128)(2,1)S(1)}, f32[2048,128]{1,0:T(8,128)S(1)}) custom-call(s32[16]{0:T(128)S(1)} %bitcast.103, s32[4]{0:T(128)S(1)} %get-tuple-element.192.place, bf16[384,512]{1,0:T(8,128)(2,1)S(1)} %get-tuple-element.127.refs_0_, f32[384,512]{1,0:T(8,128)S(1)} %get-tuple-element.118.refs_1_, ...), custom_call_target="tpu_custom_call" | custom-call | flops 1000 | bytes 1000 | tf_op jit(solution)/shard_map/attention/pallas_call | solution.py:273
  61.9 1.9 %fusion.6 = bf16[2,384,256]{2,1,0:T(8,128)(2,1)} fusion(bf16[1,2,2,384,256]{4,3,2,1,0:T(8,128)(2,1)S(1)} %add_convert_fusion, bf16[2,2,384,256]{3,2,1,0:T(8,128)(2,1)} %collective-permute-done.6), kind=kLoop, calls=%fused_computation.17 | loop fusion | flops 786432 | bytes 1179648 | tf_op jit(solution)/shard_map/convert_element_type | solution.py:753
  65.3 2.9 %collective-permute-start.7 = (bf16[384,256]{1,0:T(8,128)(2,1)S(1)}, bf16[384,256]{1,0:T(8,128)(2,1)S(1)}, u32[]{:S(2)}, u32[]{:S(2)}) collective-permute-start(bf16[384,256]{1,0:T(8,128)(2,1)S(1)} %get-tuple-element.131.mix0), channel_id=1, source_target_pairs={{0,1},{1,0},{2,3},{3,2},{4,5},{5,4},{6,7},{7,6},{8,9},{9,8},{10,11... | collective-permute-start | bytes 589832 | tf_op jit(solution)/shard_map/ppermute | solution.py:725
  68.2 16.3 %attention.3 = (bf16[384,256]{1,0:T(8,128)(2,1)S(1)}, bf16[384,256]{1,0:T(8,128)(2,1)S(1)}, bf16[2,2,256,128]{3,2,1,0:T(8,128)(2,1)S(1)}, bf16[2,2,256,128]{3,2,1,0:T(8,128)(2,1)S(1)}) custom-call(s32[16]{0:T(128)S(1)} %bitcast.104, s32[4]{0:T(128)S(1)} %get-tuple-element.191.place, bf16[384,512]{1,0:T(8,128)(2,1)S(1)} %get-tuple-element.127.refs_0_, ...), custom_call_target="tpu_custom_call" | custom-call | flops 1000 | bytes 1000 | tf_op jit(solution)/shard_map/attention/pallas_call | solution.py:273
  86.6 1.9 %late_gradients.1 = (bf16[2,2,2,144,256]{4,3,2,1,0:T(8,128)(2,1)S(1)}, bf16[2,2,2,144,256]{4,3,2,1,0:T(8,128)(2,1)S(1)}) custom-call(s32[4]{0:T(128)S(1)} %copy-done.13, bf16[512,768]{1,0:T(8,128)(2,1)S(1)} %copy-done.1, bf16[384,256]{1,0:T(8,128)(2,1)S(1)} %get-tuple-element.136.dq0, bf16[384,256]{1,0:T(8,128)(2,1)S(1)} %get-tuple-element.137.dq1, ...), custom_call_target="tpu_custom_call" | custom-call | flops 1000 | bytes 1000 | tf_op jit(solution)/shard_map/late_gradients/pallas_call | solution.py:81
  88.5 3.6 %collective-permute-done.11 = bf16[2,256,128]{2,1,0:T(8,128)(2,1)S(1)} collective-permute-done((bf16[2,256,128]{2,1,0:T(8,128)(2,1)S(1)}, bf16[2,256,128]{2,1,0:T(8,128)(2,1)S(1)}, u32[]{:S(2)}, u32[]{:S(2)}) %collective-permute-start.11) | collective-permute-done | bytes 131104 | tf_op jit(solution)/shard_map/ppermute | solution.py:733
  92.1 4.4 %collective-permute-start.13 = (bf16[2,2,2,144,256]{4,3,2,1,0:T(8,128)(2,1)S(1)}, bf16[2,2,2,144,256]{4,3,2,1,0:T(8,128)(2,1)S(1)}, u32[]{:S(2)}, u32[]{:S(2)}) collective-permute-start(bf16[2,2,2,144,256]{4,3,2,1,0:T(8,128)(2,1)S(1)} %get-tuple-element.145), channel_id=1, source_target_pairs={{0,8},{1,17},{2,10},{3,19},{4,12},{5,21},{6,14},{7,23},{8,0},{9,25... | collective-permute-start | bytes 1769480 | tf_op jit(solution)/shard_map/ppermute | solution.py:733
  97.0 7.0 %norms.1 = (f32[256,768]{1,0:T(8,128)}, bf16[256,768]{1,0:T(8,128)(2,1)}, f32[8,768]{1,0:T(8,128)}) custom-call(s32[4]{0:T(128)} %pad_add_fusion.sc, bf16[512,512]{1,0:T(8,128)(2,1)} %get-tuple-element.142.d0, bf16[512,512]{1,0:T(8,128)(2,1)} %get-tuple-element.143.d1, bf16[512,512]{1,0:T(8,128)(2,1)} %get-tuple-element.147.d2, bf16[384,256]{1,0:T(8,128)(2,1)} %copy-done.8, ...), custom_call_target="tpu_custom_call" | custom-call | flops 1000 | bytes 1000 | tf_op jit(solution)/shard_map/norms/pallas_call | solution.py:81
  104.5 4.7 %collective-permute-start.15 = (bf16[2,2,144,256]{3,2,1,0:T(8,128)(2,1)S(1)}, bf16[2,2,144,256]{3,2,1,0:T(8,128)(2,1)S(1)}, u32[]{:S(2)}, u32[]{:S(2)}) collective-permute-start(bf16[2,2,144,256]{3,2,1,0:T(8,128)(2,1)S(1)} %fusion.10), channel_id=1, source_target_pairs={{0,16},{1,9},{2,18},{3,11},{4,20},{5,13},{6,22},{7,15},{8,24},{9,1... | collective-permute-start | bytes 884744 | tf_op jit(solution)/shard_map/ppermute | solution.py:733
  111.2 2.5 %last.1 = (f32[256,768]{1,0:T(8,128)}, bf16[2,112,256]{2,1,0:T(8,128)(2,1)S(1)}, bf16[2,112,256]{2,1,0:T(8,128)(2,1)S(1)}) custom-call(s32[4]{0:T(128)S(1)} %copy-done.14, bf16[256,128]{1,0:T(8,128)(2,1)S(1)} %fusion.24.dkv_a, bf16[256,128]{1,0:T(8,128)(2,1)S(1)} %collective-permute-done.12.dkv_b, f32[8,512]{1,0:T(8,128)S(1)} %copy-done.11, ...), custom_call_target="tpu_custom_call" | custom-call | flops 1000 | bytes 1000 | tf_op jit(solution)/shard_map/last/pallas_call | solution.py:81
  115.6 2.3 %collective-permute-start.20 = (bf16[384,256]{1,0:T(8,128)(2,1)S(1)}, bf16[384,256]{1,0:T(8,128)(2,1)S(1)}, u32[]{:S(2)}, u32[]{:S(2)}) collective-permute-start(bf16[384,256]{1,0:T(8,128)(2,1)S(1)} %fusion.15), channel_id=1, source_target_pairs={{0,4},{1,5},{2,6},{3,7},{4,0},{5,1},{6,2},{7,3},{8,12},{9,13},{10,... | collective-permute-start | bytes 589832 | tf_op jit(solution)/shard_map/ppermute | solution.py:733
  117.9 6.7 %outputs.1 = (f32[256,768]{1,0:T(8,128)}, bf16[256,768]{1,0:T(8,128)(2,1)}) custom-call(s32[4]{0:T(128)} %pad_add_fusion.sc, bf16[512,512]{1,0:T(8,128)(2,1)} %get-tuple-element.161.a0, bf16[512,512]{1,0:T(8,128)(2,1)} %get-tuple-element.162.a1, bf16[512,512]{1,0:T(8,128)(2,1)} %get-tuple-element.168.a2, bf16[384,256]{1,0:T(8,128)(2,1)} %copy-done.6, ...), custom_call_target="tpu_custom_call" | custom-call | flops 1000 | bytes 1000 | tf_op jit(solution)/shard_map/outputs/pallas_call | solution.py:81
  126.7 1.8 %collective-permute-done.20 = bf16[384,256]{1,0:T(8,128)(2,1)S(1)} collective-permute-done((bf16[384,256]{1,0:T(8,128)(2,1)S(1)}, bf16[384,256]{1,0:T(8,128)(2,1)S(1)}, u32[]{:S(2)}, u32[]{:S(2)}) %collective-permute-start.20) | collective-permute-done | bytes 196640 | tf_op jit(solution)/shard_map/ppermute | solution.py:733
  129.6 4.8 %collective-permute-done.21 = bf16[384,256]{1,0:T(8,128)(2,1)S(1)} collective-permute-done((bf16[384,256]{1,0:T(8,128)(2,1)S(1)}, bf16[384,256]{1,0:T(8,128)(2,1)S(1)}, u32[]{:S(2)}, u32[]{:S(2)}) %collective-permute-start.21) | collective-permute-done | bytes 196640 | tf_op jit(solution)/shard_map/ppermute | solution.py:733
  138.3 3.3 %collective-permute-done.25 = bf16[256,256]{1,0:T(8,128)(2,1)S(1)} collective-permute-done((bf16[256,256]{1,0:T(8,128)(2,1)S(1)}, bf16[256,256]{1,0:T(8,128)(2,1)S(1)}, u32[]{:S(2)}, u32[]{:S(2)}) %collective-permute-start.25) | collective-permute-done | bytes 131104 | tf_op jit(solution)/shard_map/ppermute | solution.py:733
  144.1 4.2 %collective-permute-done.23.got_ref.b_got = bf16[768,256]{1,0:T(8,128)(2,1)S(1)} collective-permute-done((bf16[768,256]{1,0:T(8,128)(2,1)S(1)}, bf16[768,256]{1,0:T(8,128)(2,1)S(1)}, u32[]{:S(2)}, u32[]{:S(2)}) %collective-permute-start.23) | collective-permute-done | bytes 393248 | tf_op jit(solution)/shard_map/ppermute | solution.py:733
  153.2 1.9 %final.1 = (f32[96,3072]{1,0:T(8,128)}, f32[96,768]{1,0:T(8,128)}, f32[96,768]{1,0:T(8,128)}, f32[96,128]{1,0:T(8,128)}, f32[8,256]{1,0:T(8,128)S(1)}) custom-call(s32[4]{0:T(128)S(1)} %copy-done.15, bf16[920,256]{1,0:T(8,128)(2,1)S(1)} %get-tuple-element.183.own_ref, bf16[920,256]{1,0:T(8,128)(2,1)S(1)} %collective-permute-done.27.got_ref), custom_call_target="tpu_custom_call" | custom-call | flops 1000 | bytes 1000 | tf_op jit(solution)/shard_map/final/pallas_call | solution.py:81
  (145 shorter events, 36.9 us)
Async XLA Ops:
  0.6 4.4 %collective-permute-start.1 = (bf16[256,768]{1,0:T(8,128)(2,1)}, bf16[256,768]{1,0:T(8,128)(2,1)S(1)}, u32[]{:S(2)}, u32[]{:S(2)}) collective-permute-start(bf16[256,768]{1,0:T(8,128)(2,1)} %g_ref.1), channel_id=1, source_target_pairs={{0,1},{1,0},{2,3},{3,2},{4,5},{5,4},{6,7},{7,6},{8,9},{9,8},{10,11... | collective-permute-start | bytes 1179656 | tf_op jit(solution)/shard_map/ppermute | solution.py:725
  1.2 3.8 %collective-permute-start = (bf16[256,768]{1,0:T(8,128)(2,1)}, bf16[256,768]{1,0:T(8,128)(2,1)S(1)}, u32[]{:S(2)}, u32[]{:S(2)}) collective-permute-start(bf16[256,768]{1,0:T(8,128)(2,1)} %x_ref.3), channel_id=1, source_target_pairs={{0,1},{1,0},{2,3},{3,2},{4,5},{5,4},{6,7},{7,6},{8,9},{9,8},{10,11... | collective-permute-start | bytes 1179656 | tf_op jit(solution)/shard_map/ppermute | solution.py:725
  11.0 10.8 %collective-permute-start.2 = (bf16[512,128]{1,0:T(8,128)(2,1)}, bf16[512,128]{1,0:T(8,128)(2,1)S(1)}, u32[]{:S(2)}, u32[]{:S(2)}) collective-permute-start(bf16[512,128]{1,0:T(8,128)(2,1)} %get-tuple-element.104), channel_id=1, source_target_pairs={{0,2},{1,3},{2,0},{3,1},{4,6},{5,7},{6,4},{7,5},{8,10},{9,11},{10,... | collective-permute-start | bytes 393224 | tf_op jit(solution)/shard_map/ppermute | solution.py:733
  21.8 23.1 %collective-permute-start.4 = (bf16[2,2,2,384,256]{4,3,2,1,0:T(8,128)(2,1)}, bf16[2,2,2,384,256]{4,3,2,1,0:T(8,128)(2,1)S(1)}, u32[]{:S(2)}, u32[]{:S(2)}) collective-permute-start(bf16[2,2,2,384,256]{4,3,2,1,0:T(8,128)(2,1)} %get-tuple-element.105), channel_id=1, source_target_pairs={{0,8},{1,17},{2,10},{3,19},{4,12},{5,21},{6,14},{7,23},{8,0},{9,25... | collective-permute-start | bytes 4718600 | tf_op jit(solution)/shard_map/ppermute | solution.py:733
  23.4 18.0 %collective-permute-start.3 = (bf16[1024,128]{1,0:T(8,128)(2,1)S(1)}, bf16[1024,128]{1,0:T(8,128)(2,1)S(1)}, u32[]{:S(2)}, u32[]{:S(2)}) collective-permute-start(bf16[1024,128]{1,0:T(8,128)(2,1)S(1)} %constant_dynamic-update-slice_fusion.refs_4_), channel_id=1, source_target_pairs={{0,4},{1,5},{2,6},{3,7},{4,0},{5,1},{6,2},{7,3},{8,12},{9,13},{10,... | collective-permute-start | bytes 786440 | tf_op jit(solution)/shard_map/ppermute | solution.py:733
  41.4 19.1 %collective-permute-start.5 = (bf16[2,768,256]{2,1,0:T(8,128)(2,1)}, bf16[2,768,256]{2,1,0:T(8,128)(2,1)}, u32[]{:S(2)}, u32[]{:S(2)}) collective-permute-start(bf16[2,768,256]{2,1,0:T(8,128)(2,1)} %get-tuple-element.112), channel_id=1, source_target_pairs={{0,2},{1,3},{2,0},{3,1},{4,6},{5,7},{6,4},{7,5},{8,10},{9,11},{10,... | collective-permute-start | bytes 2359304 | tf_op jit(solution)/shard_map/ppermute | solution.py:733
  47.1 13.4 %collective-permute-start.6 = (bf16[2,2,384,256]{3,2,1,0:T(8,128)(2,1)}, bf16[2,2,384,256]{3,2,1,0:T(8,128)(2,1)}, u32[]{:S(2)}, u32[]{:S(2)}) collective-permute-start(bf16[2,2,384,256]{3,2,1,0:T(8,128)(2,1)} %fusion), channel_id=1, source_target_pairs={{0,16},{1,9},{2,18},{3,11},{4,20},{5,13},{6,22},{7,15},{8,24},{9,1... | collective-permute-start | bytes 2359304 | tf_op jit(solution)/shard_map/ppermute | solution.py:733
  64.9 19.6 %collective-permute-start.8 = (bf16[768,256]{1,0:T(8,128)(2,1)S(1)}, bf16[768,256]{1,0:T(8,128)(2,1)S(1)}, u32[]{:S(2)}, u32[]{:S(2)}) collective-permute-start(bf16[768,256]{1,0:T(8,128)(2,1)S(1)} %fusion.4), channel_id=1, source_target_pairs={{0,4},{1,5},{2,6},{3,7},{4,0},{5,1},{6,2},{7,3},{8,12},{9,13},{10,... | collective-permute-start | bytes 1179656 | tf_op jit(solution)/shard_map/ppermute | solution.py:733
  65.3 19.2 %collective-permute-start.7 = (bf16[384,256]{1,0:T(8,128)(2,1)S(1)}, bf16[384,256]{1,0:T(8,128)(2,1)S(1)}, u32[]{:S(2)}, u32[]{:S(2)}) collective-permute-start(bf16[384,256]{1,0:T(8,128)(2,1)S(1)} %get-tuple-element.131.mix0), channel_id=1, source_target_pairs={{0,1},{1,0},{2,3},{3,2},{4,5},{5,4},{6,7},{7,6},{8,9},{9,8},{10,11... | collective-permute-start | bytes 589832 | tf_op jit(solution)/shard_map/ppermute | solution.py:725
  86.5 5.6 %collective-permute-start.11 = (bf16[2,256,128]{2,1,0:T(8,128)(2,1)S(1)}, bf16[2,256,128]{2,1,0:T(8,128)(2,1)S(1)}, u32[]{:S(2)}, u32[]{:S(2)}) collective-permute-start(bf16[2,256,128]{2,1,0:T(8,128)(2,1)S(1)} %fusion.18), channel_id=1, source_target_pairs={{0,2},{1,3},{2,0},{3,1},{4,6},{5,7},{6,4},{7,5},{8,10},{9,11},{10,... | collective-permute-start | bytes 393224 | tf_op jit(solution)/shard_map/ppermute | solution.py:733
  92.1 12.3 %collective-permute-start.13 = (bf16[2,2,2,144,256]{4,3,2,1,0:T(8,128)(2,1)S(1)}, bf16[2,2,2,144,256]{4,3,2,1,0:T(8,128)(2,1)S(1)}, u32[]{:S(2)}, u32[]{:S(2)}) collective-permute-start(bf16[2,2,2,144,256]{4,3,2,1,0:T(8,128)(2,1)S(1)} %get-tuple-element.145), channel_id=1, source_target_pairs={{0,8},{1,17},{2,10},{3,19},{4,12},{5,21},{6,14},{7,23},{8,0},{9,25... | collective-permute-start | bytes 1769480 | tf_op jit(solution)/shard_map/ppermute | solution.py:733
  96.6 7.6 %collective-permute-start.12 = (bf16[256,128]{1,0:T(8,128)(2,1)S(1)}, bf16[256,128]{1,0:T(8,128)(2,1)S(1)}, u32[]{:S(2)}, u32[]{:S(2)}) collective-permute-start(bf16[256,128]{1,0:T(8,128)(2,1)S(1)} %fusion.25), channel_id=1, source_target_pairs={{0,4},{1,5},{2,6},{3,7},{4,0},{5,1},{6,2},{7,3},{8,12},{9,13},{10,... | collective-permute-start | bytes 196616 | tf_op jit(solution)/shard_map/ppermute | solution.py:733
  96.7 17.0 %collective-permute-start.16 = (bf16[2,384,256]{2,1,0:T(8,128)(2,1)}, bf16[2,384,256]{2,1,0:T(8,128)(2,1)S(1)}, u32[]{:S(2)}, u32[]{:S(2)}) collective-permute-start(bf16[2,384,256]{2,1,0:T(8,128)(2,1)} %fusion.6), channel_id=1, source_target_pairs={{0,2},{1,3},{2,0},{3,1},{4,6},{5,7},{6,4},{7,5},{8,10},{9,11},{10,... | collective-permute-start | bytes 1179656 | tf_op jit(solution)/shard_map/ppermute | solution.py:733
  104.5 9.4 %collective-permute-start.15 = (bf16[2,2,144,256]{3,2,1,0:T(8,128)(2,1)S(1)}, bf16[2,2,144,256]{3,2,1,0:T(8,128)(2,1)S(1)}, u32[]{:S(2)}, u32[]{:S(2)}) collective-permute-start(bf16[2,2,144,256]{3,2,1,0:T(8,128)(2,1)S(1)} %fusion.10), channel_id=1, source_target_pairs={{0,16},{1,9},{2,18},{3,11},{4,20},{5,13},{6,22},{7,15},{8,24},{9,1... | collective-permute-start | bytes 884744 | tf_op jit(solution)/shard_map/ppermute | solution.py:733
  110.4 14.3 %collective-permute-start.18 = (bf16[768,256]{1,0:T(8,128)(2,1)S(1)}, bf16[768,256]{1,0:T(8,128)(2,1)S(1)}, u32[]{:S(2)}, u32[]{:S(2)}) collective-permute-start(bf16[768,256]{1,0:T(8,128)(2,1)S(1)} %fusion.1), channel_id=1, source_target_pairs={{0,16},{1,9},{2,18},{3,11},{4,20},{5,13},{6,22},{7,15},{8,24},{9,1... | collective-permute-start | bytes 1179656 | tf_op jit(solution)/shard_map/ppermute | solution.py:733
  114.1 12.0 %collective-permute-start.17 = (bf16[2,256,256]{2,1,0:T(8,128)(2,1)S(1)}, bf16[2,256,256]{2,1,0:T(8,128)(2,1)S(1)}, u32[]{:S(2)}, u32[]{:S(2)}) collective-permute-start(bf16[2,256,256]{2,1,0:T(8,128)(2,1)S(1)} %pad_maximum_fusion.1), channel_id=1, source_target_pairs={{0,2},{1,3},{2,0},{3,1},{4,6},{5,7},{6,4},{7,5},{8,10},{9,11},{10,... | collective-permute-start | bytes 786440 | tf_op jit(solution)/shard_map/ppermute | solution.py:733
  115.6 13.0 %collective-permute-start.20 = (bf16[384,256]{1,0:T(8,128)(2,1)S(1)}, bf16[384,256]{1,0:T(8,128)(2,1)S(1)}, u32[]{:S(2)}, u32[]{:S(2)}) collective-permute-start(bf16[384,256]{1,0:T(8,128)(2,1)S(1)} %fusion.15), channel_id=1, source_target_pairs={{0,4},{1,5},{2,6},{3,7},{4,0},{5,1},{6,2},{7,3},{8,12},{9,13},{10,... | collective-permute-start | bytes 589832 | tf_op jit(solution)/shard_map/ppermute | solution.py:733
  126.1 2.5 %collective-permute-start.19 = (bf16[256,768]{1,0:T(8,128)(2,1)}, bf16[256,768]{1,0:T(8,128)(2,1)S(1)}, u32[]{:S(2)}, u32[]{:S(2)}) collective-permute-start(bf16[256,768]{1,0:T(8,128)(2,1)} %get-tuple-element.170), channel_id=1, source_target_pairs={{0,1},{1,0},{2,3},{3,2},{4,5},{5,4},{6,7},{7,6},{8,9},{9,8},{10,11... | collective-permute-start | bytes 1179656 | tf_op jit(solution)/shard_map/ppermute | solution.py:725
  126.6 8.6 %collective-permute-start.24 = (bf16[256,256]{1,0:T(8,128)(2,1)S(1)}, bf16[256,256]{1,0:T(8,128)(2,1)S(1)}, u32[]{:S(2)}, u32[]{:S(2)}) collective-permute-start(bf16[256,256]{1,0:T(8,128)(2,1)S(1)} %fusion.19), channel_id=1, source_target_pairs={{0,4},{1,5},{2,6},{3,7},{4,0},{5,1},{6,2},{7,3},{8,12},{9,13},{10,... | collective-permute-start | bytes 393224 | tf_op jit(solution)/shard_map/ppermute | solution.py:733
  128.7 5.7 %collective-permute-start.21 = (bf16[384,256]{1,0:T(8,128)(2,1)S(1)}, bf16[384,256]{1,0:T(8,128)(2,1)S(1)}, u32[]{:S(2)}, u32[]{:S(2)}) collective-permute-start(bf16[384,256]{1,0:T(8,128)(2,1)S(1)} %fusion.8), channel_id=1, source_target_pairs={{0,16},{1,9},{2,18},{3,11},{4,20},{5,13},{6,22},{7,15},{8,24},{9,1... | collective-permute-start | bytes 589832 | tf_op jit(solution)/shard_map/ppermute | solution.py:733
  135.2 6.4 %collective-permute-start.25 = (bf16[256,256]{1,0:T(8,128)(2,1)S(1)}, bf16[256,256]{1,0:T(8,128)(2,1)S(1)}, u32[]{:S(2)}, u32[]{:S(2)}) collective-permute-start(bf16[256,256]{1,0:T(8,128)(2,1)S(1)} %fusion.13), channel_id=1, source_target_pairs={{0,16},{1,9},{2,18},{3,11},{4,20},{5,13},{6,22},{7,15},{8,24},{9,1... | collective-permute-start | bytes 393224 | tf_op jit(solution)/shard_map/ppermute | solution.py:733
  136.3 7.8 %collective-permute-start.22 = (bf16[768,256]{1,0:T(8,128)(2,1)S(1)}, bf16[768,256]{1,0:T(8,128)(2,1)S(1)}, u32[]{:S(2)}, u32[]{:S(2)}) collective-permute-start(bf16[768,256]{1,0:T(8,128)(2,1)S(1)} %add_convert_fusion.3.a_send), channel_id=1, source_target_pairs={{0,8},{1,17},{2,10},{3,19},{4,12},{5,21},{6,14},{7,23},{8,0},{9,25... | collective-permute-start | bytes 1179656 | tf_op jit(solution)/shard_map/ppermute | solution.py:733
  137.3 11.0 %collective-permute-start.23 = (bf16[768,256]{1,0:T(8,128)(2,1)S(1)}, bf16[768,256]{1,0:T(8,128)(2,1)S(1)}, u32[]{:S(2)}, u32[]{:S(2)}) collective-permute-start(bf16[768,256]{1,0:T(8,128)(2,1)S(1)} %pad_maximum_fusion.send_ref.b_send), channel_id=1, source_target_pairs={{0,8},{1,17},{2,10},{3,19},{4,12},{5,21},{6,14},{7,23},{8,0},{9,25... | collective-permute-start | bytes 1179656 | tf_op jit(solution)/shard_map/ppermute | solution.py:733
  141.7 8.8 %collective-permute-start.26 = (bf16[400,256]{1,0:T(8,128)(2,1)S(1)}, bf16[400,256]{1,0:T(8,128)(2,1)S(1)}, u32[]{:S(2)}, u32[]{:S(2)}) collective-permute-start(bf16[400,256]{1,0:T(8,128)(2,1)S(1)} %pad_maximum_fusion.2.last_send), channel_id=1, source_target_pairs={{0,8},{1,17},{2,10},{3,19},{4,12},{5,21},{6,14},{7,23},{8,0},{9,25... | collective-permute-start | bytes 614408 | tf_op jit(solution)/shard_map/ppermute | solution.py:733
  (34 other events, 249.9 us)

commit v5 on v4

--- a/solution.py
+++ b/solution.py
@@ -89,7 +89,9 @@
     return placed
 
 
-def attn_kernel(table, place, *refs, blocks, heads, size, n_kv, per_chip, last_call, first_call):
+def attn_kernel(
+    table, place, *refs, blocks, heads, size, n_kv, per_chip, start, last_call, first_call
+):
     q_ref, do_ref, cos_ref, sin_ref = refs[:4]
     kv_refs = refs[4 : 4 + n_kv]
     refs = refs[4 + n_kv :]
@@ -134,7 +136,7 @@
             lax.fori_loop(0, share, place_block, 0)
         dkv_acc[...] = jnp.zeros_like(dkv_acc) if first_call else sum_ref[...]
 
-    block = table[place[0] + lax.rem(place[3] + step + place[1], per_chip)]
+    block = table[place[0] + place[4 + start + step]]
     last = block // 2
     in_prompt = block < prompt_blocks
     seg_tile = (prompt_blocks + (block - prompt_blocks) // cont_blocks * cont_blocks) // 2
@@ -267,8 +269,12 @@
     else:
         dkv_shapes = [shape((keys, 2 * size), BF)]
     extra = [] if first_call else [carried]
-    column = pl.BlockSpec((heads * size, BLK), lambda i, j, *_: (j, i + start))
-    angle = pl.BlockSpec((HALF, BLK), lambda i, j, *_: (0, i + start))
+
+    def column_of(i, scalars):
+        return lax.rem(scalars[4 + start + i] + per_chip - scalars[1], per_chip)
+
+    column = pl.BlockSpec((heads * size, BLK), lambda i, j, _, scalars: (j, column_of(i, scalars)))
+    angle = pl.BlockSpec((HALF, BLK), lambda i, j, _, scalars: (0, column_of(i, scalars)))
     out_column = pl.BlockSpec((heads * size, BLK), lambda i, j, *_: (j, i))
     return pl.pallas_call(
         functools.partial(
@@ -278,6 +284,7 @@
             size=size,
             n_kv=len(kvs),
             per_chip=per_chip,
+            start=start,
             last_call=last_call,
             first_call=first_call,
         ),
@@ -310,7 +317,7 @@
             flops=1000, bytes_accessed=1000, transcendentals=0
         ),
         name="attention",
-    )(table, place + jnp.array([0, 0, 0, start], jnp.int32), q_t, do_t, cosine, sine, *kvs, *extra)
+    )(table, place, q_t, do_t, cosine, sine, *kvs, *extra)
 
 
 def prologue_kernel(
@@ -461,18 +468,24 @@
     )(sc, h_two, g_two, w_up, w_down)
 
 
-def late_kernel(sc, h_ref, dq0, dq1, mix0, mix1, got0, got1, g_ref, send_ref, keep_ref, mix_s, dq_s, both_s, *, n_pair):
+def late_kernel(
+    sc, h_ref, dq0, dq1, mix0, mix1, got0, got1, g_ref, send_ref, keep_ref, mix_ref, dq_s, mix_s, both_s,
+    *, n_pair
+):
     half = mix0.shape[0]
     rows = mix0.shape[1]
     width = 2 * half
+    count = rows // BLK
     own = pl.multiple_of(sc[0] * half, 128)
     other = pl.multiple_of((1 - sc[0]) * half, 128)
-    mix_s[pl.ds(own, half), 0:rows] = mix0[...]
-    mix_s[pl.ds(own, half), rows : 2 * rows] = mix1[...]
-    mix_s[pl.ds(other, half), 0:rows] = got1[...]
-    mix_s[pl.ds(other, half), rows : 2 * rows] = got0[...]
-    dq_s[:, 0:rows] = dq0[...]
-    dq_s[:, rows : 2 * rows] = dq1[...]
+    for n, (mix, got, dq) in enumerate(((mix0, got0, dq0), (mix1, got1, dq1))):
+        for k in range(count):
+            source = slice(k * BLK, (k + 1) * BLK)
+            at = pl.ds(pl.multiple_of(sc[4 + n * count + k] * BLK, BLK), BLK)
+            mix_ref[:, at] = mix[:, source]
+            mix_s[pl.ds(own, half), at] = mix[:, source]
+            mix_s[pl.ds(other, half), at] = got[:, source]
+            dq_s[:, at] = dq[:, source]
     both_s[:, 0:half] = dot(h_ref[...], dq_s[...], ((0,), (1,))).astype(BF)
     both_s[:, half:width] = dot(mix_s[...], g_ref[:, pl.ds(own, half)]).astype(BF)
     block = width // n_pair
@@ -501,19 +514,18 @@
     return call(
         functools.partial(late_kernel, n_pair=n_pair),
         "late_gradients",
-        [shape((2, 2, 2, quarter, WIDE), BF)] * 2,
+        [shape((2, 2, 2, quarter, WIDE), BF)] * 2 + [shape((half, rows), BF)] * 2,
         [VM] * 8,
-        [VM] * 2,
+        [VM] * 4,
         [
             pltpu.VMEM((width, rows), BF),
-            pltpu.VMEM((half, rows), BF),
             pltpu.VMEM((width, width), BF),
         ],
         16,
     )(sc, h_one, *dqs, *mixes, *gots, g_two)
 
 
-def out_kernel(sc, a0, a1, a2, mix0, mix1, x_ref, w_down, w_out, own_ref, send_ref, down_s, out_s, sems, *, part, n_pair):
+def out_kernel(sc, a0, a1, a2, mix_ref, x_ref, w_down, w_out, own_ref, send_ref, down_s, out_s, sems, *, part, n_pair):
     half = out_s.shape[0]
     rows = x_ref.shape[0]
     span = n_pair * LANES
@@ -530,9 +542,9 @@
         copy.start()
     for copy in copies:
         copy.wait()
-    for n, mix in enumerate((mix0, mix1)):
+    for n in range(2):
         here = slice(n * rows, (n + 1) * rows)
-        total = dot(mix[...], out_s[...], ((0,), (0,)))
+        total = dot(mix_ref[:, here], out_s[...], ((0,), (0,)))
         for k, act in enumerate((a0, a1, a2)):
             total = total + dot(act[here, :], down_s[k])
         if n == 0:
@@ -541,7 +553,7 @@
             send_ref[...] = total.astype(BF)
 
 
-def hat_kernel(sc, d0, d1, d2, dq0, dq1, xo, xt, gains, w_up, w_query, own_ref, send_ref, sum_ref, up_s, query_s, sems, *, part, n_pair):
+def hat_kernel(sc, d0, d1, d2, dq_ref, xo, xt, gains, w_up, w_query, own_ref, send_ref, sum_ref, up_s, query_s, sems, *, part, n_pair):
     half = query_s.shape[1]
     rows, width = xo.shape
     copies = [
@@ -559,12 +571,12 @@
         copy.wait()
     gain_one, gain_two = gains[0:1, :].astype(F32), gains[2:3, :].astype(F32)
     sums = [jnp.zeros((1, width), F32)] * 4
-    for n, (x, dq) in enumerate(((xo, dq0), (xt, dq1))):
+    for n, x in enumerate((xo, xt)):
         here = slice(n * rows, (n + 1) * rows)
         two = dot(d0[here, :], up_s[0], ((1,), (1,)))
         two = two + dot(d1[here, :], up_s[1], ((1,), (1,)))
         two = two + dot(d2[here, :], up_s[2], ((1,), (1,)))
-        one = dot(dq[...], query_s[...], ((0,), (1,)))
+        one = dot(dq_ref[:, here], query_s[...], ((0,), (1,)))
         hat, unused = normed(x[...].astype(F32))
         for k, value in enumerate((one * hat, one, two * hat, two)):
             sums[k] = sums[k] + jnp.sum(value, 0, keepdims=True)
@@ -576,9 +588,9 @@
     sum_ref[...] = jnp.concatenate(sums + [jnp.zeros((4, width), F32)], 0)
 
 
-def last_kernel(sc, dkv_a, dkv_b, cos_ref, sin_ref, w_kv, h_ref, x_ref, gains, hat_own, hat_got, sum_ref, g_ref, grad_ref, send_ref, keep_ref, *, n_pair):
+def last_kernel(sc, dkv_a, dkv_b, dkv_c, dkv_d, cos_ref, sin_ref, w_kv, h_ref, x_ref, gains, hat_own, hat_got, sum_ref, g_ref, grad_ref, send_ref, keep_ref, *, n_pair):
     rows, width = x_ref.shape
-    dkv = (dkv_a[...].astype(F32) + dkv_b[...].astype(F32)).T
+    dkv = sum(ref[...].astype(F32) for ref in (dkv_a, dkv_b, dkv_c, dkv_d)).T
     low_t = turn(dkv, cos_ref[:, 0:rows], -sin_ref[:, 0:rows]).astype(BF)
     low = low_t.T
     weight = dot(low_t, h_ref[0:rows, :]).T.astype(BF)
@@ -749,8 +761,8 @@
         return lax.psum(jnp.sum(moved.astype(F32), 0).astype(BF), "grp")
 
 
-def add(keep, got):
-    return (keep.astype(F32) + got.astype(F32)).astype(BF)
+def add(*values):
+    return sum(value.astype(F32) for value in values).astype(BF)
 
 
 def low(value):
@@ -772,7 +784,17 @@
     half = width // 2
     per_chip = 2 * rows // BLK
     table = block_table[0]
+    count = rows // BLK
+    mine = lax.dynamic_slice_in_dim(table, chip * per_chip, per_chip)
+    rank = jnp.sum((mine[None, :] < mine[:, None]).astype(jnp.int32), 1)
+    ends = [n // 2 if n % 2 else per_chip - 1 - n // 2 for n in range(per_chip)]
+    order = jnp.stack(
+        [jnp.sum(jnp.where(rank == n, jnp.arange(per_chip, dtype=jnp.int32), 0)) for n in ends]
+    )
+    place = jnp.stack([chip * per_chip, core * count, chip, 0 * chip]).astype(jnp.int32)
+    place = jnp.concatenate([place, order])
     sc = jnp.stack([core, chip, links.bit(0), links.bit(1)]).astype(jnp.int32)
+    sc = jnp.concatenate([sc, lax.rem(order + per_chip - core * count, per_chip)])
     gains = jnp.concatenate([ln1_gain, ln1_bias, ln2_gain, ln2_bias]).reshape(4, width)
 
     x_other, g_other = links.swap(layer_input), links.swap(cotangent)
@@ -832,8 +854,6 @@
     b_send = add(b_keep[1], b_got[1])
     b_got_2 = links.cross(b_send, 1)
 
-    place = jnp.stack([chip * per_chip, core * (rows // BLK), chip, 0 * chip]).astype(jnp.int32)
-    count = rows // BLK
     attend = functools.partial(
         attention, table, place, do_t=do_t, cosine=cosine, sine=sine, kvs=(kv_near, kv_far),
         count=count, per_chip=per_chip, split=True,
@@ -841,38 +861,31 @@
     mix_0, dq_0, carried = attend(
         q_t=tie(q_t, b_send), carried=None, start=0, last_call=False
     )
-    carried, a_got, b_got_2, b_got = meet(carried, a_got, b_got_2, b_got)
-    mix_0_got = links.swap(mix_0)
-    b_keep = add(b_keep[0], b_got[0])
-    b_send = add(b_keep[1], b_got_2[1])
+    carried, a_got, b_got_2 = meet(carried, a_got, b_got_2)
+    b_send = add(b_keep[0, 1], b_got[0, 1], b_got_2[1])
     b_got_3 = links.flip(b_send, 1)
     a_send = add(a_keep[1], tie(a_got, b_send)[1])
     a_got_2 = links.flip(a_send, 2)
     mix_1, dq_1, dkv_send, dkv_keep = attend(
         q_t=tie(q_t, a_send, b_send, carried), carried=carried, start=count, last_call=True
     )
-    mix_1, dkv_send, mix_0_got, a_got_2 = meet(mix_1, dkv_send, mix_0_got, a_got_2)
+    mix_0, mix_1, dkv_send, a_got_2, b_got_3 = meet(mix_0, mix_1, dkv_send, a_got_2, b_got_3)
     dkv_got = links.swap(dkv_send)
-    mix_1_got = links.swap(mix_1)
-    dkv_got, mix_1_got = meet(dkv_got, mix_1_got)
-    dkv_send = add(dkv_keep[1], dkv_got[1])
-    dkv_got_2 = links.flip(dkv_send, 1)
-    late_send, late_keep = late_gradients(
-        sc, tie(h_one, dkv_send), (dq_0, dq_1), (mix_0, mix_1), (mix_0_got, mix_1_got), g_two, n_pair
-    )
-    late_send, dkv_got, dkv_got_2 = meet(late_send, dkv_got, dkv_got_2)
+    mix_0_got, mix_1_got = links.swap(mix_0), links.swap(mix_1)
+    dkv_got, mix_0_got, mix_1_got = meet(dkv_got, mix_0_got, mix_1_got)
+    dkv_sends = [add(dkv_keep[at], dkv_got[at]) for at in ((1, 0), (0, 1), (1, 1))]
+    dkv_gots = [links.flip(value, n + 1) for n, value in enumerate(dkv_sends)]
+    late_send, late_keep, mix_own, dq_own = late_gradients(
+        sc, tie(h_one, *dkv_sends), (dq_0, dq_1), (mix_0, mix_1), (mix_0_got, mix_1_got), g_two, n_pair
+    )
     late_got = links.cross(late_send, 0)
-    dkv_keep = add(dkv_keep[0], dkv_got[0])
-    dkv_send = add(dkv_keep[1], dkv_got_2[1])
-    dkv_got_3 = links.flip(dkv_send, 2)
-    b_got_3 = links.flip(tie(b_send, dkv_send), 1)
 
     w_specs = [HBM] * 2
     hat_own, hat_send, sums = call(
         functools.partial(hat_kernel, part=part_hidden, n_pair=n_pair),
         "norms",
         [shape((rows, width), F32), shape((rows, width), BF), shape((8, width), F32)],
-        [VM] * 8 + w_specs,
+        [VM] * 7 + w_specs,
         [VM] * 3,
         [
             pltpu.VMEM((3, width, n_pair * LANES), BF),
@@ -881,14 +894,16 @@
         ],
         56,
     )(
-        sc, dup_0, dup_1, tie(dup_2, late_send, dkv_send), dq_0, dq_1, layer_input, x_other, gains,
+        sc, dup_0, dup_1, tie(dup_2, late_send), dq_own, layer_input, x_other, gains,
         w_up, w_query,
     )
-    hat_send, dkv_got_2, dkv_got_3, late_got = meet(hat_send, dkv_got_2, dkv_got_3, late_got)
+    hat_send, late_got, *dkv_gots = meet(hat_send, late_got, *dkv_gots)
     hat_got = links.swap(hat_send)
-    dkv_keep = add(dkv_keep[0], dkv_got_2[0])
     late_send = add(late_keep[1], late_got[1])
     late_got_2 = links.cross(late_send, 1)
+    b_send = add(b_keep[0, 0, 1], b_got[0, 0, 1], b_got_2[0, 1], tie(b_got_3, late_send)[1])
+    b_got_4 = links.flip(b_send, 2)
+    dkv_own = add(dkv_keep[0, 0], dkv_got[0, 0])
     late_send, hat_got = meet(late_send, hat_got)
 
     few = part // 2 + 8
@@ -896,32 +911,28 @@
         functools.partial(last_kernel, n_pair=n_pair),
         "last",
         [shape((rows, width), F32)] + [shape((2, 2 * few, 2 * lanes), BF)] * 2,
-        [VM] * 12,
+        [VM] * 14,
         [VM] * 3,
         [],
         16,
     )(
-        sc, dkv_keep, tie(dkv_got_3, late_send), cosine, sine, w_keyval, h_one, layer_input,
-        gains, hat_own, hat_got, sums, cotangent,
-    )
-    few_send, late_got, late_got_2, b_got_2, b_got_3 = meet(
-        few_send, late_got, late_got_2, b_got_2, b_got_3
-    )
-    late_keep = add(late_keep[0], late_got[0])
-    quarter = late_keep.shape[2]
-    last_send = jnp.concatenate([add(late_keep[1], late_got_2[1]), few_send], 1)
+        sc, dkv_own, *dkv_gots, tie(cosine, late_send, b_send), sine, w_keyval, h_one,
+        layer_input, gains, hat_own, hat_got, sums, cotangent,
+    )
+    few_send, late_got_2 = meet(few_send, late_got_2)
+    quarter = late_keep.shape[3]
+    last_send = jnp.concatenate(
+        [add(late_keep[0, 1], late_got[0, 1], late_got_2[1]), few_send], 1
+    )
     last_got = links.flip(last_send, 1)
-    b_keep = add(b_keep[0], b_got_2[0])
-    b_send = add(b_keep[1], b_got_3[1])
-    b_got_4 = links.flip(b_send, 2)
-    a_sum = add(add(a_keep[0], a_got[0]), a_got_2)
+    a_sum = add(a_keep[0], a_got[0], a_got_2)
     a_got = links.cross(a_sum, 1)
 
     out_own, out_send = call(
         functools.partial(out_kernel, part=part_hidden, n_pair=n_pair),
         "outputs",
         [shape((rows, width), F32), shape((rows, width), BF)],
-        [VM] * 6 + w_specs,
+        [VM] * 5 + w_specs,
         [VM] * 2,
         [
             pltpu.VMEM((3, n_pair * LANES, width), BF),
@@ -930,27 +941,29 @@
         ],
         56,
     )(
-        sc, act_0, act_1, tie(act_2, last_send, b_send, a_sum), mix_0, mix_1,
-        layer_input, w_down, w_out,
+        sc, act_0, act_1, tie(act_2, last_send, a_sum), mix_own, layer_input, w_down, w_out,
     )
     out_send, last_got, a_got = meet(out_send, last_got, a_got)
     out_got = links.swap(out_send)
-    last_keep = jnp.concatenate([add(late_keep[0], late_got_2[0]), few_keep], 1)
+    last_keep = jnp.concatenate(
+        [add(late_keep[0, 0], late_got[0, 0], late_got_2[0]), few_keep], 1
+    )
     last_send = add(last_keep[1], last_got[1])
     last_got_2 = links.flip(last_send, 2)
     a_sum = add(a_sum, a_got)
     a_got = links.cross(a_sum, 0)
-    out_got, b_got_4 = meet(out_got, b_got_3, b_got_4, a_sum, last_send)[::2][:2]
+    out_got, b_got_4 = meet(out_got, b_got_4, a_sum, last_send)[:2]
     layer_output = low(out_own + out_got.astype(F32))
-    b_sum = add(add(b_keep[0], b_got_3[0]), b_got_4)
+    b_sum = add(b_keep[0, 0, 0], b_got[0, 0, 0], b_got_2[0, 0], b_got_3[0], b_got_4)
     b_got = links.cross(b_sum, 1)
     last_keep = add(last_keep[0], last_got[0])
-    b_got, layer_output = meet(b_got, layer_output)
+    b_got, layer_output, a_got = meet(b_got, layer_output, a_got)
     b_sum = jnp.concatenate([b_sum, b_got], 0)
     b_got = links.cross(b_sum, 0)
     last_got_2 = meet(last_got_2, b_sum)[0]
     last = add(last_keep, last_got_2)
     last_got = links.cross(last, 1)
+    last_got, b_got = meet(last_got, b_got)
     last = jnp.concatenate(
         [last[:quarter], last_got[:quarter], add(last[quarter:], last_got[quarter:])], 0
     )
@@ -1055,7 +1068,8 @@
         jax.vmap(turn, (0, None, None))(q_raw.reshape(-1, size, 2 * rows), cosine, sine)
     ).reshape(half_width, 2 * rows)
     do_t = dot(out_half, g_two, ((1,), (1,)))
-    place = jnp.stack([chip * per_chip, 0 * chip, 0 * chip, 0 * chip]).astype(jnp.int32)
+    place = jnp.stack([chip * per_chip] + [0 * chip] * 3 + [n + 0 * chip for n in range(per_chip)])
+    place = place.astype(jnp.int32)
     mix_t, dq_t, dkv_part = attention(
         table, place, q_t, do_t, cosine, sine, (kv_all,), None, 0, per_chip, per_chip, True, False
     )

time: 156 us -> 159 us (1.019); the launches traced: 156 us -> 157 us
  local copies, waits for them, and re-layouts: 4.15 us -> 7.67 us
  waiting for transfers between devices: 26.7 us -> 24.7 us
  other arithmetic: 11.6 us -> 13.5 us
    ppermute x8, starting transfers between devices: 4.74 us -> 1.3 us  [swap(): return lax.ppermute(value, 'ctx', [(i, i ^ 1) for i in range(self.n_ctx)])]
    concatenate x0 -> x2, local copies, waits for them, and re-layouts: none -> 3.2 us  [the longest x1 2.54 us: shards_small(): place = jnp.concatenate([place, order])]
    rem x0 -> x1, other arithmetic: none -> 2.54 us  [shards_small(): lax.rem(order + per_chip - core * count, per_chip)]
    ppermute x20 -> x21, waiting for transfers between devices: 23.4 us -> 21.3 us  [permute(): return lax.ppermute(value, ('grp', 'ctx'), pairs)]
    ppermute x20 -> x21, starting transfers between devices: 26.9 us -> 28.8 us  [permute(): return lax.ppermute(value, ('grp', 'ctx'), pairs)]
    convert_element_type x19 -> x13, other arithmetic: 8.3 us -> 7.62 us  [add(): return sum((value.astype(F32) for value in values)).astype(BF)]
  transfers between devices with their start and end apart: 28 -> 29, of which waited for: 15 -> 10; matrix products, arithmetic and copies ran while one was open for 6% -> 10% of each run, Pallas kernels for 47% -> 44%
where the time goes in v5:
time: 159 us; the launch traced here: 157 us
  Pallas kernels  79.7 us (50%)
  starting transfers between devices  30.1 us (19%)
  waiting for transfers between devices  24.7 us (16%)
  other arithmetic  13.5 us (8%)
  local copies, waits for them, and re-layouts  7.67 us (5%)
    pallas_call x12, Pallas kernels, placed(): made(scalars, *(pltpu.with_memory_space_constraint(v, pltpu.HBM) if spec...  53.6 us
    ppermute x21, starting transfers between devices, permute(): return lax.ppermute(value, ('grp', 'ctx'), pairs)  28.8 us
    pallas_call x2, Pallas kernels, attention(): pl.pallas_call(functools.partial(attn_kernel, blocks=blocks, heads=heads,...  26 us
    ppermute x21, waiting for transfers between devices, permute(): return lax.ppermute(value, ('grp', 'ctx'), pairs)  21.3 us
    convert_element_type x13, other arithmetic, add(): return sum((value.astype(F32) for value in values)).astype(BF)  7.62 us
    ppermute x8, waiting for transfers between devices, swap(): return lax.ppermute(value, 'ctx', [(i, i ^ 1) for i in range(self.n_ctx)])  3.42 us
  transfers between devices with their start and end apart: 29, of which 10 were waited for; matrix products, arithmetic and copies ran while one was open for 10% of the time, Pallas kernels for 44%

profile of v5, /device:TPU:0, one launch (start us, length us, event | category | flops | bytes accessed | tf_op | source)
XLA Modules:
  0.0 156.9 jit_solution(16460936609035500905)
XLA Ops:
  4.4 2.5 %compare_select_fusion.1 = s32[4]{0:T(128)S(1)} fusion(s32[1]{0:T(128)} %bitcast.8, s32[1]{0:T(128)} %bitcast.7, s32[1]{0:T(128)} %bitcast.6, s32[1]{0:T(128)} %bitcast.5, s32[]{:T(128)} %mul.38), kind=kLoop, calls=%fused_computation.54 | loop fusion | flops 44 | bytes 36 | tf_op jit(solution)/shard_map/rem | solution.py:797
  9.3 5.1 %prologue.1 = (bf16[512,768]{1,0:T(8,128)(2,1)}, bf16[512,768]{1,0:T(8,128)(2,1)}, bf16[512,768]{1,0:T(8,128)(2,1)}, bf16[512,128]{1,0:T(8,128)(2,1)}) custom-call(s32[8]{0:T(128)} %concatenate.36.sc, bf16[256,768]{1,0:T(8,128)(2,1)} %x_ref.3, bf16[256,768]{1,0:T(8,128)(2,1)} %copy-done.16, bf16[256,768]{1,0:T(8,128)(2,1)} %g_ref.1, ...), custom_call_target="tpu_custom_call" | custom-call | flops 1000 | bytes 1000 | tf_op jit(solution)/shard_map/prologue/pallas_call | solution.py:81
  14.4 3.0 %collective-permute-start.2 = (bf16[512,128]{1,0:T(8,128)(2,1)}, bf16[512,128]{1,0:T(8,128)(2,1)S(1)}, u32[]{:S(2)}, u32[]{:S(2)}) collective-permute-start(bf16[512,128]{1,0:T(8,128)(2,1)} %get-tuple-element.106), channel_id=1, source_target_pairs={{0,2},{1,3},{2,0},{3,1},{4,6},{5,7},{6,4},{7,5},{8,10},{9,11},{10,... | collective-permute-start | bytes 393224 | tf_op jit(solution)/shard_map/ppermute | solution.py:745
  17.5 7.7 %ffn_gradients.3 = (bf16[512,512]{1,0:T(8,128)(2,1)}, bf16[512,512]{1,0:T(8,128)(2,1)}, bf16[2,2,2,384,256]{4,3,2,1,0:T(8,128)(2,1)}) custom-call(s32[8]{0:T(128)} %concatenate.36.sc, bf16[512,768]{1,0:T(8,128)(2,1)} %get-tuple-element.112.h_ref, bf16[512,768]{1,0:T(8,128)(2,1)} %get-tuple-element.104.g_ref, bf16[768,3072]{1,0:T(8,128)(2,1)} %w_up.7, ...), custom_call_target="tpu_custom_call" | custom-call | flops 1000 | bytes 1000 | tf_op jit(solution)/shard_map/ffn_gradients/pallas_call | solution.py:81
  26.8 2.7 %collective-permute-start.3 = (bf16[1024,128]{1,0:T(8,128)(2,1)S(1)}, bf16[1024,128]{1,0:T(8,128)(2,1)S(1)}, u32[]{:S(2)}, u32[]{:S(2)}) collective-permute-start(bf16[1024,128]{1,0:T(8,128)(2,1)S(1)} %constant_dynamic-update-slice_fusion.refs_4_), channel_id=1, source_target_pairs={{0,4},{1,5},{2,6},{3,7},{4,0},{5,1},{6,2},{7,3},{8,12},{9,13},{10,... | collective-permute-start | bytes 786440 | tf_op jit(solution)/shard_map/ppermute | solution.py:745
  29.4 7.6 %ffn_gradients.4 = (bf16[512,512]{1,0:T(8,128)(2,1)}, bf16[512,512]{1,0:T(8,128)(2,1)}, bf16[2,2,2,384,256]{4,3,2,1,0:T(8,128)(2,1)}) custom-call(s32[8]{0:T(128)} %concatenate.36.sc, bf16[512,768]{1,0:T(8,128)(2,1)} %get-tuple-element.112.h_ref, bf16[512,768]{1,0:T(8,128)(2,1)} %get-tuple-element.104.g_ref, bf16[768,3072]{1,0:T(8,128)(2,1)} %w_up.7, ...), custom_call_target="tpu_custom_call" | custom-call | flops 1000 | bytes 1000 | tf_op jit(solution)/shard_map/ffn_gradients/pallas_call | solution.py:81
  37.1 7.7 %ffn_gradients.5 = (bf16[512,512]{1,0:T(8,128)(2,1)}, bf16[512,512]{1,0:T(8,128)(2,1)}, bf16[2,768,256]{2,1,0:T(8,128)(2,1)}, bf16[2,768,256]{2,1,0:T(8,128)(2,1)}) custom-call(s32[8]{0:T(128)} %concatenate.36.sc, bf16[512,768]{1,0:T(8,128)(2,1)} %get-tuple-element.112.h_ref, bf16[512,768]{1,0:T(8,128)(2,1)} %get-tuple-element.104.g_ref, ...), custom_call_target="tpu_custom_call" | custom-call | flops 1000 | bytes 1000 | tf_op jit(solution)/shard_map/ffn_gradients/pallas_call | solution.py:81
  45.3 2.8 %project.1 = (bf16[384,512]{1,0:T(8,128)(2,1)S(1)}, f32[384,512]{1,0:T(8,128)S(1)}) custom-call(s32[8]{0:T(128)S(1)} %copy-done.11, bf16[512,768]{1,0:T(8,128)(2,1)S(1)} %copy-done.1, bf16[512,768]{1,0:T(8,128)(2,1)S(1)} %copy-done, f32[8,512]{1,0:T(8,128)S(1)} %copy-done.7, f32[8,512]{1,0:T(8,128)S(1)} %copy-done.6, bf16[768,768]{1,0:T(8,128)(2,1)} %w_query.3, ...), custom_call_target="tpu_custom_call" | custom-call | flops 1000 | bytes 1000 | tf_op jit(solution)/shard_map/project/pallas_call | solution.py:81
  51.0 2.5 %concatenate.42.place = s32[8]{0:T(128)S(1)} concatenate(s32[1]{0:T(128)} %bitcast.14, s32[1]{0:T(128)} %bitcast.15, s32[1]{0:T(128)} %bitcast.1, s32[1]{0:T(128)} %constant.90.clone.1, s32[1]{0:T(128)} %bitcast.5, s32[1]{0:T(128)} %bitcast.6, s32[1]{0:T(128)} %bitcast.7, s32[1]{0:T(128)} %bitcast.8), dimensions={0} | concatenate | bytes 64 | tf_op jit(solution)/shard_map/concatenate | solution.py:795
  53.5 11.8 %attention.2 = (bf16[384,256]{1,0:T(8,128)(2,1)S(1)}, bf16[384,256]{1,0:T(8,128)(2,1)S(1)}, f32[2048,128]{1,0:T(8,128)S(1)}) custom-call(s32[16]{0:T(128)S(1)} %bitcast.88, s32[8]{0:T(128)S(1)} %concatenate.42.place, bf16[384,512]{1,0:T(8,128)(2,1)S(1)} %get-tuple-element.129.refs_0_, f32[384,512]{1,0:T(8,128)S(1)} %get-tuple-element.120.refs_1_, ...), custom_call_target="tpu_custom_call" | custom-call | flops 1000 | bytes 1000 | tf_op jit(solution)/shard_map/attention/pallas_call | solution.py:279
  67.7 3.8 %collective-permute-start.7 = (bf16[768,256]{1,0:T(8,128)(2,1)S(1)}, bf16[768,256]{1,0:T(8,128)(2,1)S(1)}, u32[]{:S(2)}, u32[]{:S(2)}) collective-permute-start(bf16[768,256]{1,0:T(8,128)(2,1)S(1)} %fusion.3), channel_id=1, source_target_pairs={{0,4},{1,5},{2,6},{3,7},{4,0},{5,1},{6,2},{7,3},{8,12},{9,13},{10,... | collective-permute-start | bytes 1179656 | tf_op jit(solution)/shard_map/ppermute | solution.py:745
  71.5 14.2 %attention.3 = (bf16[384,256]{1,0:T(8,128)(2,1)S(1)}, bf16[384,256]{1,0:T(8,128)(2,1)S(1)}, bf16[2,2,256,128]{3,2,1,0:T(8,128)(2,1)S(1)}, bf16[2,2,256,128]{3,2,1,0:T(8,128)(2,1)S(1)}) custom-call(s32[16]{0:T(128)S(1)} %bitcast.89, s32[8]{0:T(128)S(1)} %concatenate.42.place, bf16[384,512]{1,0:T(8,128)(2,1)S(1)} %get-tuple-element.129.refs_0_, ...), custom_call_target="tpu_custom_call" | custom-call | flops 1000 | bytes 1000 | tf_op jit(solution)/shard_map/attention/pallas_call | solution.py:279
  85.8 2.3 %collective-permute-done.7 = bf16[768,256]{1,0:T(8,128)(2,1)S(1)} collective-permute-done((bf16[768,256]{1,0:T(8,128)(2,1)S(1)}, bf16[768,256]{1,0:T(8,128)(2,1)S(1)}, u32[]{:S(2)}, u32[]{:S(2)}) %collective-permute-start.7) | collective-permute-done | bytes 393248 | tf_op jit(solution)/shard_map/ppermute | solution.py:745
  90.4 2.1 %late_gradients.1 = (bf16[2,2,2,144,256]{4,3,2,1,0:T(8,128)(2,1)S(1)}, bf16[2,2,2,144,256]{4,3,2,1,0:T(8,128)(2,1)S(1)}, bf16[384,512]{1,0:T(8,128)(2,1)S(1)}, bf16[384,512]{1,0:T(8,128)(2,1)S(1)}) custom-call(s32[8]{0:T(128)S(1)} %copy-done.11, bf16[512,768]{1,0:T(8,128)(2,1)S(1)} %copy-done.1, bf16[384,256]{1,0:T(8,128)(2,1)S(1)} %get-tuple-element.142.dq0, ...), custom_call_target="tpu_custom_call" | custom-call | flops 1000 | bytes 1000 | tf_op jit(solution)/shard_map/late_gradients/pallas_call | solution.py:81
  97.4 2.7 %collective-permute-start.13 = (bf16[256,128]{1,0:T(8,128)(2,1)S(1)}, bf16[256,128]{1,0:T(8,128)(2,1)S(1)}, u32[]{:S(2)}, u32[]{:S(2)}) collective-permute-start(bf16[256,128]{1,0:T(8,128)(2,1)S(1)} %get-tuple-element.204), channel_id=1, source_target_pairs={{0,2},{1,3},{2,0},{3,1},{4,6},{5,7},{6,4},{7,5},{8,10},{9,11},{10,... | collective-permute-start | bytes 196616 | tf_op jit(solution)/shard_map/ppermute | solution.py:745
  100.1 7.0 %norms.1 = (f32[256,768]{1,0:T(8,128)}, bf16[256,768]{1,0:T(8,128)(2,1)}, f32[8,768]{1,0:T(8,128)}) custom-call(s32[8]{0:T(128)} %concatenate.36.sc, bf16[512,512]{1,0:T(8,128)(2,1)} %get-tuple-element.147.d0, bf16[512,512]{1,0:T(8,128)(2,1)} %get-tuple-element.148.d1, bf16[512,512]{1,0:T(8,128)(2,1)} %get-tuple-element.151.d2, bf16[384,512]{1,0:T(8,128)(2,1)} %copy-done.9, ...), custom_call_target="tpu_custom_call" | custom-call | flops 1000 | bytes 1000 | tf_op jit(solution)/shard_map/norms/pallas_call | solution.py:81
  111.9 2.5 %last.1 = (f32[256,768]{1,0:T(8,128)}, bf16[2,112,256]{2,1,0:T(8,128)(2,1)S(1)}, bf16[2,112,256]{2,1,0:T(8,128)(2,1)S(1)}) custom-call(s32[8]{0:T(128)S(1)} %copy-done.12, bf16[256,128]{1,0:T(8,128)(2,1)S(1)} %get-tuple-element.202.dkv_a, bf16[256,128]{1,0:T(8,128)(2,1)S(1)} %collective-permute-done.13.dkv_b, ...), custom_call_target="tpu_custom_call" | custom-call | flops 1000 | bytes 1000 | tf_op jit(solution)/shard_map/last/pallas_call | solution.py:81
  115.9 6.7 %outputs.1 = (f32[256,768]{1,0:T(8,128)}, bf16[256,768]{1,0:T(8,128)(2,1)}) custom-call(s32[8]{0:T(128)} %concatenate.36.sc, bf16[512,512]{1,0:T(8,128)(2,1)} %get-tuple-element.133.a0, bf16[512,512]{1,0:T(8,128)(2,1)} %get-tuple-element.134.a1, bf16[512,512]{1,0:T(8,128)(2,1)} %get-tuple-element.168.a2, bf16[384,512]{1,0:T(8,128)(2,1)} %copy-done.8, ...), custom_call_target="tpu_custom_call" | custom-call | flops 1000 | bytes 1000 | tf_op jit(solution)/shard_map/outputs/pallas_call | solution.py:81
  122.6 3.1 %collective-permute-done.18 = bf16[2,256,256]{2,1,0:T(8,128)(2,1)S(1)} collective-permute-done((bf16[2,256,256]{2,1,0:T(8,128)(2,1)S(1)}, bf16[2,256,256]{2,1,0:T(8,128)(2,1)S(1)}, u32[]{:S(2)}, u32[]{:S(2)}) %collective-permute-start.18) | collective-permute-done | bytes 262176 | tf_op jit(solution)/shard_map/ppermute | solution.py:745
  131.5 5.4 %collective-permute-done.23.a_got = bf16[768,256]{1,0:T(8,128)(2,1)S(1)} collective-permute-done((bf16[768,256]{1,0:T(8,128)(2,1)S(1)}, bf16[768,256]{1,0:T(8,128)(2,1)S(1)}, u32[]{:S(2)}, u32[]{:S(2)}) %collective-permute-start.23) | collective-permute-done | bytes 393248 | tf_op jit(solution)/shard_map/ppermute | solution.py:745
  138.9 5.6 %collective-permute-done.25 = bf16[256,256]{1,0:T(8,128)(2,1)S(1)} collective-permute-done((bf16[256,256]{1,0:T(8,128)(2,1)S(1)}, bf16[256,256]{1,0:T(8,128)(2,1)S(1)}, u32[]{:S(2)}, u32[]{:S(2)}) %collective-permute-start.25) | collective-permute-done | bytes 131104 | tf_op jit(solution)/shard_map/ppermute | solution.py:745
  148.5 3.3 %collective-permute-done.27.last_got = bf16[400,256]{1,0:T(8,128)(2,1)S(1)} collective-permute-done((bf16[400,256]{1,0:T(8,128)(2,1)S(1)}, bf16[400,256]{1,0:T(8,128)(2,1)S(1)}, u32[]{:S(2)}, u32[]{:S(2)}) %collective-permute-start.27) | collective-permute-done | bytes 204832 | tf_op jit(solution)/shard_map/ppermute | solution.py:745
  152.6 1.8 %collective-permute-done.28.got_ref = bf16[920,256]{1,0:T(8,128)(2,1)S(1)} collective-permute-done((bf16[920,256]{1,0:T(8,128)(2,1)S(1)}, bf16[920,256]{1,0:T(8,128)(2,1)S(1)}, u32[]{:S(2)}, u32[]{:S(2)}) %collective-permute-start.28) | collective-permute-done | bytes 471072 | tf_op jit(solution)/shard_map/ppermute | solution.py:737
  154.5 1.9 %final.1 = (f32[96,3072]{1,0:T(8,128)}, f32[96,768]{1,0:T(8,128)}, f32[96,768]{1,0:T(8,128)}, f32[96,128]{1,0:T(8,128)}, f32[8,256]{1,0:T(8,128)S(1)}) custom-call(s32[8]{0:T(128)S(1)} %copy-done.13, bf16[920,256]{1,0:T(8,128)(2,1)S(1)} %get-tuple-element.187.own_ref, bf16[920,256]{1,0:T(8,128)(2,1)S(1)} %collective-permute-done.28.got_ref), custom_call_target="tpu_custom_call" | custom-call | flops 1000 | bytes 1000 | tf_op jit(solution)/shard_map/final/pallas_call | solution.py:81
  (141 shorter events, 39.7 us)
Async XLA Ops:
  0.6 7.8 %collective-permute-start.1 = (bf16[256,768]{1,0:T(8,128)(2,1)}, bf16[256,768]{1,0:T(8,128)(2,1)S(1)}, u32[]{:S(2)}, u32[]{:S(2)}) collective-permute-start(bf16[256,768]{1,0:T(8,128)(2,1)} %g_ref.1), channel_id=1, source_target_pairs={{0,1},{1,0},{2,3},{3,2},{4,5},{5,4},{6,7},{7,6},{8,9},{9,8},{10,11... | collective-permute-start | bytes 1179656 | tf_op jit(solution)/shard_map/ppermute | solution.py:737
  1.2 7.2 %collective-permute-start = (bf16[256,768]{1,0:T(8,128)(2,1)}, bf16[256,768]{1,0:T(8,128)(2,1)S(1)}, u32[]{:S(2)}, u32[]{:S(2)}) collective-permute-start(bf16[256,768]{1,0:T(8,128)(2,1)} %x_ref.3), channel_id=1, source_target_pairs={{0,1},{1,0},{2,3},{3,2},{4,5},{5,4},{6,7},{7,6},{8,9},{9,8},{10,11... | collective-permute-start | bytes 1179656 | tf_op jit(solution)/shard_map/ppermute | solution.py:737
  14.4 10.7 %collective-permute-start.2 = (bf16[512,128]{1,0:T(8,128)(2,1)}, bf16[512,128]{1,0:T(8,128)(2,1)S(1)}, u32[]{:S(2)}, u32[]{:S(2)}) collective-permute-start(bf16[512,128]{1,0:T(8,128)(2,1)} %get-tuple-element.106), channel_id=1, source_target_pairs={{0,2},{1,3},{2,0},{3,1},{4,6},{5,7},{6,4},{7,5},{8,10},{9,11},{10,... | collective-permute-start | bytes 393224 | tf_op jit(solution)/shard_map/ppermute | solution.py:745
  25.2 23.0 %collective-permute-start.4 = (bf16[2,2,2,384,256]{4,3,2,1,0:T(8,128)(2,1)}, bf16[2,2,2,384,256]{4,3,2,1,0:T(8,128)(2,1)S(1)}, u32[]{:S(2)}, u32[]{:S(2)}) collective-permute-start(bf16[2,2,2,384,256]{4,3,2,1,0:T(8,128)(2,1)} %get-tuple-element.107), channel_id=1, source_target_pairs={{0,8},{1,17},{2,10},{3,19},{4,12},{5,21},{6,14},{7,23},{8,0},{9,25... | collective-permute-start | bytes 4718600 | tf_op jit(solution)/shard_map/ppermute | solution.py:745
  26.8 18.0 %collective-permute-start.3 = (bf16[1024,128]{1,0:T(8,128)(2,1)S(1)}, bf16[1024,128]{1,0:T(8,128)(2,1)S(1)}, u32[]{:S(2)}, u32[]{:S(2)}) collective-permute-start(bf16[1024,128]{1,0:T(8,128)(2,1)S(1)} %constant_dynamic-update-slice_fusion.refs_4_), channel_id=1, source_target_pairs={{0,4},{1,5},{2,6},{3,7},{4,0},{5,1},{6,2},{7,3},{8,12},{9,13},{10,... | collective-permute-start | bytes 786440 | tf_op jit(solution)/shard_map/ppermute | solution.py:745
  44.8 20.6 %collective-permute-start.5 = (bf16[2,768,256]{2,1,0:T(8,128)(2,1)}, bf16[2,768,256]{2,1,0:T(8,128)(2,1)}, u32[]{:S(2)}, u32[]{:S(2)}) collective-permute-start(bf16[2,768,256]{2,1,0:T(8,128)(2,1)} %get-tuple-element.114), channel_id=1, source_target_pairs={{0,2},{1,3},{2,0},{3,1},{4,6},{5,7},{6,4},{7,5},{8,10},{9,11},{10,... | collective-permute-start | bytes 2359304 | tf_op jit(solution)/shard_map/ppermute | solution.py:745
  49.5 15.9 %collective-permute-start.6 = (bf16[2,2,384,256]{3,2,1,0:T(8,128)(2,1)}, bf16[2,2,384,256]{3,2,1,0:T(8,128)(2,1)}, u32[]{:S(2)}, u32[]{:S(2)}) collective-permute-start(bf16[2,2,384,256]{3,2,1,0:T(8,128)(2,1)} %fusion), channel_id=1, source_target_pairs={{0,16},{1,9},{2,18},{3,11},{4,20},{5,13},{6,22},{7,15},{8,24},{9,1... | collective-permute-start | bytes 2359304 | tf_op jit(solution)/shard_map/ppermute | solution.py:745
  67.7 20.3 %collective-permute-start.7 = (bf16[768,256]{1,0:T(8,128)(2,1)S(1)}, bf16[768,256]{1,0:T(8,128)(2,1)S(1)}, u32[]{:S(2)}, u32[]{:S(2)}) collective-permute-start(bf16[768,256]{1,0:T(8,128)(2,1)S(1)} %fusion.3), channel_id=1, source_target_pairs={{0,4},{1,5},{2,6},{3,7},{4,0},{5,1},{6,2},{7,3},{8,12},{9,13},{10,... | collective-permute-start | bytes 1179656 | tf_op jit(solution)/shard_map/ppermute | solution.py:745
  71.5 16.7 %collective-permute-start.8 = (bf16[2,384,256]{2,1,0:T(8,128)(2,1)S(1)}, bf16[2,384,256]{2,1,0:T(8,128)(2,1)S(1)}, u32[]{:S(2)}, u32[]{:S(2)}) collective-permute-start(bf16[2,384,256]{2,1,0:T(8,128)(2,1)S(1)} %fusion.1), channel_id=1, source_target_pairs={{0,2},{1,3},{2,0},{3,1},{4,6},{5,7},{6,4},{7,5},{8,10},{9,11},{10,... | collective-permute-start | bytes 1179656 | tf_op jit(solution)/shard_map/ppermute | solution.py:745
  94.0 13.2 %collective-permute-start.12 = (bf16[2,2,2,144,256]{4,3,2,1,0:T(8,128)(2,1)S(1)}, bf16[2,2,2,144,256]{4,3,2,1,0:T(8,128)(2,1)S(1)}, u32[]{:S(2)}, u32[]{:S(2)}) collective-permute-start(bf16[2,2,2,144,256]{4,3,2,1,0:T(8,128)(2,1)S(1)} %get-tuple-element.150), channel_id=1, source_target_pairs={{0,8},{1,17},{2,10},{3,19},{4,12},{5,21},{6,14},{7,23},{8,0},{9,25... | collective-permute-start | bytes 1769480 | tf_op jit(solution)/shard_map/ppermute | solution.py:745
  95.7 11.5 %collective-permute-start.15 = (bf16[256,128]{1,0:T(8,128)(2,1)S(1)}, bf16[256,128]{1,0:T(8,128)(2,1)S(1)}, u32[]{:S(2)}, u32[]{:S(2)}) collective-permute-start(bf16[256,128]{1,0:T(8,128)(2,1)S(1)} %get-tuple-element.201), channel_id=1, source_target_pairs={{0,6},{1,7},{2,4},{3,5},{4,2},{5,3},{6,0},{7,1},{8,14},{9,15},{10,... | collective-permute-start | bytes 196616 | tf_op jit(solution)/shard_map/ppermute | solution.py:745
  96.3 11.0 %collective-permute-start.14 = (bf16[256,128]{1,0:T(8,128)(2,1)S(1)}, bf16[256,128]{1,0:T(8,128)(2,1)S(1)}, u32[]{:S(2)}, u32[]{:S(2)}) collective-permute-start(bf16[256,128]{1,0:T(8,128)(2,1)S(1)} %get-tuple-element.203), channel_id=1, source_target_pairs={{0,4},{1,5},{2,6},{3,7},{4,0},{5,1},{6,2},{7,3},{8,12},{9,13},{10,... | collective-permute-start | bytes 196616 | tf_op jit(solution)/shard_map/ppermute | solution.py:745
  97.4 9.8 %collective-permute-start.13 = (bf16[256,128]{1,0:T(8,128)(2,1)S(1)}, bf16[256,128]{1,0:T(8,128)(2,1)S(1)}, u32[]{:S(2)}, u32[]{:S(2)}) collective-permute-start(bf16[256,128]{1,0:T(8,128)(2,1)S(1)} %get-tuple-element.204), channel_id=1, source_target_pairs={{0,2},{1,3},{2,0},{3,1},{4,6},{5,7},{6,4},{7,5},{8,10},{9,11},{10,... | collective-permute-start | bytes 196616 | tf_op jit(solution)/shard_map/ppermute | solution.py:745
  107.4 7.0 %collective-permute-start.17 = (bf16[2,2,144,256]{3,2,1,0:T(8,128)(2,1)S(1)}, bf16[2,2,144,256]{3,2,1,0:T(8,128)(2,1)S(1)}, u32[]{:S(2)}, u32[]{:S(2)}) collective-permute-start(bf16[2,2,144,256]{3,2,1,0:T(8,128)(2,1)S(1)} %fusion.7), channel_id=1, source_target_pairs={{0,16},{1,9},{2,18},{3,11},{4,20},{5,13},{6,22},{7,15},{8,24},{9,1... | collective-permute-start | bytes 884744 | tf_op jit(solution)/shard_map/ppermute | solution.py:745
  107.5 4.4 %collective-permute-start.16 = (bf16[256,768]{1,0:T(8,128)(2,1)}, bf16[256,768]{1,0:T(8,128)(2,1)S(1)}, u32[]{:S(2)}, u32[]{:S(2)}) collective-permute-start(bf16[256,768]{1,0:T(8,128)(2,1)} %get-tuple-element.161), channel_id=1, source_target_pairs={{0,1},{1,0},{2,3},{3,2},{4,5},{5,4},{6,7},{7,6},{8,9},{9,8},{10,11... | collective-permute-start | bytes 1179656 | tf_op jit(solution)/shard_map/ppermute | solution.py:737
  108.9 13.7 %collective-permute-start.19 = (bf16[768,256]{1,0:T(8,128)(2,1)S(1)}, bf16[768,256]{1,0:T(8,128)(2,1)S(1)}, u32[]{:S(2)}, u32[]{:S(2)}) collective-permute-start(bf16[768,256]{1,0:T(8,128)(2,1)S(1)} %fusion.2), channel_id=1, source_target_pairs={{0,16},{1,9},{2,18},{3,11},{4,20},{5,13},{6,22},{7,15},{8,24},{9,1... | collective-permute-start | bytes 1179656 | tf_op jit(solution)/shard_map/ppermute | solution.py:745
  114.5 11.2 %collective-permute-start.18 = (bf16[2,256,256]{2,1,0:T(8,128)(2,1)S(1)}, bf16[2,256,256]{2,1,0:T(8,128)(2,1)S(1)}, u32[]{:S(2)}, u32[]{:S(2)}) collective-permute-start(bf16[2,256,256]{2,1,0:T(8,128)(2,1)S(1)} %pad_maximum_fusion.1), channel_id=1, source_target_pairs={{0,2},{1,3},{2,0},{3,1},{4,6},{5,7},{6,4},{7,5},{8,10},{9,11},{10,... | collective-permute-start | bytes 786440 | tf_op jit(solution)/shard_map/ppermute | solution.py:745
  114.6 13.6 %collective-permute-start.21 = (bf16[384,256]{1,0:T(8,128)(2,1)S(1)}, bf16[384,256]{1,0:T(8,128)(2,1)S(1)}, u32[]{:S(2)}, u32[]{:S(2)}) collective-permute-start(bf16[384,256]{1,0:T(8,128)(2,1)S(1)} %fusion.4), channel_id=1, source_target_pairs={{0,4},{1,5},{2,6},{3,7},{4,0},{5,1},{6,2},{7,3},{8,12},{9,13},{10,... | collective-permute-start | bytes 589832 | tf_op jit(solution)/shard_map/ppermute | solution.py:745
  125.8 12.4 %collective-permute-start.24 = (bf16[256,256]{1,0:T(8,128)(2,1)S(1)}, bf16[256,256]{1,0:T(8,128)(2,1)S(1)}, u32[]{:S(2)}, u32[]{:S(2)}) collective-permute-start(bf16[256,256]{1,0:T(8,128)(2,1)S(1)} %fusion.11), channel_id=1, source_target_pairs={{0,4},{1,5},{2,6},{3,7},{4,0},{5,1},{6,2},{7,3},{8,12},{9,13},{10,... | collective-permute-start | bytes 393224 | tf_op jit(solution)/shard_map/ppermute | solution.py:745
  127.0 9.9 %collective-permute-start.23 = (bf16[768,256]{1,0:T(8,128)(2,1)S(1)}, bf16[768,256]{1,0:T(8,128)(2,1)S(1)}, u32[]{:S(2)}, u32[]{:S(2)}) collective-permute-start(bf16[768,256]{1,0:T(8,128)(2,1)S(1)} %add_convert_fusion.2.a_send), channel_id=1, source_target_pairs={{0,8},{1,17},{2,10},{3,19},{4,12},{5,21},{6,14},{7,23},{8,0},{9,25... | collective-permute-start | bytes 1179656 | tf_op jit(solution)/shard_map/ppermute | solution.py:745
  129.4 7.6 %collective-permute-start.22 = (bf16[384,256]{1,0:T(8,128)(2,1)S(1)}, bf16[384,256]{1,0:T(8,128)(2,1)S(1)}, u32[]{:S(2)}, u32[]{:S(2)}) collective-permute-start(bf16[384,256]{1,0:T(8,128)(2,1)S(1)} %fusion.6), channel_id=1, source_target_pairs={{0,16},{1,9},{2,18},{3,11},{4,20},{5,13},{6,22},{7,15},{8,24},{9,1... | collective-permute-start | bytes 589832 | tf_op jit(solution)/shard_map/ppermute | solution.py:745
  137.0 8.9 %collective-permute-start.26 = (bf16[768,256]{1,0:T(8,128)(2,1)S(1)}, bf16[768,256]{1,0:T(8,128)(2,1)S(1)}, u32[]{:S(2)}, u32[]{:S(2)}) collective-permute-start(bf16[768,256]{1,0:T(8,128)(2,1)S(1)} %pad_maximum_fusion.send_ref.b_send), channel_id=1, source_target_pairs={{0,8},{1,17},{2,10},{3,19},{4,12},{5,21},{6,14},{7,23},{8,0},{9,25... | collective-permute-start | bytes 1179656 | tf_op jit(solution)/shard_map/ppermute | solution.py:745
  138.3 6.2 %collective-permute-start.25 = (bf16[256,256]{1,0:T(8,128)(2,1)S(1)}, bf16[256,256]{1,0:T(8,128)(2,1)S(1)}, u32[]{:S(2)}, u32[]{:S(2)}) collective-permute-start(bf16[256,256]{1,0:T(8,128)(2,1)S(1)} %fusion.10), channel_id=1, source_target_pairs={{0,16},{1,9},{2,18},{3,11},{4,20},{5,13},{6,22},{7,15},{8,24},{9,1... | collective-permute-start | bytes 393224 | tf_op jit(solution)/shard_map/ppermute | solution.py:745
  146.0 5.8 %collective-permute-start.27 = (bf16[400,256]{1,0:T(8,128)(2,1)S(1)}, bf16[400,256]{1,0:T(8,128)(2,1)S(1)}, u32[]{:S(2)}, u32[]{:S(2)}) collective-permute-start(bf16[400,256]{1,0:T(8,128)(2,1)S(1)} %pad_maximum_fusion.2.last_send), channel_id=1, source_target_pairs={{0,8},{1,17},{2,10},{3,19},{4,12},{5,21},{6,14},{7,23},{8,0},{9,25... | collective-permute-start | bytes 614408 | tf_op jit(solution)/shard_map/ppermute | solution.py:745
  (34 other events, 181.2 us)

commit v6 on v5

--- a/solution.py
+++ b/solution.py
@@ -2,6 +2,7 @@
 
 import jax
 import jax.numpy as jnp
+import numpy as np
 from jax import lax
 from jax.experimental import pallas as pl
 from jax.experimental.pallas import tpu as pltpu
@@ -41,7 +42,7 @@
 
 
 def rope_tables(position):
-    inverse = 10000.0 ** (-(2.0 * jnp.arange(HALF, dtype=F32)) / ROT)
+    inverse = jnp.asarray(10000.0 ** (-2.0 * np.arange(HALF) / ROT), F32)
     angles = inverse[:, None] * position.astype(F32)[None, :]
     return (jnp.cos(angles), jnp.sin(angles))
 
@@ -66,8 +67,11 @@
 
 
 def call(kernel, name, outs, specs, out_specs, scratch, limit, flops=1000):
+    def body(table, *refs):
+        kernel(scalars(table), *refs)
+
     made = pl.pallas_call(
-        kernel,
+        body,
         out_shape=outs,
         grid_spec=pltpu.PrefetchScalarGridSpec(
             num_scalar_prefetch=1, in_specs=specs, out_specs=out_specs, scratch_shapes=scratch
@@ -77,9 +81,9 @@
         name=name,
     )
 
-    def placed(scalars, *values):
+    def placed(table, *values):
         return made(
-            scalars,
+            table,
             *(
                 pltpu.with_memory_space_constraint(v, pltpu.HBM) if spec is HBM else v
                 for v, spec in zip(values, specs)
@@ -89,8 +93,23 @@
     return placed
 
 
+def scalars(table):
+    ctx, grp = lax.axis_index("ctx"), lax.axis_index("grp")
+    per_chip = 2 * table.shape[0] // lax.axis_size("ctx")
+    core, chip = lax.rem(ctx, 2), lax.div(ctx, 2)
+    y, x = lax.div(grp, 2), lax.rem(grp, 2)
+    blocks = [table[chip * per_chip + n] for n in range(per_chip)]
+    ranks = [sum((b < a).astype(jnp.int32) for b in blocks if b is not a) for a in blocks]
+    order = []
+    for k in range(per_chip):
+        want = k // 2 if k % 2 else per_chip - 1 - k // 2
+        at = sum(jnp.where(rank == want, n, 0) for n, rank in enumerate(ranks))
+        order.append(lax.rem(at + per_chip - core * (per_chip // 2), per_chip))
+    return [core, chip, jnp.where(core == 0, x, y), jnp.where(core == 1, x, y)] + order
+
+
 def attn_kernel(
-    table, place, *refs, blocks, heads, size, n_kv, per_chip, start, last_call, first_call
+    table, *refs, blocks, heads, size, n_kv, per_chip, start, split, last_call, first_call
 ):
     q_ref, do_ref, cos_ref, sin_ref = refs[:4]
     kv_refs = refs[4 : 4 + n_kv]
@@ -101,6 +120,14 @@
     outs = refs[2:-11]
     kv_c, kv_t, s_scr, p_scr, rq, rd, rqt, rdt, o_acc, dq_acc, dkv_acc = refs[-11:]
     step, group = pl.program_id(0), pl.program_id(1)
+    core, chip, _, _, *order = scalars(table)
+    if split:
+        column = sum(
+            jnp.where(step == n, order[start + n], 0) for n in range(per_chip // 2)
+        )
+        position = lax.rem(column + core * (per_chip // 2), per_chip)
+    else:
+        column = position = step
     lanes = heads * BLK
     prompt_blocks = blocks // 2
     prompt_tiles = prompt_blocks * BLK // TILE
@@ -118,7 +145,8 @@
 
             def place_block(at, carry, n=n, kv_ref=kv_ref):
                 spot = n * share + at
-                block = table[((spot // per_chip) ^ place[2]) * per_chip + spot % per_chip]
+                owner = (spot // per_chip) ^ chip if split else spot // per_chip
+                block = table[owner * per_chip + spot % per_chip]
                 rows = kv_ref[block_rows(at), :]
                 kv_c[block_rows(block), :] = rows
                 turned = jnp.concatenate([rows.T, ones], 0)
@@ -136,7 +164,8 @@
             lax.fori_loop(0, share, place_block, 0)
         dkv_acc[...] = jnp.zeros_like(dkv_acc) if first_call else sum_ref[...]
 
-    block = table[place[0] + place[4 + start + step]]
+    block = table[chip * per_chip + position]
+    columns = pl.ds(pl.multiple_of(column * BLK, BLK), BLK)
     last = block // 2
     in_prompt = block < prompt_blocks
     seg_tile = (prompt_blocks + (block - prompt_blocks) // cont_blocks * cont_blocks) // 2
@@ -149,7 +178,7 @@
         return pl.ds(pl.multiple_of(tile * TILE, TILE), TILE)
 
     for h in range(heads):
-        rq[0:size, h * BLK : (h + 1) * BLK] = q_ref[h * size : (h + 1) * size, :]
+        rq[0:size, h * BLK : (h + 1) * BLK] = q_ref[h * size : (h + 1) * size, columns]
     rq[size : 2 * size, :] = jnp.zeros((size, lanes), BF)
 
     def scores(tile):
@@ -187,7 +216,7 @@
     for h in range(heads):
         at = slice(h * BLK, (h + 1) * BLK)
         mix_ref[h * size : (h + 1) * size, :] = mixed[:, at].astype(BF)
-        grads.append(do_ref[h * size : (h + 1) * size, :])
+        grads.append(do_ref[h * size : (h + 1) * size, columns])
     scaled = (jnp.concatenate(grads, 1) * inverse).astype(BF)
     delta = jnp.sum(mixed * scaled.astype(F32), 0, keepdims=True)
     rd[0:size, :] = jnp.zeros((size, lanes), BF)
@@ -207,7 +236,7 @@
 
     lax.fori_loop(0, full + 1, third_pass, 0)
 
-    cosine, sine = cos_ref[...], sin_ref[...]
+    cosine, sine = cos_ref[:, columns], sin_ref[:, columns]
     for h in range(heads):
         part = dq_acc[:, h * BLK : (h + 1) * BLK] * 0.125
         dq_ref[h * size : (h + 1) * size, :] = turn(part, cosine, -sine).astype(BF)
@@ -235,16 +264,16 @@
         per_core = per_chip // 2
         for low in range(2):
             for high in range(2):
-                chip = place[2] ^ (low + 2 * high)
+                owner = chip ^ (low + 2 * high)
                 for n in range(per_core):
                     here = slice(n * BLK, (n + 1) * BLK)
-                    base = chip * per_chip + n
-                    outs[0][low, high, here, :] = rows_of(base + per_core - place[1])
-                    outs[1][low, high, here, :] = rows_of(base + place[1])
+                    base = owner * per_chip + n
+                    outs[0][low, high, here, :] = rows_of(base + per_core * (1 - core))
+                    outs[1][low, high, here, :] = rows_of(base + per_core * core)
 
 
 def attention(
-    table, place, q_t, do_t, cosine, sine, kvs, carried, start, count, per_chip, last_call, split
+    table, q_t, do_t, cosine, sine, kvs, carried, start, count, per_chip, last_call, split
 ):
     width = q_t.shape[0]
     rows = count * BLK
@@ -269,12 +298,7 @@
     else:
         dkv_shapes = [shape((keys, 2 * size), BF)]
     extra = [] if first_call else [carried]
-
-    def column_of(i, scalars):
-        return lax.rem(scalars[4 + start + i] + per_chip - scalars[1], per_chip)
-
-    column = pl.BlockSpec((heads * size, BLK), lambda i, j, _, scalars: (j, column_of(i, scalars)))
-    angle = pl.BlockSpec((HALF, BLK), lambda i, j, _, scalars: (0, column_of(i, scalars)))
+    column = pl.BlockSpec((heads * size, q_t.shape[1]), lambda i, j, *_: (j, 0))
     out_column = pl.BlockSpec((heads * size, BLK), lambda i, j, *_: (j, i))
     return pl.pallas_call(
         functools.partial(
@@ -285,14 +309,15 @@
             n_kv=len(kvs),
             per_chip=per_chip,
             start=start,
+            split=split,
             last_call=last_call,
             first_call=first_call,
         ),
         out_shape=[shape((width, rows), BF)] * 2 + dkv_shapes,
         grid_spec=pltpu.PrefetchScalarGridSpec(
-            num_scalar_prefetch=2,
+            num_scalar_prefetch=1,
             grid=(count, all_heads // heads),
-            in_specs=[column, column, angle, angle]
+            in_specs=[column, column, whole(cosine.shape), whole(cosine.shape)]
             + [whole(kv.shape) for kv in kvs]
             + [whole(e.shape) for e in extra],
             out_specs=[out_column, out_column] + [whole(s.shape) for s in dkv_shapes],
@@ -317,7 +342,7 @@
             flops=1000, bytes_accessed=1000, transcendentals=0
         ),
         name="attention",
-    )(table, place, q_t, do_t, cosine, sine, *kvs, *extra)
+    )(table, q_t, do_t, cosine, sine, *kvs, *extra)
 
 
 def prologue_kernel(
@@ -444,7 +469,7 @@
                 give(low, high, 1, b * up_rows, grad_s[rows_at, b * WIDE : (b + 1) * WIDE])
 
 
-def ffn_gradients(sc, h_two, g_two, w_up, w_down, n, part, n_pair):
+def ffn_gradients(table, h_two, g_two, w_up, w_down, n, part, n_pair):
     rows, width = h_two.shape
     span = n_pair * LANES
     block = width // WIDE * LANES
@@ -465,7 +490,7 @@
             pltpu.SemaphoreType.DMA((2,)),
         ],
         56,
-    )(sc, h_two, g_two, w_up, w_down)
+    )(table, h_two, g_two, w_up, w_down)
 
 
 def late_kernel(
@@ -506,7 +531,7 @@
                         ref[second, low, high, r * unit : (r + 1) * unit, :] = both_s[source, lane]
 
 
-def late_gradients(sc, h_one, dqs, mixes, gots, g_two, n_pair):
+def late_gradients(table, h_one, dqs, mixes, gots, g_two, n_pair):
     half = dqs[0].shape[0]
     width = 2 * half
     rows = h_one.shape[0]
@@ -522,7 +547,7 @@
             pltpu.VMEM((width, width), BF),
         ],
         16,
-    )(sc, h_one, *dqs, *mixes, *gots, g_two)
+    )(table, h_one, *dqs, *mixes, *gots, g_two)
 
 
 def out_kernel(sc, a0, a1, a2, mix_ref, x_ref, w_down, w_out, own_ref, send_ref, down_s, out_s, sems, *, part, n_pair):
@@ -785,22 +810,14 @@
     per_chip = 2 * rows // BLK
     table = block_table[0]
     count = rows // BLK
-    mine = lax.dynamic_slice_in_dim(table, chip * per_chip, per_chip)
-    rank = jnp.sum((mine[None, :] < mine[:, None]).astype(jnp.int32), 1)
-    ends = [n // 2 if n % 2 else per_chip - 1 - n // 2 for n in range(per_chip)]
-    order = jnp.stack(
-        [jnp.sum(jnp.where(rank == n, jnp.arange(per_chip, dtype=jnp.int32), 0)) for n in ends]
-    )
-    place = jnp.stack([chip * per_chip, core * count, chip, 0 * chip]).astype(jnp.int32)
-    place = jnp.concatenate([place, order])
-    sc = jnp.stack([core, chip, links.bit(0), links.bit(1)]).astype(jnp.int32)
-    sc = jnp.concatenate([sc, lax.rem(order + per_chip - core * count, per_chip)])
     gains = jnp.concatenate([ln1_gain, ln1_bias, ln2_gain, ln2_bias]).reshape(4, width)
 
     x_other, g_other = links.swap(layer_input), links.swap(cotangent)
-    own_slots = lax.dynamic_slice_in_dim(table, chip * per_chip, per_chip).reshape(2, -1)
-    slots = jnp.concatenate([own_slots[core], own_slots[1 - core]])
-    canon = (slots[:, None] * BLK + jnp.arange(BLK, dtype=jnp.int32)[None, :]).reshape(2 * rows)
+    column = jnp.arange(2 * rows, dtype=jnp.int32)
+    slot = chip * per_chip + lax.rem(column // BLK + core * count, per_chip)
+    slots = jnp.arange(table.shape[0], dtype=jnp.int32)
+    canon = jnp.sum(jnp.where(slots[:, None] == slot[None, :], table[:, None], 0), 0)
+    canon = canon * BLK + column % BLK
     prompt_len = group_len // 2
     cont_span = min(CONT, prompt_len)
     position = jnp.where(
@@ -821,11 +838,11 @@
             pltpu.SemaphoreType.DMA((5,)),
         ],
         56,
-    )(sc, layer_input, x_other, cotangent, g_other, gains, w_keyval, cosine, sine)
+    )(table, layer_input, x_other, cotangent, g_other, gains, w_keyval, cosine, sine)
 
     kv_got = links.flip(kv_low, 1)
     ffn = functools.partial(
-        ffn_gradients, sc, w_up=w_up, w_down=w_down, part=part_hidden, n_pair=n_pair
+        ffn_gradients, table, w_up=w_up, w_down=w_down, part=part_hidden, n_pair=n_pair
     )
     act_1, dup_1, b_send = ffn(h_two, g_two, n=1)
     b_send, kv_got = meet(b_send, kv_got)
@@ -849,13 +866,13 @@
             pltpu.SemaphoreType.DMA((2,)),
         ],
         16,
-    )(sc, tie(h_one, a_send), g_two, cosine, sine, w_query, w_out)
+    )(table, tie(h_one, a_send), g_two, cosine, sine, w_query, w_out)
     q_t, b_got = meet(q_t, b_got)
     b_send = add(b_keep[1], b_got[1])
     b_got_2 = links.cross(b_send, 1)
 
     attend = functools.partial(
-        attention, table, place, do_t=do_t, cosine=cosine, sine=sine, kvs=(kv_near, kv_far),
+        attention, table, do_t=do_t, cosine=cosine, sine=sine, kvs=(kv_near, kv_far),
         count=count, per_chip=per_chip, split=True,
     )
     mix_0, dq_0, carried = attend(
@@ -876,7 +893,7 @@
     dkv_sends = [add(dkv_keep[at], dkv_got[at]) for at in ((1, 0), (0, 1), (1, 1))]
     dkv_gots = [links.flip(value, n + 1) for n, value in enumerate(dkv_sends)]
     late_send, late_keep, mix_own, dq_own = late_gradients(
-        sc, tie(h_one, *dkv_sends), (dq_0, dq_1), (mix_0, mix_1), (mix_0_got, mix_1_got), g_two, n_pair
+        table, tie(h_one, *dkv_sends), (dq_0, dq_1), (mix_0, mix_1), (mix_0_got, mix_1_got), g_two, n_pair
     )
     late_got = links.cross(late_send, 0)
 
@@ -892,9 +909,9 @@
             pltpu.VMEM((width, half), BF),
             pltpu.SemaphoreType.DMA((2,)),
         ],
-        56,
+        24,
     )(
-        sc, dup_0, dup_1, tie(dup_2, late_send), dq_own, layer_input, x_other, gains,
+        table, dup_0, dup_1, tie(dup_2, late_send), dq_own, layer_input, x_other, gains,
         w_up, w_query,
     )
     hat_send, late_got, *dkv_gots = meet(hat_send, late_got, *dkv_gots)
@@ -916,7 +933,7 @@
         [],
         16,
     )(
-        sc, dkv_own, *dkv_gots, tie(cosine, late_send, b_send), sine, w_keyval, h_one,
+        table, dkv_own, *dkv_gots, tie(cosine, late_send, b_send), sine, w_keyval, h_one,
         layer_input, gains, hat_own, hat_got, sums, cotangent,
     )
     few_send, late_got_2 = meet(few_send, late_got_2)
@@ -939,9 +956,9 @@
             pltpu.VMEM((half, width), BF),
             pltpu.SemaphoreType.DMA((2,)),
         ],
-        56,
+        24,
     )(
-        sc, act_0, act_1, tie(act_2, last_send, a_sum), mix_own, layer_input, w_down, w_out,
+        table, act_0, act_1, tie(act_2, last_send, a_sum), mix_own, layer_input, w_down, w_out,
     )
     out_send, last_got, a_got = meet(out_send, last_got, a_got)
     out_got = links.swap(out_send)
@@ -971,13 +988,13 @@
     total_down = call(
         functools.partial(down_kernel, width=width),
         "down", shape((part_hidden, width), F32), [VM] * 4, VM, [], 8,
-    )(sc, tie(a_sum, last), a_got, b_sum, b_got)
+    )(table, tie(a_sum, last), a_got, b_sum, b_got)
     total_down, last_got = meet(total_down, last_got)
     size_out = 9 * part + few
     other, own = call(
         functools.partial(pack_kernel, width=width, part=part, quarter=quarter),
         "pack", [shape((size_out, WIDE), BF)] * 2, [VM] * 6, [VM] * 2, [], 8,
-    )(sc, a_sum, a_got, b_sum, b_got, last, last_got)
+    )(table, a_sum, a_got, b_sum, b_got, last, last_got)
     got = links.swap(other)
     total_up, total_query, total_out, total_kv, norm = call(
         functools.partial(final_kernel, part=part, n_pair=n_pair),
@@ -993,7 +1010,7 @@
         [VM] * 5,
         [],
         8,
-    )(sc, own, got)
+    )(table, own, got)
     norms = [norm[n, :part] for n in range(4)]
     return (layer_output, in_grad, *norms, total_query, total_kv, total_out, total_up, total_down)
 
@@ -1068,10 +1085,8 @@
         jax.vmap(turn, (0, None, None))(q_raw.reshape(-1, size, 2 * rows), cosine, sine)
     ).reshape(half_width, 2 * rows)
     do_t = dot(out_half, g_two, ((1,), (1,)))
-    place = jnp.stack([chip * per_chip] + [0 * chip] * 3 + [n + 0 * chip for n in range(per_chip)])
-    place = place.astype(jnp.int32)
     mix_t, dq_t, dkv_part = attention(
-        table, place, q_t, do_t, cosine, sine, (kv_all,), None, 0, per_chip, per_chip, True, False
+        table, q_t, do_t, cosine, sine, (kv_all,), None, 0, per_chip, per_chip, True, False
     )
 
     dkv_part = dkv_part.reshape(n_pair, 2, rows, 2 * size)

time: 159 us -> 145 us (0.912); the launches traced: 157 us -> 146 us
  other arithmetic: 13.5 us -> 5.11 us
  local copies, waits for them, and re-layouts: 7.67 us -> 2.12 us
  starting transfers between devices: 30.1 us -> 34 us
    convert_element_type x13, other arithmetic: 7.62 us -> 1.31 us  [add(): return sum((value.astype(F32) for value in values)).astype(BF)]
    pallas_call x12, Pallas kernels: 53.6 us -> 48.5 us  [placed(): made(table, *(pltpu.with_memory_space_constraint(v, pltpu.HBM) if spec is...]
    pallas_call x2, Pallas kernels: 26 us -> 30.1 us  [attention(): pl.pallas_call(functools.partial(attn_kernel, blocks=blocks, heads=heads,...]
    ppermute x21, starting transfers between devices: 28.8 us -> 32.7 us  [permute(): return lax.ppermute(value, ('grp', 'ctx'), pairs)]
    concatenate x3 -> x0, local copies, waits for them, and re-layouts: 3.2 us -> none  [the longest x1 2.54 us: shards_small(): place = jnp.concatenate([place, order])]
    rem x1 -> x0, other arithmetic: 2.54 us -> none  [shards_small(): lax.rem(order + per_chip - core * count, per_chip)]
  transfers between devices with their start and end apart: 29 -> 29, of which waited for: 10 -> 10; matrix products, arithmetic and copies ran while one was open for 10% -> 4% of each run, Pallas kernels for 44% -> 47%
where the time goes in v6:
time: 145 us; the launch traced here: 146 us
  Pallas kernels  78.6 us (54%)
  starting transfers between devices  34 us (23%)
  waiting for transfers between devices  24.6 us (17%)
  other arithmetic  5.11 us (4%)
  local copies, waits for them, and re-layouts  2.12 us (1%)
    pallas_call x12, Pallas kernels, placed(): made(table, *(pltpu.with_memory_space_constraint(v, pltpu.HBM) if spec is...  48.5 us
    ppermute x21, starting transfers between devices, permute(): return lax.ppermute(value, ('grp', 'ctx'), pairs)  32.7 us
    pallas_call x2, Pallas kernels, attention(): pl.pallas_call(functools.partial(attn_kernel, blocks=blocks, heads=heads,...  30.1 us
    ppermute x21, waiting for transfers between devices, permute(): return lax.ppermute(value, ('grp', 'ctx'), pairs)  21.2 us
    ppermute x8, waiting for transfers between devices, swap(): return lax.ppermute(value, 'ctx', [(i, i ^ 1) for i in range(self.n_ctx)])  3.42 us
  transfers between devices with their start and end apart: 29, of which 10 were waited for; matrix products, arithmetic and copies ran while one was open for 4% of the time, Pallas kernels for 47%

profile of v6, /device:TPU:0, one launch (start us, length us, event | category | flops | bytes accessed | tf_op | source)
XLA Modules:
  0.0 145.6 jit_solution(16613926200512937647)
XLA Ops:
  5.7 5.1 %prologue.1 = (bf16[512,768]{1,0:T(8,128)(2,1)}, bf16[512,768]{1,0:T(8,128)(2,1)}, bf16[512,768]{1,0:T(8,128)(2,1)}, bf16[512,128]{1,0:T(8,128)(2,1)}) custom-call(s32[16]{0:T(128)} %bitcast.66, bf16[256,768]{1,0:T(8,128)(2,1)} %refs_4_.5, bf16[256,768]{1,0:T(8,128)(2,1)} %copy-done.3, bf16[256,768]{1,0:T(8,128)(2,1)} %refs_13_.1, ...), custom_call_target="tpu_custom_call" | custom-call | flops 1000 | bytes 1000 | tf_op jit(solution)/shard_map/prologue/pallas_call | solution.py:85
  10.8 3.1 %collective-permute-start.2 = (bf16[512,128]{1,0:T(8,128)(2,1)}, bf16[512,128]{1,0:T(8,128)(2,1)S(1)}, u32[]{:S(2)}, u32[]{:S(2)}) collective-permute-start(bf16[512,128]{1,0:T(8,128)(2,1)} %get-tuple-element.106), channel_id=1, source_target_pairs={{0,2},{1,3},{2,0},{3,1},{4,6},{5,7},{6,4},{7,5},{8,10},{9,11},{10,... | collective-permute-start | bytes 393224 | tf_op jit(solution)/shard_map/ppermute | solution.py:770
  13.9 7.8 %ffn_gradients.3 = (bf16[512,512]{1,0:T(8,128)(2,1)}, bf16[512,512]{1,0:T(8,128)(2,1)}, bf16[2,2,2,384,256]{4,3,2,1,0:T(8,128)(2,1)}) custom-call(s32[16]{0:T(128)} %bitcast.67, bf16[512,768]{1,0:T(8,128)(2,1)} %get-tuple-element.112.refs_0_, bf16[512,768]{1,0:T(8,128)(2,1)} %get-tuple-element.104.refs_1_.refs_7_, bf16[768,3072]{1,0:T(8,128)(2,1)} %refs_7_.1, ...), custom_call_target="tpu_custom_call" | custom-call | flops 1000 | bytes 1000 | tf_op jit(solution)/shard_map/ffn_gradients/pallas_call | solution.py:85
  23.2 2.7 %collective-permute-start.3 = (bf16[1024,128]{1,0:T(8,128)(2,1)S(1)}, bf16[1024,128]{1,0:T(8,128)(2,1)S(1)}, u32[]{:S(2)}, u32[]{:S(2)}) collective-permute-start(bf16[1024,128]{1,0:T(8,128)(2,1)S(1)} %constant_dynamic-update-slice_fusion.refs_4_), channel_id=1, source_target_pairs={{0,4},{1,5},{2,6},{3,7},{4,0},{5,1},{6,2},{7,3},{8,12},{9,13},{10,... | collective-permute-start | bytes 786440 | tf_op jit(solution)/shard_map/ppermute | solution.py:770
  25.9 7.6 %ffn_gradients.4 = (bf16[512,512]{1,0:T(8,128)(2,1)}, bf16[512,512]{1,0:T(8,128)(2,1)}, bf16[2,2,2,384,256]{4,3,2,1,0:T(8,128)(2,1)}) custom-call(s32[16]{0:T(128)} %bitcast.68, bf16[512,768]{1,0:T(8,128)(2,1)} %get-tuple-element.112.refs_0_, bf16[512,768]{1,0:T(8,128)(2,1)} %get-tuple-element.104.refs_1_.refs_7_, bf16[768,3072]{1,0:T(8,128)(2,1)} %refs_7_.1, ...), custom_call_target="tpu_custom_call" | custom-call | flops 1000 | bytes 1000 | tf_op jit(solution)/shard_map/ffn_gradients/pallas_call | solution.py:85
  33.5 7.7 %ffn_gradients.5 = (bf16[512,512]{1,0:T(8,128)(2,1)}, bf16[512,512]{1,0:T(8,128)(2,1)}, bf16[2,768,256]{2,1,0:T(8,128)(2,1)}, bf16[2,768,256]{2,1,0:T(8,128)(2,1)}) custom-call(s32[16]{0:T(128)} %bitcast.69, bf16[512,768]{1,0:T(8,128)(2,1)} %get-tuple-element.112.refs_0_, bf16[512,768]{1,0:T(8,128)(2,1)} %get-tuple-element.104.refs_1_.refs_7_, ...), custom_call_target="tpu_custom_call" | custom-call | flops 1000 | bytes 1000 | tf_op jit(solution)/shard_map/ffn_gradients/pallas_call | solution.py:85
  41.8 2.8 %project.1 = (bf16[384,512]{1,0:T(8,128)(2,1)S(1)}, f32[384,512]{1,0:T(8,128)S(1)}) custom-call(s32[16]{0:T(128)S(1)} %bitcast.70, bf16[512,768]{1,0:T(8,128)(2,1)S(1)} %copy-done.1, bf16[512,768]{1,0:T(8,128)(2,1)S(1)} %copy-done, f32[8,512]{1,0:T(8,128)S(1)} %copy-done.8, f32[8,512]{1,0:T(8,128)S(1)} %copy-done.7, bf16[768,768]{1,0:T(8,128)(2,1)} %refs_8_.2, ...), custom_call_target="tpu_custom_call" | custom-call | flops 1000 | bytes 1000 | tf_op jit(solution)/shard_map/project/pallas_call | solution.py:85
  46.4 15.0 %attention.2 = (bf16[384,256]{1,0:T(8,128)(2,1)S(1)}, bf16[384,256]{1,0:T(8,128)(2,1)S(1)}, f32[2048,128]{1,0:T(8,128)S(1)}) custom-call(s32[16]{0:T(128)S(1)} %bitcast.71, bf16[384,512]{1,0:T(8,128)(2,1)S(1)} %get-tuple-element.129.refs_0_, f32[384,512]{1,0:T(8,128)S(1)} %get-tuple-element.120.refs_1_, f32[8,512]{1,0:T(8,128)S(1)} %copy-done.8, ...), custom_call_target="tpu_custom_call" | custom-call | flops 1000 | bytes 1000 | tf_op jit(solution)/shard_map/attention/pallas_call | solution.py:303
  63.4 15.2 %attention.3 = (bf16[384,256]{1,0:T(8,128)(2,1)S(1)}, bf16[384,256]{1,0:T(8,128)(2,1)S(1)}, bf16[2,2,256,128]{3,2,1,0:T(8,128)(2,1)S(1)}, bf16[2,2,256,128]{3,2,1,0:T(8,128)(2,1)S(1)}) custom-call(s32[16]{0:T(128)S(1)} %bitcast.72, bf16[384,512]{1,0:T(8,128)(2,1)S(1)} %get-tuple-element.129.refs_0_, f32[384,512]{1,0:T(8,128)S(1)} %get-tuple-element.120.refs_1_, ...), custom_call_target="tpu_custom_call" | custom-call | flops 1000 | bytes 1000 | tf_op jit(solution)/shard_map/attention/pallas_call | solution.py:303
  78.6 2.3 %collective-permute-done.7 = bf16[768,256]{1,0:T(8,128)(2,1)S(1)} collective-permute-done((bf16[768,256]{1,0:T(8,128)(2,1)S(1)}, bf16[768,256]{1,0:T(8,128)(2,1)S(1)}, u32[]{:S(2)}, u32[]{:S(2)}) %collective-permute-start.7) | collective-permute-done | bytes 393248 | tf_op jit(solution)/shard_map/ppermute | solution.py:770
  83.1 1.9 %late_gradients.1 = (bf16[2,2,2,144,256]{4,3,2,1,0:T(8,128)(2,1)S(1)}, bf16[2,2,2,144,256]{4,3,2,1,0:T(8,128)(2,1)S(1)}, bf16[384,512]{1,0:T(8,128)(2,1)S(1)}, bf16[384,512]{1,0:T(8,128)(2,1)S(1)}) custom-call(s32[16]{0:T(128)S(1)} %bitcast.73, bf16[512,768]{1,0:T(8,128)(2,1)S(1)} %copy-done.1, bf16[384,256]{1,0:T(8,128)(2,1)S(1)} %get-tuple-element.142.refs_1_, ...), custom_call_target="tpu_custom_call" | custom-call | flops 1000 | bytes 1000 | tf_op jit(solution)/shard_map/late_gradients/pallas_call | solution.py:85
  85.1 2.0 %collective-permute-start.12 = (bf16[2,2,2,144,256]{4,3,2,1,0:T(8,128)(2,1)S(1)}, bf16[2,2,2,144,256]{4,3,2,1,0:T(8,128)(2,1)S(1)}, u32[]{:S(2)}, u32[]{:S(2)}) collective-permute-start(bf16[2,2,2,144,256]{4,3,2,1,0:T(8,128)(2,1)S(1)} %get-tuple-element.150), channel_id=1, source_target_pairs={{0,8},{1,17},{2,10},{3,19},{4,12},{5,21},{6,14},{7,23},{8,0},{9,25... | collective-permute-start | bytes 1769480 | tf_op jit(solution)/shard_map/ppermute | solution.py:770
  87.0 3.7 %collective-permute-start.15 = (bf16[256,128]{1,0:T(8,128)(2,1)S(1)}, bf16[256,128]{1,0:T(8,128)(2,1)S(1)}, u32[]{:S(2)}, u32[]{:S(2)}) collective-permute-start(bf16[256,128]{1,0:T(8,128)(2,1)S(1)} %get-tuple-element.197), channel_id=1, source_target_pairs={{0,6},{1,7},{2,4},{3,5},{4,2},{5,3},{6,0},{7,1},{8,14},{9,15},{10,... | collective-permute-start | bytes 196616 | tf_op jit(solution)/shard_map/ppermute | solution.py:770
  91.5 4.5 %norms.1 = (f32[256,768]{1,0:T(8,128)S(1)}, bf16[256,768]{1,0:T(8,128)(2,1)S(1)}, f32[8,768]{1,0:T(8,128)S(1)}) custom-call(s32[16]{0:T(128)S(1)} %bitcast.74, bf16[512,512]{1,0:T(8,128)(2,1)S(1)} %copy-done.14, bf16[512,512]{1,0:T(8,128)(2,1)S(1)} %copy-done.12, bf16[512,512]{1,0:T(8,128)(2,1)S(1)} %copy-done.13, ...), custom_call_target="tpu_custom_call" | custom-call | flops 1000 | bytes 1000 | tf_op jit(solution)/shard_map/norms/pallas_call | solution.py:85
  96.5 2.0 %collective-permute-start.19 = (bf16[768,256]{1,0:T(8,128)(2,1)S(1)}, bf16[768,256]{1,0:T(8,128)(2,1)S(1)}, u32[]{:S(2)}, u32[]{:S(2)}) collective-permute-start(bf16[768,256]{1,0:T(8,128)(2,1)S(1)} %fusion.2), channel_id=1, source_target_pairs={{0,16},{1,9},{2,18},{3,11},{4,20},{5,13},{6,22},{7,15},{8,24},{9,1... | collective-permute-start | bytes 1179656 | tf_op jit(solution)/shard_map/ppermute | solution.py:770
  98.6 2.5 %last.1 = (f32[256,768]{1,0:T(8,128)}, bf16[2,112,256]{2,1,0:T(8,128)(2,1)S(1)}, bf16[2,112,256]{2,1,0:T(8,128)(2,1)S(1)}) custom-call(s32[16]{0:T(128)S(1)} %bitcast.75, bf16[256,128]{1,0:T(8,128)(2,1)S(1)} %get-tuple-element.198.refs_0_, bf16[256,128]{1,0:T(8,128)(2,1)S(1)} %collective-permute-done.13.refs_1_, ...), custom_call_target="tpu_custom_call" | custom-call | flops 1000 | bytes 1000 | tf_op jit(solution)/shard_map/last/pallas_call | solution.py:85
  104.5 2.9 %collective-permute-start.21 = (bf16[384,256]{1,0:T(8,128)(2,1)S(1)}, bf16[384,256]{1,0:T(8,128)(2,1)S(1)}, u32[]{:S(2)}, u32[]{:S(2)}) collective-permute-start(bf16[384,256]{1,0:T(8,128)(2,1)S(1)} %fusion.4), channel_id=1, source_target_pairs={{0,4},{1,5},{2,6},{3,7},{4,0},{5,1},{6,2},{7,3},{8,12},{9,13},{10,... | collective-permute-start | bytes 589832 | tf_op jit(solution)/shard_map/ppermute | solution.py:770
  107.4 4.2 %outputs.1 = (f32[256,768]{1,0:T(8,128)S(1)}, bf16[256,768]{1,0:T(8,128)(2,1)S(1)}) custom-call(s32[16]{0:T(128)S(1)} %bitcast.76, bf16[512,512]{1,0:T(8,128)(2,1)S(1)} %copy-done.11, bf16[512,512]{1,0:T(8,128)(2,1)S(1)} %copy-done.9, bf16[512,512]{1,0:T(8,128)(2,1)S(1)} %copy-done.10, bf16[384,512]{1,0:T(8,128)(2,1)S(1)} %get-tuple-element.169.refs_3_, ...), custom_call_target="tpu_custom_call" | custom-call | flops 1000 | bytes 1000 | tf_op jit(solution)/shard_map/outputs/pallas_call | solution.py:85
  113.4 1.9 %collective-permute-start.24 = (bf16[256,256]{1,0:T(8,128)(2,1)S(1)}, bf16[256,256]{1,0:T(8,128)(2,1)S(1)}, u32[]{:S(2)}, u32[]{:S(2)}) collective-permute-start(bf16[256,256]{1,0:T(8,128)(2,1)S(1)} %fusion.11), channel_id=1, source_target_pairs={{0,4},{1,5},{2,6},{3,7},{4,0},{5,1},{6,2},{7,3},{8,12},{9,13},{10,... | collective-permute-start | bytes 393224 | tf_op jit(solution)/shard_map/ppermute | solution.py:770
  119.3 6.0 %collective-permute-done.23.refs_1_ = bf16[768,256]{1,0:T(8,128)(2,1)S(1)} collective-permute-done((bf16[768,256]{1,0:T(8,128)(2,1)S(1)}, bf16[768,256]{1,0:T(8,128)(2,1)S(1)}, u32[]{:S(2)}, u32[]{:S(2)}) %collective-permute-start.23) | collective-permute-done | bytes 393248 | tf_op jit(solution)/shard_map/ppermute | solution.py:770
  128.3 4.9 %collective-permute-done.25 = bf16[256,256]{1,0:T(8,128)(2,1)S(1)} collective-permute-done((bf16[256,256]{1,0:T(8,128)(2,1)S(1)}, bf16[256,256]{1,0:T(8,128)(2,1)S(1)}, u32[]{:S(2)}, u32[]{:S(2)}) %collective-permute-start.25) | collective-permute-done | bytes 131104 | tf_op jit(solution)/shard_map/ppermute | solution.py:770
  137.5 3.0 %collective-permute-done.27.refs_5_ = bf16[400,256]{1,0:T(8,128)(2,1)S(1)} collective-permute-done((bf16[400,256]{1,0:T(8,128)(2,1)S(1)}, bf16[400,256]{1,0:T(8,128)(2,1)S(1)}, u32[]{:S(2)}, u32[]{:S(2)}) %collective-permute-start.27) | collective-permute-done | bytes 204832 | tf_op jit(solution)/shard_map/ppermute | solution.py:770
  141.3 1.8 %collective-permute-done.28.refs_1_ = bf16[920,256]{1,0:T(8,128)(2,1)S(1)} collective-permute-done((bf16[920,256]{1,0:T(8,128)(2,1)S(1)}, bf16[920,256]{1,0:T(8,128)(2,1)S(1)}, u32[]{:S(2)}, u32[]{:S(2)}) %collective-permute-start.28) | collective-permute-done | bytes 471072 | tf_op jit(solution)/shard_map/ppermute | solution.py:762
  143.1 1.9 %final.1 = (f32[96,3072]{1,0:T(8,128)}, f32[96,768]{1,0:T(8,128)}, f32[96,768]{1,0:T(8,128)}, f32[96,128]{1,0:T(8,128)}, f32[8,256]{1,0:T(8,128)S(1)}) custom-call(s32[16]{0:T(128)S(1)} %bitcast.79, bf16[920,256]{1,0:T(8,128)(2,1)S(1)} %get-tuple-element.187.refs_0_, bf16[920,256]{1,0:T(8,128)(2,1)S(1)} %collective-permute-done.28.refs_1_), custom_call_target="tpu_custom_call" | custom-call | flops 1000 | bytes 1000 | tf_op jit(solution)/shard_map/final/pallas_call | solution.py:85
  (118 shorter events, 32.0 us)
Async XLA Ops:
  0.6 4.2 %collective-permute-start.1 = (bf16[256,768]{1,0:T(8,128)(2,1)}, bf16[256,768]{1,0:T(8,128)(2,1)S(1)}, u32[]{:S(2)}, u32[]{:S(2)}) collective-permute-start(bf16[256,768]{1,0:T(8,128)(2,1)} %refs_13_.1), channel_id=1, source_target_pairs={{0,1},{1,0},{2,3},{3,2},{4,5},{5,4},{6,7},{7,6},{8,9},{9,8},{10,11... | collective-permute-start | bytes 1179656 | tf_op jit(solution)/shard_map/ppermute | solution.py:762
  1.2 3.6 %collective-permute-start = (bf16[256,768]{1,0:T(8,128)(2,1)}, bf16[256,768]{1,0:T(8,128)(2,1)S(1)}, u32[]{:S(2)}, u32[]{:S(2)}) collective-permute-start(bf16[256,768]{1,0:T(8,128)(2,1)} %refs_4_.5), channel_id=1, source_target_pairs={{0,1},{1,0},{2,3},{3,2},{4,5},{5,4},{6,7},{7,6},{8,9},{9,8},{10,11... | collective-permute-start | bytes 1179656 | tf_op jit(solution)/shard_map/ppermute | solution.py:762
  10.8 10.8 %collective-permute-start.2 = (bf16[512,128]{1,0:T(8,128)(2,1)}, bf16[512,128]{1,0:T(8,128)(2,1)S(1)}, u32[]{:S(2)}, u32[]{:S(2)}) collective-permute-start(bf16[512,128]{1,0:T(8,128)(2,1)} %get-tuple-element.106), channel_id=1, source_target_pairs={{0,2},{1,3},{2,0},{3,1},{4,6},{5,7},{6,4},{7,5},{8,10},{9,11},{10,... | collective-permute-start | bytes 393224 | tf_op jit(solution)/shard_map/ppermute | solution.py:770
  21.6 23.0 %collective-permute-start.4 = (bf16[2,2,2,384,256]{4,3,2,1,0:T(8,128)(2,1)}, bf16[2,2,2,384,256]{4,3,2,1,0:T(8,128)(2,1)S(1)}, u32[]{:S(2)}, u32[]{:S(2)}) collective-permute-start(bf16[2,2,2,384,256]{4,3,2,1,0:T(8,128)(2,1)} %get-tuple-element.107), channel_id=1, source_target_pairs={{0,8},{1,17},{2,10},{3,19},{4,12},{5,21},{6,14},{7,23},{8,0},{9,25... | collective-permute-start | bytes 4718600 | tf_op jit(solution)/shard_map/ppermute | solution.py:770
  23.2 18.0 %collective-permute-start.3 = (bf16[1024,128]{1,0:T(8,128)(2,1)S(1)}, bf16[1024,128]{1,0:T(8,128)(2,1)S(1)}, u32[]{:S(2)}, u32[]{:S(2)}) collective-permute-start(bf16[1024,128]{1,0:T(8,128)(2,1)S(1)} %constant_dynamic-update-slice_fusion.refs_4_), channel_id=1, source_target_pairs={{0,4},{1,5},{2,6},{3,7},{4,0},{5,1},{6,2},{7,3},{8,12},{9,13},{10,... | collective-permute-start | bytes 786440 | tf_op jit(solution)/shard_map/ppermute | solution.py:770
  41.2 20.2 %collective-permute-start.5 = (bf16[2,768,256]{2,1,0:T(8,128)(2,1)}, bf16[2,768,256]{2,1,0:T(8,128)(2,1)S(1)}, u32[]{:S(2)}, u32[]{:S(2)}) collective-permute-start(bf16[2,768,256]{2,1,0:T(8,128)(2,1)} %get-tuple-element.114), channel_id=1, source_target_pairs={{0,2},{1,3},{2,0},{3,1},{4,6},{5,7},{6,4},{7,5},{8,10},{9,11},{10,... | collective-permute-start | bytes 2359304 | tf_op jit(solution)/shard_map/ppermute | solution.py:770
  44.9 16.6 %collective-permute-start.6 = (bf16[2,2,384,256]{3,2,1,0:T(8,128)(2,1)S(1)}, bf16[2,2,384,256]{3,2,1,0:T(8,128)(2,1)S(1)}, u32[]{:S(2)}, u32[]{:S(2)}) collective-permute-start(bf16[2,2,384,256]{3,2,1,0:T(8,128)(2,1)S(1)} %fusion), channel_id=1, source_target_pairs={{0,16},{1,9},{2,18},{3,11},{4,20},{5,13},{6,22},{7,15},{8,24},{9,1... | collective-permute-start | bytes 2359304 | tf_op jit(solution)/shard_map/ppermute | solution.py:770
  61.7 19.1 %collective-permute-start.7 = (bf16[768,256]{1,0:T(8,128)(2,1)S(1)}, bf16[768,256]{1,0:T(8,128)(2,1)S(1)}, u32[]{:S(2)}, u32[]{:S(2)}) collective-permute-start(bf16[768,256]{1,0:T(8,128)(2,1)S(1)} %fusion.3), channel_id=1, source_target_pairs={{0,4},{1,5},{2,6},{3,7},{4,0},{5,1},{6,2},{7,3},{8,12},{9,13},{10,... | collective-permute-start | bytes 1179656 | tf_op jit(solution)/shard_map/ppermute | solution.py:770
  62.1 18.7 %collective-permute-start.8 = (bf16[2,384,256]{2,1,0:T(8,128)(2,1)S(1)}, bf16[2,384,256]{2,1,0:T(8,128)(2,1)S(1)}, u32[]{:S(2)}, u32[]{:S(2)}) collective-permute-start(bf16[2,384,256]{2,1,0:T(8,128)(2,1)S(1)} %fusion.1), channel_id=1, source_target_pairs={{0,2},{1,3},{2,0},{3,1},{4,6},{5,7},{6,4},{7,5},{8,10},{9,11},{10,... | collective-permute-start | bytes 1179656 | tf_op jit(solution)/shard_map/ppermute | solution.py:770
  85.1 11.0 %collective-permute-start.12 = (bf16[2,2,2,144,256]{4,3,2,1,0:T(8,128)(2,1)S(1)}, bf16[2,2,2,144,256]{4,3,2,1,0:T(8,128)(2,1)S(1)}, u32[]{:S(2)}, u32[]{:S(2)}) collective-permute-start(bf16[2,2,2,144,256]{4,3,2,1,0:T(8,128)(2,1)S(1)} %get-tuple-element.150), channel_id=1, source_target_pairs={{0,8},{1,17},{2,10},{3,19},{4,12},{5,21},{6,14},{7,23},{8,0},{9,25... | collective-permute-start | bytes 1769480 | tf_op jit(solution)/shard_map/ppermute | solution.py:770
  87.0 8.9 %collective-permute-start.15 = (bf16[256,128]{1,0:T(8,128)(2,1)S(1)}, bf16[256,128]{1,0:T(8,128)(2,1)S(1)}, u32[]{:S(2)}, u32[]{:S(2)}) collective-permute-start(bf16[256,128]{1,0:T(8,128)(2,1)S(1)} %get-tuple-element.197), channel_id=1, source_target_pairs={{0,6},{1,7},{2,4},{3,5},{4,2},{5,3},{6,0},{7,1},{8,14},{9,15},{10,... | collective-permute-start | bytes 196616 | tf_op jit(solution)/shard_map/ppermute | solution.py:770
  90.7 5.3 %collective-permute-start.14 = (bf16[256,128]{1,0:T(8,128)(2,1)S(1)}, bf16[256,128]{1,0:T(8,128)(2,1)S(1)}, u32[]{:S(2)}, u32[]{:S(2)}) collective-permute-start(bf16[256,128]{1,0:T(8,128)(2,1)S(1)} %get-tuple-element.199), channel_id=1, source_target_pairs={{0,4},{1,5},{2,6},{3,7},{4,0},{5,1},{6,2},{7,3},{8,12},{9,13},{10,... | collective-permute-start | bytes 196616 | tf_op jit(solution)/shard_map/ppermute | solution.py:770
  90.7 5.3 %collective-permute-start.13 = (bf16[256,128]{1,0:T(8,128)(2,1)S(1)}, bf16[256,128]{1,0:T(8,128)(2,1)S(1)}, u32[]{:S(2)}, u32[]{:S(2)}) collective-permute-start(bf16[256,128]{1,0:T(8,128)(2,1)S(1)} %get-tuple-element.200), channel_id=1, source_target_pairs={{0,2},{1,3},{2,0},{3,1},{4,6},{5,7},{6,4},{7,5},{8,10},{9,11},{10,... | collective-permute-start | bytes 196616 | tf_op jit(solution)/shard_map/ppermute | solution.py:770
  96.1 6.8 %collective-permute-start.17 = (bf16[2,2,144,256]{3,2,1,0:T(8,128)(2,1)S(1)}, bf16[2,2,144,256]{3,2,1,0:T(8,128)(2,1)S(1)}, u32[]{:S(2)}, u32[]{:S(2)}) collective-permute-start(bf16[2,2,144,256]{3,2,1,0:T(8,128)(2,1)S(1)} %fusion.7), channel_id=1, source_target_pairs={{0,16},{1,9},{2,18},{3,11},{4,20},{5,13},{6,22},{7,15},{8,24},{9,1... | collective-permute-start | bytes 884744 | tf_op jit(solution)/shard_map/ppermute | solution.py:770
  96.5 15.1 %collective-permute-start.19 = (bf16[768,256]{1,0:T(8,128)(2,1)S(1)}, bf16[768,256]{1,0:T(8,128)(2,1)S(1)}, u32[]{:S(2)}, u32[]{:S(2)}) collective-permute-start(bf16[768,256]{1,0:T(8,128)(2,1)S(1)} %fusion.2), channel_id=1, source_target_pairs={{0,16},{1,9},{2,18},{3,11},{4,20},{5,13},{6,22},{7,15},{8,24},{9,1... | collective-permute-start | bytes 1179656 | tf_op jit(solution)/shard_map/ppermute | solution.py:770
  103.1 10.3 %collective-permute-start.18 = (bf16[2,256,256]{2,1,0:T(8,128)(2,1)S(1)}, bf16[2,256,256]{2,1,0:T(8,128)(2,1)S(1)}, u32[]{:S(2)}, u32[]{:S(2)}) collective-permute-start(bf16[2,256,256]{2,1,0:T(8,128)(2,1)S(1)} %pad_maximum_fusion.1), channel_id=1, source_target_pairs={{0,2},{1,3},{2,0},{3,1},{4,6},{5,7},{6,4},{7,5},{8,10},{9,11},{10,... | collective-permute-start | bytes 786440 | tf_op jit(solution)/shard_map/ppermute | solution.py:770
  104.5 12.5 %collective-permute-start.21 = (bf16[384,256]{1,0:T(8,128)(2,1)S(1)}, bf16[384,256]{1,0:T(8,128)(2,1)S(1)}, u32[]{:S(2)}, u32[]{:S(2)}) collective-permute-start(bf16[384,256]{1,0:T(8,128)(2,1)S(1)} %fusion.4), channel_id=1, source_target_pairs={{0,4},{1,5},{2,6},{3,7},{4,0},{5,1},{6,2},{7,3},{8,12},{9,13},{10,... | collective-permute-start | bytes 589832 | tf_op jit(solution)/shard_map/ppermute | solution.py:770
  113.3 3.6 %collective-permute-start.20 = (bf16[256,768]{1,0:T(8,128)(2,1)S(1)}, bf16[256,768]{1,0:T(8,128)(2,1)S(1)}, u32[]{:S(2)}, u32[]{:S(2)}) collective-permute-start(bf16[256,768]{1,0:T(8,128)(2,1)S(1)} %get-tuple-element.171), channel_id=1, source_target_pairs={{0,1},{1,0},{2,3},{3,2},{4,5},{5,4},{6,7},{7,6},{8,9},{9,8},{10,11... | collective-permute-start | bytes 1179656 | tf_op jit(solution)/shard_map/ppermute | solution.py:762
  113.4 13.6 %collective-permute-start.24 = (bf16[256,256]{1,0:T(8,128)(2,1)S(1)}, bf16[256,256]{1,0:T(8,128)(2,1)S(1)}, u32[]{:S(2)}, u32[]{:S(2)}) collective-permute-start(bf16[256,256]{1,0:T(8,128)(2,1)S(1)} %fusion.11), channel_id=1, source_target_pairs={{0,4},{1,5},{2,6},{3,7},{4,0},{5,1},{6,2},{7,3},{8,12},{9,13},{10,... | collective-permute-start | bytes 393224 | tf_op jit(solution)/shard_map/ppermute | solution.py:770
  115.4 9.9 %collective-permute-start.23 = (bf16[768,256]{1,0:T(8,128)(2,1)S(1)}, bf16[768,256]{1,0:T(8,128)(2,1)S(1)}, u32[]{:S(2)}, u32[]{:S(2)}) collective-permute-start(bf16[768,256]{1,0:T(8,128)(2,1)S(1)} %add_convert_fusion.2.refs_0_), channel_id=1, source_target_pairs={{0,8},{1,17},{2,10},{3,19},{4,12},{5,21},{6,14},{7,23},{8,0},{9,25... | collective-permute-start | bytes 1179656 | tf_op jit(solution)/shard_map/ppermute | solution.py:770
  117.1 8.2 %collective-permute-start.22 = (bf16[384,256]{1,0:T(8,128)(2,1)S(1)}, bf16[384,256]{1,0:T(8,128)(2,1)S(1)}, u32[]{:S(2)}, u32[]{:S(2)}) collective-permute-start(bf16[384,256]{1,0:T(8,128)(2,1)S(1)} %fusion.6), channel_id=1, source_target_pairs={{0,16},{1,9},{2,18},{3,11},{4,20},{5,13},{6,22},{7,15},{8,24},{9,1... | collective-permute-start | bytes 589832 | tf_op jit(solution)/shard_map/ppermute | solution.py:770
  125.3 9.2 %collective-permute-start.26 = (bf16[768,256]{1,0:T(8,128)(2,1)S(1)}, bf16[768,256]{1,0:T(8,128)(2,1)S(1)}, u32[]{:S(2)}, u32[]{:S(2)}) collective-permute-start(bf16[768,256]{1,0:T(8,128)(2,1)S(1)} %pad_maximum_fusion.refs_2_), channel_id=1, source_target_pairs={{0,8},{1,17},{2,10},{3,19},{4,12},{5,21},{6,14},{7,23},{8,0},{9,25... | collective-permute-start | bytes 1179656 | tf_op jit(solution)/shard_map/ppermute | solution.py:770
  127.0 6.2 %collective-permute-start.25 = (bf16[256,256]{1,0:T(8,128)(2,1)S(1)}, bf16[256,256]{1,0:T(8,128)(2,1)S(1)}, u32[]{:S(2)}, u32[]{:S(2)}) collective-permute-start(bf16[256,256]{1,0:T(8,128)(2,1)S(1)} %fusion.10), channel_id=1, source_target_pairs={{0,16},{1,9},{2,18},{3,11},{4,20},{5,13},{6,22},{7,15},{8,24},{9,1... | collective-permute-start | bytes 393224 | tf_op jit(solution)/shard_map/ppermute | solution.py:770
  134.6 5.8 %collective-permute-start.27 = (bf16[400,256]{1,0:T(8,128)(2,1)S(1)}, bf16[400,256]{1,0:T(8,128)(2,1)S(1)}, u32[]{:S(2)}, u32[]{:S(2)}) collective-permute-start(bf16[400,256]{1,0:T(8,128)(2,1)S(1)} %pad_maximum_fusion.2.refs_4_), channel_id=1, source_target_pairs={{0,8},{1,17},{2,10},{3,19},{4,12},{5,21},{6,14},{7,23},{8,0},{9,25... | collective-permute-start | bytes 614408 | tf_op jit(solution)/shard_map/ppermute | solution.py:770
  (26 other events, 154.1 us)

commit v7 on v6

--- a/solution.py
+++ b/solution.py
@@ -346,34 +346,33 @@
 
 
 def prologue_kernel(
-    sc, x_hbm, xt_hbm, g_hbm, gt_hbm, gains, w_hbm, cos_ref, sin_ref, h1_ref, h2_ref, gg_ref, kv_ref, xo, xt, w_kv, sem
+    sc, x_hbm, xt, g_hbm, gt, gains, w_hbm, cos_ref, sin_ref, h1_ref, h2_ref, gg_ref, kv_ref, xo, w_kv, sem
 ):
     rows = xt.shape[0]
     copies = [
         pltpu.make_async_copy(x_hbm, xo, sem.at[0]),
-        pltpu.make_async_copy(xt_hbm, xt, sem.at[1]),
-        pltpu.make_async_copy(w_hbm, w_kv, sem.at[2]),
-        pltpu.make_async_copy(g_hbm, gg_ref.at[0:rows, :], sem.at[3]),
-        pltpu.make_async_copy(gt_hbm, gg_ref.at[rows : 2 * rows, :], sem.at[4]),
+        pltpu.make_async_copy(w_hbm, w_kv, sem.at[1]),
+        pltpu.make_async_copy(g_hbm, gg_ref.at[0:rows, :], sem.at[2]),
     ]
     for copy in copies:
         copy.start()
+    gg_ref[rows : 2 * rows, :] = gt[...]
     gain_one, bias_one = gains[0:1, :].astype(F32), gains[1:2, :].astype(F32)
     gain_two, bias_two = gains[2:3, :].astype(F32), gains[3:4, :].astype(F32)
-    for n, x in enumerate((xo, xt)):
-        copies[n].wait()
+    for n, x in ((1, xt), (0, xo)):
+        if n == 0:
+            copies[0].wait()
         for t in range(rows // 128):
             here = slice(n * rows + t * 128, n * rows + (t + 1) * 128)
             hat, unused = normed(x[t * 128 : (t + 1) * 128, :].astype(F32))
             h1_ref[here, :] = (hat * gain_one + bias_one).astype(BF)
             h2_ref[here, :] = (hat * gain_two + bias_two).astype(BF)
-    copies[2].wait()
+    copies[1].wait()
     raw = dot(h1_ref[...], w_kv[...])
     kv = turn(raw.T, cos_ref[...], sin_ref[...]).T.astype(BF)
     kv_ref[pl.ds(pl.multiple_of(sc[0] * rows, rows), rows), :] = kv[:rows]
     kv_ref[pl.ds(pl.multiple_of((1 - sc[0]) * rows, rows), rows), :] = kv[rows:]
-    copies[3].wait()
-    copies[4].wait()
+    copies[2].wait()
 
 
 def half_copies(sc, w_query, w_out, query_s, out_s, sem):
@@ -489,7 +488,7 @@
             pltpu.VMEM((width, width), BF),
             pltpu.SemaphoreType.DMA((2,)),
         ],
-        56,
+        24,
     )(table, h_two, g_two, w_up, w_down)
 
 
@@ -829,15 +828,14 @@
         prologue_kernel,
         "prologue",
         [shape((2 * rows, width), BF)] * 3 + [shape((2 * rows, lanes), BF)],
-        [HBM] * 4 + [VM, HBM, VM, VM],
+        [HBM, VM, HBM, VM, VM, HBM, VM, VM],
         [VM] * 4,
         [
             pltpu.VMEM((rows, width), BF),
-            pltpu.VMEM((rows, width), BF),
             pltpu.VMEM((width, lanes), BF),
-            pltpu.SemaphoreType.DMA((5,)),
+            pltpu.SemaphoreType.DMA((3,)),
         ],
-        56,
+        16,
     )(table, layer_input, x_other, cotangent, g_other, gains, w_keyval, cosine, sine)
 
     kv_got = links.flip(kv_low, 1)
@@ -892,10 +890,14 @@
     dkv_got, mix_0_got, mix_1_got = meet(dkv_got, mix_0_got, mix_1_got)
     dkv_sends = [add(dkv_keep[at], dkv_got[at]) for at in ((1, 0), (0, 1), (1, 1))]
     dkv_gots = [links.flip(value, n + 1) for n, value in enumerate(dkv_sends)]
+    a_sum = add(a_keep[0], a_got[0], tie(a_got_2, *dkv_sends))
+    a_got = links.cross(a_sum, 1)
     late_send, late_keep, mix_own, dq_own = late_gradients(
-        table, tie(h_one, *dkv_sends), (dq_0, dq_1), (mix_0, mix_1), (mix_0_got, mix_1_got), g_two, n_pair
+        table, tie(h_one, a_sum, *dkv_sends), (dq_0, dq_1), (mix_0, mix_1), (mix_0_got, mix_1_got), g_two, n_pair
     )
     late_got = links.cross(late_send, 0)
+    b_send = add(b_keep[0, 0, 1], b_got[0, 0, 1], b_got_2[0, 1], tie(b_got_3, late_send)[1])
+    b_got_4 = links.flip(b_send, 2)
 
     w_specs = [HBM] * 2
     hat_own, hat_send, sums = call(
@@ -911,17 +913,17 @@
         ],
         24,
     )(
-        table, dup_0, dup_1, tie(dup_2, late_send), dq_own, layer_input, x_other, gains,
+        table, dup_0, dup_1, tie(dup_2, b_send), dq_own, layer_input, x_other, gains,
         w_up, w_query,
     )
-    hat_send, late_got, *dkv_gots = meet(hat_send, late_got, *dkv_gots)
+    hat_send, late_got, a_got, *dkv_gots = meet(hat_send, late_got, a_got, *dkv_gots)
     hat_got = links.swap(hat_send)
     late_send = add(late_keep[1], late_got[1])
     late_got_2 = links.cross(late_send, 1)
-    b_send = add(b_keep[0, 0, 1], b_got[0, 0, 1], b_got_2[0, 1], tie(b_got_3, late_send)[1])
-    b_got_4 = links.flip(b_send, 2)
+    a_sum = add(a_sum, tie(a_got, late_send))
+    a_got = links.cross(a_sum, 0)
     dkv_own = add(dkv_keep[0, 0], dkv_got[0, 0])
-    late_send, hat_got = meet(late_send, hat_got)
+    a_sum, hat_got = meet(a_sum, hat_got)
 
     few = part // 2 + 8
     in_grad, few_send, few_keep = call(
@@ -933,17 +935,19 @@
         [],
         16,
     )(
-        table, dkv_own, *dkv_gots, tie(cosine, late_send, b_send), sine, w_keyval, h_one,
+        table, dkv_own, *dkv_gots, tie(cosine, a_sum), sine, w_keyval, h_one,
         layer_input, gains, hat_own, hat_got, sums, cotangent,
     )
-    few_send, late_got_2 = meet(few_send, late_got_2)
+    few_send, late_got_2, b_got_4 = meet(few_send, late_got_2, b_got_4)
     quarter = late_keep.shape[3]
     last_send = jnp.concatenate(
         [add(late_keep[0, 1], late_got[0, 1], late_got_2[1]), few_send], 1
     )
     last_got = links.flip(last_send, 1)
-    a_sum = add(a_keep[0], a_got[0], a_got_2)
-    a_got = links.cross(a_sum, 1)
+    b_sum = add(
+        b_keep[0, 0, 0], b_got[0, 0, 0], b_got_2[0, 0], b_got_3[0], tie(b_got_4, last_send)
+    )
+    b_got = links.cross(b_sum, 1)
 
     out_own, out_send = call(
         functools.partial(out_kernel, part=part_hidden, n_pair=n_pair),
@@ -958,38 +962,31 @@
         ],
         24,
     )(
-        table, act_0, act_1, tie(act_2, last_send, a_sum), mix_own, layer_input, w_down, w_out,
-    )
-    out_send, last_got, a_got = meet(out_send, last_got, a_got)
+        table, act_0, act_1, tie(act_2, b_sum), mix_own, layer_input, w_down, w_out,
+    )
+    out_send, last_got, a_got, b_got = meet(out_send, last_got, a_got, b_got)
     out_got = links.swap(out_send)
     last_keep = jnp.concatenate(
         [add(late_keep[0, 0], late_got[0, 0], late_got_2[0]), few_keep], 1
     )
     last_send = add(last_keep[1], last_got[1])
     last_got_2 = links.flip(last_send, 2)
-    a_sum = add(a_sum, a_got)
-    a_got = links.cross(a_sum, 0)
-    out_got, b_got_4 = meet(out_got, b_got_4, a_sum, last_send)[:2]
+    b_sum = jnp.concatenate([b_sum, b_got], 0)
+    b_got = links.cross(tie(b_sum, last_send), 0)
+    out_got = tie(out_got, b_sum, last_send)
     layer_output = low(out_own + out_got.astype(F32))
-    b_sum = add(b_keep[0, 0, 0], b_got[0, 0, 0], b_got_2[0, 0], b_got_3[0], b_got_4)
-    b_got = links.cross(b_sum, 1)
-    last_keep = add(last_keep[0], last_got[0])
-    b_got, layer_output, a_got = meet(b_got, layer_output, a_got)
-    b_sum = jnp.concatenate([b_sum, b_got], 0)
-    b_got = links.cross(b_sum, 0)
-    last_got_2 = meet(last_got_2, b_sum)[0]
-    last = add(last_keep, last_got_2)
+    last_got_2, b_got, layer_output = meet(last_got_2, b_got, layer_output)
+    last = add(last_keep[0], last_got[0], last_got_2)
     last_got = links.cross(last, 1)
-    last_got, b_got = meet(last_got, b_got)
-    last = jnp.concatenate(
-        [last[:quarter], last_got[:quarter], add(last[quarter:], last_got[quarter:])], 0
-    )
-    last_got = links.cross(last, 0)
     total_down = call(
         functools.partial(down_kernel, width=width),
         "down", shape((part_hidden, width), F32), [VM] * 4, VM, [], 8,
     )(table, tie(a_sum, last), a_got, b_sum, b_got)
     total_down, last_got = meet(total_down, last_got)
+    last = jnp.concatenate(
+        [last[:quarter], last_got[:quarter], add(last[quarter:], last_got[quarter:])], 0
+    )
+    last_got = links.cross(last, 0)
     size_out = 9 * part + few
     other, own = call(
         functools.partial(pack_kernel, width=width, part=part, quarter=quarter),

time: 145 us -> 139 us (0.959); the launches traced: 146 us -> 138 us
  Pallas kernels: 78.6 us -> 57.9 us
  waiting for transfers between devices: 24.6 us -> 44.8 us
  starting transfers between devices: 34 us -> 28.1 us
    ppermute x21, waiting for transfers between devices: 21.2 us -> 41.4 us  [permute(): return lax.ppermute(value, ('grp', 'ctx'), pairs)]
    pallas_call x12, Pallas kernels: 48.5 us -> 37.9 us  [placed(): made(table, *(pltpu.with_memory_space_constraint(v, pltpu.HBM) if spec is...]
    pallas_call x2, Pallas kernels: 30.1 us -> 20 us  [attention(): pl.pallas_call(functools.partial(attn_kernel, blocks=blocks, heads=heads,...]
    ppermute x21, starting transfers between devices: 32.7 us -> 26.8 us  [permute(): return lax.ppermute(value, ('grp', 'ctx'), pairs)]
  transfers between devices with their start and end apart: 29 -> 29, of which waited for: 10 -> 16; matrix products, arithmetic and copies ran while one was open for 4% -> 3% of each run, Pallas kernels for 47% -> 37%
where the time goes in v7:
time: 139 us; the launch traced here: 138 us
  Pallas kernels  57.9 us (42%)
  waiting for transfers between devices  44.8 us (32%)
  starting transfers between devices  28.1 us (20%)
  other arithmetic  4.59 us (3%)
    ppermute x21, waiting for transfers between devices, permute(): return lax.ppermute(value, ('grp', 'ctx'), pairs)  41.4 us
    pallas_call x12, Pallas kernels, placed(): made(table, *(pltpu.with_memory_space_constraint(v, pltpu.HBM) if spec is...  37.9 us
    ppermute x21, starting transfers between devices, permute(): return lax.ppermute(value, ('grp', 'ctx'), pairs)  26.8 us
    pallas_call x2, Pallas kernels, attention(): pl.pallas_call(functools.partial(attn_kernel, blocks=blocks, heads=heads,...  20 us
    ppermute x8, waiting for transfers between devices, swap(): return lax.ppermute(value, 'ctx', [(i, i ^ 1) for i in range(self.n_ctx)])  3.42 us
  transfers between devices with their start and end apart: 29, of which 16 were waited for; matrix products, arithmetic and copies ran while one was open for 3% of the time, Pallas kernels for 37%

profile of v7, /device:TPU:0, one launch (start us, length us, event | category | flops | bytes accessed | tf_op | source)
XLA Modules:
  0.0 137.6 jit_solution(9320903589196697940)
XLA Ops:
  4.3 2.6 %prologue.1 = (bf16[512,768]{1,0:T(8,128)(2,1)S(1)}, bf16[512,768]{1,0:T(8,128)(2,1)S(1)}, bf16[512,768]{1,0:T(8,128)(2,1)S(1)}, bf16[512,128]{1,0:T(8,128)(2,1)S(1)}) custom-call(s32[16]{0:T(128)S(1)} %bitcast.65, bf16[256,768]{1,0:T(8,128)(2,1)} %refs_4_.5, bf16[256,768]{1,0:T(8,128)(2,1)S(1)} %collective-permute-done.refs_1_.refs_5_, ...), custom_call_target="tpu_custom_call" | custom-call | flops 1000 | bytes 1000 | tf_op jit(solution)/shard_map/prologue/pallas_call | solution.py:85
  7.0 3.1 %collective-permute-start.2 = (bf16[512,128]{1,0:T(8,128)(2,1)S(1)}, bf16[512,128]{1,0:T(8,128)(2,1)S(1)}, u32[]{:S(2)}, u32[]{:S(2)}) collective-permute-start(bf16[512,128]{1,0:T(8,128)(2,1)S(1)} %get-tuple-element.111), channel_id=1, source_target_pairs={{0,2},{1,3},{2,0},{3,1},{4,6},{5,7},{6,4},{7,5},{8,10},{9,11},{10,... | collective-permute-start | bytes 393224 | tf_op jit(solution)/shard_map/ppermute | solution.py:769
  10.0 5.0 %ffn_gradients.3 = (bf16[512,512]{1,0:T(8,128)(2,1)S(1)}, bf16[512,512]{1,0:T(8,128)(2,1)S(1)}, bf16[2,2,2,384,256]{4,3,2,1,0:T(8,128)(2,1)S(1)}) custom-call(s32[16]{0:T(128)S(1)} %bitcast.66, bf16[512,768]{1,0:T(8,128)(2,1)S(1)} %get-tuple-element.116.refs_0_, bf16[512,768]{1,0:T(8,128)(2,1)S(1)} %get-tuple-element.109.refs_1_.refs_7_, ...), custom_call_target="tpu_custom_call" | custom-call | flops 1000 | bytes 1000 | tf_op jit(solution)/shard_map/ffn_gradients/pallas_call | solution.py:85
  16.6 2.6 %collective-permute-start.3 = (bf16[1024,128]{1,0:T(8,128)(2,1)S(1)}, bf16[1024,128]{1,0:T(8,128)(2,1)S(1)}, u32[]{:S(2)}, u32[]{:S(2)}) collective-permute-start(bf16[1024,128]{1,0:T(8,128)(2,1)S(1)} %constant_dynamic-update-slice_fusion.refs_4_), channel_id=1, source_target_pairs={{0,4},{1,5},{2,6},{3,7},{4,0},{5,1},{6,2},{7,3},{8,12},{9,13},{10,... | collective-permute-start | bytes 786440 | tf_op jit(solution)/shard_map/ppermute | solution.py:769
  19.2 5.0 %ffn_gradients.4 = (bf16[512,512]{1,0:T(8,128)(2,1)S(1)}, bf16[512,512]{1,0:T(8,128)(2,1)S(1)}, bf16[2,2,2,384,256]{4,3,2,1,0:T(8,128)(2,1)S(1)}) custom-call(s32[16]{0:T(128)S(1)} %bitcast.67, bf16[512,768]{1,0:T(8,128)(2,1)S(1)} %get-tuple-element.116.refs_0_, bf16[512,768]{1,0:T(8,128)(2,1)S(1)} %get-tuple-element.109.refs_1_.refs_7_, ...), custom_call_target="tpu_custom_call" | custom-call | flops 1000 | bytes 1000 | tf_op jit(solution)/shard_map/ffn_gradients/pallas_call | solution.py:85
  24.2 5.0 %ffn_gradients.5 = (bf16[512,512]{1,0:T(8,128)(2,1)S(1)}, bf16[512,512]{1,0:T(8,128)(2,1)S(1)}, bf16[2,768,256]{2,1,0:T(8,128)(2,1)S(1)}, bf16[2,768,256]{2,1,0:T(8,128)(2,1)S(1)}) custom-call(s32[16]{0:T(128)S(1)} %bitcast.68, bf16[512,768]{1,0:T(8,128)(2,1)S(1)} %get-tuple-element.116.refs_0_, bf16[512,768]{1,0:T(8,128)(2,1)S(1)} %get-tuple-element.109.refs_1_.refs_7_, ...), custom_call_target="tpu_custom_call" | custom-call | flops 1000 | bytes 1000 | tf_op jit(solution)/shard_map/ffn_gradients/pallas_call | solution.py:85
  30.8 2.9 %project.1 = (bf16[384,512]{1,0:T(8,128)(2,1)S(1)}, f32[384,512]{1,0:T(8,128)S(1)}) custom-call(s32[16]{0:T(128)S(1)} %bitcast.69, bf16[512,768]{1,0:T(8,128)(2,1)S(1)} %get-tuple-element.143.refs_0_.refs_7_, bf16[512,768]{1,0:T(8,128)(2,1)S(1)} %get-tuple-element.109.refs_1_.refs_7_, f32[8,512]{1,0:T(8,128)S(1)} %get-tuple-element.166.refs_6_.refs_2_.refs_4_, ...), custom_call_target="tpu_custom_call" | custom-call | flops 1000 | bytes 1000 | tf_op jit(solution)/shard_map/project/pallas_call | solution.py:85
  37.3 11.6 %attention.2 = (bf16[384,256]{1,0:T(8,128)(2,1)S(1)}, bf16[384,256]{1,0:T(8,128)(2,1)S(1)}, f32[2048,128]{1,0:T(8,128)S(1)}) custom-call(s32[16]{0:T(128)S(1)} %bitcast.70, bf16[384,512]{1,0:T(8,128)(2,1)S(1)} %get-tuple-element.133.refs_0_, f32[384,512]{1,0:T(8,128)S(1)} %get-tuple-element.125.refs_1_, ...), custom_call_target="tpu_custom_call" | custom-call | flops 1000 | bytes 1000 | tf_op jit(solution)/shard_map/attention/pallas_call | solution.py:303
  50.6 3.6 %collective-permute-start.7 = (bf16[768,256]{1,0:T(8,128)(2,1)S(1)}, bf16[768,256]{1,0:T(8,128)(2,1)S(1)}, u32[]{:S(2)}, u32[]{:S(2)}) collective-permute-start(bf16[768,256]{1,0:T(8,128)(2,1)S(1)} %fusion.3), channel_id=1, source_target_pairs={{0,4},{1,5},{2,6},{3,7},{4,0},{5,1},{6,2},{7,3},{8,12},{9,13},{10,... | collective-permute-start | bytes 1179656 | tf_op jit(solution)/shard_map/ppermute | solution.py:769
  54.1 8.4 %attention.3 = (bf16[384,256]{1,0:T(8,128)(2,1)S(1)}, bf16[384,256]{1,0:T(8,128)(2,1)S(1)}, bf16[2,2,256,128]{3,2,1,0:T(8,128)(2,1)S(1)}, bf16[2,2,256,128]{3,2,1,0:T(8,128)(2,1)S(1)}) custom-call(s32[16]{0:T(128)S(1)} %bitcast.71, bf16[384,512]{1,0:T(8,128)(2,1)S(1)} %get-tuple-element.133.refs_0_, f32[384,512]{1,0:T(8,128)S(1)} %get-tuple-element.125.refs_1_, ...), custom_call_target="tpu_custom_call" | custom-call | flops 1000 | bytes 1000 | tf_op jit(solution)/shard_map/attention/pallas_call | solution.py:303
  62.6 7.7 %collective-permute-done.7 = bf16[768,256]{1,0:T(8,128)(2,1)S(1)} collective-permute-done((bf16[768,256]{1,0:T(8,128)(2,1)S(1)}, bf16[768,256]{1,0:T(8,128)(2,1)S(1)}, u32[]{:S(2)}, u32[]{:S(2)}) %collective-permute-start.7) | collective-permute-done | bytes 393248 | tf_op jit(solution)/shard_map/ppermute | solution.py:769
  74.2 1.9 %late_gradients.1 = (bf16[2,2,2,144,256]{4,3,2,1,0:T(8,128)(2,1)S(1)}, bf16[2,2,2,144,256]{4,3,2,1,0:T(8,128)(2,1)S(1)}, bf16[384,512]{1,0:T(8,128)(2,1)S(1)}, bf16[384,512]{1,0:T(8,128)(2,1)S(1)}) custom-call(s32[16]{0:T(128)S(1)} %bitcast.72, bf16[512,768]{1,0:T(8,128)(2,1)S(1)} %get-tuple-element.143.refs_0_.refs_7_, ...), custom_call_target="tpu_custom_call" | custom-call | flops 1000 | bytes 1000 | tf_op jit(solution)/shard_map/late_gradients/pallas_call | solution.py:85
  77.8 3.0 %collective-permute-start.16 = (bf16[256,128]{1,0:T(8,128)(2,1)S(1)}, bf16[256,128]{1,0:T(8,128)(2,1)S(1)}, u32[]{:S(2)}, u32[]{:S(2)}) collective-permute-start(bf16[256,128]{1,0:T(8,128)(2,1)S(1)} %get-tuple-element.205), channel_id=1, source_target_pairs={{0,6},{1,7},{2,4},{3,5},{4,2},{5,3},{6,0},{7,1},{8,14},{9,15},{10,... | collective-permute-start | bytes 196616 | tf_op jit(solution)/shard_map/ppermute | solution.py:769
  82.3 4.5 %norms.1 = (f32[256,768]{1,0:T(8,128)S(1)}, bf16[256,768]{1,0:T(8,128)(2,1)S(1)}, f32[8,768]{1,0:T(8,128)S(1)}) custom-call(s32[16]{0:T(128)S(1)} %bitcast.73, bf16[512,512]{1,0:T(8,128)(2,1)S(1)} %get-tuple-element.149.refs_0_, bf16[512,512]{1,0:T(8,128)(2,1)S(1)} %get-tuple-element.150.refs_1_, bf16[512,512]{1,0:T(8,128)(2,1)S(1)} %get-tuple-element.155.refs_2_, ...), custom_call_target="tpu_custom_call" | custom-call | flops 1000 | bytes 1000 | tf_op jit(solution)/shard_map/norms/pallas_call | solution.py:85
  88.3 2.0 %collective-permute-done.12 = bf16[2,2,2,144,256]{4,3,2,1,0:T(8,128)(2,1)S(1)} collective-permute-done((bf16[2,2,2,144,256]{4,3,2,1,0:T(8,128)(2,1)S(1)}, bf16[2,2,2,144,256]{4,3,2,1,0:T(8,128)(2,1)S(1)}, u32[]{:S(2)}, u32[]{:S(2)}) %collective-permute-start.12) | collective-permute-done | bytes 589856 | tf_op jit(solution)/shard_map/ppermute | solution.py:769
  91.5 1.8 %collective-permute-start.21 = (bf16[768,256]{1,0:T(8,128)(2,1)S(1)}, bf16[768,256]{1,0:T(8,128)(2,1)S(1)}, u32[]{:S(2)}, u32[]{:S(2)}) collective-permute-start(bf16[768,256]{1,0:T(8,128)(2,1)S(1)} %add_convert_fusion.2.refs_0_), channel_id=1, source_target_pairs={{0,8},{1,17},{2,10},{3,19},{4,12},{5,21},{6,14},{7,23},{8,0},{9,25... | collective-permute-start | bytes 1179656 | tf_op jit(solution)/shard_map/ppermute | solution.py:769
  93.4 2.5 %last.1 = (f32[256,768]{1,0:T(8,128)}, bf16[2,112,256]{2,1,0:T(8,128)(2,1)S(1)}, bf16[2,112,256]{2,1,0:T(8,128)(2,1)S(1)}) custom-call(s32[16]{0:T(128)S(1)} %bitcast.74, bf16[256,128]{1,0:T(8,128)(2,1)S(1)} %get-tuple-element.206.refs_0_, bf16[256,128]{1,0:T(8,128)(2,1)S(1)} %collective-permute-done.14.refs_1_, ...), custom_call_target="tpu_custom_call" | custom-call | flops 1000 | bytes 1000 | tf_op jit(solution)/shard_map/last/pallas_call | solution.py:85
  95.9 6.9 %collective-permute-done.19 = bf16[384,256]{1,0:T(8,128)(2,1)S(1)} collective-permute-done((bf16[384,256]{1,0:T(8,128)(2,1)S(1)}, bf16[384,256]{1,0:T(8,128)(2,1)S(1)}, u32[]{:S(2)}, u32[]{:S(2)}) %collective-permute-start.19) | collective-permute-done | bytes 196640 | tf_op jit(solution)/shard_map/ppermute | solution.py:769
  104.3 4.1 %outputs.1 = (f32[256,768]{1,0:T(8,128)S(1)}, bf16[256,768]{1,0:T(8,128)(2,1)S(1)}) custom-call(s32[16]{0:T(128)S(1)} %bitcast.75, bf16[512,512]{1,0:T(8,128)(2,1)S(1)} %get-tuple-element.173.refs_0_, bf16[512,512]{1,0:T(8,128)(2,1)S(1)} %get-tuple-element.174.refs_1_, bf16[512,512]{1,0:T(8,128)(2,1)S(1)} %get-tuple-element.179.refs_2_, ...), custom_call_target="tpu_custom_call" | custom-call | flops 1000 | bytes 1000 | tf_op jit(solution)/shard_map/outputs/pallas_call | solution.py:85
  108.9 2.3 %collective-permute-done.20 = bf16[2,256,256]{2,1,0:T(8,128)(2,1)S(1)} collective-permute-done((bf16[2,256,256]{2,1,0:T(8,128)(2,1)S(1)}, bf16[2,256,256]{2,1,0:T(8,128)(2,1)S(1)}, u32[]{:S(2)}, u32[]{:S(2)}) %collective-permute-start.20) | collective-permute-done | bytes 262176 | tf_op jit(solution)/shard_map/ppermute | solution.py:769
  113.9 7.6 %collective-permute-done.23 = bf16[256,256]{1,0:T(8,128)(2,1)S(1)} collective-permute-done((bf16[256,256]{1,0:T(8,128)(2,1)S(1)}, bf16[256,256]{1,0:T(8,128)(2,1)S(1)}, u32[]{:S(2)}, u32[]{:S(2)}) %collective-permute-start.23) | collective-permute-done | bytes 131104 | tf_op jit(solution)/shard_map/ppermute | solution.py:769
  124.3 2.3 %collective-permute-done.26 = bf16[256,256]{1,0:T(8,128)(2,1)S(1)} collective-permute-done((bf16[256,256]{1,0:T(8,128)(2,1)S(1)}, bf16[256,256]{1,0:T(8,128)(2,1)S(1)}, u32[]{:S(2)}, u32[]{:S(2)}) %collective-permute-start.26) | collective-permute-done | bytes 131104 | tf_op jit(solution)/shard_map/ppermute | solution.py:769
  128.2 4.3 %collective-permute-done.27.refs_5_ = bf16[400,256]{1,0:T(8,128)(2,1)S(1)} collective-permute-done((bf16[400,256]{1,0:T(8,128)(2,1)S(1)}, bf16[400,256]{1,0:T(8,128)(2,1)S(1)}, u32[]{:S(2)}, u32[]{:S(2)}) %collective-permute-start.27) | collective-permute-done | bytes 204832 | tf_op jit(solution)/shard_map/ppermute | solution.py:769
  135.1 1.9 %final.1 = (f32[96,3072]{1,0:T(8,128)}, f32[96,768]{1,0:T(8,128)}, f32[96,768]{1,0:T(8,128)}, f32[96,128]{1,0:T(8,128)}, f32[8,256]{1,0:T(8,128)S(1)}) custom-call(s32[16]{0:T(128)S(1)} %bitcast.78, bf16[920,256]{1,0:T(8,128)(2,1)S(1)} %get-tuple-element.195.refs_0_, bf16[920,256]{1,0:T(8,128)(2,1)S(1)} %collective-permute-done.28.refs_1_), custom_call_target="tpu_custom_call" | custom-call | flops 1000 | bytes 1000 | tf_op jit(solution)/shard_map/final/pallas_call | solution.py:85
  (86 shorter events, 33.9 us)
Async XLA Ops:
  0.6 3.0 %collective-permute-start.1 = (bf16[256,768]{1,0:T(8,128)(2,1)}, bf16[256,768]{1,0:T(8,128)(2,1)S(1)}, u32[]{:S(2)}, u32[]{:S(2)}) collective-permute-start(bf16[256,768]{1,0:T(8,128)(2,1)} %refs_13_.1), channel_id=1, source_target_pairs={{0,1},{1,0},{2,3},{3,2},{4,5},{5,4},{6,7},{7,6},{8,9},{9,8},{10,11... | collective-permute-start | bytes 1179656 | tf_op jit(solution)/shard_map/ppermute | solution.py:761
  1.2 2.4 %collective-permute-start = (bf16[256,768]{1,0:T(8,128)(2,1)}, bf16[256,768]{1,0:T(8,128)(2,1)S(1)}, u32[]{:S(2)}, u32[]{:S(2)}) collective-permute-start(bf16[256,768]{1,0:T(8,128)(2,1)} %refs_4_.5), channel_id=1, source_target_pairs={{0,1},{1,0},{2,3},{3,2},{4,5},{5,4},{6,7},{7,6},{8,9},{9,8},{10,11... | collective-permute-start | bytes 1179656 | tf_op jit(solution)/shard_map/ppermute | solution.py:761
  7.0 8.0 %collective-permute-start.2 = (bf16[512,128]{1,0:T(8,128)(2,1)S(1)}, bf16[512,128]{1,0:T(8,128)(2,1)S(1)}, u32[]{:S(2)}, u32[]{:S(2)}) collective-permute-start(bf16[512,128]{1,0:T(8,128)(2,1)S(1)} %get-tuple-element.111), channel_id=1, source_target_pairs={{0,2},{1,3},{2,0},{3,1},{4,6},{5,7},{6,4},{7,5},{8,10},{9,11},{10,... | collective-permute-start | bytes 393224 | tf_op jit(solution)/shard_map/ppermute | solution.py:769
  15.0 20.5 %collective-permute-start.4 = (bf16[2,2,2,384,256]{4,3,2,1,0:T(8,128)(2,1)S(1)}, bf16[2,2,2,384,256]{4,3,2,1,0:T(8,128)(2,1)S(1)}, u32[]{:S(2)}, u32[]{:S(2)}) collective-permute-start(bf16[2,2,2,384,256]{4,3,2,1,0:T(8,128)(2,1)S(1)} %get-tuple-element.112), channel_id=1, source_target_pairs={{0,8},{1,17},{2,10},{3,19},{4,12},{5,21},{6,14},{7,23},{8,0},{9,25... | collective-permute-start | bytes 4718600 | tf_op jit(solution)/shard_map/ppermute | solution.py:769
  16.6 14.2 %collective-permute-start.3 = (bf16[1024,128]{1,0:T(8,128)(2,1)S(1)}, bf16[1024,128]{1,0:T(8,128)(2,1)S(1)}, u32[]{:S(2)}, u32[]{:S(2)}) collective-permute-start(bf16[1024,128]{1,0:T(8,128)(2,1)S(1)} %constant_dynamic-update-slice_fusion.refs_4_), channel_id=1, source_target_pairs={{0,4},{1,5},{2,6},{3,7},{4,0},{5,1},{6,2},{7,3},{8,12},{9,13},{10,... | collective-permute-start | bytes 786440 | tf_op jit(solution)/shard_map/ppermute | solution.py:769
  30.8 19.5 %collective-permute-start.5 = (bf16[2,768,256]{2,1,0:T(8,128)(2,1)S(1)}, bf16[2,768,256]{2,1,0:T(8,128)(2,1)S(1)}, u32[]{:S(2)}, u32[]{:S(2)}) collective-permute-start(bf16[2,768,256]{2,1,0:T(8,128)(2,1)S(1)} %get-tuple-element.119), channel_id=1, source_target_pairs={{0,2},{1,3},{2,0},{3,1},{4,6},{5,7},{6,4},{7,5},{8,10},{9,11},{10,... | collective-permute-start | bytes 2359304 | tf_op jit(solution)/shard_map/ppermute | solution.py:769
  35.7 14.6 %collective-permute-start.6 = (bf16[2,2,384,256]{3,2,1,0:T(8,128)(2,1)S(1)}, bf16[2,2,384,256]{3,2,1,0:T(8,128)(2,1)S(1)}, u32[]{:S(2)}, u32[]{:S(2)}) collective-permute-start(bf16[2,2,384,256]{3,2,1,0:T(8,128)(2,1)S(1)} %fusion), channel_id=1, source_target_pairs={{0,16},{1,9},{2,18},{3,11},{4,20},{5,13},{6,22},{7,15},{8,24},{9,1... | collective-permute-start | bytes 2359304 | tf_op jit(solution)/shard_map/ppermute | solution.py:769
  50.6 19.7 %collective-permute-start.7 = (bf16[768,256]{1,0:T(8,128)(2,1)S(1)}, bf16[768,256]{1,0:T(8,128)(2,1)S(1)}, u32[]{:S(2)}, u32[]{:S(2)}) collective-permute-start(bf16[768,256]{1,0:T(8,128)(2,1)S(1)} %fusion.3), channel_id=1, source_target_pairs={{0,4},{1,5},{2,6},{3,7},{4,0},{5,1},{6,2},{7,3},{8,12},{9,13},{10,... | collective-permute-start | bytes 1179656 | tf_op jit(solution)/shard_map/ppermute | solution.py:769
  54.1 17.7 %collective-permute-start.8 = (bf16[2,384,256]{2,1,0:T(8,128)(2,1)S(1)}, bf16[2,384,256]{2,1,0:T(8,128)(2,1)S(1)}, u32[]{:S(2)}, u32[]{:S(2)}) collective-permute-start(bf16[2,384,256]{2,1,0:T(8,128)(2,1)S(1)} %fusion.1), channel_id=1, source_target_pairs={{0,2},{1,3},{2,0},{3,1},{4,6},{5,7},{6,4},{7,5},{8,10},{9,11},{10,... | collective-permute-start | bytes 1179656 | tf_op jit(solution)/shard_map/ppermute | solution.py:769
  76.1 14.2 %collective-permute-start.12 = (bf16[2,2,2,144,256]{4,3,2,1,0:T(8,128)(2,1)S(1)}, bf16[2,2,2,144,256]{4,3,2,1,0:T(8,128)(2,1)S(1)}, u32[]{:S(2)}, u32[]{:S(2)}) collective-permute-start(bf16[2,2,2,144,256]{4,3,2,1,0:T(8,128)(2,1)S(1)} %get-tuple-element.153), channel_id=1, source_target_pairs={{0,8},{1,17},{2,10},{3,19},{4,12},{5,21},{6,14},{7,23},{8,0},{9,25... | collective-permute-start | bytes 1769480 | tf_op jit(solution)/shard_map/ppermute | solution.py:769
  76.2 12.1 %collective-permute-start.13 = (bf16[768,256]{1,0:T(8,128)(2,1)S(1)}, bf16[768,256]{1,0:T(8,128)(2,1)S(1)}, u32[]{:S(2)}, u32[]{:S(2)}) collective-permute-start(bf16[768,256]{1,0:T(8,128)(2,1)S(1)} %fusion.2), channel_id=1, source_target_pairs={{0,16},{1,9},{2,18},{3,11},{4,20},{5,13},{6,22},{7,15},{8,24},{9,1... | collective-permute-start | bytes 1179656 | tf_op jit(solution)/shard_map/ppermute | solution.py:769
  77.8 9.1 %collective-permute-start.16 = (bf16[256,128]{1,0:T(8,128)(2,1)S(1)}, bf16[256,128]{1,0:T(8,128)(2,1)S(1)}, u32[]{:S(2)}, u32[]{:S(2)}) collective-permute-start(bf16[256,128]{1,0:T(8,128)(2,1)S(1)} %get-tuple-element.205), channel_id=1, source_target_pairs={{0,6},{1,7},{2,4},{3,5},{4,2},{5,3},{6,0},{7,1},{8,14},{9,15},{10,... | collective-permute-start | bytes 196616 | tf_op jit(solution)/shard_map/ppermute | solution.py:769
  80.8 6.0 %collective-permute-start.15 = (bf16[256,128]{1,0:T(8,128)(2,1)S(1)}, bf16[256,128]{1,0:T(8,128)(2,1)S(1)}, u32[]{:S(2)}, u32[]{:S(2)}) collective-permute-start(bf16[256,128]{1,0:T(8,128)(2,1)S(1)} %get-tuple-element.207), channel_id=1, source_target_pairs={{0,4},{1,5},{2,6},{3,7},{4,0},{5,1},{6,2},{7,3},{8,12},{9,13},{10,... | collective-permute-start | bytes 196616 | tf_op jit(solution)/shard_map/ppermute | solution.py:769
  80.9 6.0 %collective-permute-start.14 = (bf16[256,128]{1,0:T(8,128)(2,1)S(1)}, bf16[256,128]{1,0:T(8,128)(2,1)S(1)}, u32[]{:S(2)}, u32[]{:S(2)}) collective-permute-start(bf16[256,128]{1,0:T(8,128)(2,1)S(1)} %get-tuple-element.208), channel_id=1, source_target_pairs={{0,2},{1,3},{2,0},{3,1},{4,6},{5,7},{6,4},{7,5},{8,10},{9,11},{10,... | collective-permute-start | bytes 196616 | tf_op jit(solution)/shard_map/ppermute | solution.py:769
  90.3 3.0 %collective-permute-start.17 = (bf16[256,768]{1,0:T(8,128)(2,1)S(1)}, bf16[256,768]{1,0:T(8,128)(2,1)S(1)}, u32[]{:S(2)}, u32[]{:S(2)}) collective-permute-start(bf16[256,768]{1,0:T(8,128)(2,1)S(1)} %get-tuple-element.164), channel_id=1, source_target_pairs={{0,1},{1,0},{2,3},{3,2},{4,5},{5,4},{6,7},{7,6},{8,9},{9,8},{10,11... | collective-permute-start | bytes 1179656 | tf_op jit(solution)/shard_map/ppermute | solution.py:761
  90.4 12.4 %collective-permute-start.18 = (bf16[2,2,144,256]{3,2,1,0:T(8,128)(2,1)S(1)}, bf16[2,2,144,256]{3,2,1,0:T(8,128)(2,1)S(1)}, u32[]{:S(2)}, u32[]{:S(2)}) collective-permute-start(bf16[2,2,144,256]{3,2,1,0:T(8,128)(2,1)S(1)} %fusion.7), channel_id=1, source_target_pairs={{0,16},{1,9},{2,18},{3,11},{4,20},{5,13},{6,22},{7,15},{8,24},{9,1... | collective-permute-start | bytes 884744 | tf_op jit(solution)/shard_map/ppermute | solution.py:769
  91.4 11.5 %collective-permute-start.19 = (bf16[384,256]{1,0:T(8,128)(2,1)S(1)}, bf16[384,256]{1,0:T(8,128)(2,1)S(1)}, u32[]{:S(2)}, u32[]{:S(2)}) collective-permute-start(bf16[384,256]{1,0:T(8,128)(2,1)S(1)} %fusion.6), channel_id=1, source_target_pairs={{0,4},{1,5},{2,6},{3,7},{4,0},{5,1},{6,2},{7,3},{8,12},{9,13},{10,... | collective-permute-start | bytes 589832 | tf_op jit(solution)/shard_map/ppermute | solution.py:769
  91.5 16.9 %collective-permute-start.21 = (bf16[768,256]{1,0:T(8,128)(2,1)S(1)}, bf16[768,256]{1,0:T(8,128)(2,1)S(1)}, u32[]{:S(2)}, u32[]{:S(2)}) collective-permute-start(bf16[768,256]{1,0:T(8,128)(2,1)S(1)} %add_convert_fusion.2.refs_0_), channel_id=1, source_target_pairs={{0,8},{1,17},{2,10},{3,19},{4,12},{5,21},{6,14},{7,23},{8,0},{9,25... | collective-permute-start | bytes 1179656 | tf_op jit(solution)/shard_map/ppermute | solution.py:769
  103.0 8.3 %collective-permute-start.20 = (bf16[2,256,256]{2,1,0:T(8,128)(2,1)S(1)}, bf16[2,256,256]{2,1,0:T(8,128)(2,1)S(1)}, u32[]{:S(2)}, u32[]{:S(2)}) collective-permute-start(bf16[2,256,256]{2,1,0:T(8,128)(2,1)S(1)} %pad_maximum_fusion.1), channel_id=1, source_target_pairs={{0,2},{1,3},{2,0},{3,1},{4,6},{5,7},{6,4},{7,5},{8,10},{9,11},{10,... | collective-permute-start | bytes 786440 | tf_op jit(solution)/shard_map/ppermute | solution.py:769
  103.2 5.7 %collective-permute-start.22 = (bf16[384,256]{1,0:T(8,128)(2,1)S(1)}, bf16[384,256]{1,0:T(8,128)(2,1)S(1)}, u32[]{:S(2)}, u32[]{:S(2)}) collective-permute-start(bf16[384,256]{1,0:T(8,128)(2,1)S(1)} %fusion.5), channel_id=1, source_target_pairs={{0,16},{1,9},{2,18},{3,11},{4,20},{5,13},{6,22},{7,15},{8,24},{9,1... | collective-permute-start | bytes 589832 | tf_op jit(solution)/shard_map/ppermute | solution.py:769
  111.3 10.2 %collective-permute-start.24 = (bf16[768,256]{1,0:T(8,128)(2,1)S(1)}, bf16[768,256]{1,0:T(8,128)(2,1)S(1)}, u32[]{:S(2)}, u32[]{:S(2)}) collective-permute-start(bf16[768,256]{1,0:T(8,128)(2,1)S(1)} %pad_maximum_fusion.refs_2_), channel_id=1, source_target_pairs={{0,8},{1,17},{2,10},{3,19},{4,12},{5,21},{6,14},{7,23},{8,0},{9,25... | collective-permute-start | bytes 1179656 | tf_op jit(solution)/shard_map/ppermute | solution.py:769
  113.1 8.4 %collective-permute-start.23 = (bf16[256,256]{1,0:T(8,128)(2,1)S(1)}, bf16[256,256]{1,0:T(8,128)(2,1)S(1)}, u32[]{:S(2)}, u32[]{:S(2)}) collective-permute-start(bf16[256,256]{1,0:T(8,128)(2,1)S(1)} %fusion.11), channel_id=1, source_target_pairs={{0,4},{1,5},{2,6},{3,7},{4,0},{5,1},{6,2},{7,3},{8,12},{9,13},{10,... | collective-permute-start | bytes 393224 | tf_op jit(solution)/shard_map/ppermute | solution.py:769
  121.5 5.0 %collective-permute-start.26 = (bf16[256,256]{1,0:T(8,128)(2,1)S(1)}, bf16[256,256]{1,0:T(8,128)(2,1)S(1)}, u32[]{:S(2)}, u32[]{:S(2)}) collective-permute-start(bf16[256,256]{1,0:T(8,128)(2,1)S(1)} %fusion.10), channel_id=1, source_target_pairs={{0,16},{1,9},{2,18},{3,11},{4,20},{5,13},{6,22},{7,15},{8,24},{9,1... | collective-permute-start | bytes 393224 | tf_op jit(solution)/shard_map/ppermute | solution.py:769
  126.6 5.8 %collective-permute-start.27 = (bf16[400,256]{1,0:T(8,128)(2,1)S(1)}, bf16[400,256]{1,0:T(8,128)(2,1)S(1)}, u32[]{:S(2)}, u32[]{:S(2)}) collective-permute-start(bf16[400,256]{1,0:T(8,128)(2,1)S(1)} %pad_maximum_fusion.2.refs_4_), channel_id=1, source_target_pairs={{0,8},{1,17},{2,10},{3,19},{4,12},{5,21},{6,14},{7,23},{8,0},{9,25... | collective-permute-start | bytes 614408 | tf_op jit(solution)/shard_map/ppermute | solution.py:769
  (10 other events, 40.3 us)

commit v8 on v7

--- a/solution.py
+++ b/solution.py
@@ -700,7 +700,7 @@
     return jnp.concatenate(pieces, 0)
 
 
-def pack_kernel(sc, a_send, a_got, b_send, b_got, last_send, last_got, out_ref, own_ref, *, width, part, quarter):
+def pack_up_kernel(sc, a_send, a_got, b_send, b_got, out_ref, own_ref, *, width, part):
     for which, ref in ((1, out_ref), (0, own_ref)):
         parity = sc[0] if which == 0 else 1 - sc[0]
         at = 0
@@ -710,6 +710,12 @@
                     sc, k, b, parity, a_send, a_got, b_send, b_got, width, part
                 ).astype(BF)
                 at += part
+
+
+def pack_late_kernel(sc, last_send, last_got, out_ref, own_ref, *, width, part, quarter):
+    for which, ref in ((1, out_ref), (0, own_ref)):
+        parity = sc[0] if which == 0 else 1 - sc[0]
+        at = 0
         for b in range(width // WIDE):
             ref[at : at + part, :] = late_block(
                 sc, b, parity, last_send, last_got, part, quarter
@@ -722,25 +728,28 @@
         ).astype(BF)
 
 
-def final_kernel(sc, own_ref, got_ref, up_ref, query_ref, proj_ref, kv_ref, norm_ref, *, part, n_pair):
+def final_up_kernel(sc, own_ref, got_ref, up_ref, *, part, n_pair):
     part_hidden = up_ref.shape[1] // (2 * n_pair)
-    half = query_ref.shape[1] // 2
     for which, ref in enumerate((own_ref, got_ref)):
         core = sc[0] if which == 0 else 1 - sc[0]
-        at = 0
         for k in range(3):
             for j in range(n_pair):
                 lane = (2 * j + core) * part_hidden + k * LANES
                 rows = slice((2 * k + j // 2) * part, (2 * k + j // 2 + 1) * part)
                 cols = slice(j % 2 * LANES, (j % 2 + 1) * LANES)
                 up_ref[:, pl.ds(pl.multiple_of(lane, LANES), LANES)] = ref[rows, cols].astype(F32)
-        base = 6 * part
+
+
+def final_late_kernel(sc, own_ref, got_ref, query_ref, proj_ref, kv_ref, norm_ref, *, part):
+    half = query_ref.shape[1] // 2
+    for which, ref in enumerate((own_ref, got_ref)):
+        core = sc[0] if which == 0 else 1 - sc[0]
         for n in range(2 * half // LANES):
-            rows = slice(base + n // 2 * part, base + (n // 2 + 1) * part)
+            rows = slice(n // 2 * part, (n // 2 + 1) * part)
             value = ref[rows, n % 2 * LANES : (n % 2 + 1) * LANES].astype(F32)
             to, m = (query_ref, n) if n < half // LANES else (proj_ref, n - half // LANES)
             to[:, pl.ds(pl.multiple_of(core * half + m * LANES, LANES), LANES)] = value
-    base = 9 * part
+    base = 2 * half // WIDE * part
     few = own_ref[base:, :].astype(F32) + got_ref[base:, :].astype(F32)
     kv_ref[0 : part // 2, :] = few[0 : part // 2, 0:LANES]
     kv_ref[part // 2 : part, :] = few[0 : part // 2, LANES:WIDE]
@@ -975,36 +984,45 @@
     b_got = links.cross(tie(b_sum, last_send), 0)
     out_got = tie(out_got, b_sum, last_send)
     layer_output = low(out_own + out_got.astype(F32))
-    last_got_2, b_got, layer_output = meet(last_got_2, b_got, layer_output)
+    b_got, layer_output = meet(b_got, layer_output)
+    up_send, up_own = call(
+        functools.partial(pack_up_kernel, width=width, part=part),
+        "pack_up", [shape((6 * part, WIDE), BF)] * 2, [VM] * 4, [VM] * 2, [], 8,
+    )(table, a_sum, a_got, b_sum, b_got)
+    up_got = links.swap(up_send)
+    last_got_2 = tie(last_got_2, up_send)
     last = add(last_keep[0], last_got[0], last_got_2)
     last_got = links.cross(last, 1)
     total_down = call(
         functools.partial(down_kernel, width=width),
         "down", shape((part_hidden, width), F32), [VM] * 4, VM, [], 8,
     )(table, tie(a_sum, last), a_got, b_sum, b_got)
-    total_down, last_got = meet(total_down, last_got)
+    total_down, last_got, up_got = meet(total_down, last_got, up_got)
     last = jnp.concatenate(
         [last[:quarter], last_got[:quarter], add(last[quarter:], last_got[quarter:])], 0
     )
     last_got = links.cross(last, 0)
-    size_out = 9 * part + few
+    total_up = call(
+        functools.partial(final_up_kernel, part=part, n_pair=n_pair),
+        "final_up", shape((part, hidden), F32), [VM] * 2, VM, [], 8,
+    )(table, tie(up_own, last), up_got)
+    total_up, last_got = meet(total_up, last_got)
     other, own = call(
-        functools.partial(pack_kernel, width=width, part=part, quarter=quarter),
-        "pack", [shape((size_out, WIDE), BF)] * 2, [VM] * 6, [VM] * 2, [], 8,
-    )(table, a_sum, a_got, b_sum, b_got, last, last_got)
+        functools.partial(pack_late_kernel, width=width, part=part, quarter=quarter),
+        "pack_late", [shape((width // WIDE * part + few, WIDE), BF)] * 2, [VM] * 2, [VM] * 2, [], 8,
+    )(table, last, last_got)
     got = links.swap(other)
-    total_up, total_query, total_out, total_kv, norm = call(
-        functools.partial(final_kernel, part=part, n_pair=n_pair),
-        "final",
+    total_query, total_out, total_kv, norm = call(
+        functools.partial(final_late_kernel, part=part),
+        "final_late",
         [
-            shape((part, hidden), F32),
             shape((part, width), F32),
             shape((part, width), F32),
             shape((part, lanes), F32),
             shape((8, WIDE), F32),
         ],
         [VM] * 2,
-        [VM] * 5,
+        [VM] * 4,
         [],
         8,
     )(table, own, got)

time: 139 us -> 138 us (level); the launches traced: 138 us -> 138 us
  waiting for transfers between devices: 44.8 us -> 32.4 us
  starting transfers between devices: 28.1 us -> 39.2 us
  Pallas kernels: 57.9 us -> 59.7 us
    ppermute x21, waiting for transfers between devices: 41.4 us -> 29.4 us  [permute(): return lax.ppermute(value, ('grp', 'ctx'), pairs)]
    ppermute x21, starting transfers between devices: 26.8 us -> 37.9 us  [permute(): return lax.ppermute(value, ('grp', 'ctx'), pairs)]
    pallas_call x12 -> x14, Pallas kernels: 37.9 us -> 39.7 us  [placed(): made(table, *(pltpu.with_memory_space_constraint(v, pltpu.HBM) if spec is...]
    ppermute x8 -> x9, waiting for transfers between devices: 3.42 us -> 3 us  [swap(): return lax.ppermute(value, 'ctx', [(i, i ^ 1) for i in range(self.n_ctx)])]
  transfers between devices with their start and end apart: 29 -> 30, of which waited for: 16 -> 16; matrix products, arithmetic and copies ran while one was open for 3% -> 3% of each run, Pallas kernels for 37% -> 38%
where the time goes in v8:
time: 138 us
  Pallas kernels  59.7 us (43%)
  starting transfers between devices  39.2 us (28%)
  waiting for transfers between devices  32.4 us (23%)
  other arithmetic  4.59 us (3%)
    pallas_call x14, Pallas kernels, placed(): made(table, *(pltpu.with_memory_space_constraint(v, pltpu.HBM) if spec is...  39.7 us
    ppermute x21, starting transfers between devices, permute(): return lax.ppermute(value, ('grp', 'ctx'), pairs)  37.9 us
    ppermute x21, waiting for transfers between devices, permute(): return lax.ppermute(value, ('grp', 'ctx'), pairs)  29.4 us
    pallas_call x2, Pallas kernels, attention(): pl.pallas_call(functools.partial(attn_kernel, blocks=blocks, heads=heads,...  20 us
    ppermute x9, waiting for transfers between devices, swap(): return lax.ppermute(value, 'ctx', [(i, i ^ 1) for i in range(self.n_ctx)])  3 us
  transfers between devices with their start and end apart: 30, of which 16 were waited for; matrix products, arithmetic and copies ran while one was open for 3% of the time, Pallas kernels for 38%

profile of v8, /device:TPU:0, one launch (start us, length us, event | category | flops | bytes accessed | tf_op | source)
XLA Modules:
  0.0 138.1 jit_solution(2922454912627805788)
XLA Ops:
  4.3 2.6 %prologue.1 = (bf16[512,768]{1,0:T(8,128)(2,1)S(1)}, bf16[512,768]{1,0:T(8,128)(2,1)S(1)}, bf16[512,768]{1,0:T(8,128)(2,1)S(1)}, bf16[512,128]{1,0:T(8,128)(2,1)S(1)}) custom-call(s32[16]{0:T(128)S(1)} %bitcast.65, bf16[256,768]{1,0:T(8,128)(2,1)} %refs_4_.5, bf16[256,768]{1,0:T(8,128)(2,1)S(1)} %collective-permute-done.refs_1_.refs_5_, ...), custom_call_target="tpu_custom_call" | custom-call | flops 1000 | bytes 1000 | tf_op jit(solution)/shard_map/prologue/pallas_call | solution.py:85
  7.0 3.1 %collective-permute-start.2 = (bf16[512,128]{1,0:T(8,128)(2,1)S(1)}, bf16[512,128]{1,0:T(8,128)(2,1)S(1)}, u32[]{:S(2)}, u32[]{:S(2)}) collective-permute-start(bf16[512,128]{1,0:T(8,128)(2,1)S(1)} %get-tuple-element.115), channel_id=1, source_target_pairs={{0,2},{1,3},{2,0},{3,1},{4,6},{5,7},{6,4},{7,5},{8,10},{9,11},{10,... | collective-permute-start | bytes 393224 | tf_op jit(solution)/shard_map/ppermute | solution.py:778
  10.0 5.0 %ffn_gradients.3 = (bf16[512,512]{1,0:T(8,128)(2,1)S(1)}, bf16[512,512]{1,0:T(8,128)(2,1)S(1)}, bf16[2,2,2,384,256]{4,3,2,1,0:T(8,128)(2,1)S(1)}) custom-call(s32[16]{0:T(128)S(1)} %bitcast.66, bf16[512,768]{1,0:T(8,128)(2,1)S(1)} %get-tuple-element.121.refs_0_, bf16[512,768]{1,0:T(8,128)(2,1)S(1)} %get-tuple-element.113.refs_1_.refs_7_, ...), custom_call_target="tpu_custom_call" | custom-call | flops 1000 | bytes 1000 | tf_op jit(solution)/shard_map/ffn_gradients/pallas_call | solution.py:85
  16.6 2.6 %collective-permute-start.3 = (bf16[1024,128]{1,0:T(8,128)(2,1)S(1)}, bf16[1024,128]{1,0:T(8,128)(2,1)S(1)}, u32[]{:S(2)}, u32[]{:S(2)}) collective-permute-start(bf16[1024,128]{1,0:T(8,128)(2,1)S(1)} %constant_dynamic-update-slice_fusion.refs_4_), channel_id=1, source_target_pairs={{0,4},{1,5},{2,6},{3,7},{4,0},{5,1},{6,2},{7,3},{8,12},{9,13},{10,... | collective-permute-start | bytes 786440 | tf_op jit(solution)/shard_map/ppermute | solution.py:778
  19.2 5.0 %ffn_gradients.4 = (bf16[512,512]{1,0:T(8,128)(2,1)S(1)}, bf16[512,512]{1,0:T(8,128)(2,1)S(1)}, bf16[2,2,2,384,256]{4,3,2,1,0:T(8,128)(2,1)S(1)}) custom-call(s32[16]{0:T(128)S(1)} %bitcast.67, bf16[512,768]{1,0:T(8,128)(2,1)S(1)} %get-tuple-element.121.refs_0_, bf16[512,768]{1,0:T(8,128)(2,1)S(1)} %get-tuple-element.113.refs_1_.refs_7_, ...), custom_call_target="tpu_custom_call" | custom-call | flops 1000 | bytes 1000 | tf_op jit(solution)/shard_map/ffn_gradients/pallas_call | solution.py:85
  24.2 5.0 %ffn_gradients.5 = (bf16[512,512]{1,0:T(8,128)(2,1)S(1)}, bf16[512,512]{1,0:T(8,128)(2,1)S(1)}, bf16[2,768,256]{2,1,0:T(8,128)(2,1)S(1)}, bf16[2,768,256]{2,1,0:T(8,128)(2,1)S(1)}) custom-call(s32[16]{0:T(128)S(1)} %bitcast.68, bf16[512,768]{1,0:T(8,128)(2,1)S(1)} %get-tuple-element.121.refs_0_, bf16[512,768]{1,0:T(8,128)(2,1)S(1)} %get-tuple-element.113.refs_1_.refs_7_, ...), custom_call_target="tpu_custom_call" | custom-call | flops 1000 | bytes 1000 | tf_op jit(solution)/shard_map/ffn_gradients/pallas_call | solution.py:85
  30.8 2.9 %project.1 = (bf16[384,512]{1,0:T(8,128)(2,1)S(1)}, f32[384,512]{1,0:T(8,128)S(1)}) custom-call(s32[16]{0:T(128)S(1)} %bitcast.69, bf16[512,768]{1,0:T(8,128)(2,1)S(1)} %get-tuple-element.152.refs_0_.refs_7_, bf16[512,768]{1,0:T(8,128)(2,1)S(1)} %get-tuple-element.113.refs_1_.refs_7_, f32[8,512]{1,0:T(8,128)S(1)} %get-tuple-element.171.refs_6_.refs_2_.refs_4_, ...), custom_call_target="tpu_custom_call" | custom-call | flops 1000 | bytes 1000 | tf_op jit(solution)/shard_map/project/pallas_call | solution.py:85
  37.3 9.4 %attention.2 = (bf16[384,256]{1,0:T(8,128)(2,1)S(1)}, bf16[384,256]{1,0:T(8,128)(2,1)S(1)}, f32[2048,128]{1,0:T(8,128)S(1)}) custom-call(s32[16]{0:T(128)S(1)} %bitcast.70, bf16[384,512]{1,0:T(8,128)(2,1)S(1)} %get-tuple-element.138.refs_0_, f32[384,512]{1,0:T(8,128)S(1)} %get-tuple-element.129.refs_1_, ...), custom_call_target="tpu_custom_call" | custom-call | flops 1000 | bytes 1000 | tf_op jit(solution)/shard_map/attention/pallas_call | solution.py:303
  46.7 3.6 %collective-permute-done.5 = bf16[2,768,256]{2,1,0:T(8,128)(2,1)S(1)} collective-permute-done((bf16[2,768,256]{2,1,0:T(8,128)(2,1)S(1)}, bf16[2,768,256]{2,1,0:T(8,128)(2,1)S(1)}, u32[]{:S(2)}, u32[]{:S(2)}) %collective-permute-start.5) | collective-permute-done | bytes 786464 | tf_op jit(solution)/shard_map/ppermute | solution.py:778
  51.0 8.1 %collective-permute-start.8 = (bf16[2,384,256]{2,1,0:T(8,128)(2,1)S(1)}, bf16[2,384,256]{2,1,0:T(8,128)(2,1)S(1)}, u32[]{:S(2)}, u32[]{:S(2)}) collective-permute-start(bf16[2,384,256]{2,1,0:T(8,128)(2,1)S(1)} %fusion.1), channel_id=1, source_target_pairs={{0,2},{1,3},{2,0},{3,1},{4,6},{5,7},{6,4},{7,5},{8,10},{9,11},{10,... | collective-permute-start | bytes 1179656 | tf_op jit(solution)/shard_map/ppermute | solution.py:778
  59.1 10.7 %attention.3 = (bf16[384,256]{1,0:T(8,128)(2,1)S(1)}, bf16[384,256]{1,0:T(8,128)(2,1)S(1)}, bf16[2,2,256,128]{3,2,1,0:T(8,128)(2,1)S(1)}, bf16[2,2,256,128]{3,2,1,0:T(8,128)(2,1)S(1)}) custom-call(s32[16]{0:T(128)S(1)} %bitcast.71, bf16[384,512]{1,0:T(8,128)(2,1)S(1)} %get-tuple-element.138.refs_0_, f32[384,512]{1,0:T(8,128)S(1)} %get-tuple-element.129.refs_1_, ...), custom_call_target="tpu_custom_call" | custom-call | flops 1000 | bytes 1000 | tf_op jit(solution)/shard_map/attention/pallas_call | solution.py:303
  74.6 5.5 %collective-permute-start.12 = (bf16[2,2,2,144,256]{4,3,2,1,0:T(8,128)(2,1)S(1)}, bf16[2,2,2,144,256]{4,3,2,1,0:T(8,128)(2,1)S(1)}, u32[]{:S(2)}, u32[]{:S(2)}) collective-permute-start(bf16[2,2,2,144,256]{4,3,2,1,0:T(8,128)(2,1)S(1)} %get-tuple-element.157), channel_id=1, source_target_pairs={{0,8},{1,17},{2,10},{3,19},{4,12},{5,21},{6,14},{7,23},{8,0},{9,25... | collective-permute-start | bytes 1769480 | tf_op jit(solution)/shard_map/ppermute | solution.py:778
  80.1 2.6 %collective-permute-start.16 = (bf16[256,128]{1,0:T(8,128)(2,1)S(1)}, bf16[256,128]{1,0:T(8,128)(2,1)S(1)}, u32[]{:S(2)}, u32[]{:S(2)}) collective-permute-start(bf16[256,128]{1,0:T(8,128)(2,1)S(1)} %get-tuple-element.215), channel_id=1, source_target_pairs={{0,6},{1,7},{2,4},{3,5},{4,2},{5,3},{6,0},{7,1},{8,14},{9,15},{10,... | collective-permute-start | bytes 196616 | tf_op jit(solution)/shard_map/ppermute | solution.py:778
  84.6 4.5 %norms.1 = (f32[256,768]{1,0:T(8,128)S(1)}, bf16[256,768]{1,0:T(8,128)(2,1)S(1)}, f32[8,768]{1,0:T(8,128)S(1)}) custom-call(s32[16]{0:T(128)S(1)} %bitcast.73, bf16[512,512]{1,0:T(8,128)(2,1)S(1)} %get-tuple-element.147.refs_0_, bf16[512,512]{1,0:T(8,128)(2,1)S(1)} %get-tuple-element.148.refs_1_, bf16[512,512]{1,0:T(8,128)(2,1)S(1)} %get-tuple-element.159.refs_2_, ...), custom_call_target="tpu_custom_call" | custom-call | flops 1000 | bytes 1000 | tf_op jit(solution)/shard_map/norms/pallas_call | solution.py:85
  89.2 2.5 %collective-permute-done.12 = bf16[2,2,2,144,256]{4,3,2,1,0:T(8,128)(2,1)S(1)} collective-permute-done((bf16[2,2,2,144,256]{4,3,2,1,0:T(8,128)(2,1)S(1)}, bf16[2,2,2,144,256]{4,3,2,1,0:T(8,128)(2,1)S(1)}, u32[]{:S(2)}, u32[]{:S(2)}) %collective-permute-start.12) | collective-permute-done | bytes 589856 | tf_op jit(solution)/shard_map/ppermute | solution.py:778
  91.9 2.2 %collective-permute-start.19 = (bf16[384,256]{1,0:T(8,128)(2,1)S(1)}, bf16[384,256]{1,0:T(8,128)(2,1)S(1)}, u32[]{:S(2)}, u32[]{:S(2)}) collective-permute-start(bf16[384,256]{1,0:T(8,128)(2,1)S(1)} %fusion.4), channel_id=1, source_target_pairs={{0,4},{1,5},{2,6},{3,7},{4,0},{5,1},{6,2},{7,3},{8,12},{9,13},{10,... | collective-permute-start | bytes 589832 | tf_op jit(solution)/shard_map/ppermute | solution.py:778
  94.2 2.1 %collective-permute-start.21 = (bf16[768,256]{1,0:T(8,128)(2,1)S(1)}, bf16[768,256]{1,0:T(8,128)(2,1)S(1)}, u32[]{:S(2)}, u32[]{:S(2)}) collective-permute-start(bf16[768,256]{1,0:T(8,128)(2,1)S(1)} %add_convert_fusion.2.refs_0_), channel_id=1, source_target_pairs={{0,8},{1,17},{2,10},{3,19},{4,12},{5,21},{6,14},{7,23},{8,0},{9,25... | collective-permute-start | bytes 1179656 | tf_op jit(solution)/shard_map/ppermute | solution.py:778
  96.3 2.5 %last.1 = (f32[256,768]{1,0:T(8,128)}, bf16[2,112,256]{2,1,0:T(8,128)(2,1)S(1)}, bf16[2,112,256]{2,1,0:T(8,128)(2,1)S(1)}) custom-call(s32[16]{0:T(128)S(1)} %bitcast.74, bf16[256,128]{1,0:T(8,128)(2,1)S(1)} %get-tuple-element.218.refs_0_, bf16[256,128]{1,0:T(8,128)(2,1)S(1)} %collective-permute-done.14.refs_1_, ...), custom_call_target="tpu_custom_call" | custom-call | flops 1000 | bytes 1000 | tf_op jit(solution)/shard_map/last/pallas_call | solution.py:85
  98.8 5.1 %collective-permute-done.19 = bf16[384,256]{1,0:T(8,128)(2,1)S(1)} collective-permute-done((bf16[384,256]{1,0:T(8,128)(2,1)S(1)}, bf16[384,256]{1,0:T(8,128)(2,1)S(1)}, u32[]{:S(2)}, u32[]{:S(2)}) %collective-permute-start.19) | collective-permute-done | bytes 196640 | tf_op jit(solution)/shard_map/ppermute | solution.py:778
  106.3 4.1 %outputs.1 = (f32[256,768]{1,0:T(8,128)S(1)}, bf16[256,768]{1,0:T(8,128)(2,1)S(1)}) custom-call(s32[16]{0:T(128)S(1)} %bitcast.75, bf16[512,512]{1,0:T(8,128)(2,1)S(1)} %get-tuple-element.180.refs_0_, bf16[512,512]{1,0:T(8,128)(2,1)S(1)} %get-tuple-element.181.refs_1_, bf16[512,512]{1,0:T(8,128)(2,1)S(1)} %get-tuple-element.183.refs_2_, ...), custom_call_target="tpu_custom_call" | custom-call | flops 1000 | bytes 1000 | tf_op jit(solution)/shard_map/outputs/pallas_call | solution.py:85
  110.7 2.4 %collective-permute-done.20 = bf16[2,256,256]{2,1,0:T(8,128)(2,1)S(1)} collective-permute-done((bf16[2,256,256]{2,1,0:T(8,128)(2,1)S(1)}, bf16[2,256,256]{2,1,0:T(8,128)(2,1)S(1)}, u32[]{:S(2)}, u32[]{:S(2)}) %collective-permute-start.20) | collective-permute-done | bytes 262176 | tf_op jit(solution)/shard_map/ppermute | solution.py:778
  116.7 4.3 %collective-permute-done.23.refs_3_ = bf16[768,256]{1,0:T(8,128)(2,1)S(1)} collective-permute-done((bf16[768,256]{1,0:T(8,128)(2,1)S(1)}, bf16[768,256]{1,0:T(8,128)(2,1)S(1)}, u32[]{:S(2)}, u32[]{:S(2)}) %collective-permute-start.23) | collective-permute-done | bytes 393248 | tf_op jit(solution)/shard_map/ppermute | solution.py:778
  125.3 2.8 %collective-permute-done.26 = bf16[256,256]{1,0:T(8,128)(2,1)S(1)} collective-permute-done((bf16[256,256]{1,0:T(8,128)(2,1)S(1)}, bf16[256,256]{1,0:T(8,128)(2,1)S(1)}, u32[]{:S(2)}, u32[]{:S(2)}) %collective-permute-start.26) | collective-permute-done | bytes 131104 | tf_op jit(solution)/shard_map/ppermute | solution.py:778
  130.8 3.2 %collective-permute-done.28.refs_1_ = bf16[400,256]{1,0:T(8,128)(2,1)S(1)} collective-permute-done((bf16[400,256]{1,0:T(8,128)(2,1)S(1)}, bf16[400,256]{1,0:T(8,128)(2,1)S(1)}, u32[]{:S(2)}, u32[]{:S(2)}) %collective-permute-start.28) | collective-permute-done | bytes 204832 | tf_op jit(solution)/shard_map/ppermute | solution.py:778
  (90 shorter events, 35.5 us)
Async XLA Ops:
  0.6 3.0 %collective-permute-start.1 = (bf16[256,768]{1,0:T(8,128)(2,1)}, bf16[256,768]{1,0:T(8,128)(2,1)S(1)}, u32[]{:S(2)}, u32[]{:S(2)}) collective-permute-start(bf16[256,768]{1,0:T(8,128)(2,1)} %refs_13_.1), channel_id=1, source_target_pairs={{0,1},{1,0},{2,3},{3,2},{4,5},{5,4},{6,7},{7,6},{8,9},{9,8},{10,11... | collective-permute-start | bytes 1179656 | tf_op jit(solution)/shard_map/ppermute | solution.py:770
  7.0 8.0 %collective-permute-start.2 = (bf16[512,128]{1,0:T(8,128)(2,1)S(1)}, bf16[512,128]{1,0:T(8,128)(2,1)S(1)}, u32[]{:S(2)}, u32[]{:S(2)}) collective-permute-start(bf16[512,128]{1,0:T(8,128)(2,1)S(1)} %get-tuple-element.115), channel_id=1, source_target_pairs={{0,2},{1,3},{2,0},{3,1},{4,6},{5,7},{6,4},{7,5},{8,10},{9,11},{10,... | collective-permute-start | bytes 393224 | tf_op jit(solution)/shard_map/ppermute | solution.py:778
  15.0 20.5 %collective-permute-start.4 = (bf16[2,2,2,384,256]{4,3,2,1,0:T(8,128)(2,1)S(1)}, bf16[2,2,2,384,256]{4,3,2,1,0:T(8,128)(2,1)S(1)}, u32[]{:S(2)}, u32[]{:S(2)}) collective-permute-start(bf16[2,2,2,384,256]{4,3,2,1,0:T(8,128)(2,1)S(1)} %get-tuple-element.116), channel_id=1, source_target_pairs={{0,8},{1,17},{2,10},{3,19},{4,12},{5,21},{6,14},{7,23},{8,0},{9,25... | collective-permute-start | bytes 4718600 | tf_op jit(solution)/shard_map/ppermute | solution.py:778
  16.6 14.2 %collective-permute-start.3 = (bf16[1024,128]{1,0:T(8,128)(2,1)S(1)}, bf16[1024,128]{1,0:T(8,128)(2,1)S(1)}, u32[]{:S(2)}, u32[]{:S(2)}) collective-permute-start(bf16[1024,128]{1,0:T(8,128)(2,1)S(1)} %constant_dynamic-update-slice_fusion.refs_4_), channel_id=1, source_target_pairs={{0,4},{1,5},{2,6},{3,7},{4,0},{5,1},{6,2},{7,3},{8,12},{9,13},{10,... | collective-permute-start | bytes 786440 | tf_op jit(solution)/shard_map/ppermute | solution.py:778
  30.8 19.5 %collective-permute-start.5 = (bf16[2,768,256]{2,1,0:T(8,128)(2,1)S(1)}, bf16[2,768,256]{2,1,0:T(8,128)(2,1)S(1)}, u32[]{:S(2)}, u32[]{:S(2)}) collective-permute-start(bf16[2,768,256]{2,1,0:T(8,128)(2,1)S(1)} %get-tuple-element.123), channel_id=1, source_target_pairs={{0,2},{1,3},{2,0},{3,1},{4,6},{5,7},{6,4},{7,5},{8,10},{9,11},{10,... | collective-permute-start | bytes 2359304 | tf_op jit(solution)/shard_map/ppermute | solution.py:778
  35.7 14.6 %collective-permute-start.6 = (bf16[2,2,384,256]{3,2,1,0:T(8,128)(2,1)S(1)}, bf16[2,2,384,256]{3,2,1,0:T(8,128)(2,1)S(1)}, u32[]{:S(2)}, u32[]{:S(2)}) collective-permute-start(bf16[2,2,384,256]{3,2,1,0:T(8,128)(2,1)S(1)} %fusion), channel_id=1, source_target_pairs={{0,16},{1,9},{2,18},{3,11},{4,20},{5,13},{6,22},{7,15},{8,24},{9,1... | collective-permute-start | bytes 2359304 | tf_op jit(solution)/shard_map/ppermute | solution.py:778
  50.6 19.7 %collective-permute-start.7 = (bf16[768,256]{1,0:T(8,128)(2,1)S(1)}, bf16[768,256]{1,0:T(8,128)(2,1)S(1)}, u32[]{:S(2)}, u32[]{:S(2)}) collective-permute-start(bf16[768,256]{1,0:T(8,128)(2,1)S(1)} %fusion.3), channel_id=1, source_target_pairs={{0,4},{1,5},{2,6},{3,7},{4,0},{5,1},{6,2},{7,3},{8,12},{9,13},{10,... | collective-permute-start | bytes 1179656 | tf_op jit(solution)/shard_map/ppermute | solution.py:778
  51.0 19.3 %collective-permute-start.8 = (bf16[2,384,256]{2,1,0:T(8,128)(2,1)S(1)}, bf16[2,384,256]{2,1,0:T(8,128)(2,1)S(1)}, u32[]{:S(2)}, u32[]{:S(2)}) collective-permute-start(bf16[2,384,256]{2,1,0:T(8,128)(2,1)S(1)} %fusion.1), channel_id=1, source_target_pairs={{0,2},{1,3},{2,0},{3,1},{4,6},{5,7},{6,4},{7,5},{8,10},{9,11},{10,... | collective-permute-start | bytes 1179656 | tf_op jit(solution)/shard_map/ppermute | solution.py:778
  74.6 17.1 %collective-permute-start.12 = (bf16[2,2,2,144,256]{4,3,2,1,0:T(8,128)(2,1)S(1)}, bf16[2,2,2,144,256]{4,3,2,1,0:T(8,128)(2,1)S(1)}, u32[]{:S(2)}, u32[]{:S(2)}) collective-permute-start(bf16[2,2,2,144,256]{4,3,2,1,0:T(8,128)(2,1)S(1)} %get-tuple-element.157), channel_id=1, source_target_pairs={{0,8},{1,17},{2,10},{3,19},{4,12},{5,21},{6,14},{7,23},{8,0},{9,25... | collective-permute-start | bytes 1769480 | tf_op jit(solution)/shard_map/ppermute | solution.py:778
  80.1 9.1 %collective-permute-start.13 = (bf16[768,256]{1,0:T(8,128)(2,1)S(1)}, bf16[768,256]{1,0:T(8,128)(2,1)S(1)}, u32[]{:S(2)}, u32[]{:S(2)}) collective-permute-start(bf16[768,256]{1,0:T(8,128)(2,1)S(1)} %fusion.2), channel_id=1, source_target_pairs={{0,16},{1,9},{2,18},{3,11},{4,20},{5,13},{6,22},{7,15},{8,24},{9,1... | collective-permute-start | bytes 1179656 | tf_op jit(solution)/shard_map/ppermute | solution.py:778
  80.1 9.1 %collective-permute-start.16 = (bf16[256,128]{1,0:T(8,128)(2,1)S(1)}, bf16[256,128]{1,0:T(8,128)(2,1)S(1)}, u32[]{:S(2)}, u32[]{:S(2)}) collective-permute-start(bf16[256,128]{1,0:T(8,128)(2,1)S(1)} %get-tuple-element.215), channel_id=1, source_target_pairs={{0,6},{1,7},{2,4},{3,5},{4,2},{5,3},{6,0},{7,1},{8,14},{9,15},{10,... | collective-permute-start | bytes 196616 | tf_op jit(solution)/shard_map/ppermute | solution.py:778
  82.7 6.5 %collective-permute-start.15 = (bf16[256,128]{1,0:T(8,128)(2,1)S(1)}, bf16[256,128]{1,0:T(8,128)(2,1)S(1)}, u32[]{:S(2)}, u32[]{:S(2)}) collective-permute-start(bf16[256,128]{1,0:T(8,128)(2,1)S(1)} %get-tuple-element.216), channel_id=1, source_target_pairs={{0,4},{1,5},{2,6},{3,7},{4,0},{5,1},{6,2},{7,3},{8,12},{9,13},{10,... | collective-permute-start | bytes 196616 | tf_op jit(solution)/shard_map/ppermute | solution.py:778
  82.7 6.5 %collective-permute-start.14 = (bf16[256,128]{1,0:T(8,128)(2,1)S(1)}, bf16[256,128]{1,0:T(8,128)(2,1)S(1)}, u32[]{:S(2)}, u32[]{:S(2)}) collective-permute-start(bf16[256,128]{1,0:T(8,128)(2,1)S(1)} %get-tuple-element.217), channel_id=1, source_target_pairs={{0,2},{1,3},{2,0},{3,1},{4,6},{5,7},{6,4},{7,5},{8,10},{9,11},{10,... | collective-permute-start | bytes 196616 | tf_op jit(solution)/shard_map/ppermute | solution.py:778
  91.7 4.6 %collective-permute-start.17 = (bf16[256,768]{1,0:T(8,128)(2,1)S(1)}, bf16[256,768]{1,0:T(8,128)(2,1)S(1)}, u32[]{:S(2)}, u32[]{:S(2)}) collective-permute-start(bf16[256,768]{1,0:T(8,128)(2,1)S(1)} %get-tuple-element.169), channel_id=1, source_target_pairs={{0,1},{1,0},{2,3},{3,2},{4,5},{5,4},{6,7},{7,6},{8,9},{9,8},{10,11... | collective-permute-start | bytes 1179656 | tf_op jit(solution)/shard_map/ppermute | solution.py:770
  91.8 12.1 %collective-permute-start.18 = (bf16[2,2,144,256]{3,2,1,0:T(8,128)(2,1)S(1)}, bf16[2,2,144,256]{3,2,1,0:T(8,128)(2,1)S(1)}, u32[]{:S(2)}, u32[]{:S(2)}) collective-permute-start(bf16[2,2,144,256]{3,2,1,0:T(8,128)(2,1)S(1)} %fusion.7), channel_id=1, source_target_pairs={{0,16},{1,9},{2,18},{3,11},{4,20},{5,13},{6,22},{7,15},{8,24},{9,1... | collective-permute-start | bytes 884744 | tf_op jit(solution)/shard_map/ppermute | solution.py:778
  91.9 12.1 %collective-permute-start.19 = (bf16[384,256]{1,0:T(8,128)(2,1)S(1)}, bf16[384,256]{1,0:T(8,128)(2,1)S(1)}, u32[]{:S(2)}, u32[]{:S(2)}) collective-permute-start(bf16[384,256]{1,0:T(8,128)(2,1)S(1)} %fusion.4), channel_id=1, source_target_pairs={{0,4},{1,5},{2,6},{3,7},{4,0},{5,1},{6,2},{7,3},{8,12},{9,13},{10,... | collective-permute-start | bytes 589832 | tf_op jit(solution)/shard_map/ppermute | solution.py:778
  94.2 16.2 %collective-permute-start.21 = (bf16[768,256]{1,0:T(8,128)(2,1)S(1)}, bf16[768,256]{1,0:T(8,128)(2,1)S(1)}, u32[]{:S(2)}, u32[]{:S(2)}) collective-permute-start(bf16[768,256]{1,0:T(8,128)(2,1)S(1)} %add_convert_fusion.2.refs_0_), channel_id=1, source_target_pairs={{0,8},{1,17},{2,10},{3,19},{4,12},{5,21},{6,14},{7,23},{8,0},{9,25... | collective-permute-start | bytes 1179656 | tf_op jit(solution)/shard_map/ppermute | solution.py:778
  104.1 9.0 %collective-permute-start.20 = (bf16[2,256,256]{2,1,0:T(8,128)(2,1)S(1)}, bf16[2,256,256]{2,1,0:T(8,128)(2,1)S(1)}, u32[]{:S(2)}, u32[]{:S(2)}) collective-permute-start(bf16[2,256,256]{2,1,0:T(8,128)(2,1)S(1)} %pad_maximum_fusion.1), channel_id=1, source_target_pairs={{0,2},{1,3},{2,0},{3,1},{4,6},{5,7},{6,4},{7,5},{8,10},{9,11},{10,... | collective-permute-start | bytes 786440 | tf_op jit(solution)/shard_map/ppermute | solution.py:778
  105.0 5.7 %collective-permute-start.22 = (bf16[384,256]{1,0:T(8,128)(2,1)S(1)}, bf16[384,256]{1,0:T(8,128)(2,1)S(1)}, u32[]{:S(2)}, u32[]{:S(2)}) collective-permute-start(bf16[384,256]{1,0:T(8,128)(2,1)S(1)} %fusion.6), channel_id=1, source_target_pairs={{0,16},{1,9},{2,18},{3,11},{4,20},{5,13},{6,22},{7,15},{8,24},{9,1... | collective-permute-start | bytes 589832 | tf_op jit(solution)/shard_map/ppermute | solution.py:778
  113.2 7.8 %collective-permute-start.23 = (bf16[768,256]{1,0:T(8,128)(2,1)S(1)}, bf16[768,256]{1,0:T(8,128)(2,1)S(1)}, u32[]{:S(2)}, u32[]{:S(2)}) collective-permute-start(bf16[768,256]{1,0:T(8,128)(2,1)S(1)} %pad_maximum_fusion.refs_2_), channel_id=1, source_target_pairs={{0,8},{1,17},{2,10},{3,19},{4,12},{5,21},{6,14},{7,23},{8,0},{9,25... | collective-permute-start | bytes 1179656 | tf_op jit(solution)/shard_map/ppermute | solution.py:778
  114.2 8.8 %collective-permute-start.25 = (bf16[256,256]{1,0:T(8,128)(2,1)S(1)}, bf16[256,256]{1,0:T(8,128)(2,1)S(1)}, u32[]{:S(2)}, u32[]{:S(2)}) collective-permute-start(bf16[256,256]{1,0:T(8,128)(2,1)S(1)} %fusion.11), channel_id=1, source_target_pairs={{0,4},{1,5},{2,6},{3,7},{4,0},{5,1},{6,2},{7,3},{8,12},{9,13},{10,... | collective-permute-start | bytes 393224 | tf_op jit(solution)/shard_map/ppermute | solution.py:778
  121.7 6.4 %collective-permute-start.27 = (bf16[576,256]{1,0:T(8,128)(2,1)S(1)}, bf16[576,256]{1,0:T(8,128)(2,1)S(1)}, u32[]{:S(2)}, u32[]{:S(2)}) collective-permute-start(bf16[576,256]{1,0:T(8,128)(2,1)S(1)} %get-tuple-element.197), channel_id=1, source_target_pairs={{0,1},{1,0},{2,3},{3,2},{4,5},{5,4},{6,7},{7,6},{8,9},{9,8},{10,11... | collective-permute-start | bytes 884744 | tf_op jit(solution)/shard_map/ppermute | solution.py:770
  123.0 5.0 %collective-permute-start.26 = (bf16[256,256]{1,0:T(8,128)(2,1)S(1)}, bf16[256,256]{1,0:T(8,128)(2,1)S(1)}, u32[]{:S(2)}, u32[]{:S(2)}) collective-permute-start(bf16[256,256]{1,0:T(8,128)(2,1)S(1)} %fusion.10), channel_id=1, source_target_pairs={{0,16},{1,9},{2,18},{3,11},{4,20},{5,13},{6,22},{7,15},{8,24},{9,1... | collective-permute-start | bytes 393224 | tf_op jit(solution)/shard_map/ppermute | solution.py:778
  128.1 5.8 %collective-permute-start.28 = (bf16[400,256]{1,0:T(8,128)(2,1)S(1)}, bf16[400,256]{1,0:T(8,128)(2,1)S(1)}, u32[]{:S(2)}, u32[]{:S(2)}) collective-permute-start(bf16[400,256]{1,0:T(8,128)(2,1)S(1)} %pad_maximum_fusion.2.refs_0_), channel_id=1, source_target_pairs={{0,8},{1,17},{2,10},{3,19},{4,12},{5,21},{6,14},{7,23},{8,0},{9,25... | collective-permute-start | bytes 614408 | tf_op jit(solution)/shard_map/ppermute | solution.py:778
  (11 other events, 48.3 us)

commit v9 on v8

--- a/solution.py
+++ b/solution.py
@@ -357,8 +357,10 @@
     for copy in copies:
         copy.start()
     gg_ref[rows : 2 * rows, :] = gt[...]
-    gain_one, bias_one = gains[0:1, :].astype(F32), gains[1:2, :].astype(F32)
-    gain_two, bias_two = gains[2:3, :].astype(F32), gains[3:4, :].astype(F32)
+    width = xt.shape[1]
+    gain_one, bias_one, gain_two, bias_two = (
+        gains[:, n * width : (n + 1) * width] for n in range(4)
+    )
     for n, x in ((1, xt), (0, xo)):
         if n == 0:
             copies[0].wait()
@@ -593,7 +595,7 @@
         copy.start()
     for copy in copies:
         copy.wait()
-    gain_one, gain_two = gains[0:1, :].astype(F32), gains[2:3, :].astype(F32)
+    gain_one, gain_two = gains[:, 0:width], gains[:, 2 * width : 3 * width]
     sums = [jnp.zeros((1, width), F32)] * 4
     for n, x in enumerate((xo, xt)):
         here = slice(n * rows, (n + 1) * rows)
@@ -620,7 +622,7 @@
     weight = dot(low_t, h_ref[0:rows, :]).T.astype(BF)
     d_kv = dot(low, w_kv[...], ((1,), (1,)))
     hat, scale = normed(x_ref[...].astype(F32))
-    gain = gains[0:1, :].astype(F32)
+    gain = gains[:, 0:width]
     total = hat_own[...] + hat_got[...].astype(F32) + d_kv * gain
     grad_ref[...] = g_ref[...].astype(F32) + scale * (
         total
@@ -818,7 +820,9 @@
     per_chip = 2 * rows // BLK
     table = block_table[0]
     count = rows // BLK
-    gains = jnp.concatenate([ln1_gain, ln1_bias, ln2_gain, ln2_bias]).reshape(4, width)
+    gains = jnp.concatenate(
+        [v.astype(F32) for v in (ln1_gain, ln1_bias, ln2_gain, ln2_bias)]
+    ).reshape(1, 4 * width)
 
     x_other, g_other = links.swap(layer_input), links.swap(cotangent)
     column = jnp.arange(2 * rows, dtype=jnp.int32)

time: 138 us -> 136 us (0.986)
  starting transfers between devices: 39.2 us -> 35.2 us
  waiting for transfers between devices: 32.4 us -> 34.2 us
    ppermute x21, starting transfers between devices: 37.9 us -> 33.6 us  [permute(): return lax.ppermute(value, ('grp', 'ctx'), pairs)]
    ppermute x21, waiting for transfers between devices: 29.4 us -> 31.2 us  [permute(): return lax.ppermute(value, ('grp', 'ctx'), pairs)]
  transfers between devices with their start and end apart: 30 -> 30, of which waited for: 16 -> 18; matrix products, arithmetic and copies ran while one was open for 3% -> 3% of each run, Pallas kernels for 38% -> 39%
where the time goes in v9:
time: 136 us
  Pallas kernels  59.5 us (44%)
  starting transfers between devices  35.2 us (26%)
  waiting for transfers between devices  34.2 us (25%)
  other arithmetic  4.57 us (3%)
    pallas_call x14, Pallas kernels, placed(): made(table, *(pltpu.with_memory_space_constraint(v, pltpu.HBM) if spec is...  39.5 us
    ppermute x21, starting transfers between devices, permute(): return lax.ppermute(value, ('grp', 'ctx'), pairs)  33.6 us
    ppermute x21, waiting for transfers between devices, permute(): return lax.ppermute(value, ('grp', 'ctx'), pairs)  31.2 us
    pallas_call x2, Pallas kernels, attention(): pl.pallas_call(functools.partial(attn_kernel, blocks=blocks, heads=heads,...  20 us
    ppermute x9, waiting for transfers between devices, swap(): return lax.ppermute(value, 'ctx', [(i, i ^ 1) for i in range(self.n_ctx)])  3 us
  transfers between devices with their start and end apart: 30, of which 18 were waited for; matrix products, arithmetic and copies ran while one was open for 3% of the time, Pallas kernels for 39%

profile of v9, /device:TPU:0, one launch (start us, length us, event | category | flops | bytes accessed | tf_op | source)
XLA Modules:
  0.0 135.7 jit_solution(17943554236301268347)
XLA Ops:
  4.3 2.4 %prologue.1 = (bf16[512,768]{1,0:T(8,128)(2,1)S(1)}, bf16[512,768]{1,0:T(8,128)(2,1)S(1)}, bf16[512,768]{1,0:T(8,128)(2,1)S(1)}, bf16[512,128]{1,0:T(8,128)(2,1)S(1)}) custom-call(s32[16]{0:T(128)S(1)} %bitcast.69, bf16[256,768]{1,0:T(8,128)(2,1)} %refs_4_.5, bf16[256,768]{1,0:T(8,128)(2,1)S(1)} %collective-permute-done.refs_1_.refs_5_, ...), custom_call_target="tpu_custom_call" | custom-call | flops 1000 | bytes 1000 | tf_op jit(solution)/shard_map/prologue/pallas_call | solution.py:85
  6.7 3.1 %collective-permute-start.2 = (bf16[512,128]{1,0:T(8,128)(2,1)S(1)}, bf16[512,128]{1,0:T(8,128)(2,1)S(1)}, u32[]{:S(2)}, u32[]{:S(2)}) collective-permute-start(bf16[512,128]{1,0:T(8,128)(2,1)S(1)} %get-tuple-element.115), channel_id=1, source_target_pairs={{0,2},{1,3},{2,0},{3,1},{4,6},{5,7},{6,4},{7,5},{8,10},{9,11},{10,... | collective-permute-start | bytes 393224 | tf_op jit(solution)/shard_map/ppermute | solution.py:780
  9.8 5.0 %ffn_gradients.3 = (bf16[512,512]{1,0:T(8,128)(2,1)S(1)}, bf16[512,512]{1,0:T(8,128)(2,1)S(1)}, bf16[2,2,2,384,256]{4,3,2,1,0:T(8,128)(2,1)S(1)}) custom-call(s32[16]{0:T(128)S(1)} %bitcast.70, bf16[512,768]{1,0:T(8,128)(2,1)S(1)} %get-tuple-element.121.refs_0_, bf16[512,768]{1,0:T(8,128)(2,1)S(1)} %get-tuple-element.113.refs_1_.refs_7_, ...), custom_call_target="tpu_custom_call" | custom-call | flops 1000 | bytes 1000 | tf_op jit(solution)/shard_map/ffn_gradients/pallas_call | solution.py:85
  16.3 2.7 %collective-permute-start.3 = (bf16[1024,128]{1,0:T(8,128)(2,1)S(1)}, bf16[1024,128]{1,0:T(8,128)(2,1)S(1)}, u32[]{:S(2)}, u32[]{:S(2)}) collective-permute-start(bf16[1024,128]{1,0:T(8,128)(2,1)S(1)} %constant_dynamic-update-slice_fusion.refs_4_), channel_id=1, source_target_pairs={{0,4},{1,5},{2,6},{3,7},{4,0},{5,1},{6,2},{7,3},{8,12},{9,13},{10,... | collective-permute-start | bytes 786440 | tf_op jit(solution)/shard_map/ppermute | solution.py:780
  19.0 5.0 %ffn_gradients.4 = (bf16[512,512]{1,0:T(8,128)(2,1)S(1)}, bf16[512,512]{1,0:T(8,128)(2,1)S(1)}, bf16[2,2,2,384,256]{4,3,2,1,0:T(8,128)(2,1)S(1)}) custom-call(s32[16]{0:T(128)S(1)} %bitcast.71, bf16[512,768]{1,0:T(8,128)(2,1)S(1)} %get-tuple-element.121.refs_0_, bf16[512,768]{1,0:T(8,128)(2,1)S(1)} %get-tuple-element.113.refs_1_.refs_7_, ...), custom_call_target="tpu_custom_call" | custom-call | flops 1000 | bytes 1000 | tf_op jit(solution)/shard_map/ffn_gradients/pallas_call | solution.py:85
  24.0 5.0 %ffn_gradients.5 = (bf16[512,512]{1,0:T(8,128)(2,1)S(1)}, bf16[512,512]{1,0:T(8,128)(2,1)S(1)}, bf16[2,768,256]{2,1,0:T(8,128)(2,1)S(1)}, bf16[2,768,256]{2,1,0:T(8,128)(2,1)S(1)}) custom-call(s32[16]{0:T(128)S(1)} %bitcast.72, bf16[512,768]{1,0:T(8,128)(2,1)S(1)} %get-tuple-element.121.refs_0_, bf16[512,768]{1,0:T(8,128)(2,1)S(1)} %get-tuple-element.113.refs_1_.refs_7_, ...), custom_call_target="tpu_custom_call" | custom-call | flops 1000 | bytes 1000 | tf_op jit(solution)/shard_map/ffn_gradients/pallas_call | solution.py:85
  30.6 2.9 %project.1 = (bf16[384,512]{1,0:T(8,128)(2,1)S(1)}, f32[384,512]{1,0:T(8,128)S(1)}) custom-call(s32[16]{0:T(128)S(1)} %bitcast.73, bf16[512,768]{1,0:T(8,128)(2,1)S(1)} %get-tuple-element.152.refs_0_.refs_7_, bf16[512,768]{1,0:T(8,128)(2,1)S(1)} %get-tuple-element.113.refs_1_.refs_7_, f32[8,512]{1,0:T(8,128)S(1)} %get-tuple-element.171.refs_6_.refs_2_.refs_4_, ...), custom_call_target="tpu_custom_call" | custom-call | flops 1000 | bytes 1000 | tf_op jit(solution)/shard_map/project/pallas_call | solution.py:85
  33.4 1.8 %collective-permute-done.4 = bf16[2,2,2,384,256]{4,3,2,1,0:T(8,128)(2,1)S(1)} collective-permute-done((bf16[2,2,2,384,256]{4,3,2,1,0:T(8,128)(2,1)S(1)}, bf16[2,2,2,384,256]{4,3,2,1,0:T(8,128)(2,1)S(1)}, u32[]{:S(2)}, u32[]{:S(2)}) %collective-permute-start.4) | collective-permute-done | bytes 1572896 | tf_op jit(solution)/shard_map/ppermute | solution.py:780
  37.0 12.7 %attention.2 = (bf16[384,256]{1,0:T(8,128)(2,1)S(1)}, bf16[384,256]{1,0:T(8,128)(2,1)S(1)}, f32[2048,128]{1,0:T(8,128)S(1)}) custom-call(s32[16]{0:T(128)S(1)} %bitcast.74, bf16[384,512]{1,0:T(8,128)(2,1)S(1)} %get-tuple-element.138.refs_0_, f32[384,512]{1,0:T(8,128)S(1)} %get-tuple-element.129.refs_1_, ...), custom_call_target="tpu_custom_call" | custom-call | flops 1000 | bytes 1000 | tf_op jit(solution)/shard_map/attention/pallas_call | solution.py:303
  51.6 4.9 %collective-permute-start.8 = (bf16[2,384,256]{2,1,0:T(8,128)(2,1)S(1)}, bf16[2,384,256]{2,1,0:T(8,128)(2,1)S(1)}, u32[]{:S(2)}, u32[]{:S(2)}) collective-permute-start(bf16[2,384,256]{2,1,0:T(8,128)(2,1)S(1)} %fusion.1), channel_id=1, source_target_pairs={{0,2},{1,3},{2,0},{3,1},{4,6},{5,7},{6,4},{7,5},{8,10},{9,11},{10,... | collective-permute-start | bytes 1179656 | tf_op jit(solution)/shard_map/ppermute | solution.py:780
  56.6 7.3 %attention.3 = (bf16[384,256]{1,0:T(8,128)(2,1)S(1)}, bf16[384,256]{1,0:T(8,128)(2,1)S(1)}, bf16[2,2,256,128]{3,2,1,0:T(8,128)(2,1)S(1)}, bf16[2,2,256,128]{3,2,1,0:T(8,128)(2,1)S(1)}) custom-call(s32[16]{0:T(128)S(1)} %bitcast.75, bf16[384,512]{1,0:T(8,128)(2,1)S(1)} %get-tuple-element.138.refs_0_, f32[384,512]{1,0:T(8,128)S(1)} %get-tuple-element.129.refs_1_, ...), custom_call_target="tpu_custom_call" | custom-call | flops 1000 | bytes 1000 | tf_op jit(solution)/shard_map/attention/pallas_call | solution.py:303
  63.9 6.1 %collective-permute-done.7 = bf16[768,256]{1,0:T(8,128)(2,1)S(1)} collective-permute-done((bf16[768,256]{1,0:T(8,128)(2,1)S(1)}, bf16[768,256]{1,0:T(8,128)(2,1)S(1)}, u32[]{:S(2)}, u32[]{:S(2)}) %collective-permute-start.7) | collective-permute-done | bytes 393248 | tf_op jit(solution)/shard_map/ppermute | solution.py:780
  72.4 1.9 %late_gradients.1 = (bf16[2,2,2,144,256]{4,3,2,1,0:T(8,128)(2,1)S(1)}, bf16[2,2,2,144,256]{4,3,2,1,0:T(8,128)(2,1)S(1)}, bf16[384,512]{1,0:T(8,128)(2,1)S(1)}, bf16[384,512]{1,0:T(8,128)(2,1)S(1)}) custom-call(s32[16]{0:T(128)S(1)} %bitcast.76, bf16[512,768]{1,0:T(8,128)(2,1)S(1)} %get-tuple-element.152.refs_0_.refs_7_, ...), custom_call_target="tpu_custom_call" | custom-call | flops 1000 | bytes 1000 | tf_op jit(solution)/shard_map/late_gradients/pallas_call | solution.py:85
  77.6 2.9 %collective-permute-start.16 = (bf16[256,128]{1,0:T(8,128)(2,1)S(1)}, bf16[256,128]{1,0:T(8,128)(2,1)S(1)}, u32[]{:S(2)}, u32[]{:S(2)}) collective-permute-start(bf16[256,128]{1,0:T(8,128)(2,1)S(1)} %get-tuple-element.215), channel_id=1, source_target_pairs={{0,6},{1,7},{2,4},{3,5},{4,2},{5,3},{6,0},{7,1},{8,14},{9,15},{10,... | collective-permute-start | bytes 196616 | tf_op jit(solution)/shard_map/ppermute | solution.py:780
  82.1 4.5 %norms.1 = (f32[256,768]{1,0:T(8,128)S(1)}, bf16[256,768]{1,0:T(8,128)(2,1)S(1)}, f32[8,768]{1,0:T(8,128)S(1)}) custom-call(s32[16]{0:T(128)S(1)} %bitcast.77, bf16[512,512]{1,0:T(8,128)(2,1)S(1)} %get-tuple-element.147.refs_0_, bf16[512,512]{1,0:T(8,128)(2,1)S(1)} %get-tuple-element.148.refs_1_, bf16[512,512]{1,0:T(8,128)(2,1)S(1)} %get-tuple-element.159.refs_2_, ...), custom_call_target="tpu_custom_call" | custom-call | flops 1000 | bytes 1000 | tf_op jit(solution)/shard_map/norms/pallas_call | solution.py:85
  88.9 2.1 %collective-permute-start.18 = (bf16[2,2,144,256]{3,2,1,0:T(8,128)(2,1)S(1)}, bf16[2,2,144,256]{3,2,1,0:T(8,128)(2,1)S(1)}, u32[]{:S(2)}, u32[]{:S(2)}) collective-permute-start(bf16[2,2,144,256]{3,2,1,0:T(8,128)(2,1)S(1)} %fusion.7), channel_id=1, source_target_pairs={{0,16},{1,9},{2,18},{3,11},{4,20},{5,13},{6,22},{7,15},{8,24},{9,1... | collective-permute-start | bytes 884744 | tf_op jit(solution)/shard_map/ppermute | solution.py:780
  93.2 2.5 %last.1 = (f32[256,768]{1,0:T(8,128)}, bf16[2,112,256]{2,1,0:T(8,128)(2,1)S(1)}, bf16[2,112,256]{2,1,0:T(8,128)(2,1)S(1)}) custom-call(s32[16]{0:T(128)S(1)} %bitcast.78, bf16[256,128]{1,0:T(8,128)(2,1)S(1)} %get-tuple-element.218.refs_0_, bf16[256,128]{1,0:T(8,128)(2,1)S(1)} %collective-permute-done.14.refs_1_, ...), custom_call_target="tpu_custom_call" | custom-call | flops 1000 | bytes 1000 | tf_op jit(solution)/shard_map/last/pallas_call | solution.py:85
  95.7 6.6 %collective-permute-done.19 = bf16[384,256]{1,0:T(8,128)(2,1)S(1)} collective-permute-done((bf16[384,256]{1,0:T(8,128)(2,1)S(1)}, bf16[384,256]{1,0:T(8,128)(2,1)S(1)}, u32[]{:S(2)}, u32[]{:S(2)}) %collective-permute-start.19) | collective-permute-done | bytes 196640 | tf_op jit(solution)/shard_map/ppermute | solution.py:780
  103.9 4.1 %outputs.1 = (f32[256,768]{1,0:T(8,128)S(1)}, bf16[256,768]{1,0:T(8,128)(2,1)S(1)}) custom-call(s32[16]{0:T(128)S(1)} %bitcast.79, bf16[512,512]{1,0:T(8,128)(2,1)S(1)} %get-tuple-element.180.refs_0_, bf16[512,512]{1,0:T(8,128)(2,1)S(1)} %get-tuple-element.181.refs_1_, bf16[512,512]{1,0:T(8,128)(2,1)S(1)} %get-tuple-element.183.refs_2_, ...), custom_call_target="tpu_custom_call" | custom-call | flops 1000 | bytes 1000 | tf_op jit(solution)/shard_map/outputs/pallas_call | solution.py:85
  110.7 2.6 %collective-permute-start.25 = (bf16[256,256]{1,0:T(8,128)(2,1)S(1)}, bf16[256,256]{1,0:T(8,128)(2,1)S(1)}, u32[]{:S(2)}, u32[]{:S(2)}) collective-permute-start(bf16[256,256]{1,0:T(8,128)(2,1)S(1)} %fusion.11), channel_id=1, source_target_pairs={{0,4},{1,5},{2,6},{3,7},{4,0},{5,1},{6,2},{7,3},{8,12},{9,13},{10,... | collective-permute-start | bytes 393224 | tf_op jit(solution)/shard_map/ppermute | solution.py:780
  114.2 3.7 %collective-permute-done.23.refs_3_ = bf16[768,256]{1,0:T(8,128)(2,1)S(1)} collective-permute-done((bf16[768,256]{1,0:T(8,128)(2,1)S(1)}, bf16[768,256]{1,0:T(8,128)(2,1)S(1)}, u32[]{:S(2)}, u32[]{:S(2)}) %collective-permute-start.23) | collective-permute-done | bytes 393248 | tf_op jit(solution)/shard_map/ppermute | solution.py:780
  118.7 2.0 %collective-permute-done.25 = bf16[256,256]{1,0:T(8,128)(2,1)S(1)} collective-permute-done((bf16[256,256]{1,0:T(8,128)(2,1)S(1)}, bf16[256,256]{1,0:T(8,128)(2,1)S(1)}, u32[]{:S(2)}, u32[]{:S(2)}) %collective-permute-start.25) | collective-permute-done | bytes 131104 | tf_op jit(solution)/shard_map/ppermute | solution.py:780
  123.3 2.4 %collective-permute-done.26 = bf16[256,256]{1,0:T(8,128)(2,1)S(1)} collective-permute-done((bf16[256,256]{1,0:T(8,128)(2,1)S(1)}, bf16[256,256]{1,0:T(8,128)(2,1)S(1)}, u32[]{:S(2)}, u32[]{:S(2)}) %collective-permute-start.26) | collective-permute-done | bytes 131104 | tf_op jit(solution)/shard_map/ppermute | solution.py:780
  128.8 2.8 %collective-permute-done.28.refs_1_ = bf16[400,256]{1,0:T(8,128)(2,1)S(1)} collective-permute-done((bf16[400,256]{1,0:T(8,128)(2,1)S(1)}, bf16[400,256]{1,0:T(8,128)(2,1)S(1)}, u32[]{:S(2)}, u32[]{:S(2)}) %collective-permute-start.28) | collective-permute-done | bytes 204832 | tf_op jit(solution)/shard_map/ppermute | solution.py:780
  (89 shorter events, 37.7 us)
Async XLA Ops:
  6.7 8.0 %collective-permute-start.2 = (bf16[512,128]{1,0:T(8,128)(2,1)S(1)}, bf16[512,128]{1,0:T(8,128)(2,1)S(1)}, u32[]{:S(2)}, u32[]{:S(2)}) collective-permute-start(bf16[512,128]{1,0:T(8,128)(2,1)S(1)} %get-tuple-element.115), channel_id=1, source_target_pairs={{0,2},{1,3},{2,0},{3,1},{4,6},{5,7},{6,4},{7,5},{8,10},{9,11},{10,... | collective-permute-start | bytes 393224 | tf_op jit(solution)/shard_map/ppermute | solution.py:780
  14.8 20.5 %collective-permute-start.4 = (bf16[2,2,2,384,256]{4,3,2,1,0:T(8,128)(2,1)S(1)}, bf16[2,2,2,384,256]{4,3,2,1,0:T(8,128)(2,1)S(1)}, u32[]{:S(2)}, u32[]{:S(2)}) collective-permute-start(bf16[2,2,2,384,256]{4,3,2,1,0:T(8,128)(2,1)S(1)} %get-tuple-element.116), channel_id=1, source_target_pairs={{0,8},{1,17},{2,10},{3,19},{4,12},{5,21},{6,14},{7,23},{8,0},{9,25... | collective-permute-start | bytes 4718600 | tf_op jit(solution)/shard_map/ppermute | solution.py:780
  16.3 14.2 %collective-permute-start.3 = (bf16[1024,128]{1,0:T(8,128)(2,1)S(1)}, bf16[1024,128]{1,0:T(8,128)(2,1)S(1)}, u32[]{:S(2)}, u32[]{:S(2)}) collective-permute-start(bf16[1024,128]{1,0:T(8,128)(2,1)S(1)} %constant_dynamic-update-slice_fusion.refs_4_), channel_id=1, source_target_pairs={{0,4},{1,5},{2,6},{3,7},{4,0},{5,1},{6,2},{7,3},{8,12},{9,13},{10,... | collective-permute-start | bytes 786440 | tf_op jit(solution)/shard_map/ppermute | solution.py:780
  30.6 19.5 %collective-permute-start.5 = (bf16[2,768,256]{2,1,0:T(8,128)(2,1)S(1)}, bf16[2,768,256]{2,1,0:T(8,128)(2,1)S(1)}, u32[]{:S(2)}, u32[]{:S(2)}) collective-permute-start(bf16[2,768,256]{2,1,0:T(8,128)(2,1)S(1)} %get-tuple-element.123), channel_id=1, source_target_pairs={{0,2},{1,3},{2,0},{3,1},{4,6},{5,7},{6,4},{7,5},{8,10},{9,11},{10,... | collective-permute-start | bytes 2359304 | tf_op jit(solution)/shard_map/ppermute | solution.py:780
  35.5 14.6 %collective-permute-start.6 = (bf16[2,2,384,256]{3,2,1,0:T(8,128)(2,1)S(1)}, bf16[2,2,384,256]{3,2,1,0:T(8,128)(2,1)S(1)}, u32[]{:S(2)}, u32[]{:S(2)}) collective-permute-start(bf16[2,2,384,256]{3,2,1,0:T(8,128)(2,1)S(1)} %fusion), channel_id=1, source_target_pairs={{0,16},{1,9},{2,18},{3,11},{4,20},{5,13},{6,22},{7,15},{8,24},{9,1... | collective-permute-start | bytes 2359304 | tf_op jit(solution)/shard_map/ppermute | solution.py:780
  50.3 19.7 %collective-permute-start.7 = (bf16[768,256]{1,0:T(8,128)(2,1)S(1)}, bf16[768,256]{1,0:T(8,128)(2,1)S(1)}, u32[]{:S(2)}, u32[]{:S(2)}) collective-permute-start(bf16[768,256]{1,0:T(8,128)(2,1)S(1)} %fusion.3), channel_id=1, source_target_pairs={{0,4},{1,5},{2,6},{3,7},{4,0},{5,1},{6,2},{7,3},{8,12},{9,13},{10,... | collective-permute-start | bytes 1179656 | tf_op jit(solution)/shard_map/ppermute | solution.py:780
  51.6 18.4 %collective-permute-start.8 = (bf16[2,384,256]{2,1,0:T(8,128)(2,1)S(1)}, bf16[2,384,256]{2,1,0:T(8,128)(2,1)S(1)}, u32[]{:S(2)}, u32[]{:S(2)}) collective-permute-start(bf16[2,384,256]{2,1,0:T(8,128)(2,1)S(1)} %fusion.1), channel_id=1, source_target_pairs={{0,2},{1,3},{2,0},{3,1},{4,6},{5,7},{6,4},{7,5},{8,10},{9,11},{10,... | collective-permute-start | bytes 1179656 | tf_op jit(solution)/shard_map/ppermute | solution.py:780
  74.4 14.2 %collective-permute-start.12 = (bf16[2,2,2,144,256]{4,3,2,1,0:T(8,128)(2,1)S(1)}, bf16[2,2,2,144,256]{4,3,2,1,0:T(8,128)(2,1)S(1)}, u32[]{:S(2)}, u32[]{:S(2)}) collective-permute-start(bf16[2,2,2,144,256]{4,3,2,1,0:T(8,128)(2,1)S(1)} %get-tuple-element.157), channel_id=1, source_target_pairs={{0,8},{1,17},{2,10},{3,19},{4,12},{5,21},{6,14},{7,23},{8,0},{9,25... | collective-permute-start | bytes 1769480 | tf_op jit(solution)/shard_map/ppermute | solution.py:780
  75.9 12.0 %collective-permute-start.13 = (bf16[768,256]{1,0:T(8,128)(2,1)S(1)}, bf16[768,256]{1,0:T(8,128)(2,1)S(1)}, u32[]{:S(2)}, u32[]{:S(2)}) collective-permute-start(bf16[768,256]{1,0:T(8,128)(2,1)S(1)} %fusion.2), channel_id=1, source_target_pairs={{0,16},{1,9},{2,18},{3,11},{4,20},{5,13},{6,22},{7,15},{8,24},{9,1... | collective-permute-start | bytes 1179656 | tf_op jit(solution)/shard_map/ppermute | solution.py:780
  77.6 9.1 %collective-permute-start.16 = (bf16[256,128]{1,0:T(8,128)(2,1)S(1)}, bf16[256,128]{1,0:T(8,128)(2,1)S(1)}, u32[]{:S(2)}, u32[]{:S(2)}) collective-permute-start(bf16[256,128]{1,0:T(8,128)(2,1)S(1)} %get-tuple-element.215), channel_id=1, source_target_pairs={{0,6},{1,7},{2,4},{3,5},{4,2},{5,3},{6,0},{7,1},{8,14},{9,15},{10,... | collective-permute-start | bytes 196616 | tf_op jit(solution)/shard_map/ppermute | solution.py:780
  80.5 7.0 %collective-permute-start.15 = (bf16[256,128]{1,0:T(8,128)(2,1)S(1)}, bf16[256,128]{1,0:T(8,128)(2,1)S(1)}, u32[]{:S(2)}, u32[]{:S(2)}) collective-permute-start(bf16[256,128]{1,0:T(8,128)(2,1)S(1)} %get-tuple-element.216), channel_id=1, source_target_pairs={{0,4},{1,5},{2,6},{3,7},{4,0},{5,1},{6,2},{7,3},{8,12},{9,13},{10,... | collective-permute-start | bytes 196616 | tf_op jit(solution)/shard_map/ppermute | solution.py:780
  81.9 5.6 %collective-permute-start.14 = (bf16[256,128]{1,0:T(8,128)(2,1)S(1)}, bf16[256,128]{1,0:T(8,128)(2,1)S(1)}, u32[]{:S(2)}, u32[]{:S(2)}) collective-permute-start(bf16[256,128]{1,0:T(8,128)(2,1)S(1)} %get-tuple-element.217), channel_id=1, source_target_pairs={{0,2},{1,3},{2,0},{3,1},{4,6},{5,7},{6,4},{7,5},{8,10},{9,11},{10,... | collective-permute-start | bytes 196616 | tf_op jit(solution)/shard_map/ppermute | solution.py:780
  88.6 4.6 %collective-permute-start.17 = (bf16[256,768]{1,0:T(8,128)(2,1)S(1)}, bf16[256,768]{1,0:T(8,128)(2,1)S(1)}, u32[]{:S(2)}, u32[]{:S(2)}) collective-permute-start(bf16[256,768]{1,0:T(8,128)(2,1)S(1)} %get-tuple-element.169), channel_id=1, source_target_pairs={{0,1},{1,0},{2,3},{3,2},{4,5},{5,4},{6,7},{7,6},{8,9},{9,8},{10,11... | collective-permute-start | bytes 1179656 | tf_op jit(solution)/shard_map/ppermute | solution.py:772
  88.9 13.4 %collective-permute-start.18 = (bf16[2,2,144,256]{3,2,1,0:T(8,128)(2,1)S(1)}, bf16[2,2,144,256]{3,2,1,0:T(8,128)(2,1)S(1)}, u32[]{:S(2)}, u32[]{:S(2)}) collective-permute-start(bf16[2,2,144,256]{3,2,1,0:T(8,128)(2,1)S(1)} %fusion.7), channel_id=1, source_target_pairs={{0,16},{1,9},{2,18},{3,11},{4,20},{5,13},{6,22},{7,15},{8,24},{9,1... | collective-permute-start | bytes 884744 | tf_op jit(solution)/shard_map/ppermute | solution.py:780
  91.0 11.3 %collective-permute-start.19 = (bf16[384,256]{1,0:T(8,128)(2,1)S(1)}, bf16[384,256]{1,0:T(8,128)(2,1)S(1)}, u32[]{:S(2)}, u32[]{:S(2)}) collective-permute-start(bf16[384,256]{1,0:T(8,128)(2,1)S(1)} %fusion.4), channel_id=1, source_target_pairs={{0,4},{1,5},{2,6},{3,7},{4,0},{5,1},{6,2},{7,3},{8,12},{9,13},{10,... | collective-permute-start | bytes 589832 | tf_op jit(solution)/shard_map/ppermute | solution.py:780
  91.8 16.3 %collective-permute-start.21 = (bf16[768,256]{1,0:T(8,128)(2,1)S(1)}, bf16[768,256]{1,0:T(8,128)(2,1)S(1)}, u32[]{:S(2)}, u32[]{:S(2)}) collective-permute-start(bf16[768,256]{1,0:T(8,128)(2,1)S(1)} %add_convert_fusion.2.refs_0_), channel_id=1, source_target_pairs={{0,8},{1,17},{2,10},{3,19},{4,12},{5,21},{6,14},{7,23},{8,0},{9,25... | collective-permute-start | bytes 1179656 | tf_op jit(solution)/shard_map/ppermute | solution.py:780
  102.4 7.5 %collective-permute-start.20 = (bf16[2,256,256]{2,1,0:T(8,128)(2,1)S(1)}, bf16[2,256,256]{2,1,0:T(8,128)(2,1)S(1)}, u32[]{:S(2)}, u32[]{:S(2)}) collective-permute-start(bf16[2,256,256]{2,1,0:T(8,128)(2,1)S(1)} %pad_maximum_fusion.1), channel_id=1, source_target_pairs={{0,2},{1,3},{2,0},{3,1},{4,6},{5,7},{6,4},{7,5},{8,10},{9,11},{10,... | collective-permute-start | bytes 786440 | tf_op jit(solution)/shard_map/ppermute | solution.py:780
  102.6 5.7 %collective-permute-start.22 = (bf16[384,256]{1,0:T(8,128)(2,1)S(1)}, bf16[384,256]{1,0:T(8,128)(2,1)S(1)}, u32[]{:S(2)}, u32[]{:S(2)}) collective-permute-start(bf16[384,256]{1,0:T(8,128)(2,1)S(1)} %fusion.6), channel_id=1, source_target_pairs={{0,16},{1,9},{2,18},{3,11},{4,20},{5,13},{6,22},{7,15},{8,24},{9,1... | collective-permute-start | bytes 589832 | tf_op jit(solution)/shard_map/ppermute | solution.py:780
  110.0 3.4 %collective-permute-start.24 = (bf16[256,768]{1,0:T(8,128)(2,1)S(1)}, bf16[256,768]{1,0:T(8,128)(2,1)S(1)}, u32[]{:S(2)}, u32[]{:S(2)}) collective-permute-start(bf16[256,768]{1,0:T(8,128)(2,1)S(1)} %get-tuple-element.191), channel_id=1, source_target_pairs={{0,1},{1,0},{2,3},{3,2},{4,5},{5,4},{6,7},{7,6},{8,9},{9,8},{10,11... | collective-permute-start | bytes 1179656 | tf_op jit(solution)/shard_map/ppermute | solution.py:772
  110.0 7.8 %collective-permute-start.23 = (bf16[768,256]{1,0:T(8,128)(2,1)S(1)}, bf16[768,256]{1,0:T(8,128)(2,1)S(1)}, u32[]{:S(2)}, u32[]{:S(2)}) collective-permute-start(bf16[768,256]{1,0:T(8,128)(2,1)S(1)} %pad_maximum_fusion.refs_2_), channel_id=1, source_target_pairs={{0,8},{1,17},{2,10},{3,19},{4,12},{5,21},{6,14},{7,23},{8,0},{9,25... | collective-permute-start | bytes 1179656 | tf_op jit(solution)/shard_map/ppermute | solution.py:780
  110.7 9.9 %collective-permute-start.25 = (bf16[256,256]{1,0:T(8,128)(2,1)S(1)}, bf16[256,256]{1,0:T(8,128)(2,1)S(1)}, u32[]{:S(2)}, u32[]{:S(2)}) collective-permute-start(bf16[256,256]{1,0:T(8,128)(2,1)S(1)} %fusion.11), channel_id=1, source_target_pairs={{0,4},{1,5},{2,6},{3,7},{4,0},{5,1},{6,2},{7,3},{8,12},{9,13},{10,... | collective-permute-start | bytes 393224 | tf_op jit(solution)/shard_map/ppermute | solution.py:780
  118.6 7.1 %collective-permute-start.27 = (bf16[576,256]{1,0:T(8,128)(2,1)S(1)}, bf16[576,256]{1,0:T(8,128)(2,1)S(1)}, u32[]{:S(2)}, u32[]{:S(2)}) collective-permute-start(bf16[576,256]{1,0:T(8,128)(2,1)S(1)} %get-tuple-element.197), channel_id=1, source_target_pairs={{0,1},{1,0},{2,3},{3,2},{4,5},{5,4},{6,7},{7,6},{8,9},{9,8},{10,11... | collective-permute-start | bytes 884744 | tf_op jit(solution)/shard_map/ppermute | solution.py:772
  120.7 5.0 %collective-permute-start.26 = (bf16[256,256]{1,0:T(8,128)(2,1)S(1)}, bf16[256,256]{1,0:T(8,128)(2,1)S(1)}, u32[]{:S(2)}, u32[]{:S(2)}) collective-permute-start(bf16[256,256]{1,0:T(8,128)(2,1)S(1)} %fusion.10), channel_id=1, source_target_pairs={{0,16},{1,9},{2,18},{3,11},{4,20},{5,13},{6,22},{7,15},{8,24},{9,1... | collective-permute-start | bytes 393224 | tf_op jit(solution)/shard_map/ppermute | solution.py:780
  125.8 5.8 %collective-permute-start.28 = (bf16[400,256]{1,0:T(8,128)(2,1)S(1)}, bf16[400,256]{1,0:T(8,128)(2,1)S(1)}, u32[]{:S(2)}, u32[]{:S(2)}) collective-permute-start(bf16[400,256]{1,0:T(8,128)(2,1)S(1)} %pad_maximum_fusion.2.refs_0_), channel_id=1, source_target_pairs={{0,8},{1,17},{2,10},{3,19},{4,12},{5,21},{6,14},{7,23},{8,0},{9,25... | collective-permute-start | bytes 614408 | tf_op jit(solution)/shard_map/ppermute | solution.py:780
  (11 other events, 44.9 us)
